TPU v7x, 256 devices: a whole 4x4x8 slice. The times are simulated.
256 devices in a mesh: section: 2 (over core), seq: 16 (over x, y), tensor: 8 (over z).
Axes of the slice: x: 4, y: 4, z: 8, core: 2. Of those that a mesh axis runs over, the one named last changes fastest.
Arguments:
- x_in: bfloat16 [2, 32768, 2048], P(None, 'seq', 'tensor'), may hold values from -6 to 6
- norm_gain: float32 [2, 2048], P('section', 'tensor'), may hold values from 0.5 to 1.5
- right_blocks: bfloat16 [2, 128, 256, 256], P('section', 'seq'), may hold values from -0.375 to 0.375
- left_blocks: bfloat16 [2, 256, 128, 128], P('section', 'seq'), may hold values from -0.5 to 0.5
- gate_first: bfloat16 [2, 32, 64, 64], P('section'), may hold values from -0.75 to 0.75
- gate_second: bfloat16 [2, 64, 32, 32], P('section'), may hold values from -1 to 1
- out_first: bfloat16 [2, 32, 64, 64], P('section'), may hold values from -0.75 to 0.75
- out_second: bfloat16 [2, 64, 32, 32], P('section'), may hold values from -1 to 1
- head: bfloat16 [2, 2048, 32768], P('section', None, ('seq', 'tensor')), may hold values from -0.375 to 0.375
- targets: int32 [2, 256], replicated, may hold values from 0 to 32767
Outputs:
- block_out: bfloat16 [2, 2, 32768, 2048], P('section', None, 'seq', 'tensor')
- aux_losses: float32 [2, 2, 256], P('section')
All inputs are finite; a program needn't handle non-finite values.
Results may differ from a plain program's by a relative error of at most 0.011.
Values may be sent and summed in bfloat16 or wider, within the bound.
No kernel may reach another device: no remote copies, remote signals or barrier semaphores. Data moves between devices by JAX's collectives and lax.ppermute only.
A program may use at most 128 MiB of HBM per device.

v0:
```python
import jax
import jax.numpy as jnp
from jax import lax
from jax.sharding import PartitionSpec as P

C1 = 32
C2 = 64
D = 2048
STRIDE = 128


epsilon = 1e-05


def from_behind(block, axis, distance):
    devices = range(lax.axis_size(axis))
    route = [(i - distance, i) for i in devices if i - distance in devices]
    return lax.ppermute(block, axis, route)


def first_map(factor_local):
    c_one, c_two, _ = factor_local.shape
    identity = jnp.eye(c_one, dtype=factor_local.dtype)
    dense_map = identity[None, :, :, None] * jnp.transpose(factor_local, (1, 0, 2))[:, :, None, :]
    return dense_map.reshape(c_two * c_one, c_one * c_two)


def second_map(factor_local, groups, c_one):
    k_dev = factor_local.shape[0]
    split_view = factor_local.reshape(k_dev, groups, c_one, groups, c_one)
    split_view = jnp.transpose(split_view, (1, 2, 0, 3, 4))
    identity = jnp.eye(k_dev, dtype=factor_local.dtype)
    dense_map = split_view[:, :, :, :, None, :] * identity[None, None, :, None, :, None]
    return dense_map.reshape(groups * c_one * k_dev, groups * k_dev * c_one)


def restore_rows(returned, groups, c_one, k_dev, token_count):
    ordered = returned.reshape(groups, c_one, k_dev, token_count)
    return jnp.transpose(ordered, (3, 1, 0, 2)).reshape(token_count, c_one * groups * k_dev)


def gate_channels(normed, one_map, two_map, groups, c_one, k_dev):
    token_count = normed.shape[0]
    first_mix = jnp.einsum("oc,tc->ot", one_map, normed, preferred_element_type=jnp.float32).astype(
        jnp.bfloat16
    )
    first_mix = first_mix.reshape(groups, k_dev * c_one, token_count)
    incoming = lax.all_to_all(first_mix, "tensor", split_axis=0, concat_axis=0, tiled=True)
    count_here = incoming.shape[2]
    flat_in = incoming.reshape(groups * k_dev * c_one, count_here)
    second_mix = jnp.dot(two_map, flat_in, preferred_element_type=jnp.float32).astype(jnp.bfloat16)
    returned = lax.all_to_all(
        second_mix.reshape(groups, c_one * k_dev, count_here),
        "tensor",
        split_axis=0,
        concat_axis=0,
        tiled=True,
    )
    return restore_rows(returned, groups, c_one, k_dev, token_count)


def out_channels(values, one_map, two_map, groups, c_one, k_dev):
    token_count = values.shape[0]
    first_mix = jnp.einsum("oc,tc->ot", one_map, values, preferred_element_type=jnp.float32).astype(
        jnp.bfloat16
    )
    first_mix = first_mix.reshape(groups, k_dev * c_one, token_count)
    incoming = lax.all_to_all(first_mix, "tensor", split_axis=0, concat_axis=0, tiled=True)
    count_here = incoming.shape[2]
    flat_in = incoming.reshape(groups * k_dev * c_one, count_here)
    second_mix = jnp.dot(two_map, flat_in, preferred_element_type=jnp.float32).astype(jnp.bfloat16)
    returned = lax.all_to_all(
        second_mix.reshape(groups, c_one * k_dev, count_here),
        "tensor",
        split_axis=0,
        concat_axis=0,
        tiled=True,
    )
    return restore_rows(returned, groups, c_one, k_dev, token_count)


def sequence_mix(normed, right_local, left_local, row_count, col_count):
    chan_count = normed.shape[1]
    seq_view = normed.reshape(row_count, col_count, chan_count)
    row_mix = jnp.einsum(
        "pjq,pqc->pjc", right_local, seq_view, preferred_element_type=jnp.float32
    ).astype(jnp.bfloat16)
    col_mix = jnp.einsum(
        "jip,pjc->ijc",
        left_local,
        lax.all_to_all(row_mix, "seq", split_axis=1, concat_axis=0, tiled=True),
        preferred_element_type=jnp.float32,
    ).astype(jnp.bfloat16)
    returned = lax.all_to_all(col_mix, "seq", split_axis=0, concat_axis=1, tiled=True)
    return returned.reshape(row_count * col_count, chan_count)


def body(
    x_in,
    norm_gain,
    right_blocks,
    left_blocks,
    gate_first,
    gate_second,
    out_first,
    out_second,
    head,
    targets,
):
    section_index = lax.axis_index("section")
    tensor_count = lax.axis_size("tensor")
    tensor_index = lax.axis_index("tensor")
    micro_count = x_in.shape[0]
    tok_dev = x_in.shape[1]
    chan_dev = x_in.shape[2]
    row_count = right_blocks.shape[1]
    col_count = right_blocks.shape[2]
    c_one = C1 // tensor_count
    k_dev = C2 // tensor_count
    norm_scale = norm_gain[0]
    right_local = right_blocks[0]
    left_local = left_blocks[0]
    gate_first_all = gate_first[0]
    gate_second_all = gate_second[0]
    out_first_all = out_first[0]
    out_second_all = out_second[0]
    gate_one = first_map(lax.dynamic_slice_in_dim(gate_first_all, tensor_index * c_one, c_one, 0))
    gate_two = second_map(
        lax.dynamic_slice_in_dim(gate_second_all, tensor_index * k_dev, k_dev, 0),
        tensor_count,
        c_one,
    )
    out_one = first_map(lax.dynamic_slice_in_dim(out_first_all, tensor_index * c_one, c_one, 0))
    out_two = second_map(
        lax.dynamic_slice_in_dim(out_second_all, tensor_index * k_dev, k_dev, 0),
        tensor_count,
        c_one,
    )
    head_local = head[0]
    vocab_dev = head_local.shape[1]
    vocab_offset = lax.axis_index(("seq", "tensor")) * vocab_dev
    handed = jnp.zeros((tok_dev, chan_dev), jnp.bfloat16)
    first_outputs, second_outputs, first_losses, second_losses = ([], [], [], [])
    for step_index in range(micro_count + 1):
        feed_rows = x_in[min(step_index, micro_count - 1)]
        x_val = jnp.where(section_index == 0, feed_rows, handed)
        labels = jnp.where(
            section_index == 0,
            targets[min(step_index, micro_count - 1)],
            targets[max(step_index - 1, 0)],
        )
        x_float = x_val.astype(jnp.float32)
        square_part = jnp.sum(x_float * x_float, axis=1)
        square_total = lax.psum(square_part, "tensor")
        row_scale = lax.rsqrt(square_total / D + epsilon)
        normed = (x_float * row_scale[:, None] * norm_scale[None, :]).astype(jnp.bfloat16)
        seq_out = sequence_mix(normed, right_local, left_local, row_count, col_count)
        gate_pre = gate_channels(normed, gate_one, gate_two, tensor_count, c_one, k_dev)
        gated_mix = (
            seq_out.astype(jnp.float32) * jax.nn.sigmoid(gate_pre.astype(jnp.float32))
        ).astype(jnp.bfloat16)
        out_pre = out_channels(gated_mix, out_one, out_two, tensor_count, c_one, k_dev)
        result = (x_float + out_pre.astype(jnp.float32)).astype(jnp.bfloat16)
        scored = result.reshape(row_count, col_count, chan_dev)[:, ::STRIDE, :].reshape(
            -1, chan_dev
        )
        wide_rows = lax.all_gather(scored, "tensor", axis=1, tiled=True)
        logits = jnp.dot(
            lax.all_gather(wide_rows, "seq", axis=0, tiled=True),
            head_local,
            preferred_element_type=jnp.float32,
        )
        exp_sums = jnp.sum(jnp.exp(logits), axis=1)
        vocab_ids = jnp.arange(vocab_dev, dtype=jnp.int32)[None, :] + vocab_offset
        is_target = vocab_ids == labels[:, None]
        target_part = jnp.sum(jnp.where(is_target, logits, 0.0), axis=1)
        exp_total, target_logit = lax.psum((exp_sums, target_part), ("seq", "tensor"))
        result, aux_loss = (result, jnp.log(exp_total) - target_logit)
        if step_index < micro_count:
            first_outputs.append(result)
            first_losses.append(aux_loss)
            handed = from_behind(result, "section", 1)
        if step_index > 0:
            second_outputs.append(result)
            second_losses.append(aux_loss)
    block_out = jnp.where(section_index == 0, jnp.stack(first_outputs), jnp.stack(second_outputs))[
        None
    ]
    aux_losses = jnp.where(section_index == 0, jnp.stack(first_losses), jnp.stack(second_losses))[
        None
    ]
    return (block_out, aux_losses)


def solution(mesh):
    in_specs = (
        P(None, "seq", "tensor"),
        P("section", "tensor"),
        P("section", "seq", None, None),
        P("section", "seq", None, None),
        P("section", None, None, None),
        P("section", None, None, None),
        P("section", None, None, None),
        P("section", None, None, None),
        P("section", None, ("seq", "tensor")),
        P(),
    )
    out_specs = (P("section", None, "seq", "tensor"), P("section", None, None))
    return jax.shard_map(body, mesh=mesh, in_specs=in_specs, out_specs=out_specs, check_vma=False)
```

profile of v0, /device:TPU:0, one launch (start us, length us, event | category | flops | bytes accessed | tf_op | source)
XLA Modules:
  0.0 1093.3 jit_solution(17827740526057056564)
XLA Ops:
  13.2 18.5 %psum.63 = f32[2048]{0:T(1024)S(1)} all-reduce(f32[2048]{0:T(1024)S(1)} %fusion.18), channel_id=1, replica_groups=mesh['section'=2,'seq'=16,'tensor'=8] {'tensor'}, use_global_device_ids=true, to_apply=%region_1.2 | all-reduce | flops 2048 | bytes 16384 | tf_op jit(solution)/shard_map/psum | solution.py:154
  43.1 19.9 %all-to-all-done.2 = bf16[8,32,2048]{2,1,0:T(8,128)(2,1)} async-done(((bf16[8,32,2048]{2,1,0:T(8,128)(2,1)}), bf16[8,32,2048]{2,1,0:T(8,128)(2,1)}, u32[]{:S(2)}, u32[]{:S(2)}) %all-to-all-start.2) | async-done | bytes 1048608 | tf_op jit(solution)/shard_map/all_to_all | solution.py:48
  93.4 17.9 %all-to-all-done.3 = bf16[8,32,2048]{2,1,0:T(8,128)(2,1)S(1)} async-done(((bf16[8,32,2048]{2,1,0:T(8,128)(2,1)}), bf16[8,32,2048]{2,1,0:T(8,128)(2,1)S(1)}, u32[]{:S(2)}, u32[]{:S(2)}) %all-to-all-start.3) | async-done | bytes 1048608 | tf_op jit(solution)/shard_map/all_to_all | solution.py:52
  126.0 11.8 %copy.100 = f32[8,16,16,256]{3,2,0,1:T(8,128)S(1)} copy(f32[8,16,16,256]{2,1,0,3:T(8,128)} %reshape.474) | data formatting | bytes 4194304 | tf_op jit(solution)/shard_map/div | solution.py:160
  148.0 22.8 %all-to-all-done.4 = bf16[8,32,2048]{2,1,0:T(8,128)(2,1)} async-done(((bf16[8,32,2048]{2,1,0:T(8,128)(2,1)}), bf16[8,32,2048]{2,1,0:T(8,128)(2,1)}, u32[]{:S(2)}, u32[]{:S(2)}) %all-to-all-start.4) | async-done | bytes 1048608 | tf_op jit(solution)/shard_map/all_to_all | solution.py:68
  172.6 28.1 %all_to_all.141 = bf16[8,32,2048]{2,1,0:T(8,128)(2,1)S(1)} all-to-all(bf16[8,32,2048]{2,1,0:T(8,128)(2,1)S(1)} %bitcast.255), channel_id=1, replica_groups=mesh['section'=2,'seq'=16,'tensor'=8] {'tensor'}, dimensions={0} | all-to-all | bytes 2097152 | tf_op jit(solution)/shard_map/all_to_all | solution.py:72
  210.7 14.9 %psum.64 = f32[2048]{0:T(1024)S(1)} all-reduce(f32[2048]{0:T(1024)S(1)} %get-tuple-element.22), channel_id=1, replica_groups=mesh['section'=2,'seq'=16,'tensor'=8] {'tensor'}, use_global_device_ids=true, to_apply=%region_3.4 | all-reduce | flops 2048 | bytes 16384 | tf_op jit(solution)/shard_map/psum | solution.py:154
  239.2 20.1 %all-to-all-done.8 = bf16[8,32,2048]{2,1,0:T(8,128)(2,1)} async-done(((bf16[8,32,2048]{2,1,0:T(8,128)(2,1)}), bf16[8,32,2048]{2,1,0:T(8,128)(2,1)}, u32[]{:S(2)}, u32[]{:S(2)}) %all-to-all-start.8) | async-done | bytes 1048608 | tf_op jit(solution)/shard_map/all_to_all | solution.py:48
  269.0 11.2 %all-to-all-done.6 = bf16[8,256,256]{2,0,1:T(8,128)(2,1)} async-done(((bf16[8,256,256]{2,0,1:T(8,128)(2,1)}), bf16[8,256,256]{2,0,1:T(8,128)(2,1)}, u32[]{:S(2)}, u32[]{:S(2)}) %all-to-all-start.6) | async-done | bytes 1048608 | tf_op jit(solution)/shard_map/all_to_all | solution.py:91
  290.2 17.9 %all-to-all-done.9 = bf16[8,32,2048]{2,1,0:T(8,128)(2,1)} async-done(((bf16[8,32,2048]{2,1,0:T(8,128)(2,1)}), bf16[8,32,2048]{2,1,0:T(8,128)(2,1)}, u32[]{:S(2)}, u32[]{:S(2)}) %all-to-all-start.9) | async-done | bytes 1048608 | tf_op jit(solution)/shard_map/all_to_all | solution.py:52
  326.5 12.9 %copy.112 = f32[8,16,16,256]{3,2,0,1:T(8,128)} copy(f32[8,16,16,256]{2,1,0,3:T(8,128)} %reshape.479) | data formatting | bytes 4194304 | tf_op jit(solution)/shard_map/div | solution.py:160
  342.2 28.1 %all_to_all.142 = bf16[8,32,2048]{2,1,0:T(8,128)(2,1)S(1)} all-to-all(bf16[8,32,2048]{2,1,0:T(8,128)(2,1)S(1)} %bitcast.258), channel_id=1, replica_groups=mesh['section'=2,'seq'=16,'tensor'=8] {'tensor'}, dimensions={0} | all-to-all | bytes 2097152 | tf_op jit(solution)/shard_map/all_to_all | solution.py:68
  370.8 27.4 %all_to_all.143 = bf16[8,32,2048]{2,1,0:T(8,128)(2,1)S(1)} all-to-all(bf16[8,32,2048]{2,1,0:T(8,128)(2,1)S(1)} %bitcast.260), channel_id=1, replica_groups=mesh['section'=2,'seq'=16,'tensor'=8] {'tensor'}, dimensions={0} | all-to-all | bytes 2097152 | tf_op jit(solution)/shard_map/all_to_all | solution.py:72
  404.9 15.0 %psum.65 = f32[2048]{0:T(1024)S(1)} all-reduce(f32[2048]{0:T(1024)S(1)} %get-tuple-element.20), channel_id=1, replica_groups=mesh['section'=2,'seq'=16,'tensor'=8] {'tensor'}, use_global_device_ids=true, to_apply=%region_5.6 | all-reduce | flops 2048 | bytes 16384 | tf_op jit(solution)/shard_map/psum | solution.py:154
  433.4 20.5 %all-to-all-done.14 = bf16[8,32,2048]{2,1,0:T(8,128)(2,1)} async-done(((bf16[8,32,2048]{2,1,0:T(8,128)(2,1)}), bf16[8,32,2048]{2,1,0:T(8,128)(2,1)}, u32[]{:S(2)}, u32[]{:S(2)}) %all-to-all-start.14) | async-done | bytes 1048608 | tf_op jit(solution)/shard_map/all_to_all | solution.py:48
  463.4 11.3 %all-to-all-done.12 = bf16[8,256,256]{2,0,1:T(8,128)(2,1)} async-done(((bf16[8,256,256]{2,0,1:T(8,128)(2,1)}), bf16[8,256,256]{2,0,1:T(8,128)(2,1)}, u32[]{:S(2)}, u32[]{:S(2)}) %all-to-all-start.12) | async-done | bytes 1048608 | tf_op jit(solution)/shard_map/all_to_all | solution.py:91
  484.7 18.1 %all-to-all-done.15 = bf16[8,32,2048]{2,1,0:T(8,128)(2,1)} async-done(((bf16[8,32,2048]{2,1,0:T(8,128)(2,1)}), bf16[8,32,2048]{2,1,0:T(8,128)(2,1)}, u32[]{:S(2)}, u32[]{:S(2)}) %all-to-all-start.15) | async-done | bytes 1048608 | tf_op jit(solution)/shard_map/all_to_all | solution.py:52
  521.2 12.9 %copy.122 = f32[8,16,16,256]{3,2,0,1:T(8,128)} copy(f32[8,16,16,256]{2,1,0,3:T(8,128)} %reshape.483) | data formatting | bytes 4194304 | tf_op jit(solution)/shard_map/div | solution.py:160
  552.8 32.3 %all_gather.18 = bf16[16,2048]{1,0:T(8,128)(2,1)} all-gather(bf16[16,256]{1,0:T(8,128)(2,1)S(1)} %reshape.465), channel_id=1, replica_groups=mesh['section'=2,'seq'=16,'tensor'=8] {'tensor'}, dimensions={1}, use_global_device_ids=true | all-gather | bytes 73728 | tf_op jit(solution)/shard_map/all_gather | solution.py:167
  597.1 35.3 %all_gather.20 = bf16[16,2048]{1,0:T(8,128)(2,1)} all-gather(bf16[16,256]{1,0:T(8,128)(2,1)S(1)} %reshape.467), channel_id=1, replica_groups=mesh['section'=2,'seq'=16,'tensor'=8] {'tensor'}, dimensions={1}, use_global_device_ids=true | all-gather | bytes 73728 | tf_op jit(solution)/shard_map/all_gather | solution.py:167
  640.1 26.5 %all_gather.22 = bf16[16,2048]{1,0:T(8,128)(2,1)} all-gather(bf16[16,256]{1,0:T(8,128)(2,1)S(1)} %reshape.469), channel_id=1, replica_groups=mesh['section'=2,'seq'=16,'tensor'=8] {'tensor'}, dimensions={1}, use_global_device_ids=true | all-gather | bytes 73728 | tf_op jit(solution)/shard_map/all_gather | solution.py:167
  671.5 11.2 %all-gather.6.cloned.1.call-done = bf16[256,2048]{1,0:T(8,128)(2,1)} async-done(((bf16[16,2048]{1,0:T(8,128)(2,1)}), bf16[256,2048]{1,0:T(8,128)(2,1)}) %all-gather.6.cloned.1.call-update) | async-done | bytes 1048592 | tf_op jit(solution)/shard_map/all_gather | solution.py:169
  691.3 40.9 %all-gather.8.cloned.1.call-done = bf16[256,2048]{1,0:T(8,128)(2,1)} async-done(((bf16[16,2048]{1,0:T(8,128)(2,1)}), bf16[256,2048]{1,0:T(8,128)(2,1)}) %all-gather.8.cloned.1.call-update) | async-done | bytes 1048592 | tf_op jit(solution)/shard_map/all_gather | solution.py:169
  734.0 351.8 %all-reduce = (f32[256]{0:T(256)S(1)}, f32[256]{0:T(256)S(1)}, f32[256]{0:T(256)S(1)}, f32[256]{0:T(256)S(1)}, f32[256]{0:T(256)S(1)}, /*index=5*/f32[256]{0:T(256)S(1)}) all-reduce(f32[256]{0:T(256)S(1)} %get-tuple-element.30, f32[256]{0:T(256)S(1)} %get-tuple-element.31, ...), channel_id=1, replica_groups=mesh['section'=2,'seq'=16,'tensor'=8] {'seq','tensor'}, use_global_device_ids=true, to_apply=%region_13.14 | all-reduce | flops 1536 | bytes 12288 | tf_op jit(solution)/shard_map/psum | solution.py:177
  (192 shorter events, 251.2 us)
Async XLA Ops:
  7.2 31.8 %copy-start = (bf16[1,8,256,256]{3,2,1,0:T(8,128)(2,1)S(1)}, bf16[1,8,256,256]{3,2,1,0:T(8,128)(2,1)}, u32[]{:S(2)}) copy-start(bf16[1,8,256,256]{3,2,1,0:T(8,128)(2,1)} %param.12) | copy-start | bytes 3145732
  33.3 29.7 %all-to-all-start.2 = ((bf16[8,32,2048]{2,1,0:T(8,128)(2,1)}), bf16[8,32,2048]{2,1,0:T(8,128)(2,1)}, u32[]{:S(2)}, u32[]{:S(2)}) async-start(bf16[8,32,2048]{2,1,0:T(8,128)(2,1)} %bitcast.21), calls=%async_computation.2 | async-start | bytes 2097152 | tf_op jit(solution)/shard_map/all_to_all | solution.py:48
  63.0 21.0 %all-to-all-start = ((bf16[8,256,256]{2,0,1:T(8,128)(2,1)}), bf16[8,256,256]{2,0,1:T(8,128)(2,1)}, u32[]{:S(2)}, u32[]{:S(2)}) async-start(bf16[8,256,256]{2,0,1:T(8,128)(2,1)} %copy.92), calls=%async_computation | async-start | bytes 2097152 | tf_op jit(solution)/shard_map/all_to_all | solution.py:91
  84.0 27.3 %all-to-all-start.3 = ((bf16[8,32,2048]{2,1,0:T(8,128)(2,1)}), bf16[8,32,2048]{2,1,0:T(8,128)(2,1)S(1)}, u32[]{:S(2)}, u32[]{:S(2)}) async-start(bf16[8,32,2048]{2,1,0:T(8,128)(2,1)} %bitcast.247), calls=%async_computation.3 | async-start | bytes 2097152 | tf_op jit(solution)/shard_map/all_to_all | solution.py:52
  111.3 26.5 %all-to-all-start.1 = ((bf16[128,16,256]{2,1,0:T(8,128)(2,1)}), bf16[128,16,256]{2,1,0:T(8,128)(2,1)}, u32[]{:S(2)}, u32[]{:S(2)}) async-start(bf16[128,16,256]{2,1,0:T(8,128)(2,1)} %copy.96), calls=%async_computation.1 | async-start | bytes 2097152 | tf_op jit(solution)/shard_map/all_to_all | solution.py:94
  140.9 30.0 %all-to-all-start.4 = ((bf16[8,32,2048]{2,1,0:T(8,128)(2,1)}), bf16[8,32,2048]{2,1,0:T(8,128)(2,1)}, u32[]{:S(2)}, u32[]{:S(2)}) async-start(bf16[8,32,2048]{2,1,0:T(8,128)(2,1)} %bitcast.250), calls=%async_computation.4 | async-start | bytes 2097152 | tf_op jit(solution)/shard_map/all_to_all | solution.py:68
  203.5 4.6 collective-permute-start
  229.6 29.7 %all-to-all-start.8 = ((bf16[8,32,2048]{2,1,0:T(8,128)(2,1)}), bf16[8,32,2048]{2,1,0:T(8,128)(2,1)}, u32[]{:S(2)}, u32[]{:S(2)}) async-start(bf16[8,32,2048]{2,1,0:T(8,128)(2,1)} %bitcast.251), calls=%async_computation.8 | async-start | bytes 2097152 | tf_op jit(solution)/shard_map/all_to_all | solution.py:48
  259.3 20.8 %all-to-all-start.6 = ((bf16[8,256,256]{2,0,1:T(8,128)(2,1)}), bf16[8,256,256]{2,0,1:T(8,128)(2,1)}, u32[]{:S(2)}, u32[]{:S(2)}) async-start(bf16[8,256,256]{2,0,1:T(8,128)(2,1)} %copy.106), calls=%async_computation.6 | async-start | bytes 2097152 | tf_op jit(solution)/shard_map/all_to_all | solution.py:91
  280.2 27.9 %all-to-all-start.9 = ((bf16[8,32,2048]{2,1,0:T(8,128)(2,1)}), bf16[8,32,2048]{2,1,0:T(8,128)(2,1)}, u32[]{:S(2)}, u32[]{:S(2)}) async-start(bf16[8,32,2048]{2,1,0:T(8,128)(2,1)} %bitcast.248), calls=%async_computation.9 | async-start | bytes 2097152 | tf_op jit(solution)/shard_map/all_to_all | solution.py:52
  308.1 31.3 %all-to-all-start.7 = ((bf16[128,16,256]{2,1,0:T(8,128)(2,1)}), bf16[128,16,256]{2,1,0:T(8,128)(2,1)}, u32[]{:S(2)}, u32[]{:S(2)}) async-start(bf16[128,16,256]{2,1,0:T(8,128)(2,1)} %copy.110), calls=%async_computation.7 | async-start | bytes 2097152 | tf_op jit(solution)/shard_map/all_to_all | solution.py:94
  399.9 3.6 collective-permute-start.1
  423.8 30.1 %all-to-all-start.14 = ((bf16[8,32,2048]{2,1,0:T(8,128)(2,1)}), bf16[8,32,2048]{2,1,0:T(8,128)(2,1)}, u32[]{:S(2)}, u32[]{:S(2)}) async-start(bf16[8,32,2048]{2,1,0:T(8,128)(2,1)} %bitcast.249), calls=%async_computation.14 | async-start | bytes 2097152 | tf_op jit(solution)/shard_map/all_to_all | solution.py:48
  453.9 20.8 %all-to-all-start.12 = ((bf16[8,256,256]{2,0,1:T(8,128)(2,1)}), bf16[8,256,256]{2,0,1:T(8,128)(2,1)}, u32[]{:S(2)}, u32[]{:S(2)}) async-start(bf16[8,256,256]{2,0,1:T(8,128)(2,1)} %copy.116), calls=%async_computation.12 | async-start | bytes 2097152 | tf_op jit(solution)/shard_map/all_to_all | solution.py:91
  474.7 28.1 %all-to-all-start.15 = ((bf16[8,32,2048]{2,1,0:T(8,128)(2,1)}), bf16[8,32,2048]{2,1,0:T(8,128)(2,1)}, u32[]{:S(2)}, u32[]{:S(2)}) async-start(bf16[8,32,2048]{2,1,0:T(8,128)(2,1)} %bitcast.246), calls=%async_computation.15 | async-start | bytes 2097152 | tf_op jit(solution)/shard_map/all_to_all | solution.py:52
  502.8 31.3 %all-to-all-start.13 = ((bf16[128,16,256]{2,1,0:T(8,128)(2,1)}), bf16[128,16,256]{2,1,0:T(8,128)(2,1)}, u32[]{:S(2)}, u32[]{:S(2)}) async-start(bf16[128,16,256]{2,1,0:T(8,128)(2,1)} %copy.120), calls=%async_computation.13 | async-start | bytes 2097152 | tf_op jit(solution)/shard_map/all_to_all | solution.py:94
  537.8 47.2 %all-to-all-start.16 = ((bf16[8,32,2048]{2,1,0:T(8,128)(2,1)}), bf16[8,32,2048]{2,1,0:T(8,128)(2,1)}, u32[]{:S(2)}, u32[]{:S(2)}) async-start(bf16[8,32,2048]{2,1,0:T(8,128)(2,1)} %bitcast.244), calls=%async_computation.16 | async-start | bytes 2097152 | tf_op jit(solution)/shard_map/all_to_all | solution.py:68
  542.1 127.1 %all-gather.4.cloned.1.call-start = ((), (), s32[]{:S(2)}) async-start(), calls=%async_computation.18 | async-start | bytes 1114112 | tf_op jit(solution)/shard_map/all_gather | solution.py:169
  587.7 44.8 %all-to-all-start.17 = ((bf16[8,32,2048]{2,1,0:T(8,128)(2,1)}), bf16[8,32,2048]{2,1,0:T(8,128)(2,1)}, u32[]{:S(2)}, u32[]{:S(2)}) async-start(bf16[8,32,2048]{2,1,0:T(8,128)(2,1)} %bitcast.245), calls=%async_computation.17 | async-start | bytes 2097152 | tf_op jit(solution)/shard_map/all_to_all | solution.py:72
  593.5 89.2 %all-gather.6.cloned.1.call-start = ((), (), s32[]{:S(2)}) async-start(), calls=%async_computation.19 | async-start | bytes 1114112 | tf_op jit(solution)/shard_map/all_gather | solution.py:169
  632.5 99.7 %all-gather.8.cloned.1.call-start = ((), (), s32[]{:S(2)}) async-start(), calls=%async_computation.20 | async-start | bytes 1114112 | tf_op jit(solution)/shard_map/all_gather | solution.py:169
  636.5 30.1 %copy-start.27 = (s32[2,256]{1,0:T(2,128)S(1)}, s32[2,256]{1,0:T(2,128)}, u32[]{:S(2)}) copy-start(s32[2,256]{1,0:T(2,128)} %param.19) | copy-start | bytes 6148
  687.2 44.9 %copy-start.17 = (bf16[1,2048,256]{2,1,0:T(8,128)(2,1)S(1)}, bf16[1,2048,256]{2,1,0:T(8,128)(2,1)}, u32[]{:S(2)}) copy-start(bf16[1,2048,256]{2,1,0:T(8,128)(2,1)} %param.18) | copy-start | bytes 3145732
  687.2 44.9 %copy-start.23 = (f32[256,256]{0,1:T(8,128)S(1)}, f32[256,256]{0,1:T(8,128)}, u32[]{:S(2)}) copy-start(f32[256,256]{0,1:T(8,128)} %fusion.34) | copy-start | bytes 786436
  (24 other events, 221.0 us)
Sparse Core Ops, SparseCore 0:
  585.2 47.9 all-gather.3
  635.6 47.0 all-gather.5
  685.1 47.0 all-gather.7
where the time goes:
time: 1100 us; the launch traced here: 1090 us
  blocking collectives  578 us (53%)
  waiting for transfers between devices  219 us (20%)
  local copies, waits for them, and re-layouts  132 us (12%)
  starting transfers between devices  78 us (7%)
  matrix products  38.8 us (4%)
  other arithmetic  32.9 us (3%)
  between operations  15 us (1%)
    psum x1, blocking collectives, body(): lax.psum((exp_sums, target_part), ('seq', 'tensor'))  352 us
    all_gather x3, blocking collectives, body(): wide_rows = lax.all_gather(scored, 'tensor', axis=1, tiled=True)  94.1 us
    div x9, local copies, waits for them, and re-layouts, body(): jax.nn.sigmoid(gate_pre.astype(jnp.float32))  70.5 us
    all_to_all x3, waiting for transfers between devices, gate_channels(): lax.all_to_all(first_mix, 'tensor', split_axis=0, concat_axis=0, tiled=True)  60.5 us
    all_to_all x2, blocking collectives, out_channels(): lax.all_to_all(second_mix.reshape(groups, c_one * k_dev, count_here), 'te...  55.5 us
    all_to_all x3, waiting for transfers between devices, gate_channels(): lax.all_to_all(second_mix.reshape(groups, c_one * k_dev, count_here), 'te...  53.8 us
    all_gather x3, waiting for transfers between devices, body(): lax.all_gather(wide_rows, 'seq', axis=0, tiled=True)  52.1 us
    psum x3, blocking collectives, body(): square_total = lax.psum(square_part, 'tensor')  48.4 us
  transfers between devices with their start and end apart: 20, of which 13 were waited for; matrix products, arithmetic and copies ran while one was open for 15% of the time, Pallas kernels for 0%

commit v1 on v0

v1 whole, which is shorter than its diff:
```python
import jax
import jax.numpy as jnp
from jax import lax
from jax.experimental import pallas as pl
from jax.experimental.pallas import tpu as pltpu
from jax.sharding import PartitionSpec as P

C1 = 32
C2 = 64
D = 2048
STRIDE = 128
EPS = 1e-05
BLK = 256
VMEM_LIMIT = 48 * 1024 * 1024


def params():
    return pltpu.CompilerParams(vmem_limit_bytes=VMEM_LIMIT)


def whole(shape):
    return pl.BlockSpec(shape, lambda *_: (0,) * len(shape))


def gather_by_exchange(block, axis):
    count = lax.axis_size(axis)
    copies = jnp.broadcast_to(block[None], (count,) + block.shape)
    return lax.all_to_all(copies, axis, split_axis=0, concat_axis=0, tiled=True)


def channel_map(first_t, second_rows, n_blk):
    def kernel(first_ref, second_ref, out_ref):
        first = first_ref[...].astype(jnp.float32)
        second = second_ref[...].astype(jnp.float32)
        out_ref[0] = (first * second[:, None, :]).astype(jnp.bfloat16).reshape(D, BLK)

    return pl.pallas_call(
        kernel,
        grid=(n_blk,),
        in_specs=[whole((C1, C2, BLK)), pl.BlockSpec((C1, BLK), lambda n: (0, n))],
        out_specs=pl.BlockSpec((1, D, BLK), lambda n: (n, 0, 0)),
        out_shape=jax.ShapeDtypeStruct((n_blk, D, BLK), jnp.bfloat16),
        compiler_params=params(),
    )(first_t, second_rows)


def left_map(left_rows, j_count):
    rows, p_count = left_rows.shape
    cols = p_count * j_count

    def kernel(left_ref, out_ref):
        lane = lax.broadcasted_iota(jnp.int32, (p_count, cols), 1) // j_count
        spread = (lane == lax.broadcasted_iota(jnp.int32, (p_count, cols), 0)).astype(jnp.bfloat16)
        wide = jnp.dot(left_ref[...], spread, preferred_element_type=jnp.float32)
        same = (lax.broadcasted_iota(jnp.int32, (BLK, cols), 0) % j_count) == (
            lax.broadcasted_iota(jnp.int32, (BLK, cols), 1) % j_count
        )
        out_ref[...] = jnp.where(same, wide, 0.0).astype(jnp.bfloat16)

    return pl.pallas_call(
        kernel,
        grid=(rows // BLK,),
        in_specs=[pl.BlockSpec((BLK, p_count), lambda n: (n, 0))],
        out_specs=pl.BlockSpec((BLK, cols), lambda n: (n, 0)),
        out_shape=jax.ShapeDtypeStruct((rows, cols), jnp.bfloat16),
        compiler_params=params(),
    )(left_rows)


def norm_and_right(x_ref, gain_ref, right_ref, normed_ref, mix_ref):
    n_blk, tokens, _ = x_ref.shape
    total = jnp.zeros((tokens, 1), jnp.float32)
    for n in range(n_blk):
        xf = x_ref[n].astype(jnp.float32)
        total = total + jnp.sum(xf * xf, axis=1, keepdims=True)
    scale = lax.rsqrt(total / D + EPS)
    groups, _, width, _ = mix_ref.shape
    for n in range(n_blk):
        normed = (x_ref[n].astype(jnp.float32) * scale * gain_ref[n]).astype(jnp.bfloat16)
        normed_ref[n] = normed
        mix = jnp.dot(right_ref[...], normed, preferred_element_type=jnp.float32)
        mix_ref[:, n] = mix.astype(jnp.bfloat16).reshape(groups, width, BLK)


def first_stage(x_tok, gain, right_row, groups):
    n_blk, tokens, _ = x_tok.shape
    return pl.pallas_call(
        norm_and_right,
        out_shape=(
            jax.ShapeDtypeStruct(x_tok.shape, jnp.bfloat16),
            jax.ShapeDtypeStruct((groups, n_blk, tokens // groups, BLK), jnp.bfloat16),
        ),
        compiler_params=params(),
    )(x_tok, gain, right_row)


def gate_stage(normed, gate_map):
    n_blk, tokens, _ = normed.shape

    def kernel(normed_ref, map_ref, out_ref):
        acc = jnp.zeros((tokens, BLK), jnp.float32)
        for z in range(n_blk):
            acc = acc + jnp.dot(
                normed_ref[z], map_ref[0, z * BLK : (z + 1) * BLK], preferred_element_type=jnp.float32
            )
        out_ref[0] = jax.nn.sigmoid(acc.astype(jnp.bfloat16).astype(jnp.float32))

    return pl.pallas_call(
        kernel,
        grid=(n_blk,),
        in_specs=[whole(normed.shape), pl.BlockSpec((1, D, BLK), lambda n: (n, 0, 0))],
        out_specs=pl.BlockSpec((1, tokens, BLK), lambda n: (n, 0, 0)),
        out_shape=jax.ShapeDtypeStruct(normed.shape, jnp.float32),
        compiler_params=params(),
    )(normed, gate_map)


def left_stage(left_dense, mix):
    rows, cols = left_dense.shape

    def kernel(left_ref, mix_ref, out_ref):
        out_ref[...] = jnp.dot(
            left_ref[...], mix_ref[...], preferred_element_type=jnp.float32
        ).astype(jnp.bfloat16)

    return pl.pallas_call(
        kernel,
        grid=(rows // BLK,),
        in_specs=[pl.BlockSpec((BLK, cols), lambda n: (n, 0)), whole(mix.shape)],
        out_specs=pl.BlockSpec((BLK, BLK), lambda n: (n, 0)),
        out_shape=jax.ShapeDtypeStruct((rows, BLK), jnp.bfloat16),
        compiler_params=params(),
    )(left_dense, mix)


def out_stage(seq_out, gate, x_tok, out_map, following=None):
    groups, n_blk, width, _ = seq_out.shape
    tokens = groups * width

    def kernel(seq_ref, gate_ref, x_ref, map_ref, *refs):
        if following is None:
            res_ref, gated_ref = refs
        else:
            gain_ref, right_ref, res_ref, normed_ref, mix_ref, gated_ref = refs
        n = pl.program_id(0)

        @pl.when(n == 0)
        def _():
            for z in range(n_blk):
                seq = seq_ref[:, z].reshape(tokens, BLK).astype(jnp.float32)
                gated_ref[z] = (seq * gate_ref[z]).astype(jnp.bfloat16)

        acc = jnp.zeros((tokens, BLK), jnp.float32)
        for z in range(n_blk):
            acc = acc + jnp.dot(
                gated_ref[z], map_ref[0, z * BLK : (z + 1) * BLK], preferred_element_type=jnp.float32
            )
        mixed = acc.astype(jnp.bfloat16).astype(jnp.float32)
        res_ref[n] = (x_ref[n].astype(jnp.float32) + mixed).astype(jnp.bfloat16)
        if following is not None:

            @pl.when(n == n_blk - 1)
            def _():
                norm_and_right(res_ref, gain_ref, right_ref, normed_ref, mix_ref)

    tok_shape = (n_blk, tokens, BLK)
    in_specs = [
        whole(seq_out.shape),
        whole(tok_shape),
        whole(tok_shape),
        pl.BlockSpec((1, D, BLK), lambda n: (n, 0, 0)),
    ]
    out_shape = [jax.ShapeDtypeStruct(tok_shape, jnp.bfloat16)]
    operands = [seq_out, gate, x_tok, out_map]
    if following is not None:
        gain, right_row = following
        operands += [gain, right_row]
        in_specs += [whole(gain.shape), whole(right_row.shape)]
        out_shape += [
            jax.ShapeDtypeStruct(tok_shape, jnp.bfloat16),
            jax.ShapeDtypeStruct(seq_out.shape, jnp.bfloat16),
        ]
    return pl.pallas_call(
        kernel,
        grid=(n_blk,),
        in_specs=in_specs,
        out_specs=[whole(s.shape) for s in out_shape],
        out_shape=out_shape,
        scratch_shapes=[pltpu.VMEM(tok_shape, jnp.bfloat16)],
        compiler_params=params(),
    )(*operands)


def body(
    x_in,
    norm_gain,
    right_blocks,
    left_blocks,
    gate_first,
    gate_second,
    out_first,
    out_second,
    head,
    targets,
):
    section = lax.axis_index("section")
    tensor_index = lax.axis_index("tensor")
    seq_count = lax.axis_size("seq")
    n_blk = lax.axis_size("tensor")
    everyone = ("seq", "tensor")
    swap = [(0, 1), (1, 0)]
    tokens = right_blocks.shape[2]
    j_dev = left_blocks.shape[1]
    p_count = left_blocks.shape[2]

    x_own = lax.dynamic_index_in_dim(x_in, section, 0, keepdims=False)
    x_tok = lax.all_to_all(
        x_own.reshape(n_blk, tokens, BLK), "tensor", split_axis=0, concat_axis=0, tiled=True
    )

    gains = gather_by_exchange(norm_gain, ("section", "tensor")).reshape(2, n_blk, 1, BLK)

    def spread_first(factor):
        return jnp.tile(jnp.transpose(factor[0], (0, 2, 1)), (1, 1, BLK // C2))

    def rows_second(factor):
        return jnp.transpose(factor[0], (2, 1, 0)).reshape(C1, D)

    own = (
        lax.dynamic_index_in_dim(right_blocks[0], tensor_index, 0, keepdims=False),
        jnp.transpose(left_blocks[0], (1, 0, 2)).reshape(p_count * j_dev, p_count),
        spread_first(gate_first),
        rows_second(gate_second),
        spread_first(out_first),
        rows_second(out_second),
    )
    other = tuple(lax.ppermute(w, "section", swap) for w in own)
    weights = []
    for b in range(2):
        right_row, left_rows, g1, g2, o1, o2 = (
            jnp.where(section == b, a, c) for a, c in zip(own, other)
        )
        weights.append(
            (
                right_row,
                left_map(left_rows, j_dev),
                channel_map(g1, g2, n_blk),
                channel_map(o1, o2, n_blk),
            )
        )

    head_local = head[0]
    vocab_dev = head_local.shape[1]
    vocab_offset = lax.axis_index(everyone) * vocab_dev

    normed, mix = first_stage(x_tok, gains[0], weights[0][0], seq_count)
    current = x_tok
    results, rows = [], []
    for b in range(2):
        _, left_dense, gate_map, out_map = weights[b]
        mix_cols = lax.all_to_all(
            mix.reshape(seq_count * n_blk, j_dev, BLK),
            everyone,
            split_axis=0,
            concat_axis=0,
            tiled=True,
        )
        gate = gate_stage(normed, gate_map)
        col_out = left_stage(left_dense, mix_cols.reshape(p_count * j_dev, BLK))
        seq_out = lax.all_to_all(
            col_out.reshape(p_count, j_dev, BLK), everyone, split_axis=0, concat_axis=0, tiled=True
        ).reshape(seq_count, n_blk, j_dev, BLK)
        if b == 0:
            current, normed, mix = out_stage(
                seq_out, gate, current, out_map, (gains[1], weights[1][0])
            )
        else:
            (current,) = out_stage(seq_out, gate, current, out_map)
        scored = jnp.transpose(current[:, ::STRIDE], (1, 0, 2)).reshape(-1, D)
        near = gather_by_exchange(scored, "tensor").reshape(-1, D)
        rows.append(gather_by_exchange(near, "seq").reshape(-1, D))
        results.append(
            lax.all_to_all(current, "tensor", split_axis=0, concat_axis=0, tiled=True).reshape(
                n_blk * tokens, BLK
            )
        )

    first = section == 0
    got_rows = lax.ppermute(jnp.where(first, rows[1], rows[0]), "section", swap)
    own_rows = jnp.where(first, rows[0], rows[1])
    scored_all = jnp.where(
        first, jnp.concatenate([own_rows, got_rows]), jnp.concatenate([got_rows, own_rows])
    )
    logits = jnp.dot(scored_all, head_local, preferred_element_type=jnp.float32)
    exp_sums = jnp.sum(jnp.exp(logits), axis=1)
    vocab_ids = jnp.arange(vocab_dev, dtype=jnp.int32)[None, :] + vocab_offset
    is_target = vocab_ids == targets.reshape(-1)[:, None]
    target_part = jnp.sum(jnp.where(is_target, logits, 0.0), axis=1)
    parts = jnp.stack([exp_sums, target_part]).reshape(-1, 128)
    totals = jnp.sum(gather_by_exchange(parts, everyone), axis=0).reshape(2, -1)
    aux_losses = (jnp.log(totals[0]) - totals[1]).reshape(1, 2, -1)

    got = lax.ppermute(jnp.where(first, results[1], results[0]), "section", swap)
    kept = jnp.where(first, results[0], results[1])
    block_out = jnp.where(first, jnp.stack([kept, got]), jnp.stack([got, kept]))[None]
    return (block_out, aux_losses)


def solution(mesh):
    in_specs = (
        P(None, "seq", "tensor"),
        P("section", "tensor"),
        P("section", "seq", None, None),
        P("section", "seq", None, None),
        P("section", None, None, None),
        P("section", None, None, None),
        P("section", None, None, None),
        P("section", None, None, None),
        P("section", None, ("seq", "tensor")),
        P(),
    )
    out_specs = (P("section", None, "seq", "tensor"), P("section", None, None))
    return jax.shard_map(body, mesh=mesh, in_specs=in_specs, out_specs=out_specs, check_vma=False)
```

time: 1100 us -> 425 us (0.39)
  the two profiles are of different devices: /device:TPU:0 before, /device:TPU:1 now
where the time goes in v1:
time: 425 us; the launch traced here: 423 us
  waiting for transfers between devices  170 us (40%)
  starting transfers between devices  90.4 us (21%)
  Pallas kernels  84.4 us (20%)
  local copies, waits for them, and re-layouts  31.9 us (8%)
  blocking collectives  28.1 us (7%)
  other arithmetic  15.1 us (4%)
    all_to_all x2, waiting for transfers between devices, body(): lax.all_to_all(mix.reshape(seq_count * n_blk, j_dev, BLK), everyone, spli...  50.4 us
    all_to_all x2, waiting for transfers between devices, body(): lax.all_to_all(current, 'tensor', split_axis=0, concat_axis=0, tiled=True)  41.3 us
    all_to_all x2, waiting for transfers between devices, body(): lax.all_to_all(col_out.reshape(p_count, j_dev, BLK), everyone, split_axis...  28.5 us
    all_to_all x2, blocking collectives, gather_by_exchange(): return lax.all_to_all(copies, axis, split_axis=0, concat_axis=0, tiled=True)  28.1 us
    all_to_all x1, waiting for transfers between devices, body(): lax.all_to_all(x_own.reshape(n_blk, tokens, BLK), 'tensor', split_axis=0,...  25.4 us
    all_to_all x4, starting transfers between devices, gather_by_exchange(): return lax.all_to_all(copies, axis, split_axis=0, concat_axis=0, tiled=True)  25.2 us
    all_to_all x2, starting transfers between devices, body(): lax.all_to_all(mix.reshape(seq_count * n_blk, j_dev, BLK), everyone, spli...  22.3 us
    all_to_all x4, waiting for transfers between devices, gather_by_exchange(): return lax.all_to_all(copies, axis, split_axis=0, concat_axis=0, tiled=True)  21.3 us
  transfers between devices with their start and end apart: 19, of which 11 were waited for; matrix products, arithmetic and copies ran while one was open for 9% of the time, Pallas kernels for 15%

profile of v1, /device:TPU:1, one launch (start us, length us, event | category | flops | bytes accessed | tf_op | source)
XLA Modules:
  0.0 423.2 jit_solution(2691373008208366701)
XLA Ops:
  2.1 10.0 %all-to-all-start.1 = ((f32[16,1,256]{2,1,0:T(1,128)}), f32[16,1,256]{2,1,0:T(1,128)S(1)}, u32[]{:S(2)}, u32[]{:S(2)}) async-start(f32[16,1,256]{2,1,0:T(1,128)} %broadcast_in_dim.50), calls=%async_computation.1 | async-start | bytes 32768 | tf_op jit(solution)/shard_map/all_to_all | solution.py:28
  26.4 25.4 %all-to-all-done.x_ref = bf16[8,256,256]{2,1,0:T(8,128)(2,1)S(1)} async-done(((bf16[8,256,256]{2,1,0:T(8,128)(2,1)}), bf16[8,256,256]{2,1,0:T(8,128)(2,1)S(1)}, u32[]{:S(2)}, u32[]{:S(2)}) %all-to-all-start) | async-done | bytes 1048608 | tf_op jit(solution)/shard_map/all_to_all | solution.py:217
  54.6 8.9 %all-to-all-start.2 = ((bf16[128,16,256]{2,1,0:T(8,128)(2,1)}), bf16[128,16,256]{2,1,0:T(8,128)(2,1)S(1)}, u32[]{:S(2)}, u32[]{:S(2)}) async-start(bf16[128,16,256]{2,1,0:T(8,128)(2,1)} %bitcast.6), calls=%async_computation.2 | async-start | bytes 2097152 | tf_op jit(solution)/shard_map/all_to_all | solution.py:261
  67.1 6.1 %shard_map.113.left_ref = bf16[2048,2048]{1,0:T(8,128)(2,1)} custom-call(bf16[2048,128]{1,0:T(8,128)(2,1)S(1)} %get-tuple-element.22.left_ref), custom_call_target="tpu_custom_call" | custom-call | tf_op jit(solution)/shard_map/pallas_call | solution.py:60
  73.2 20.9 %all-to-all-done.2 = bf16[128,16,256]{2,1,0:T(8,128)(2,1)S(1)} async-done(((bf16[128,16,256]{2,1,0:T(8,128)(2,1)}), bf16[128,16,256]{2,1,0:T(8,128)(2,1)S(1)}, u32[]{:S(2)}, u32[]{:S(2)}) %all-to-all-start.2) | async-done | bytes 1048608 | tf_op jit(solution)/shard_map/all_to_all | solution.py:261
  94.0 8.3 %shard_map.115 = bf16[2048,256]{1,0:T(8,128)(2,1)} custom-call(bf16[2048,2048]{1,0:T(8,128)(2,1)} %shard_map.113.left_ref, bf16[2048,256]{1,0:T(8,128)(2,1)S(1)} %bitcast.52), custom_call_target="tpu_custom_call" | custom-call | tf_op jit(solution)/shard_map/pallas_call | solution.py:126
  102.3 7.4 %all-to-all-start.3 = ((bf16[128,16,256]{2,1,0:T(8,128)(2,1)}), bf16[128,16,256]{2,1,0:T(8,128)(2,1)}, u32[]{:S(2)}, u32[]{:S(2)}) async-start(bf16[128,16,256]{2,1,0:T(8,128)(2,1)} %bitcast.8), calls=%async_computation.3 | async-start | bytes 2097152 | tf_op jit(solution)/shard_map/all_to_all | solution.py:270
  143.7 7.4 %shard_map.117.gate_ref = f32[8,256,256]{2,1,0:T(8,128)S(1)} custom-call(bf16[8,256,256]{2,1,0:T(8,128)(2,1)S(1)} %copy-done.9, bf16[8,2048,256]{2,1,0:T(8,128)(2,1)} %shard_map.116.map_ref), custom_call_target="tpu_custom_call" | custom-call | tf_op jit(solution)/shard_map/pallas_call | solution.py:108
  152.5 10.4 %shard_map.119 = (bf16[8,256,256]{2,1,0:T(8,128)(2,1)}, bf16[8,256,256]{2,1,0:T(8,128)(2,1)S(1)}, bf16[16,8,16,256]{3,2,1,0:T(8,128)(2,1)S(1)}) custom-call(bf16[16,8,16,256]{3,2,1,0:T(8,128)(2,1)} %bitcast.9.seq_ref, f32[8,256,256]{2,1,0:T(8,128)} %copy-done.2, bf16[8,256,256]{2,1,0:T(8,128)(2,1)S(1)} %all-to-all-done.x_ref, ...), custom_call_target="tpu_custom_call" | custom-call | tf_op jit(solution)/shard_map/pallas_call | solution.py:183
  164.8 13.5 %all-to-all-start.5 = ((bf16[128,16,256]{2,1,0:T(8,128)(2,1)}), bf16[128,16,256]{2,1,0:T(8,128)(2,1)S(1)}, u32[]{:S(2)}, u32[]{:S(2)}) async-start(bf16[128,16,256]{2,1,0:T(8,128)(2,1)} %bitcast.56), calls=%async_computation.5 | async-start | bytes 2097152 | tf_op jit(solution)/shard_map/all_to_all | solution.py:261
  179.6 29.6 %all-to-all-done.5 = bf16[128,16,256]{2,1,0:T(8,128)(2,1)S(1)} async-done(((bf16[128,16,256]{2,1,0:T(8,128)(2,1)}), bf16[128,16,256]{2,1,0:T(8,128)(2,1)S(1)}, u32[]{:S(2)}, u32[]{:S(2)}) %all-to-all-start.5) | async-done | bytes 1048608 | tf_op jit(solution)/shard_map/all_to_all | solution.py:261
  214.2 6.1 %shard_map.120.left_ref = bf16[2048,2048]{1,0:T(8,128)(2,1)} custom-call(bf16[2048,128]{1,0:T(8,128)(2,1)S(1)} %copy-done.6), custom_call_target="tpu_custom_call" | custom-call | tf_op jit(solution)/shard_map/pallas_call | solution.py:60
  220.3 7.4 %shard_map.121 = bf16[2048,256]{1,0:T(8,128)(2,1)S(1)} custom-call(bf16[2048,2048]{1,0:T(8,128)(2,1)} %shard_map.120.left_ref, bf16[2048,256]{1,0:T(8,128)(2,1)S(1)} %bitcast.53), custom_call_target="tpu_custom_call" | custom-call | tf_op jit(solution)/shard_map/pallas_call | solution.py:126
  228.7 9.1 %all-to-all-start.6 = ((bf16[128,16,256]{2,1,0:T(8,128)(2,1)}), bf16[128,16,256]{2,1,0:T(8,128)(2,1)S(1)}, u32[]{:S(2)}, u32[]{:S(2)}) async-start(bf16[128,16,256]{2,1,0:T(8,128)(2,1)} %bitcast.54), calls=%async_computation.6 | async-start | bytes 2097152 | tf_op jit(solution)/shard_map/all_to_all | solution.py:270
  237.8 28.5 %all-to-all-done.6 = bf16[128,16,256]{2,1,0:T(8,128)(2,1)S(1)} async-done(((bf16[128,16,256]{2,1,0:T(8,128)(2,1)}), bf16[128,16,256]{2,1,0:T(8,128)(2,1)S(1)}, u32[]{:S(2)}, u32[]{:S(2)}) %all-to-all-start.6) | async-done | bytes 1048608 | tf_op jit(solution)/shard_map/all_to_all | solution.py:270
  283.3 7.5 %shard_map.123.gate_ref = f32[8,256,256]{2,1,0:T(8,128)S(1)} custom-call(bf16[8,256,256]{2,1,0:T(8,128)(2,1)S(1)} %copy-done.11, bf16[8,2048,256]{2,1,0:T(8,128)(2,1)} %shard_map.122.map_ref), custom_call_target="tpu_custom_call" | custom-call | tf_op jit(solution)/shard_map/pallas_call | solution.py:108
  290.8 8.9 %shard_map.125 = bf16[8,256,256]{2,1,0:T(8,128)(2,1)} custom-call(bf16[16,8,16,256]{3,2,1,0:T(8,128)(2,1)S(1)} %bitcast.55, f32[8,256,256]{2,1,0:T(8,128)S(1)} %shard_map.123.gate_ref, bf16[8,256,256]{2,1,0:T(8,128)(2,1)} %get-tuple-element.9.x_ref, bf16[8,2048,256]{2,1,0:T(8,128)(2,1)} %shard_map.124.map_ref), custom_call_target="tpu_custom_call" | custom-call | tf_op jit(solution)/shard_map/pallas_call | solution.py:183
  301.0 10.0 %all_to_all.65 = bf16[8,2,2048]{2,1,0:T(2,128)(2,1)S(1)} all-to-all(bf16[8,2,2048]{2,1,0:T(2,128)(2,1)S(1)} %broadcast_in_dim.56), channel_id=1, replica_groups=mesh['section'=2,'seq'=16,'tensor'=8] {'tensor'}, dimensions={0} | all-to-all | bytes 131072 | tf_op jit(solution)/shard_map/all_to_all | solution.py:28
  314.6 25.0 %all-to-all-done.4 = bf16[8,256,256]{2,1,0:T(8,128)(2,1)S(1)} async-done(((bf16[8,256,256]{2,1,0:T(8,128)(2,1)}), bf16[8,256,256]{2,1,0:T(8,128)(2,1)S(1)}, u32[]{:S(2)}, u32[]{:S(2)}) %all-to-all-start.4) | async-done | bytes 1048608 | tf_op jit(solution)/shard_map/all_to_all | solution.py:283
  339.7 18.1 %all_to_all.66 = bf16[16,16,2048]{2,1,0:T(8,128)(2,1)S(1)} all-to-all(bf16[16,16,2048]{2,1,0:T(8,128)(2,1)S(1)} %broadcast_in_dim.58), channel_id=1, replica_groups=mesh['section'=2,'seq'=16,'tensor'=8] {'seq'}, dimensions={0} | all-to-all | bytes 2097152 | tf_op jit(solution)/shard_map/all_to_all | solution.py:28
  364.1 6.0 %collective-permute-start.7 = (bf16[256,2048]{1,0:T(8,128)(2,1)}, bf16[256,2048]{1,0:T(8,128)(2,1)}, u32[]{:S(2)}, u32[]{:S(2)}) collective-permute-start(bf16[256,2048]{1,0:T(8,128)(2,1)} %bitcast.30), channel_id=1, source_target_pairs={{0,128},{128,0},{1,129},{129,1},{2,130},{130,2},{3,131},{131,3},{4... | collective-permute-start | bytes 3145736 | tf_op jit(solution)/shard_map/ppermute | solution.py:289
  370.1 16.3 %all-to-all-done.7 = bf16[8,256,256]{2,1,0:T(8,128)(2,1)S(1)} async-done(((bf16[8,256,256]{2,1,0:T(8,128)(2,1)}), bf16[8,256,256]{2,1,0:T(8,128)(2,1)S(1)}, u32[]{:S(2)}, u32[]{:S(2)}) %all-to-all-start.7) | async-done | bytes 1048608 | tf_op jit(solution)/shard_map/all_to_all | solution.py:283
  395.4 7.3 %all-to-all-start.12 = ((f32[128,8,128]{2,1,0:T(8,128)}), f32[128,8,128]{2,1,0:T(8,128)}, u32[]{:S(2)}, u32[]{:S(2)}) async-start(f32[128,8,128]{2,1,0:T(8,128)} %broadcast_in_dim.61), calls=%async_computation.12 | async-start | bytes 1048576 | tf_op jit(solution)/shard_map/all_to_all | solution.py:28
  406.1 15.4 %all-to-all-done.12 = f32[128,8,128]{2,1,0:T(8,128)} async-done(((f32[128,8,128]{2,1,0:T(8,128)}), f32[128,8,128]{2,1,0:T(8,128)}, u32[]{:S(2)}, u32[]{:S(2)}) %all-to-all-start.12) | async-done | bytes 524320 | tf_op jit(solution)/shard_map/all_to_all | solution.py:28
  (114 shorter events, 108.7 us)
Async XLA Ops:
  0.6 11.4 %copy-start = (bf16[2,2048,256]{2,1,0:T(8,128)(2,1)S(1)}, bf16[2,2048,256]{2,1,0:T(8,128)(2,1)}, u32[]{:S(2)}) copy-start(bf16[2,2048,256]{2,1,0:T(8,128)(2,1)} %param.10) | copy-start | bytes 6291460
  2.1 17.0 %all-to-all-start.1 = ((f32[16,1,256]{2,1,0:T(1,128)}), f32[16,1,256]{2,1,0:T(1,128)S(1)}, u32[]{:S(2)}, u32[]{:S(2)}) async-start(f32[16,1,256]{2,1,0:T(1,128)} %broadcast_in_dim.50), calls=%async_computation.1 | async-start | bytes 32768 | tf_op jit(solution)/shard_map/all_to_all | solution.py:28
  19.1 32.7 %all-to-all-start = ((bf16[8,256,256]{2,1,0:T(8,128)(2,1)}), bf16[8,256,256]{2,1,0:T(8,128)(2,1)S(1)}, u32[]{:S(2)}, u32[]{:S(2)}) async-start(bf16[8,256,256]{2,1,0:T(8,128)(2,1)} %bitcast.3), calls=%async_computation | async-start | bytes 2097152 | tf_op jit(solution)/shard_map/all_to_all | solution.py:217
  22.6 40.8 %copy-start.16 = (bf16[1,16,128,128]{3,2,1,0:T(8,128)(2,1)S(1)}, bf16[1,16,128,128]{3,2,1,0:T(8,128)(2,1)}, u32[]{:S(2)}) copy-start(bf16[1,16,128,128]{3,2,1,0:T(8,128)(2,1)} %param.13) | copy-start | bytes 1572868
  23.6 1.8 collective-permute-start.1
  54.6 39.5 %all-to-all-start.2 = ((bf16[128,16,256]{2,1,0:T(8,128)(2,1)}), bf16[128,16,256]{2,1,0:T(8,128)(2,1)S(1)}, u32[]{:S(2)}, u32[]{:S(2)}) async-start(bf16[128,16,256]{2,1,0:T(8,128)(2,1)} %bitcast.6), calls=%async_computation.2 | async-start | bytes 2097152 | tf_op jit(solution)/shard_map/all_to_all | solution.py:261
  63.8 2.4 collective-permute-start
  102.3 10.8 %copy-start.17 = (bf16[1,32,64,64]{3,2,1,0:T(8,128)(2,1)S(1)}, bf16[1,32,64,64]{3,2,1,0:T(8,128)(2,1)}, u32[]{:S(2)}) copy-start(bf16[1,32,64,64]{3,2,1,0:T(8,128)(2,1)} %param.14) | copy-start | bytes 786436
  102.3 50.1 %all-to-all-start.3 = ((bf16[128,16,256]{2,1,0:T(8,128)(2,1)}), bf16[128,16,256]{2,1,0:T(8,128)(2,1)}, u32[]{:S(2)}, u32[]{:S(2)}) async-start(bf16[128,16,256]{2,1,0:T(8,128)(2,1)} %bitcast.8), calls=%async_computation.3 | async-start | bytes 2097152 | tf_op jit(solution)/shard_map/all_to_all | solution.py:270
  110.8 17.2 %collective-permute-start.3 = (bf16[32,2048]{1,0:T(8,128)(2,1)}, bf16[32,2048]{1,0:T(8,128)(2,1)}, u32[]{:S(2)}, u32[]{:S(2)}) collective-permute-start(bf16[32,2048]{1,0:T(8,128)(2,1)} %reshape.197), channel_id=1, source_target_pairs={{0,128},{128,0},{1,129},{129,1},{2,130},{130,2},{3,131},{131,3},{4... | collective-permute-start | bytes 393224 | tf_op jit(solution)/shard_map/ppermute | solution.py:237
  119.1 11.2 %collective-permute-start.2 = (bf16[32,64,256]{2,1,0:T(8,128)(2,1)S(1)}, bf16[32,64,256]{2,1,0:T(8,128)(2,1)}, u32[]{:S(2)}, u32[]{:S(2)}) collective-permute-start(bf16[32,64,256]{2,1,0:T(8,128)(2,1)S(1)} %tile.9), channel_id=1, source_target_pairs={{0,128},{128,0},{1,129},{129,1},{2,130},{130,2},{3,131},{131,3},{4... | collective-permute-start | bytes 3145736 | tf_op jit(solution)/shard_map/ppermute | solution.py:237
  125.3 11.9 %collective-permute-start.4 = (bf16[32,64,256]{2,1,0:T(8,128)(2,1)S(1)}, bf16[32,64,256]{2,1,0:T(8,128)(2,1)}, u32[]{:S(2)}, u32[]{:S(2)}) collective-permute-start(bf16[32,64,256]{2,1,0:T(8,128)(2,1)S(1)} %tile.21), channel_id=1, source_target_pairs={{0,128},{128,0},{1,129},{129,1},{2,130},{130,2},{3,131},{131,3},{4... | collective-permute-start | bytes 3145736 | tf_op jit(solution)/shard_map/ppermute | solution.py:237
  127.8 1.6 collective-permute-start.5
  164.8 44.3 %all-to-all-start.5 = ((bf16[128,16,256]{2,1,0:T(8,128)(2,1)}), bf16[128,16,256]{2,1,0:T(8,128)(2,1)S(1)}, u32[]{:S(2)}, u32[]{:S(2)}) async-start(bf16[128,16,256]{2,1,0:T(8,128)(2,1)} %bitcast.56), calls=%async_computation.5 | async-start | bytes 2097152 | tf_op jit(solution)/shard_map/all_to_all | solution.py:261
  209.8 18.8 %all-to-all-start.8 = ((bf16[8,2,2048]{2,1,0:T(2,128)(2,1)}), bf16[8,2,2048]{2,1,0:T(2,128)(2,1)S(1)}, u32[]{:S(2)}, u32[]{:S(2)}) async-start(bf16[8,2,2048]{2,1,0:T(2,128)(2,1)} %broadcast_in_dim.52), calls=%async_computation.8 | async-start | bytes 131072 | tf_op jit(solution)/shard_map/all_to_all | solution.py:28
  228.7 37.7 %all-to-all-start.6 = ((bf16[128,16,256]{2,1,0:T(8,128)(2,1)}), bf16[128,16,256]{2,1,0:T(8,128)(2,1)S(1)}, u32[]{:S(2)}, u32[]{:S(2)}) async-start(bf16[128,16,256]{2,1,0:T(8,128)(2,1)} %bitcast.54), calls=%async_computation.6 | async-start | bytes 2097152 | tf_op jit(solution)/shard_map/all_to_all | solution.py:270
  268.4 32.5 %all-to-all-start.9 = ((bf16[16,16,2048]{2,1,0:T(8,128)(2,1)}), bf16[16,16,2048]{2,1,0:T(8,128)(2,1)}, u32[]{:S(2)}, u32[]{:S(2)}) async-start(bf16[16,16,2048]{2,1,0:T(8,128)(2,1)} %broadcast_in_dim.54), calls=%async_computation.9 | async-start | bytes 2097152 | tf_op jit(solution)/shard_map/all_to_all | solution.py:28
  311.0 28.6 %all-to-all-start.4 = ((bf16[8,256,256]{2,1,0:T(8,128)(2,1)}), bf16[8,256,256]{2,1,0:T(8,128)(2,1)S(1)}, u32[]{:S(2)}, u32[]{:S(2)}) async-start(bf16[8,256,256]{2,1,0:T(8,128)(2,1)} %get-tuple-element.9.x_ref), calls=%async_computation.4 | async-start | bytes 2097152 | tf_op jit(solution)/shard_map/all_to_all | solution.py:283
  357.8 28.6 %all-to-all-start.7 = ((bf16[8,256,256]{2,1,0:T(8,128)(2,1)}), bf16[8,256,256]{2,1,0:T(8,128)(2,1)S(1)}, u32[]{:S(2)}, u32[]{:S(2)}) async-start(bf16[8,256,256]{2,1,0:T(8,128)(2,1)} %shard_map.125), calls=%async_computation.7 | async-start | bytes 2097152 | tf_op jit(solution)/shard_map/all_to_all | solution.py:283
  361.4 8.7 %copy-start.20 = (s32[2,256]{1,0:T(2,128)S(1)}, s32[2,256]{1,0:T(2,128)}, u32[]{:S(2)}) copy-start(s32[2,256]{1,0:T(2,128)} %param.19) | copy-start | bytes 6148
  364.1 28.1 %collective-permute-start.7 = (bf16[256,2048]{1,0:T(8,128)(2,1)}, bf16[256,2048]{1,0:T(8,128)(2,1)}, u32[]{:S(2)}, u32[]{:S(2)}) collective-permute-start(bf16[256,2048]{1,0:T(8,128)(2,1)} %bitcast.30), channel_id=1, source_target_pairs={{0,128},{128,0},{1,129},{129,1},{2,130},{130,2},{3,131},{131,3},{4... | collective-permute-start | bytes 3145736 | tf_op jit(solution)/shard_map/ppermute | solution.py:289
  387.5 15.2 %collective-permute-start.6 = (bf16[2048,256]{1,0:T(8,128)(2,1)}, bf16[2048,256]{1,0:T(8,128)(2,1)}, u32[]{:S(2)}, u32[]{:S(2)}) collective-permute-start(bf16[2048,256]{1,0:T(8,128)(2,1)} %bitcast.23), channel_id=1, source_target_pairs={{0,128},{128,0},{1,129},{129,1},{2,130},{130,2},{3,131},{131,3},{4... | collective-permute-start | bytes 3145736 | tf_op jit(solution)/shard_map/ppermute | solution.py:303
  395.4 26.0 %all-to-all-start.12 = ((f32[128,8,128]{2,1,0:T(8,128)}), f32[128,8,128]{2,1,0:T(8,128)}, u32[]{:S(2)}, u32[]{:S(2)}) async-start(f32[128,8,128]{2,1,0:T(8,128)} %broadcast_in_dim.61), calls=%async_computation.12 | async-start | bytes 1048576 | tf_op jit(solution)/shard_map/all_to_all | solution.py:28
  402.7 20.5 %copy-start.1 = (bf16[2,2048,256]{2,1,0:T(8,128)(2,1)S(1)}, bf16[2,2048,256]{2,1,0:T(8,128)(2,1)}, u32[]{:S(2)}) copy-start(bf16[2,2048,256]{2,1,0:T(8,128)(2,1)} %param.10) | copy-start | bytes 6291460
  (17 other events, 65.9 us)

commit v2 on v1

v2 whole, which is shorter than its diff:
```python
import jax
import jax.numpy as jnp
from jax import lax
from jax.experimental import pallas as pl
from jax.experimental.pallas import tpu as pltpu
from jax.sharding import PartitionSpec as P

C1 = 32
C2 = 64
D = 2048
STRIDE = 128
EPS = 1e-05
BLK = 256
EXTRA = 16
VMEM_LIMIT = 48 * 1024 * 1024
F32 = jnp.float32
BF16 = jnp.bfloat16


def params():
    return pltpu.CompilerParams(vmem_limit_bytes=VMEM_LIMIT)


def whole(shape):
    return pl.BlockSpec(shape, lambda *_: (0,) * len(shape))


def scalar_spec():
    return pl.BlockSpec(memory_space=pltpu.SMEM)


def shape_of(shape, dtype=BF16):
    return jax.ShapeDtypeStruct(shape, dtype)


def dot(a, b):
    return jnp.dot(a, b, preferred_element_type=F32)


def gather_by_exchange(block, axis):
    count = lax.axis_size(axis)
    copies = jnp.broadcast_to(block[None], (count,) + block.shape)
    return lax.all_to_all(copies, axis, split_axis=0, concat_axis=0, tiled=True)


def xor_route(axis, mask):
    return [(i, i ^ mask) for i in range(lax.axis_size(axis))]


def sum_over(block, axis, masks):
    got = [lax.ppermute(block, axis, xor_route(axis, mask)) for mask in masks]
    if len(got) == 1:
        return block + got[0]
    return (block + got[0]) + (got[1] + got[2])


def squares_by_lane(x_blocks):
    ones = jnp.ones((8, BLK), BF16)
    dims = (((1,), (1,)), ((), ()))
    total = None
    for x in x_blocks:
        xf = x.astype(F32)
        square = xf * xf
        high = square.astype(BF16)
        low = (square - high.astype(F32)).astype(BF16)
        part = lax.dot_general(ones, high, dims, preferred_element_type=F32) + lax.dot_general(
            ones, low, dims, preferred_element_type=F32
        )
        total = part if total is None else total + part
    return total


def split_stage(x_own, tensor_index):
    rows, tokens, _ = x_own.shape

    def kernel(z_ref, x_ref, squares_ref, *send_refs):
        z = z_ref[0]
        row = lax.broadcasted_iota(jnp.int32, (8, tokens), 0)
        squares = jnp.zeros((8, tokens), F32)
        for p in range(rows):
            squares = jnp.where(row == p, squares_by_lane([x_ref[p]]), squares)
        squares_ref[...] = squares
        for d in range(rows):
            send_refs[d][...] = x_ref[(z + d) % rows]

    outs = [shape_of((rows, tokens), F32)] + [shape_of((tokens, BLK))] * rows
    return pl.pallas_call(
        kernel,
        in_specs=[scalar_spec(), whole(x_own.shape)],
        out_shape=outs,
        compiler_params=params(),
    )(tensor_index, x_own)


def right_stage(x_chan, squares, gain_local, right, groups):
    rows = right.shape[0]
    tokens = right.shape[1]
    width = tokens // groups
    operands = [x_chan, gain_local, right] + ([] if squares is None else [squares])

    def kernel(x_ref, gain_ref, right_ref, *refs):
        out_ref = refs[-1]
        for p in range(rows):
            if squares is None:
                extra = x_ref[p, tokens:].astype(F32)
                total = extra[0:1] + extra[1:2] + extra[2:3]
            else:
                total = refs[0][p : p + 1]
            scale = lax.rsqrt(total / D + EPS)
            scaled = (right_ref[p].astype(F32) * scale).astype(BF16)
            mix = dot(scaled, x_ref[p, :tokens]) * gain_ref[...]
            out_ref[:, p] = mix.astype(BF16).reshape(groups, width, BLK)

    return pl.pallas_call(
        kernel,
        out_shape=shape_of((groups, rows, width, BLK)),
        compiler_params=params(),
    )(*operands)


def left_stage(left, mix):
    j_count, i_count, p_count = left.shape

    half = BLK // 2

    def kernel(left_ref, mix_ref, out_ref, wide_ref, acc_ref):
        for h in range(2):
            wide_ref[h] = mix_ref[:, h * half : (h + 1) * half].astype(F32)
        for j in range(j_count):
            column = jnp.concatenate(
                [wide_ref[h, pl.ds(j, p_count, stride=j_count), :] for h in range(2)], axis=1
            ).astype(BF16)
            mixed = dot(left_ref[j], column)
            for h in range(2):
                acc_ref[h, pl.ds(j, i_count, stride=j_count), :] = mixed[:, h * half : (h + 1) * half]
        for h in range(2):
            out_ref[:, h * half : (h + 1) * half] = acc_ref[h].astype(BF16)

    return pl.pallas_call(
        kernel,
        out_shape=shape_of((i_count * j_count, BLK)),
        scratch_shapes=[
            pltpu.VMEM((2, p_count * j_count, half), F32),
            pltpu.VMEM((2, i_count * j_count, half), F32),
        ],
        compiler_params=params(),
    )(left, mix)


def channel_map(first, second_rows, n_blk):
    def kernel(first_ref, second_ref, out_ref, spread_ref):
        @pl.when(pl.program_id(0) == 0)
        def _():
            lane = lax.broadcasted_iota(jnp.int32, (C2, BLK), 1) % C2
            pick = (lane == lax.broadcasted_iota(jnp.int32, (C2, BLK), 0)).astype(BF16)
            for r in range(C1):
                spread_ref[r] = lax.dot_general(
                    first_ref[r], pick, (((0,), (0,)), ((), ())), preferred_element_type=F32
                ).astype(BF16)

        for r in range(C1):
            row = second_ref[r : r + 1].astype(F32)
            out_ref[0, r * C2 : (r + 1) * C2] = (spread_ref[r].astype(F32) * row).astype(BF16)

    return pl.pallas_call(
        kernel,
        grid=(n_blk,),
        in_specs=[whole((C1, C2, C2)), pl.BlockSpec((C1, BLK), lambda n: (0, n))],
        out_specs=pl.BlockSpec((1, D, BLK), lambda n: (n, 0, 0)),
        out_shape=shape_of((n_blk, D, BLK)),
        scratch_shapes=[pltpu.VMEM((C1, C2, BLK), BF16)],
        compiler_params=params(),
    )(first, second_rows)


def normalize(x_blocks, gain_ref, tokens, store):
    total = jnp.zeros((tokens, 1), F32)
    for x in x_blocks:
        xf = x.astype(F32)
        total = total + jnp.sum(xf * xf, axis=1, keepdims=True)
    scale = lax.rsqrt(total / D + EPS)
    for n, x in enumerate(x_blocks):
        store(n, (x.astype(F32) * scale * gain_ref[n]).astype(BF16))


def token_stage(received, gain, tensor_index):
    n_blk = len(received)
    tokens = received[0].shape[0]

    def kernel(z_ref, gain_ref, *refs):
        x_ref, normed_ref = refs[n_blk:]
        for d in range(n_blk):
            x_ref[(z_ref[0] + n_blk - d) % n_blk] = refs[d][...]

        def store(n, value):
            normed_ref[:, n * BLK : (n + 1) * BLK] = value

        normalize([x_ref[n] for n in range(n_blk)], gain_ref, tokens, store)

    return pl.pallas_call(
        kernel,
        in_specs=[scalar_spec(), whole(gain.shape)] + [whole((tokens, BLK))] * n_blk,
        out_shape=(shape_of((n_blk, tokens, BLK)), shape_of((tokens, D))),
        compiler_params=params(),
    )(tensor_index, gain, *received)


def gate_stage(normed, gate_map):
    tokens = normed.shape[0]
    n_blk = gate_map.shape[0]

    def kernel(normed_ref, map_ref, out_ref):
        pre = dot(normed_ref[...], map_ref[0]).astype(BF16)
        out_ref[0] = jax.nn.sigmoid(pre.astype(F32))

    return pl.pallas_call(
        kernel,
        grid=(n_blk,),
        in_specs=[whole(normed.shape), pl.BlockSpec((1, D, BLK), lambda n: (n, 0, 0))],
        out_specs=pl.BlockSpec((1, tokens, BLK), lambda n: (n, 0, 0)),
        out_shape=shape_of((n_blk, tokens, BLK), F32),
        compiler_params=params(),
    )(normed, gate_map)


def out_stage(seq_out, gate, x_tok, out_map, gain=None):
    groups, n_blk, width, _ = seq_out.shape
    tokens = groups * width
    extra = 0 if gain is None else EXTRA

    def kernel(seq_ref, gate_ref, x_ref, map_ref, *refs):
        if gain is None:
            res_ref, gated_ref = refs
        else:
            gain_ref, res_ref, normed_ref, gated_ref = refs
        n = pl.program_id(0)

        @pl.when(n == 0)
        def _():
            for z in range(n_blk):
                seq = seq_ref[:, z].reshape(tokens, BLK).astype(F32)
                gated_ref[:, z * BLK : (z + 1) * BLK] = (seq * gate_ref[z]).astype(BF16)

        mixed = dot(gated_ref[...], map_ref[0]).astype(BF16).astype(F32)
        res_ref[n, :tokens] = (x_ref[n].astype(F32) + mixed).astype(BF16)
        if gain is not None:

            @pl.when(n == n_blk - 1)
            def _():
                blocks = [res_ref[z, :tokens] for z in range(n_blk)]

                def store(z, value):
                    normed_ref[:, z * BLK : (z + 1) * BLK] = value

                normalize(blocks, gain_ref, tokens, store)
                total = squares_by_lane(blocks)
                total = jnp.concatenate([total, total], axis=0)
                high = total.astype(BF16).astype(F32)
                mid = (total - high).astype(BF16).astype(F32)
                row = lax.broadcasted_iota(jnp.int32, (EXTRA, tokens), 0)
                rest = jnp.where(row == 1, mid, jnp.where(row == 2, total - high - mid, 0.0))
                packed = jnp.where(row == 0, high, rest).astype(BF16)
                for z in range(n_blk):
                    res_ref[z, tokens:] = packed

    tok_shape = (n_blk, tokens, BLK)
    in_specs = [
        whole(seq_out.shape),
        whole(tok_shape),
        whole(x_tok.shape),
        pl.BlockSpec((1, D, BLK), lambda n: (n, 0, 0)),
    ]
    out_shape = [shape_of((n_blk, tokens + extra, BLK))]
    operands = [seq_out, gate, x_tok, out_map]
    if gain is not None:
        operands.append(gain)
        in_specs.append(whole(gain.shape))
        out_shape.append(shape_of((tokens, D)))
    if x_tok.shape != tok_shape:
        in_specs[2] = whole(x_tok.shape)

        def wrapped(seq_ref, gate_ref, x_ref, *refs):
            kernel(seq_ref, gate_ref, x_ref.at[:, :tokens], *refs)
    else:
        wrapped = kernel
    return pl.pallas_call(
        wrapped,
        grid=(n_blk,),
        in_specs=in_specs,
        out_specs=[whole(s.shape) for s in out_shape],
        out_shape=out_shape,
        scratch_shapes=[pltpu.VMEM((tokens, D), BF16)],
        compiler_params=params(),
    )(*operands)


def body(
    x_in,
    norm_gain,
    right_blocks,
    left_blocks,
    gate_first,
    gate_second,
    out_first,
    out_second,
    head,
    targets,
):
    section = lax.axis_index("section")
    first = section == 0
    tensor_index = lax.axis_index("tensor")
    z_scalar = tensor_index.astype(jnp.int32).reshape(1)
    seq_count = lax.axis_size("seq")
    n_blk = lax.axis_size("tensor")
    everyone = ("seq", "tensor")
    swap = [(0, 1), (1, 0)]
    rows_dev, tokens = right_blocks.shape[1], right_blocks.shape[2]
    j_dev = left_blocks.shape[1]
    p_count = left_blocks.shape[2]

    def by_block(own):
        other = lax.ppermute(own, "section", swap)
        return jnp.where(first, own, other), jnp.where(first, other, own)

    x_own = lax.dynamic_index_in_dim(x_in, section, 0, keepdims=False).reshape(
        rows_dev, tokens, BLK
    )
    squares, *sends = split_stage(x_own, z_scalar)
    gain_local = by_block(norm_gain)
    gain_pair = jnp.concatenate(gain_local, axis=0)
    shared = jnp.concatenate([squares, gain_pair, jnp.zeros((6, BLK), F32)], axis=0)
    shared = gather_by_exchange(shared, "tensor")
    squares = jnp.sum(shared[:, :rows_dev], axis=0)
    gains = [shared[:, rows_dev + b][:, None, :] for b in range(2)]
    rights = by_block(right_blocks[0])
    lefts = by_block(left_blocks[0])

    received = [sends[0]] + [
        lax.ppermute(sends[d], "tensor", [(i, (i + d) % n_blk) for i in range(n_blk)])
        for d in range(1, n_blk)
    ]

    def rows_second(factor):
        return jnp.transpose(factor[0], (2, 1, 0)).reshape(C1, D)

    gate_maps = [
        channel_map(a, c, n_blk)
        for a, c in zip(by_block(gate_first[0]), by_block(rows_second(gate_second)))
    ]
    out_maps = [
        channel_map(a, c, n_blk)
        for a, c in zip(by_block(out_first[0]), by_block(rows_second(out_second)))
    ]

    head_local = head[0]
    vocab_dev = head_local.shape[1]
    vocab_offset = lax.axis_index(everyone) * vocab_dev

    def sequence_mix(x_chan, squares, b):
        mix = right_stage(x_chan, squares, gain_local[b], rights[b], seq_count)
        cols = lax.all_to_all(mix, "seq", split_axis=0, concat_axis=0, tiled=True)
        col_out = left_stage(lefts[b], cols.reshape(p_count * j_dev, BLK))
        seq_out = lax.all_to_all(
            col_out.reshape(p_count, j_dev, BLK), everyone, split_axis=0, concat_axis=0, tiled=True
        )
        return seq_out.reshape(seq_count, n_blk, j_dev, BLK)

    def scored_rows(result):
        return jnp.transpose(result[:, :tokens:STRIDE], (1, 0, 2)).reshape(-1, D)

    def to_channels(result):
        return lax.all_to_all(result, "tensor", split_axis=0, concat_axis=0, tiled=True)

    seq_out = sequence_mix(x_own, squares, 0)
    x_tok, normed = token_stage(received, gains[0], z_scalar)
    gate = gate_stage(normed, gate_maps[0])
    packed, normed = out_stage(seq_out, gate, x_tok, out_maps[0], gains[1])
    rows_one = scored_rows(packed)
    chan_one = to_channels(packed)

    gate = gate_stage(normed, gate_maps[1])
    seq_out = sequence_mix(chan_one, None, 1)
    (result,) = out_stage(seq_out, gate, packed, out_maps[1])
    rows_two = scored_rows(result)

    kept = jnp.where(first, rows_one, rows_two)
    got = lax.ppermute(jnp.where(first, rows_two, rows_one), "section", swap)
    pair = jnp.where(first, jnp.concatenate([kept, got]), jnp.concatenate([got, kept]))
    near = gather_by_exchange(pair, "tensor").reshape(-1, D)
    scored = gather_by_exchange(near, "seq").reshape(-1, D)
    scored, result = lax.optimization_barrier((scored, result))
    chan_two = to_channels(result)

    logits = jnp.dot(scored, head_local, preferred_element_type=F32)
    exp_sums = jnp.sum(jnp.exp(logits), axis=1)
    vocab_ids = jnp.arange(vocab_dev, dtype=jnp.int32)[None, :] + vocab_offset
    labels = jnp.transpose(targets.reshape(2, p_count, -1), (1, 0, 2)).reshape(-1)
    is_target = vocab_ids == labels[:, None]
    target_part = jnp.sum(jnp.where(is_target, logits, 0.0), axis=1)
    total = jnp.stack([exp_sums, target_part]).reshape(-1, 128)
    total = sum_over(total, "seq", (1, 2, 3))
    total = sum_over(total, "seq", (4, 8, 12))
    total = sum_over(total, "tensor", (2, 4, 6))
    total = sum_over(total, "tensor", (1,)).reshape(2, -1)
    losses = jnp.log(total[0]) - total[1]
    aux_losses = jnp.transpose(losses.reshape(p_count, 2, -1), (1, 0, 2)).reshape(1, 2, -1)

    chan_one = chan_one[:, :tokens].reshape(rows_dev * tokens, BLK)
    chan_two = chan_two.reshape(rows_dev * tokens, BLK)
    got_one = lax.ppermute(chan_one, "section", [(1, 0)])
    got_two = lax.ppermute(chan_two, "section", [(0, 1)])
    block_out = jnp.stack(
        [jnp.where(first, chan_one, got_two), jnp.where(first, got_one, chan_two)]
    )[None]
    return (block_out, aux_losses)


def solution(mesh):
    in_specs = (
        P(None, "seq", "tensor"),
        P("section", "tensor"),
        P("section", "seq", None, None),
        P("section", "seq", None, None),
        P("section", None, None, None),
        P("section", None, None, None),
        P("section", None, None, None),
        P("section", None, None, None),
        P("section", None, ("seq", "tensor")),
        P(),
    )
    out_specs = (P("section", None, "seq", "tensor"), P("section", None, None))
    return jax.shard_map(body, mesh=mesh, in_specs=in_specs, out_specs=out_specs, check_vma=False)
```

time: 425 us -> 338 us (0.80)
  waiting for transfers between devices: 170 us -> 55.5 us
  blocking collectives: 28.1 us -> 104 us
  local copies, waits for them, and re-layouts: 31.9 us -> 11.6 us
  Pallas kernels: 84.4 us -> 64.4 us
  other arithmetic: 15.1 us -> 9.22 us
  starting transfers between devices: 90.4 us -> 84.8 us
    all_to_all x11 -> x4, waiting for transfers between devices: 167 us -> 24.2 us  [the longest x1 9.3 us: sequence_mix(): cols = lax.all_to_all(mix, 'seq', split_axis=0, concat_axis=0, tiled=True)]
    all_to_all x0 -> x2, blocking collectives: none -> 49.5 us  [the longest x1 29.3 us: to_channels(): lax.all_to_all(result, 'tensor', split_axis=0, concat_axis=0, tiled=True)]
    all_to_all x11 -> x4, starting transfers between devices: 74.8 us -> 27.7 us  [the longest x2 17.2 us: sequence_mix(): lax.all_to_all(col_out.reshape(p_count, j_dev, BLK), everyone, split_axis...]
    ppermute x8 -> x27, starting transfers between devices: 15.7 us -> 57.1 us  [the longest x7 17.1 us: body(): lax.ppermute(sends[d], 'tensor', [(i, (i + d) % n_blk) for i in range(n_b...]
    ppermute x8 -> x27, waiting for transfers between devices: 2.87 us -> 31.4 us  [the longest x7 22 us: body(): lax.ppermute(sends[d], 'tensor', [(i, (i + d) % n_blk) for i in range(n_b...]
    all_to_all x2 -> x3, blocking collectives: 28.1 us -> 54 us  [gather_by_exchange(): return lax.all_to_all(copies, axis, split_axis=0, concat_axis=0, tiled=True)]
    pallas_call x11 -> x12, Pallas kernels: 69.4 us -> 49.5 us  [the longest x4 22.6 us: channel_map(): pl.pallas_call(kernel, grid=(n_blk,), in_specs=[whole((C1, C2, C2)), pl.B...]
    another operation x4 -> x0, local copies, waits for them, and re-layouts: 11.3 us -> none  [spread_first(): return jnp.tile(jnp.transpose(factor[0], (0, 2, 1)), (1, 1, BLK // C2))]
  transfers between devices with their start and end apart: 19 -> 31, of which waited for: 11 -> 16; matrix products, arithmetic and copies ran while one was open for 9% -> 3% of each run, Pallas kernels for 15% -> 12%
where the time goes in v2:
time: 338 us; the launch traced here: 332 us
  blocking collectives  104 us (31%)
  starting transfers between devices  84.8 us (25%)
  Pallas kernels  64.4 us (19%)
  waiting for transfers between devices  55.5 us (16%)
  local copies, waits for them, and re-layouts  11.6 us (3%)
  other arithmetic  9.22 us (3%)
    all_to_all x3, blocking collectives, gather_by_exchange(): return lax.all_to_all(copies, axis, split_axis=0, concat_axis=0, tiled=True)  54 us
    all_to_all x1, blocking collectives, to_channels(): lax.all_to_all(result, 'tensor', split_axis=0, concat_axis=0, tiled=True)  29.3 us
    pallas_call x4, Pallas kernels, channel_map(): pl.pallas_call(kernel, grid=(n_blk,), in_specs=[whole((C1, C2, C2)), pl.B...  22.6 us
    ppermute x7, waiting for transfers between devices, body(): lax.ppermute(sends[d], 'tensor', [(i, (i + d) % n_blk) for i in range(n_b...  22 us
    all_to_all x1, blocking collectives, sequence_mix(): cols = lax.all_to_all(mix, 'seq', split_axis=0, concat_axis=0, tiled=True)  20.3 us
    pallas_call x2, Pallas kernels, out_stage(): pl.pallas_call(wrapped, grid=(n_blk,), in_specs=in_specs, out_specs=[whol...  18.1 us
    all_to_all x2, starting transfers between devices, sequence_mix(): lax.all_to_all(col_out.reshape(p_count, j_dev, BLK), everyone, split_axis...  17.2 us
    ppermute x7, starting transfers between devices, body(): lax.ppermute(sends[d], 'tensor', [(i, (i + d) % n_blk) for i in range(n_b...  17.1 us
  transfers between devices with their start and end apart: 31, of which 16 were waited for; matrix products, arithmetic and copies ran while one was open for 3% of the time, Pallas kernels for 12%

profile of v2, /device:TPU:1, one launch (start us, length us, event | category | flops | bytes accessed | tf_op | source)
XLA Modules:
  0.0 332.3 jit_solution(6397159404942637057)
XLA Ops:
  6.4 14.0 %all_to_all.45 = f32[8,16,256]{2,1,0:T(8,128)S(1)} all-to-all(f32[8,16,256]{2,1,0:T(8,128)S(1)} %broadcast_in_dim.31), channel_id=1, replica_groups=mesh['section'=2,'seq'=16,'tensor'=8] {'tensor'}, dimensions={0} | all-to-all | bytes 262144 | tf_op jit(solution)/shard_map/all_to_all | solution.py:43
  24.3 6.8 %all-to-all-start.1 = ((bf16[16,8,16,256]{3,2,1,0:T(8,128)(2,1)}), bf16[16,8,16,256]{3,2,1,0:T(8,128)(2,1)S(1)}, u32[]{:S(2)}, u32[]{:S(2)}) async-start(bf16[16,8,16,256]{3,2,1,0:T(8,128)(2,1)} %shard_map.114), calls=%async_computation.1 | async-start | bytes 2097152 | tf_op jit(solution)/shard_map/all_to_all | solution.py:361
  36.3 9.3 %all-to-all-done.1 = bf16[16,8,16,256]{3,2,1,0:T(8,128)(2,1)S(1)} async-done(((bf16[16,8,16,256]{3,2,1,0:T(8,128)(2,1)}), bf16[16,8,16,256]{3,2,1,0:T(8,128)(2,1)S(1)}, u32[]{:S(2)}, u32[]{:S(2)}) %all-to-all-start.1) | async-done | bytes 1048608 | tf_op jit(solution)/shard_map/all_to_all | solution.py:361
  48.1 7.5 %all-to-all-start.2 = ((bf16[128,16,256]{2,1,0:T(8,128)(2,1)}), bf16[128,16,256]{2,1,0:T(8,128)(2,1)S(1)}, u32[]{:S(2)}, u32[]{:S(2)}) async-start(bf16[128,16,256]{2,1,0:T(8,128)(2,1)} %bitcast.5), calls=%async_computation.2 | async-start | bytes 2097152 | tf_op jit(solution)/shard_map/all_to_all | solution.py:363
  69.1 11.0 %collective-permute-done.3.refs_1_ = bf16[256,256]{1,0:T(8,128)(2,1)S(1)} collective-permute-done((bf16[256,256]{1,0:T(8,128)(2,1)}, bf16[256,256]{1,0:T(8,128)(2,1)S(1)}, u32[]{:S(2)}, u32[]{:S(2)}) %collective-permute-start.3) | collective-permute-done | bytes 131104 | tf_op jit(solution)/shard_map/ppermute | solution.py:339
  80.1 4.4 %collective-permute-start.7 = (bf16[256,256]{1,0:T(8,128)(2,1)S(1)}, bf16[256,256]{1,0:T(8,128)(2,1)S(1)}, u32[]{:S(2)}, u32[]{:S(2)}) collective-permute-start(bf16[256,256]{1,0:T(8,128)(2,1)S(1)} %get-tuple-element.23), channel_id=1, source_target_pairs={{0,5},{1,6},{2,7},{3,0},{4,1},{5,2},{6,3},{7,4},{8,13},{9,14},{10,... | collective-permute-start | bytes 393224 | tf_op jit(solution)/shard_map/ppermute | solution.py:339
  95.9 5.8 %collective-permute-done.6.refs_4_ = bf16[256,256]{1,0:T(8,128)(2,1)S(1)} collective-permute-done((bf16[256,256]{1,0:T(8,128)(2,1)S(1)}, bf16[256,256]{1,0:T(8,128)(2,1)S(1)}, u32[]{:S(2)}, u32[]{:S(2)}) %collective-permute-start.6) | collective-permute-done | bytes 131104 | tf_op jit(solution)/shard_map/ppermute | solution.py:339
  108.3 5.7 %shard_map.117.map_ref = bf16[8,2048,256]{2,1,0:T(8,128)(2,1)} custom-call(bf16[32,64,64]{2,1,0:T(8,128)(2,1)S(1)} %get-tuple-element.39.first_ref, bf16[32,2048]{1,0:T(8,128)(2,1)S(1)} %get-tuple-element.45.second_ref), custom_call_target="tpu_custom_call" | custom-call | tf_op jit(solution)/shard_map/pallas_call | solution.py:165
  114.0 7.5 %shard_map.118.gate_ref = f32[8,256,256]{2,1,0:T(8,128)S(1)} custom-call(bf16[256,2048]{1,0:T(8,128)(2,1)S(1)} %get-tuple-element.26.normed_ref, bf16[8,2048,256]{2,1,0:T(8,128)(2,1)} %shard_map.117.map_ref), custom_call_target="tpu_custom_call" | custom-call | tf_op jit(solution)/shard_map/pallas_call | solution.py:216
  123.6 5.7 %shard_map.119.map_ref = bf16[8,2048,256]{2,1,0:T(8,128)(2,1)} custom-call(bf16[32,64,64]{2,1,0:T(8,128)(2,1)S(1)} %get-tuple-element.37.first_ref, bf16[32,2048]{1,0:T(8,128)(2,1)S(1)} %get-tuple-element.43.second_ref), custom_call_target="tpu_custom_call" | custom-call | tf_op jit(solution)/shard_map/pallas_call | solution.py:165
  130.5 9.2 %shard_map.120 = (bf16[8,272,256]{2,1,0:T(8,128)(2,1)S(1)}, bf16[256,2048]{1,0:T(8,128)(2,1)S(1)}) custom-call(bf16[16,8,16,256]{3,2,1,0:T(8,128)(2,1)S(1)} %bitcast.61, f32[8,256,256]{2,1,0:T(8,128)} %copy-done.2, bf16[8,256,256]{2,1,0:T(8,128)(2,1)S(1)} %copy-done.8, bf16[8,2048,256]{2,1,0:T(8,128)(2,1)} %shard_map.119.map_ref, ...), custom_call_target="tpu_custom_call" | custom-call | tf_op jit(solution)/shard_map/pallas_call | solution.py:286
  139.8 29.3 %all_to_all.46.x_ref = bf16[8,272,256]{2,1,0:T(8,128)(2,1)S(1)} all-to-all(bf16[8,272,256]{2,1,0:T(8,128)(2,1)S(1)} %get-tuple-element.28.x_ref), channel_id=1, replica_groups=mesh['section'=2,'seq'=16,'tensor'=8] {'tensor'}, dimensions={0} | all-to-all | bytes 2228224 | tf_op jit(solution)/shard_map/all_to_all | solution.py:372
  169.6 20.3 %all_to_all.47 = bf16[16,8,16,256]{3,2,1,0:T(8,128)(2,1)S(1)} all-to-all(bf16[16,8,16,256]{3,2,1,0:T(8,128)(2,1)S(1)} %shard_map.121), channel_id=1, replica_groups=mesh['section'=2,'seq'=16,'tensor'=8] {'seq'}, dimensions={0} | all-to-all | bytes 2097152 | tf_op jit(solution)/shard_map/all_to_all | solution.py:361
  192.3 9.7 %all-to-all-start.5 = ((bf16[128,16,256]{2,1,0:T(8,128)(2,1)}), bf16[128,16,256]{2,1,0:T(8,128)(2,1)}, u32[]{:S(2)}, u32[]{:S(2)}) async-start(bf16[128,16,256]{2,1,0:T(8,128)(2,1)} %bitcast.15), calls=%async_computation.5 | async-start | bytes 2097152 | tf_op jit(solution)/shard_map/all_to_all | solution.py:363
  202.1 5.6 %shard_map.123.map_ref = bf16[8,2048,256]{2,1,0:T(8,128)(2,1)} custom-call(bf16[32,64,64]{2,1,0:T(8,128)(2,1)S(1)} %get-tuple-element.38.first_ref, bf16[32,2048]{1,0:T(8,128)(2,1)S(1)} %get-tuple-element.44.second_ref), custom_call_target="tpu_custom_call" | custom-call | tf_op jit(solution)/shard_map/pallas_call | solution.py:165
  207.7 5.7 %shard_map.125.refs_0_ = bf16[8,2048,256]{2,1,0:T(8,128)(2,1)} custom-call(bf16[32,64,64]{2,1,0:T(8,128)(2,1)S(1)} %copy-done.6, bf16[32,2048]{1,0:T(8,128)(2,1)S(1)} %get-tuple-element.42.second_ref), custom_call_target="tpu_custom_call" | custom-call | tf_op jit(solution)/shard_map/pallas_call | solution.py:165
  214.6 7.4 %shard_map.124.gate_ref = f32[8,256,256]{2,1,0:T(8,128)S(1)} custom-call(bf16[256,2048]{1,0:T(8,128)(2,1)S(1)} %copy-done.10, bf16[8,2048,256]{2,1,0:T(8,128)(2,1)} %shard_map.123.map_ref), custom_call_target="tpu_custom_call" | custom-call | tf_op jit(solution)/shard_map/pallas_call | solution.py:216
  222.1 5.9 %all-to-all-done.5 = bf16[128,16,256]{2,1,0:T(8,128)(2,1)} async-done(((bf16[128,16,256]{2,1,0:T(8,128)(2,1)}), bf16[128,16,256]{2,1,0:T(8,128)(2,1)}, u32[]{:S(2)}, u32[]{:S(2)}) %all-to-all-start.5) | async-done | bytes 1048608 | tf_op jit(solution)/shard_map/all_to_all | solution.py:363
  229.2 8.9 %shard_map.126 = bf16[8,256,256]{2,1,0:T(8,128)(2,1)} custom-call(bf16[16,8,16,256]{3,2,1,0:T(8,128)(2,1)} %bitcast.16.seq_ref, f32[8,256,256]{2,1,0:T(8,128)S(1)} %shard_map.124.gate_ref, bf16[8,272,256]{2,1,0:T(8,128)(2,1)S(1)} %copy-done.4, bf16[8,2048,256]{2,1,0:T(8,128)(2,1)} %shard_map.125.refs_0_), custom_call_target="tpu_custom_call" | custom-call | tf_op jit(solution)/shard_map/pallas_call | solution.py:286
  239.4 6.4 %collective-permute-start.14 = (bf16[2,2048]{1,0:T(2,128)(2,1)S(1)}, bf16[2,2048]{1,0:T(2,128)(2,1)S(1)}, u32[]{:S(2)}, u32[]{:S(2)}) collective-permute-start(bf16[2,2048]{1,0:T(2,128)(2,1)S(1)} %bitcast.76), channel_id=1, source_target_pairs={{0,128},{128,0},{1,129},{129,1},{2,130},{130,2},{3,131},{131,3},{4... | collective-permute-start | bytes 24584 | tf_op jit(solution)/shard_map/ppermute | solution.py:387
  246.7 10.8 %all_to_all.48 = bf16[8,4,2048]{2,1,0:T(4,128)(2,1)S(1)} all-to-all(bf16[8,4,2048]{2,1,0:T(4,128)(2,1)S(1)} %broadcast_in_dim.32), channel_id=1, replica_groups=mesh['section'=2,'seq'=16,'tensor'=8] {'tensor'}, dimensions={0} | all-to-all | bytes 262144 | tf_op jit(solution)/shard_map/all_to_all | solution.py:43
  257.8 29.2 %all_to_all.49 = bf16[16,32,2048]{2,1,0:T(8,128)(2,1)} all-to-all(bf16[16,32,2048]{2,1,0:T(8,128)(2,1)S(1)} %broadcast_in_dim.34), channel_id=1, replica_groups=mesh['section'=2,'seq'=16,'tensor'=8] {'seq'}, dimensions={0} | all-to-all | bytes 4194304 | tf_op jit(solution)/shard_map/all_to_all | solution.py:43
  291.3 5.5 %collective-permute-start.16 = (bf16[2048,256]{1,0:T(8,128)(2,1)S(1)}, bf16[2048,256]{1,0:T(8,128)(2,1)S(1)}, u32[]{:S(2)}, u32[]{:S(2)}) collective-permute-start(bf16[2048,256]{1,0:T(8,128)(2,1)S(1)} %bitcast.63), channel_id=1, source_target_pairs={{128,0},{129,1},{130,2},{131,3},{132,4},{133,5},{134,6},{135,7},{1... | collective-permute-start | bytes 3145736 | tf_op jit(solution)/shard_map/ppermute | solution.py:410
  308.3 9.0 %all-to-all-done.8 = bf16[8,256,256]{2,1,0:T(8,128)(2,1)S(1)} async-done(((bf16[8,256,256]{2,1,0:T(8,128)(2,1)}), bf16[8,256,256]{2,1,0:T(8,128)(2,1)S(1)}, u32[]{:S(2)}, u32[]{:S(2)}) %all-to-all-start.8) | async-done | bytes 1048608 | tf_op jit(solution)/shard_map/all_to_all | solution.py:372
  (145 shorter events, 90.7 us)
Async XLA Ops:
  0.7 19.8 %collective-permute-start.2 = (bf16[8,256,256]{2,1,0:T(8,128)(2,1)}, bf16[8,256,256]{2,1,0:T(8,128)(2,1)}, u32[]{:S(2)}, u32[]{:S(2)}) collective-permute-start(bf16[8,256,256]{2,1,0:T(8,128)(2,1)} %bitcast.65), channel_id=1, source_target_pairs={{0,128},{128,0},{1,129},{129,1},{2,130},{130,2},{3,131},{131,3},{4... | collective-permute-start | bytes 3145736 | tf_op jit(solution)/shard_map/ppermute | solution.py:322
  24.3 21.4 %all-to-all-start.1 = ((bf16[16,8,16,256]{3,2,1,0:T(8,128)(2,1)}), bf16[16,8,16,256]{3,2,1,0:T(8,128)(2,1)S(1)}, u32[]{:S(2)}, u32[]{:S(2)}) async-start(bf16[16,8,16,256]{3,2,1,0:T(8,128)(2,1)} %shard_map.114), calls=%async_computation.1 | async-start | bytes 2097152 | tf_op jit(solution)/shard_map/all_to_all | solution.py:361
  48.1 81.2 %all-to-all-start.2 = ((bf16[128,16,256]{2,1,0:T(8,128)(2,1)}), bf16[128,16,256]{2,1,0:T(8,128)(2,1)S(1)}, u32[]{:S(2)}, u32[]{:S(2)}) async-start(bf16[128,16,256]{2,1,0:T(8,128)(2,1)} %bitcast.5), calls=%async_computation.2 | async-start | bytes 2097152 | tf_op jit(solution)/shard_map/all_to_all | solution.py:363
  56.0 10.4 %collective-permute-start.11 = (bf16[32,2048]{1,0:T(8,128)(2,1)S(1)}, bf16[32,2048]{1,0:T(8,128)(2,1)S(1)}, u32[]{:S(2)}, u32[]{:S(2)}) collective-permute-start(bf16[32,2048]{1,0:T(8,128)(2,1)S(1)} %reshape.113), channel_id=1, source_target_pairs={{0,128},{128,0},{1,129},{129,1},{2,130},{130,2},{3,131},{131,3},{4... | collective-permute-start | bytes 393224 | tf_op jit(solution)/shard_map/ppermute | solution.py:322
  58.6 21.5 %collective-permute-start.3 = (bf16[256,256]{1,0:T(8,128)(2,1)}, bf16[256,256]{1,0:T(8,128)(2,1)S(1)}, u32[]{:S(2)}, u32[]{:S(2)}) collective-permute-start(bf16[256,256]{1,0:T(8,128)(2,1)} %get-tuple-element.19), channel_id=1, source_target_pairs={{0,1},{1,2},{2,3},{3,4},{4,5},{5,6},{6,7},{7,0},{8,9},{9,10},{10,1... | collective-permute-start | bytes 393224 | tf_op jit(solution)/shard_map/ppermute | solution.py:339
  59.5 26.6 %collective-permute-start.4 = (bf16[256,256]{1,0:T(8,128)(2,1)}, bf16[256,256]{1,0:T(8,128)(2,1)S(1)}, u32[]{:S(2)}, u32[]{:S(2)}) collective-permute-start(bf16[256,256]{1,0:T(8,128)(2,1)} %get-tuple-element.20), channel_id=1, source_target_pairs={{0,2},{1,3},{2,4},{3,5},{4,6},{5,7},{6,0},{7,1},{8,10},{9,11},{10,... | collective-permute-start | bytes 393224 | tf_op jit(solution)/shard_map/ppermute | solution.py:339
  61.6 30.6 %collective-permute-start.5 = (bf16[256,256]{1,0:T(8,128)(2,1)}, bf16[256,256]{1,0:T(8,128)(2,1)S(1)}, u32[]{:S(2)}, u32[]{:S(2)}) collective-permute-start(bf16[256,256]{1,0:T(8,128)(2,1)} %get-tuple-element.21), channel_id=1, source_target_pairs={{0,3},{1,4},{2,5},{3,6},{4,7},{5,0},{6,1},{7,2},{8,11},{9,12},{10,... | collective-permute-start | bytes 393224 | tf_op jit(solution)/shard_map/ppermute | solution.py:339
  64.0 37.7 %collective-permute-start.6 = (bf16[256,256]{1,0:T(8,128)(2,1)S(1)}, bf16[256,256]{1,0:T(8,128)(2,1)S(1)}, u32[]{:S(2)}, u32[]{:S(2)}) collective-permute-start(bf16[256,256]{1,0:T(8,128)(2,1)S(1)} %get-tuple-element.22), channel_id=1, source_target_pairs={{0,4},{1,5},{2,6},{3,7},{4,0},{5,1},{6,2},{7,3},{8,12},{9,13},{10,... | collective-permute-start | bytes 393224 | tf_op jit(solution)/shard_map/ppermute | solution.py:339
  68.7 38.1 %collective-permute-start.10 = (bf16[32,64,64]{2,1,0:T(8,128)(2,1)}, bf16[32,64,64]{2,1,0:T(8,128)(2,1)S(1)}, u32[]{:S(2)}, u32[]{:S(2)}) collective-permute-start(bf16[32,64,64]{2,1,0:T(8,128)(2,1)} %bitcast.67), channel_id=1, source_target_pairs={{0,128},{128,0},{1,129},{129,1},{2,130},{130,2},{3,131},{131,3},{4... | collective-permute-start | bytes 786440 | tf_op jit(solution)/shard_map/ppermute | solution.py:322
  80.1 25.1 %collective-permute-start.7 = (bf16[256,256]{1,0:T(8,128)(2,1)S(1)}, bf16[256,256]{1,0:T(8,128)(2,1)S(1)}, u32[]{:S(2)}, u32[]{:S(2)}) collective-permute-start(bf16[256,256]{1,0:T(8,128)(2,1)S(1)} %get-tuple-element.23), channel_id=1, source_target_pairs={{0,5},{1,6},{2,7},{3,0},{4,1},{5,2},{6,3},{7,4},{8,13},{9,14},{10,... | collective-permute-start | bytes 393224 | tf_op jit(solution)/shard_map/ppermute | solution.py:339
  86.1 19.1 %collective-permute-start.8 = (bf16[256,256]{1,0:T(8,128)(2,1)S(1)}, bf16[256,256]{1,0:T(8,128)(2,1)S(1)}, u32[]{:S(2)}, u32[]{:S(2)}) collective-permute-start(bf16[256,256]{1,0:T(8,128)(2,1)S(1)} %get-tuple-element.24), channel_id=1, source_target_pairs={{0,6},{1,7},{2,0},{3,1},{4,2},{5,3},{6,4},{7,5},{8,14},{9,15},{10,... | collective-permute-start | bytes 393224 | tf_op jit(solution)/shard_map/ppermute | solution.py:339
  92.2 13.1 %collective-permute-start.9 = (bf16[256,256]{1,0:T(8,128)(2,1)S(1)}, bf16[256,256]{1,0:T(8,128)(2,1)S(1)}, u32[]{:S(2)}, u32[]{:S(2)}) collective-permute-start(bf16[256,256]{1,0:T(8,128)(2,1)S(1)} %get-tuple-element.25), channel_id=1, source_target_pairs={{0,7},{1,0},{2,1},{3,2},{4,3},{5,4},{6,5},{7,6},{8,15},{9,8},{10,9... | collective-permute-start | bytes 393224 | tf_op jit(solution)/shard_map/ppermute | solution.py:339
  102.3 20.5 %collective-permute-start.12 = (bf16[32,64,64]{2,1,0:T(8,128)(2,1)}, bf16[32,64,64]{2,1,0:T(8,128)(2,1)S(1)}, u32[]{:S(2)}, u32[]{:S(2)}) collective-permute-start(bf16[32,64,64]{2,1,0:T(8,128)(2,1)} %bitcast.68), channel_id=1, source_target_pairs={{0,128},{128,0},{1,129},{129,1},{2,130},{130,2},{3,131},{131,3},{4... | collective-permute-start | bytes 786440 | tf_op jit(solution)/shard_map/ppermute | solution.py:322
  192.3 35.6 %all-to-all-start.5 = ((bf16[128,16,256]{2,1,0:T(8,128)(2,1)}), bf16[128,16,256]{2,1,0:T(8,128)(2,1)}, u32[]{:S(2)}, u32[]{:S(2)}) async-start(bf16[128,16,256]{2,1,0:T(8,128)(2,1)} %bitcast.15), calls=%async_computation.5 | async-start | bytes 2097152 | tf_op jit(solution)/shard_map/all_to_all | solution.py:363
  239.4 7.3 %collective-permute-start.14 = (bf16[2,2048]{1,0:T(2,128)(2,1)S(1)}, bf16[2,2048]{1,0:T(2,128)(2,1)S(1)}, u32[]{:S(2)}, u32[]{:S(2)}) collective-permute-start(bf16[2,2048]{1,0:T(2,128)(2,1)S(1)} %bitcast.76), channel_id=1, source_target_pairs={{0,128},{128,0},{1,129},{129,1},{2,130},{130,2},{3,131},{131,3},{4... | collective-permute-start | bytes 24584 | tf_op jit(solution)/shard_map/ppermute | solution.py:387
  287.0 30.2 %all-to-all-start.8 = ((bf16[8,256,256]{2,1,0:T(8,128)(2,1)}), bf16[8,256,256]{2,1,0:T(8,128)(2,1)S(1)}, u32[]{:S(2)}, u32[]{:S(2)}) async-start(bf16[8,256,256]{2,1,0:T(8,128)(2,1)} %shard_map.126), calls=%async_computation.8 | async-start | bytes 2097152 | tf_op jit(solution)/shard_map/all_to_all | solution.py:372
  291.3 37.8 %collective-permute-start.16 = (bf16[2048,256]{1,0:T(8,128)(2,1)S(1)}, bf16[2048,256]{1,0:T(8,128)(2,1)S(1)}, u32[]{:S(2)}, u32[]{:S(2)}) collective-permute-start(bf16[2048,256]{1,0:T(8,128)(2,1)S(1)} %bitcast.63), channel_id=1, source_target_pairs={{128,0},{129,1},{130,2},{131,3},{132,4},{133,5},{134,6},{135,7},{1... | collective-permute-start | bytes 3145736 | tf_op jit(solution)/shard_map/ppermute | solution.py:410
  304.4 14.1 %collective-permute-start.20 = (f32[8,128]{1,0:T(8,128)S(1)}, f32[8,128]{1,0:T(8,128)S(1)}, u32[]{:S(2)}, u32[]{:S(2)}) collective-permute-start(f32[8,128]{1,0:T(8,128)S(1)} %add_add_fusion.2), channel_id=1, source_target_pairs={{0,32},{8,40},{16,48},{24,56},{32,0},{40,8},{48,16},{56,24},{64,96... | collective-permute-start | bytes 12296 | tf_op jit(solution)/shard_map/ppermute | solution.py:51
  304.4 14.1 %collective-permute-start.21 = (f32[8,128]{1,0:T(8,128)S(1)}, f32[8,128]{1,0:T(8,128)S(1)}, u32[]{:S(2)}, u32[]{:S(2)}) collective-permute-start(f32[8,128]{1,0:T(8,128)S(1)} %add_add_fusion.2), channel_id=1, source_target_pairs={{0,64},{8,72},{16,80},{24,88},{32,96},{40,104},{48,112},{56,120},{... | collective-permute-start | bytes 12296 | tf_op jit(solution)/shard_map/ppermute | solution.py:51
  306.5 12.0 %collective-permute-start.22 = (f32[8,128]{1,0:T(8,128)S(1)}, f32[8,128]{1,0:T(8,128)S(1)}, u32[]{:S(2)}, u32[]{:S(2)}) collective-permute-start(f32[8,128]{1,0:T(8,128)S(1)} %add_add_fusion.2), channel_id=1, source_target_pairs={{0,96},{8,104},{16,112},{24,120},{32,64},{40,72},{48,80},{56,88},{... | collective-permute-start | bytes 12296 | tf_op jit(solution)/shard_map/ppermute | solution.py:51
  317.2 12.0 %collective-permute-start.15 = (bf16[2048,256]{1,0:T(8,128)(2,1)S(1)}, bf16[2048,256]{1,0:T(8,128)(2,1)}, u32[]{:S(2)}, u32[]{:S(2)}) collective-permute-start(bf16[2048,256]{1,0:T(8,128)(2,1)S(1)} %bitcast.62), channel_id=1, source_target_pairs={{0,128},{1,129},{2,130},{3,131},{4,132},{5,133},{6,134},{7,135},{8... | collective-permute-start | bytes 3145736 | tf_op jit(solution)/shard_map/ppermute | solution.py:411
  318.6 5.7 %collective-permute-start.23 = (f32[8,128]{1,0:T(8,128)S(1)}, f32[8,128]{1,0:T(8,128)S(1)}, u32[]{:S(2)}, u32[]{:S(2)}) collective-permute-start(f32[8,128]{1,0:T(8,128)S(1)} %add_add_fusion.1), channel_id=1, source_target_pairs={{0,2},{1,3},{2,0},{3,1},{4,6},{5,7},{6,4},{7,5},{8,10},{9,11},{10,... | collective-permute-start | bytes 12296 | tf_op jit(solution)/shard_map/ppermute | solution.py:51
  318.7 6.5 %collective-permute-start.24 = (f32[8,128]{1,0:T(8,128)S(1)}, f32[8,128]{1,0:T(8,128)S(1)}, u32[]{:S(2)}, u32[]{:S(2)}) collective-permute-start(f32[8,128]{1,0:T(8,128)S(1)} %add_add_fusion.1), channel_id=1, source_target_pairs={{0,4},{1,5},{2,6},{3,7},{4,0},{5,1},{6,2},{7,3},{8,12},{9,13},{10,... | collective-permute-start | bytes 12296 | tf_op jit(solution)/shard_map/ppermute | solution.py:51
  320.0 5.4 %collective-permute-start.25 = (f32[8,128]{1,0:T(8,128)S(1)}, f32[8,128]{1,0:T(8,128)S(1)}, u32[]{:S(2)}, u32[]{:S(2)}) collective-permute-start(f32[8,128]{1,0:T(8,128)S(1)} %add_add_fusion.1), channel_id=1, source_target_pairs={{0,6},{1,7},{2,4},{3,5},{4,2},{5,3},{6,0},{7,1},{8,14},{9,15},{10,... | collective-permute-start | bytes 12296 | tf_op jit(solution)/shard_map/ppermute | solution.py:51
  (29 other events, 260.4 us)

commit v3 on v2

--- a/solution.py
+++ b/solution.py
@@ -41,17 +41,6 @@
     count = lax.axis_size(axis)
     copies = jnp.broadcast_to(block[None], (count,) + block.shape)
     return lax.all_to_all(copies, axis, split_axis=0, concat_axis=0, tiled=True)
-
-
-def xor_route(axis, mask):
-    return [(i, i ^ mask) for i in range(lax.axis_size(axis))]
-
-
-def sum_over(block, axis, masks):
-    got = [lax.ppermute(block, axis, xor_route(axis, mask)) for mask in masks]
-    if len(got) == 1:
-        return block + got[0]
-    return (block + got[0]) + (got[1] + got[2])
 
 
 def squares_by_lane(x_blocks):
@@ -153,14 +142,16 @@
         def _():
             lane = lax.broadcasted_iota(jnp.int32, (C2, BLK), 1) % C2
             pick = (lane == lax.broadcasted_iota(jnp.int32, (C2, BLK), 0)).astype(BF16)
-            for r in range(C1):
+
+            @pl.loop(0, C1)
+            def _(r):
                 spread_ref[r] = lax.dot_general(
                     first_ref[r], pick, (((0,), (0,)), ((), ())), preferred_element_type=F32
                 ).astype(BF16)
 
         for r in range(C1):
-            row = second_ref[r : r + 1].astype(F32)
-            out_ref[0, r * C2 : (r + 1) * C2] = (spread_ref[r].astype(F32) * row).astype(BF16)
+            row = second_ref[r : r + 1]
+            out_ref[0, r * C2 : (r + 1) * C2] = spread_ref[r] * row
 
     return pl.pallas_call(
         kernel,
@@ -223,17 +214,16 @@
     )(normed, gate_map)
 
 
-def out_stage(seq_out, gate, x_tok, out_map, gain=None):
+def out_stage(seq_out, gate, x_tok, out_map, gain=None, tensor_index=None):
     groups, n_blk, width, _ = seq_out.shape
     tokens = groups * width
-    extra = 0 if gain is None else EXTRA
 
     def kernel(seq_ref, gate_ref, x_ref, map_ref, *refs):
-        if gain is None:
-            res_ref, gated_ref = refs
+        n = pl.program_id(0)
+        if gain is not None:
+            gain_ref, res_ref, normed_ref, gated_ref = refs
         else:
-            gain_ref, res_ref, normed_ref, gated_ref = refs
-        n = pl.program_id(0)
+            z_ref, *send_refs, rows_ref, res_ref, gated_ref = refs
 
         @pl.when(n == 0)
         def _():
@@ -242,56 +232,77 @@
                 gated_ref[:, z * BLK : (z + 1) * BLK] = (seq * gate_ref[z]).astype(BF16)
 
         mixed = dot(gated_ref[...], map_ref[0]).astype(BF16).astype(F32)
-        res_ref[n, :tokens] = (x_ref[n].astype(F32) + mixed).astype(BF16)
-        if gain is not None:
-
-            @pl.when(n == n_blk - 1)
-            def _():
-                blocks = [res_ref[z, :tokens] for z in range(n_blk)]
-
-                def store(z, value):
-                    normed_ref[:, z * BLK : (z + 1) * BLK] = value
-
-                normalize(blocks, gain_ref, tokens, store)
-                total = squares_by_lane(blocks)
-                total = jnp.concatenate([total, total], axis=0)
-                high = total.astype(BF16).astype(F32)
-                mid = (total - high).astype(BF16).astype(F32)
-                row = lax.broadcasted_iota(jnp.int32, (EXTRA, tokens), 0)
-                rest = jnp.where(row == 1, mid, jnp.where(row == 2, total - high - mid, 0.0))
-                packed = jnp.where(row == 0, high, rest).astype(BF16)
+        res_ref[n, :tokens] = (x_ref[n, :tokens].astype(F32) + mixed).astype(BF16)
+
+        @pl.when(n == n_blk - 1)
+        def _():
+            if gain is None:
+                for d in range(n_blk):
+                    send_refs[d][...] = res_ref[(z_ref[0] + d) % n_blk]
                 for z in range(n_blk):
-                    res_ref[z, tokens:] = packed
-
-    tok_shape = (n_blk, tokens, BLK)
+                    for q in range(tokens // STRIDE):
+                        rows_ref[q : q + 1, z * BLK : (z + 1) * BLK] = res_ref[
+                            z, q * STRIDE : q * STRIDE + 1
+                        ]
+                return
+            blocks = [res_ref[z, :tokens] for z in range(n_blk)]
+
+            def store(z, value):
+                normed_ref[:, z * BLK : (z + 1) * BLK] = value
+
+            normalize(blocks, gain_ref, tokens, store)
+            total = squares_by_lane(blocks)
+            total = jnp.concatenate([total, total], axis=0)
+            high = total.astype(BF16).astype(F32)
+            mid = (total - high).astype(BF16).astype(F32)
+            row = lax.broadcasted_iota(jnp.int32, (EXTRA, tokens), 0)
+            rest = jnp.where(row == 1, mid, jnp.where(row == 2, total - high - mid, 0.0))
+            packed = jnp.where(row == 0, high, rest).astype(BF16)
+            for z in range(n_blk):
+                res_ref[z, tokens:] = packed
+
     in_specs = [
         whole(seq_out.shape),
-        whole(tok_shape),
+        whole(gate.shape),
         whole(x_tok.shape),
         pl.BlockSpec((1, D, BLK), lambda n: (n, 0, 0)),
     ]
-    out_shape = [shape_of((n_blk, tokens + extra, BLK))]
     operands = [seq_out, gate, x_tok, out_map]
+    scratch = [pltpu.VMEM((tokens, D), BF16)]
     if gain is not None:
         operands.append(gain)
         in_specs.append(whole(gain.shape))
-        out_shape.append(shape_of((tokens, D)))
-    if x_tok.shape != tok_shape:
-        in_specs[2] = whole(x_tok.shape)
-
-        def wrapped(seq_ref, gate_ref, x_ref, *refs):
-            kernel(seq_ref, gate_ref, x_ref.at[:, :tokens], *refs)
+        out_shape = [shape_of((n_blk, tokens + EXTRA, BLK)), shape_of((tokens, D))]
     else:
-        wrapped = kernel
-    return pl.pallas_call(
-        wrapped,
+        operands.append(tensor_index)
+        in_specs.append(scalar_spec())
+        out_shape = [shape_of((tokens, BLK))] * n_blk + [shape_of((tokens // STRIDE, D))]
+        scratch = [pltpu.VMEM((n_blk, tokens, BLK), BF16)] + scratch
+    return pl.pallas_call(
+        kernel,
         grid=(n_blk,),
         in_specs=in_specs,
         out_specs=[whole(s.shape) for s in out_shape],
         out_shape=out_shape,
-        scratch_shapes=[pltpu.VMEM((tokens, D), BF16)],
+        scratch_shapes=scratch,
         compiler_params=params(),
     )(*operands)
+
+
+def place_stage(received, tensor_index):
+    n_blk = len(received)
+    tokens = received[0].shape[0]
+
+    def kernel(z_ref, *refs):
+        for d in range(n_blk):
+            refs[n_blk][(z_ref[0] + n_blk - d) % n_blk] = refs[d][...]
+
+    return pl.pallas_call(
+        kernel,
+        in_specs=[scalar_spec()] + [whole((tokens, BLK))] * n_blk,
+        out_shape=shape_of((n_blk, tokens, BLK)),
+        compiler_params=params(),
+    )(tensor_index, *received)
 
 
 def body(
@@ -322,91 +333,108 @@
         other = lax.ppermute(own, "section", swap)
         return jnp.where(first, own, other), jnp.where(first, other, own)
 
+    def by_distance(blocks):
+        return [blocks[0]] + [
+            lax.ppermute(blocks[d], "tensor", [(i, (i + d) % n_blk) for i in range(n_blk)])
+            for d in range(1, n_blk)
+        ]
+
+    def rows_second(factor):
+        return jnp.transpose(factor[0], (2, 1, 0)).reshape(C1, D)
+
+    tie = lax.optimization_barrier
+
     x_own = lax.dynamic_index_in_dim(x_in, section, 0, keepdims=False).reshape(
         rows_dev, tokens, BLK
     )
     squares, *sends = split_stage(x_own, z_scalar)
+    rights = by_block(right_blocks[0])
     gain_local = by_block(norm_gain)
-    gain_pair = jnp.concatenate(gain_local, axis=0)
-    shared = jnp.concatenate([squares, gain_pair, jnp.zeros((6, BLK), F32)], axis=0)
+    shared = jnp.concatenate([squares, *gain_local, jnp.zeros((6, BLK), F32)], axis=0)
+
+    shared, gate_own, out_own, second_own = tie(
+        (shared, gate_first[0], out_first[0], (gate_second, out_second))
+    )
+    gate_one, gate_two = by_block(gate_own)
+    out_one, out_two = by_block(out_own)
+    gate_sec = by_block(rows_second(second_own[0]))
+    out_sec = by_block(rows_second(second_own[1]))
     shared = gather_by_exchange(shared, "tensor")
+    gate_map_one = channel_map(gate_one, gate_sec[0], n_blk)
     squares = jnp.sum(shared[:, :rows_dev], axis=0)
     gains = [shared[:, rows_dev + b][:, None, :] for b in range(2)]
-    rights = by_block(right_blocks[0])
-    lefts = by_block(left_blocks[0])
-
-    received = [sends[0]] + [
-        lax.ppermute(sends[d], "tensor", [(i, (i + d) % n_blk) for i in range(n_blk)])
-        for d in range(1, n_blk)
-    ]
-
-    def rows_second(factor):
-        return jnp.transpose(factor[0], (2, 1, 0)).reshape(C1, D)
-
-    gate_maps = [
-        channel_map(a, c, n_blk)
-        for a, c in zip(by_block(gate_first[0]), by_block(rows_second(gate_second)))
-    ]
-    out_maps = [
-        channel_map(a, c, n_blk)
-        for a, c in zip(by_block(out_first[0]), by_block(rows_second(out_second)))
-    ]
-
-    head_local = head[0]
-    vocab_dev = head_local.shape[1]
+
+    def mix_right(x_chan, squares, b):
+        return right_stage(x_chan, squares, gain_local[b], rights[b], seq_count)
+
+    def exchange_seq(mix):
+        return lax.all_to_all(mix, "seq", split_axis=0, concat_axis=0, tiled=True)
+
+    def mix_left(cols, b):
+        out = left_stage(lefts[b], cols.reshape(p_count * j_dev, BLK))
+        return out.reshape(p_count, j_dev, BLK)
+
+    def exchange_all(cols):
+        out = lax.all_to_all(cols, everyone, split_axis=0, concat_axis=0, tiled=True)
+        return out.reshape(seq_count, n_blk, j_dev, BLK)
+
+    mix = mix_right(x_own, squares, 0)
+    mix, left_own, gate_map_one, out_one = tie((mix, left_blocks[0], gate_map_one, out_one))
+    cols = exchange_seq(mix)
+    lefts = by_block(left_own)
+    received = by_distance(sends)
+    out_map_one = channel_map(out_one, out_sec[0], n_blk)
+
+    cols = mix_left(cols, 0)
+    cols, received, out_map_one, gate_two, out_two, head_own = tie(
+        (cols, received, out_map_one, gate_two, out_two, head[0])
+    )
+    seq_out = exchange_all(cols)
+    x_tok, normed = token_stage(received, gains[0], z_scalar)
+    gate = gate_stage(normed, gate_map_one)
+    gate_map_two = channel_map(gate_two, gate_sec[1], n_blk)
+    out_map_two = channel_map(out_two, out_sec[1], n_blk)
+    heads = by_block(head_own)
+    packed, normed = out_stage(seq_out, gate, x_tok, out_map_one, gain=gains[1])
+
+    rows_one = jnp.transpose(packed[:, :tokens:STRIDE], (1, 0, 2)).reshape(-1, D)
+    chan_one = lax.all_to_all(packed, "tensor", split_axis=0, concat_axis=0, tiled=True)
+    gate = gate_stage(normed, gate_map_two)
+    cols = exchange_seq(mix_right(chan_one, None, 1))
+    seq_out = exchange_all(mix_left(cols, 1))
+    *sends, rows_two = out_stage(seq_out, gate, packed, out_map_two, tensor_index=z_scalar)
+
+    pair = jnp.concatenate([rows_one, rows_two], axis=0)
+    near = gather_by_exchange(pair, "tensor").reshape(-1, D)
+    received = by_distance(sends)
+    scored = gather_by_exchange(near, "seq")
+    scored, received = tie((scored, received))
+    scored = scored.reshape(-1, D)
+
+    vocab_dev = head.shape[2]
     vocab_offset = lax.axis_index(everyone) * vocab_dev
-
-    def sequence_mix(x_chan, squares, b):
-        mix = right_stage(x_chan, squares, gain_local[b], rights[b], seq_count)
-        cols = lax.all_to_all(mix, "seq", split_axis=0, concat_axis=0, tiled=True)
-        col_out = left_stage(lefts[b], cols.reshape(p_count * j_dev, BLK))
-        seq_out = lax.all_to_all(
-            col_out.reshape(p_count, j_dev, BLK), everyone, split_axis=0, concat_axis=0, tiled=True
-        )
-        return seq_out.reshape(seq_count, n_blk, j_dev, BLK)
-
-    def scored_rows(result):
-        return jnp.transpose(result[:, :tokens:STRIDE], (1, 0, 2)).reshape(-1, D)
-
-    def to_channels(result):
-        return lax.all_to_all(result, "tensor", split_axis=0, concat_axis=0, tiled=True)
-
-    seq_out = sequence_mix(x_own, squares, 0)
-    x_tok, normed = token_stage(received, gains[0], z_scalar)
-    gate = gate_stage(normed, gate_maps[0])
-    packed, normed = out_stage(seq_out, gate, x_tok, out_maps[0], gains[1])
-    rows_one = scored_rows(packed)
-    chan_one = to_channels(packed)
-
-    gate = gate_stage(normed, gate_maps[1])
-    seq_out = sequence_mix(chan_one, None, 1)
-    (result,) = out_stage(seq_out, gate, packed, out_maps[1])
-    rows_two = scored_rows(result)
-
-    kept = jnp.where(first, rows_one, rows_two)
-    got = lax.ppermute(jnp.where(first, rows_two, rows_one), "section", swap)
-    pair = jnp.where(first, jnp.concatenate([kept, got]), jnp.concatenate([got, kept]))
-    near = gather_by_exchange(pair, "tensor").reshape(-1, D)
-    scored = gather_by_exchange(near, "seq").reshape(-1, D)
-    scored, result = lax.optimization_barrier((scored, result))
-    chan_two = to_channels(result)
-
-    logits = jnp.dot(scored, head_local, preferred_element_type=F32)
-    exp_sums = jnp.sum(jnp.exp(logits), axis=1)
     vocab_ids = jnp.arange(vocab_dev, dtype=jnp.int32)[None, :] + vocab_offset
-    labels = jnp.transpose(targets.reshape(2, p_count, -1), (1, 0, 2)).reshape(-1)
-    is_target = vocab_ids == labels[:, None]
-    target_part = jnp.sum(jnp.where(is_target, logits, 0.0), axis=1)
-    total = jnp.stack([exp_sums, target_part]).reshape(-1, 128)
-    total = sum_over(total, "seq", (1, 2, 3))
-    total = sum_over(total, "seq", (4, 8, 12))
-    total = sum_over(total, "tensor", (2, 4, 6))
-    total = sum_over(total, "tensor", (1,)).reshape(2, -1)
-    losses = jnp.log(total[0]) - total[1]
-    aux_losses = jnp.transpose(losses.reshape(p_count, 2, -1), (1, 0, 2)).reshape(1, 2, -1)
+    labels = jnp.where(first, targets[0], targets[1]).reshape(p_count, 1, -1)
+    labels = jnp.broadcast_to(labels, (p_count, 2, labels.shape[2]))
+    row_shape = labels.shape
+    is_target = vocab_ids == labels.reshape(-1)[:, None]
+    parts = []
+    for b in range(2):
+        logits = jnp.dot(scored, heads[b], preferred_element_type=F32)
+        exp_sums = jnp.sum(jnp.exp(logits), axis=1)
+        target_part = jnp.sum(jnp.where(is_target, logits, 0.0), axis=1)
+        parts.append(jnp.stack([exp_sums, target_part]))
+    row_block = lax.broadcasted_iota(jnp.int32, row_shape, 1).reshape(1, -1)
+    parts = jnp.where(row_block == 0, parts[0], parts[1]).reshape(-1, 128)
+    totals = jnp.sum(gather_by_exchange(parts, everyone), axis=0).reshape(2, -1)
+    losses = (jnp.log(totals[0]) - totals[1]).reshape(row_shape)
+    losses = [losses[:, b].reshape(-1) for b in range(2)]
+    kept = jnp.where(first, losses[0], losses[1])
+    got = lax.ppermute(jnp.where(first, losses[1], losses[0]), "section", swap)
+    aux_losses = jnp.where(first, jnp.stack([kept, got]), jnp.stack([got, kept]))[None]
 
     chan_one = chan_one[:, :tokens].reshape(rows_dev * tokens, BLK)
-    chan_two = chan_two.reshape(rows_dev * tokens, BLK)
+    chan_two = place_stage(received, z_scalar).reshape(rows_dev * tokens, BLK)
     got_one = lax.ppermute(chan_one, "section", [(1, 0)])
     got_two = lax.ppermute(chan_two, "section", [(0, 1)])
     block_out = jnp.stack(

time: 338 us -> 363 us (1.074)
  blocking collectives: 104 us -> 58.9 us
  starting transfers between devices: 84.8 us -> 104 us
  Pallas kernels: 64.4 us -> 83.1 us
  waiting for transfers between devices: 55.5 us -> 68.6 us
  local copies, waits for them, and re-layouts: 11.6 us -> 22.1 us
  other arithmetic: 9.22 us -> 13.5 us
    all_to_all x3 -> x1, blocking collectives: 54 us -> 13.4 us  [gather_by_exchange(): return lax.all_to_all(copies, axis, split_axis=0, concat_axis=0, tiled=True)]
    all_to_all x4 -> x6, starting transfers between devices: 27.7 us -> 63 us  [the longest x3 35.9 us: gather_by_exchange(): return lax.all_to_all(copies, axis, split_axis=0, concat_axis=0, tiled=True)]
    pallas_call x4, Pallas kernels: 22.6 us -> 42.1 us  [channel_map(): pl.pallas_call(kernel, grid=(n_blk,), in_specs=[whole((C1, C2, C2)), pl.B...]
    ppermute x18 -> x15, starting transfers between devices: 37 us -> 22 us  [the longest x14 19.4 us: by_distance(): lax.ppermute(blocks[d], 'tensor', [(i, (i + d) % n_blk) for i in range(n_...]
    all_to_all x4 -> x6, waiting for transfers between devices: 24.2 us -> 35.5 us  [the longest x3 19.3 us: gather_by_exchange(): return lax.all_to_all(copies, axis, split_axis=0, concat_axis=0, tiled=True)]
    unnamed x44 -> x86, local copies, waits for them, and re-layouts: 6.64 us -> 14.3 us
    ppermute x18 -> x15, waiting for transfers between devices: 28.1 us -> 33.1 us  [the longest x14 33.1 us: by_distance(): lax.ppermute(blocks[d], 'tensor', [(i, (i + d) % n_blk) for i in range(n_...]
    all_to_all x2, blocking collectives: 49.5 us -> 45.5 us  [the longest x1 29.5 us: body(): lax.all_to_all(packed, 'tensor', split_axis=0, concat_axis=0, tiled=True)]
  transfers between devices with their start and end apart: 31 -> 31, of which waited for: 16 -> 10; matrix products, arithmetic and copies ran while one was open for 3% -> 4% of each run, Pallas kernels for 12% -> 17%
where the time goes in v3:
time: 363 us; the launch traced here: 357 us
  starting transfers between devices  104 us (29%)
  Pallas kernels  83.1 us (23%)
  waiting for transfers between devices  68.6 us (19%)
  blocking collectives  58.9 us (16%)
  local copies, waits for them, and re-layouts  22.1 us (6%)
  other arithmetic  13.5 us (4%)
  matrix products  5.17 us (1%)
    pallas_call x4, Pallas kernels, channel_map(): pl.pallas_call(kernel, grid=(n_blk,), in_specs=[whole((C1, C2, C2)), pl.B...  42.1 us
    all_to_all x3, starting transfers between devices, gather_by_exchange(): return lax.all_to_all(copies, axis, split_axis=0, concat_axis=0, tiled=True)  35.9 us
    ppermute x14, waiting for transfers between devices, by_distance(): lax.ppermute(blocks[d], 'tensor', [(i, (i + d) % n_blk) for i in range(n_...  33.1 us
    all_to_all x1, blocking collectives, body(): lax.all_to_all(packed, 'tensor', split_axis=0, concat_axis=0, tiled=True)  29.5 us
    all_to_all x2, starting transfers between devices, exchange_all(): lax.all_to_all(cols, everyone, split_axis=0, concat_axis=0, tiled=True)  20.1 us
    ppermute x14, starting transfers between devices, by_distance(): lax.ppermute(blocks[d], 'tensor', [(i, (i + d) % n_blk) for i in range(n_...  19.4 us
    all_to_all x3, waiting for transfers between devices, gather_by_exchange(): return lax.all_to_all(copies, axis, split_axis=0, concat_axis=0, tiled=True)  19.3 us
    pallas_call x2, Pallas kernels, out_stage(): pl.pallas_call(kernel, grid=(n_blk,), in_specs=in_specs, out_specs=[whole...  17.2 us
  transfers between devices with their start and end apart: 31, of which 10 were waited for; matrix products, arithmetic and copies ran while one was open for 4% of the time, Pallas kernels for 17%

profile of v3, /device:TPU:1, one launch (start us, length us, event | category | flops | bytes accessed | tf_op | source)
XLA Modules:
  0.0 357.1 jit_solution(14678983424587725568)
XLA Ops:
  9.9 6.5 %all-to-all-start = ((f32[8,16,256]{2,1,0:T(8,128)}), f32[8,16,256]{2,1,0:T(8,128)S(1)}, u32[]{:S(2)}, u32[]{:S(2)}) async-start(f32[8,16,256]{2,1,0:T(8,128)} %broadcast_in_dim.53), calls=%async_computation | async-start | bytes 262144 | tf_op jit(solution)/shard_map/all_to_all | solution.py:43
  18.2 6.0 %all-to-all-done = f32[8,16,256]{2,1,0:T(8,128)S(1)} async-done(((f32[8,16,256]{2,1,0:T(8,128)}), f32[8,16,256]{2,1,0:T(8,128)S(1)}, u32[]{:S(2)}, u32[]{:S(2)}) %all-to-all-start) | async-done | bytes 131104 | tf_op jit(solution)/shard_map/all_to_all | solution.py:43
  26.2 10.5 %shard_map.115.map_ref = bf16[8,2048,256]{2,1,0:T(8,128)(2,1)} custom-call(bf16[32,64,64]{2,1,0:T(8,128)(2,1)S(1)} %get-tuple-element.121.first_ref, bf16[32,2048]{1,0:T(8,128)(2,1)S(1)} %get-tuple-element.125.second_ref), custom_call_target="tpu_custom_call" | custom-call | tf_op jit(solution)/shard_map/pallas_call | solution.py:156
  41.4 6.9 %all-to-all-start.1 = ((bf16[16,8,16,256]{3,2,1,0:T(8,128)(2,1)}), bf16[16,8,16,256]{3,2,1,0:T(8,128)(2,1)S(1)}, u32[]{:S(2)}, u32[]{:S(2)}) async-start(bf16[16,8,16,256]{3,2,1,0:T(8,128)(2,1)} %shard_map.114), calls=%async_computation.1 | async-start | bytes 2097152 | tf_op jit(solution)/shard_map/all_to_all | solution.py:371
  58.5 10.5 %shard_map.117.map_ref = bf16[8,2048,256]{2,1,0:T(8,128)(2,1)} custom-call(bf16[32,64,64]{2,1,0:T(8,128)(2,1)S(1)} %get-tuple-element.70.first_ref, bf16[32,2048]{1,0:T(8,128)(2,1)S(1)} %get-tuple-element.123.second_ref), custom_call_target="tpu_custom_call" | custom-call | tf_op jit(solution)/shard_map/pallas_call | solution.py:156
  78.8 7.3 %collective-permute-done.11.refs_6_ = bf16[256,256]{1,0:T(8,128)(2,1)S(1)} collective-permute-done((bf16[256,256]{1,0:T(8,128)(2,1)}, bf16[256,256]{1,0:T(8,128)(2,1)S(1)}, u32[]{:S(2)}, u32[]{:S(2)}) %collective-permute-start.11) | collective-permute-done | bytes 131104 | tf_op jit(solution)/shard_map/ppermute | solution.py:338
  89.4 11.3 %all-to-all-start.2 = ((bf16[128,16,256]{2,1,0:T(8,128)(2,1)}), bf16[128,16,256]{2,1,0:T(8,128)(2,1)S(1)}, u32[]{:S(2)}, u32[]{:S(2)}) async-start(bf16[128,16,256]{2,1,0:T(8,128)(2,1)} %bitcast.9), calls=%async_computation.2 | async-start | bytes 2097152 | tf_op jit(solution)/shard_map/all_to_all | solution.py:378
  106.0 7.4 %shard_map.119.gate_ref = f32[8,256,256]{2,1,0:T(8,128)S(1)} custom-call(bf16[256,2048]{1,0:T(8,128)(2,1)S(1)} %get-tuple-element.81.normed_ref, bf16[8,2048,256]{2,1,0:T(8,128)(2,1)} %shard_map.115.map_ref), custom_call_target="tpu_custom_call" | custom-call | tf_op jit(solution)/shard_map/pallas_call | solution.py:207
  114.7 16.2 %all-to-all-done.2 = bf16[128,16,256]{2,1,0:T(8,128)(2,1)S(1)} async-done(((bf16[128,16,256]{2,1,0:T(8,128)(2,1)}), bf16[128,16,256]{2,1,0:T(8,128)(2,1)S(1)}, u32[]{:S(2)}, u32[]{:S(2)}) %all-to-all-start.2) | async-done | bytes 1048608 | tf_op jit(solution)/shard_map/all_to_all | solution.py:378
  132.1 9.2 %shard_map.120 = (bf16[8,272,256]{2,1,0:T(8,128)(2,1)S(1)}, bf16[256,2048]{1,0:T(8,128)(2,1)S(1)}) custom-call(bf16[16,8,16,256]{3,2,1,0:T(8,128)(2,1)S(1)} %bitcast.48, f32[8,256,256]{2,1,0:T(8,128)} %copy-done.2, bf16[8,256,256]{2,1,0:T(8,128)(2,1)S(1)} %copy-done.11, bf16[8,2048,256]{2,1,0:T(8,128)(2,1)} %shard_map.117.map_ref, ...), custom_call_target="tpu_custom_call" | custom-call | tf_op jit(solution)/shard_map/pallas_call | solution.py:281
  142.4 29.5 %all_to_all.45.x_ref = bf16[8,272,256]{2,1,0:T(8,128)(2,1)S(1)} all-to-all(bf16[8,272,256]{2,1,0:T(8,128)(2,1)S(1)} %get-tuple-element.85.x_ref), channel_id=1, replica_groups=mesh['section'=2,'seq'=16,'tensor'=8] {'tensor'}, dimensions={0} | all-to-all | bytes 2228224 | tf_op jit(solution)/shard_map/all_to_all | solution.py:401
  172.3 16.1 %all_to_all.46 = bf16[16,8,16,256]{3,2,1,0:T(8,128)(2,1)S(1)} all-to-all(bf16[16,8,16,256]{3,2,1,0:T(8,128)(2,1)S(1)} %shard_map.121), channel_id=1, replica_groups=mesh['section'=2,'seq'=16,'tensor'=8] {'seq'}, dimensions={0} | all-to-all | bytes 2097152 | tf_op jit(solution)/shard_map/all_to_all | solution.py:371
  190.9 8.8 %all-to-all-start.5 = ((bf16[128,16,256]{2,1,0:T(8,128)(2,1)}), bf16[128,16,256]{2,1,0:T(8,128)(2,1)}, u32[]{:S(2)}, u32[]{:S(2)}) async-start(bf16[128,16,256]{2,1,0:T(8,128)(2,1)} %bitcast.18), calls=%async_computation.5 | async-start | bytes 2097152 | tf_op jit(solution)/shard_map/all_to_all | solution.py:378
  199.7 10.5 %shard_map.123.map_ref = bf16[8,2048,256]{2,1,0:T(8,128)(2,1)} custom-call(bf16[32,64,64]{2,1,0:T(8,128)(2,1)S(1)} %copy-done.6, bf16[32,2048]{1,0:T(8,128)(2,1)S(1)} %get-tuple-element.124.second_ref), custom_call_target="tpu_custom_call" | custom-call | tf_op jit(solution)/shard_map/pallas_call | solution.py:156
  210.2 10.5 %shard_map.125.map_ref = bf16[8,2048,256]{2,1,0:T(8,128)(2,1)} custom-call(bf16[32,64,64]{2,1,0:T(8,128)(2,1)S(1)} %copy-done.7, bf16[32,2048]{1,0:T(8,128)(2,1)S(1)} %get-tuple-element.122.second_ref), custom_call_target="tpu_custom_call" | custom-call | tf_op jit(solution)/shard_map/pallas_call | solution.py:156
  222.1 7.4 %shard_map.124.gate_ref = f32[8,256,256]{2,1,0:T(8,128)S(1)} custom-call(bf16[256,2048]{1,0:T(8,128)(2,1)S(1)} %copy-done.9, bf16[8,2048,256]{2,1,0:T(8,128)(2,1)} %shard_map.123.map_ref), custom_call_target="tpu_custom_call" | custom-call | tf_op jit(solution)/shard_map/pallas_call | solution.py:207
  230.8 8.0 %shard_map.126 = (bf16[256,256]{1,0:T(8,128)(2,1)S(1)}, bf16[256,256]{1,0:T(8,128)(2,1)S(1)}, bf16[256,256]{1,0:T(8,128)(2,1)S(1)}, bf16[256,256]{1,0:T(8,128)(2...) custom-call(bf16[16,8,16,256]{3,2,1,0:T(8,128)(2,1)} %bitcast.19.seq, ...), custom_call_target="tpu_custom_call" | custom-call | tf_op jit(solution)/shard_map/pallas_call | solution.py:281
  242.8 13.4 %all_to_all.47 = bf16[8,4,2048]{2,1,0:T(4,128)(2,1)S(1)} all-to-all(bf16[8,4,2048]{2,1,0:T(4,128)(2,1)S(1)} %broadcast_in_dim.54), channel_id=1, replica_groups=mesh['section'=2,'seq'=16,'tensor'=8] {'tensor'}, dimensions={0} | all-to-all | bytes 262144 | tf_op jit(solution)/shard_map/all_to_all | solution.py:43
  257.8 16.0 %all-to-all-start.7 = ((bf16[16,32,2048]{2,1,0:T(8,128)(2,1)}), bf16[16,32,2048]{2,1,0:T(8,128)(2,1)}, u32[]{:S(2)}, u32[]{:S(2)}) async-start(bf16[16,32,2048]{2,1,0:T(8,128)(2,1)} %broadcast_in_dim.56), calls=%async_computation.7 | async-start | bytes 4194304 | tf_op jit(solution)/shard_map/all_to_all | solution.py:43
  273.8 5.7 %collective-permute-start.23 = (bf16[2048,256]{1,0:T(8,128)(2,1)}, bf16[2048,256]{1,0:T(8,128)(2,1)}, u32[]{:S(2)}, u32[]{:S(2)}) collective-permute-start(bf16[2048,256]{1,0:T(8,128)(2,1)} %bitcast.66), channel_id=1, source_target_pairs={{0,128},{128,0},{1,129},{129,1},{2,130},{130,2},{3,131},{131,3},{4... | collective-permute-start | bytes 3145736 | tf_op jit(solution)/shard_map/ppermute | solution.py:333
  289.0 12.5 %collective-permute-done.16.refs_3_ = bf16[256,256]{1,0:T(8,128)(2,1)S(1)} collective-permute-done((bf16[256,256]{1,0:T(8,128)(2,1)S(1)}, bf16[256,256]{1,0:T(8,128)(2,1)S(1)}, u32[]{:S(2)}, u32[]{:S(2)}) %collective-permute-start.16) | collective-permute-done | bytes 131104 | tf_op jit(solution)/shard_map/ppermute | solution.py:338
  315.3 13.5 %all-to-all-start.8 = ((f32[128,8,128]{2,1,0:T(8,128)}), f32[128,8,128]{2,1,0:T(8,128)}, u32[]{:S(2)}, u32[]{:S(2)}) async-start(f32[128,8,128]{2,1,0:T(8,128)} %broadcast_in_dim.62), calls=%async_computation.8 | async-start | bytes 1048576 | tf_op jit(solution)/shard_map/all_to_all | solution.py:43
  328.9 4.0 %collective-permute-start.22 = (bf16[2048,256]{1,0:T(8,128)(2,1)S(1)}, bf16[2048,256]{1,0:T(8,128)(2,1)}, u32[]{:S(2)}, u32[]{:S(2)}) collective-permute-start(bf16[2048,256]{1,0:T(8,128)(2,1)S(1)} %bitcast.49), channel_id=1, source_target_pairs={{128,0},{129,1},{130,2},{131,3},{132,4},{133,5},{134,6},{135,7},{1... | collective-permute-start | bytes 3145736 | tf_op jit(solution)/shard_map/ppermute | solution.py:438
  334.2 13.3 %all-to-all-done.8 = f32[128,8,128]{2,1,0:T(8,128)} async-done(((f32[128,8,128]{2,1,0:T(8,128)}), f32[128,8,128]{2,1,0:T(8,128)}, u32[]{:S(2)}, u32[]{:S(2)}) %all-to-all-start.8) | async-done | bytes 524320 | tf_op jit(solution)/shard_map/all_to_all | solution.py:43
  (192 shorter events, 94.7 us)
Async XLA Ops:
  7.6 9.7 %collective-permute-start.3 = (bf16[32,2048]{1,0:T(8,128)(2,1)S(1)}, bf16[32,2048]{1,0:T(8,128)(2,1)}, u32[]{:S(2)}, u32[]{:S(2)}) collective-permute-start(bf16[32,2048]{1,0:T(8,128)(2,1)S(1)} %reshape.192), channel_id=1, source_target_pairs={{0,128},{128,0},{1,129},{129,1},{2,130},{130,2},{3,131},{131,3},{4... | collective-permute-start | bytes 393224 | tf_op jit(solution)/shard_map/ppermute | solution.py:333
  9.2 29.6 %collective-permute-start.1 = (bf16[8,256,256]{2,1,0:T(8,128)(2,1)}, bf16[8,256,256]{2,1,0:T(8,128)(2,1)S(1)}, u32[]{:S(2)}, u32[]{:S(2)}) collective-permute-start(bf16[8,256,256]{2,1,0:T(8,128)(2,1)} %bitcast.50), channel_id=1, source_target_pairs={{0,128},{128,0},{1,129},{129,1},{2,130},{130,2},{3,131},{131,3},{4... | collective-permute-start | bytes 3145736 | tf_op jit(solution)/shard_map/ppermute | solution.py:333
  9.9 14.3 %all-to-all-start = ((f32[8,16,256]{2,1,0:T(8,128)}), f32[8,16,256]{2,1,0:T(8,128)S(1)}, u32[]{:S(2)}, u32[]{:S(2)}) async-start(f32[8,16,256]{2,1,0:T(8,128)} %broadcast_in_dim.53), calls=%async_computation | async-start | bytes 262144 | tf_op jit(solution)/shard_map/all_to_all | solution.py:43
  17.2 19.6 %collective-permute-start.4 = (bf16[32,64,64]{2,1,0:T(8,128)(2,1)}, bf16[32,64,64]{2,1,0:T(8,128)(2,1)}, u32[]{:S(2)}, u32[]{:S(2)}) collective-permute-start(bf16[32,64,64]{2,1,0:T(8,128)(2,1)} %bitcast.53), channel_id=1, source_target_pairs={{0,128},{128,0},{1,129},{129,1},{2,130},{130,2},{3,131},{131,3},{4... | collective-permute-start | bytes 786440 | tf_op jit(solution)/shard_map/ppermute | solution.py:333
  41.4 32.0 %all-to-all-start.1 = ((bf16[16,8,16,256]{3,2,1,0:T(8,128)(2,1)}), bf16[16,8,16,256]{3,2,1,0:T(8,128)(2,1)S(1)}, u32[]{:S(2)}, u32[]{:S(2)}) async-start(bf16[16,8,16,256]{3,2,1,0:T(8,128)(2,1)} %shard_map.114), calls=%async_computation.1 | async-start | bytes 2097152 | tf_op jit(solution)/shard_map/all_to_all | solution.py:371
  51.8 20.8 %collective-permute-start.5 = (bf16[16,128,128]{2,1,0:T(8,128)(2,1)S(1)}, bf16[16,128,128]{2,1,0:T(8,128)(2,1)S(1)}, u32[]{:S(2)}, u32[]{:S(2)}) collective-permute-start(bf16[16,128,128]{2,1,0:T(8,128)(2,1)S(1)} %bitcast.55), channel_id=1, source_target_pairs={{0,128},{128,0},{1,129},{129,1},{2,130},{130,2},{3,131},{131,3},{4... | collective-permute-start | bytes 1572872 | tf_op jit(solution)/shard_map/ppermute | solution.py:333
  51.8 17.2 %collective-permute-start.6 = (bf16[256,256]{1,0:T(8,128)(2,1)S(1)}, bf16[256,256]{1,0:T(8,128)(2,1)S(1)}, u32[]{:S(2)}, u32[]{:S(2)}) collective-permute-start(bf16[256,256]{1,0:T(8,128)(2,1)S(1)} %get-tuple-element.63), channel_id=1, source_target_pairs={{0,1},{1,2},{2,3},{3,4},{4,5},{5,6},{6,7},{7,0},{8,9},{9,10},{10,1... | collective-permute-start | bytes 393224 | tf_op jit(solution)/shard_map/ppermute | solution.py:338
  52.1 18.2 %collective-permute-start.7 = (bf16[256,256]{1,0:T(8,128)(2,1)S(1)}, bf16[256,256]{1,0:T(8,128)(2,1)S(1)}, u32[]{:S(2)}, u32[]{:S(2)}) collective-permute-start(bf16[256,256]{1,0:T(8,128)(2,1)S(1)} %get-tuple-element.64), channel_id=1, source_target_pairs={{0,2},{1,3},{2,4},{3,5},{4,6},{5,7},{6,0},{7,1},{8,10},{9,11},{10,... | collective-permute-start | bytes 393224 | tf_op jit(solution)/shard_map/ppermute | solution.py:338
  52.2 23.7 %collective-permute-start.8 = (bf16[256,256]{1,0:T(8,128)(2,1)}, bf16[256,256]{1,0:T(8,128)(2,1)S(1)}, u32[]{:S(2)}, u32[]{:S(2)}) collective-permute-start(bf16[256,256]{1,0:T(8,128)(2,1)} %get-tuple-element.65), channel_id=1, source_target_pairs={{0,3},{1,4},{2,5},{3,6},{4,7},{5,0},{6,1},{7,2},{8,11},{9,12},{10,... | collective-permute-start | bytes 393224 | tf_op jit(solution)/shard_map/ppermute | solution.py:338
  54.3 21.6 %collective-permute-start.9 = (bf16[256,256]{1,0:T(8,128)(2,1)}, bf16[256,256]{1,0:T(8,128)(2,1)S(1)}, u32[]{:S(2)}, u32[]{:S(2)}) collective-permute-start(bf16[256,256]{1,0:T(8,128)(2,1)} %get-tuple-element.66), channel_id=1, source_target_pairs={{0,4},{1,5},{2,6},{3,7},{4,0},{5,1},{6,2},{7,3},{8,12},{9,13},{10,... | collective-permute-start | bytes 393224 | tf_op jit(solution)/shard_map/ppermute | solution.py:338
  69.0 9.8 %collective-permute-start.10 = (bf16[256,256]{1,0:T(8,128)(2,1)}, bf16[256,256]{1,0:T(8,128)(2,1)S(1)}, u32[]{:S(2)}, u32[]{:S(2)}) collective-permute-start(bf16[256,256]{1,0:T(8,128)(2,1)} %get-tuple-element.67), channel_id=1, source_target_pairs={{0,5},{1,6},{2,7},{3,0},{4,1},{5,2},{6,3},{7,4},{8,13},{9,14},{10,... | collective-permute-start | bytes 393224 | tf_op jit(solution)/shard_map/ppermute | solution.py:338
  70.3 15.8 %collective-permute-start.11 = (bf16[256,256]{1,0:T(8,128)(2,1)}, bf16[256,256]{1,0:T(8,128)(2,1)S(1)}, u32[]{:S(2)}, u32[]{:S(2)}) collective-permute-start(bf16[256,256]{1,0:T(8,128)(2,1)} %get-tuple-element.68), channel_id=1, source_target_pairs={{0,6},{1,7},{2,0},{3,1},{4,2},{5,3},{6,4},{7,5},{8,14},{9,15},{10,... | collective-permute-start | bytes 393224 | tf_op jit(solution)/shard_map/ppermute | solution.py:338
  72.6 16.8 %collective-permute-start.12 = (bf16[256,256]{1,0:T(8,128)(2,1)S(1)}, bf16[256,256]{1,0:T(8,128)(2,1)S(1)}, u32[]{:S(2)}, u32[]{:S(2)}) collective-permute-start(bf16[256,256]{1,0:T(8,128)(2,1)S(1)} %get-tuple-element.69), channel_id=1, source_target_pairs={{0,7},{1,0},{2,1},{3,2},{4,3},{5,4},{6,5},{7,6},{8,15},{9,8},{10,9... | collective-permute-start | bytes 393224 | tf_op jit(solution)/shard_map/ppermute | solution.py:338
  89.4 41.5 %all-to-all-start.2 = ((bf16[128,16,256]{2,1,0:T(8,128)(2,1)}), bf16[128,16,256]{2,1,0:T(8,128)(2,1)S(1)}, u32[]{:S(2)}, u32[]{:S(2)}) async-start(bf16[128,16,256]{2,1,0:T(8,128)(2,1)} %bitcast.9), calls=%async_computation.2 | async-start | bytes 2097152 | tf_op jit(solution)/shard_map/all_to_all | solution.py:378
  190.9 38.6 %all-to-all-start.5 = ((bf16[128,16,256]{2,1,0:T(8,128)(2,1)}), bf16[128,16,256]{2,1,0:T(8,128)(2,1)}, u32[]{:S(2)}, u32[]{:S(2)}) async-start(bf16[128,16,256]{2,1,0:T(8,128)(2,1)} %bitcast.18), calls=%async_computation.5 | async-start | bytes 2097152 | tf_op jit(solution)/shard_map/all_to_all | solution.py:378
  257.8 51.3 %all-to-all-start.7 = ((bf16[16,32,2048]{2,1,0:T(8,128)(2,1)}), bf16[16,32,2048]{2,1,0:T(8,128)(2,1)}, u32[]{:S(2)}, u32[]{:S(2)}) async-start(bf16[16,32,2048]{2,1,0:T(8,128)(2,1)} %broadcast_in_dim.56), calls=%async_computation.7 | async-start | bytes 4194304 | tf_op jit(solution)/shard_map/all_to_all | solution.py:43
  273.8 35.3 %collective-permute-start.23 = (bf16[2048,256]{1,0:T(8,128)(2,1)}, bf16[2048,256]{1,0:T(8,128)(2,1)}, u32[]{:S(2)}, u32[]{:S(2)}) collective-permute-start(bf16[2048,256]{1,0:T(8,128)(2,1)} %bitcast.66), channel_id=1, source_target_pairs={{0,128},{128,0},{1,129},{129,1},{2,130},{130,2},{3,131},{131,3},{4... | collective-permute-start | bytes 3145736 | tf_op jit(solution)/shard_map/ppermute | solution.py:333
  279.8 21.7 %collective-permute-start.16 = (bf16[256,256]{1,0:T(8,128)(2,1)S(1)}, bf16[256,256]{1,0:T(8,128)(2,1)S(1)}, u32[]{:S(2)}, u32[]{:S(2)}) collective-permute-start(bf16[256,256]{1,0:T(8,128)(2,1)S(1)} %copy-done.27), channel_id=1, source_target_pairs={{0,3},{1,4},{2,5},{3,6},{4,7},{5,0},{6,1},{7,2},{8,11},{9,12},{10,... | collective-permute-start | bytes 393224 | tf_op jit(solution)/shard_map/ppermute | solution.py:338
  282.0 23.1 %collective-permute-start.17 = (bf16[256,256]{1,0:T(8,128)(2,1)S(1)}, bf16[256,256]{1,0:T(8,128)(2,1)S(1)}, u32[]{:S(2)}, u32[]{:S(2)}) collective-permute-start(bf16[256,256]{1,0:T(8,128)(2,1)S(1)} %copy-done.25), channel_id=1, source_target_pairs={{0,4},{1,5},{2,6},{3,7},{4,0},{5,1},{6,2},{7,3},{8,12},{9,13},{10,... | collective-permute-start | bytes 393224 | tf_op jit(solution)/shard_map/ppermute | solution.py:338
  288.5 16.6 %collective-permute-start.18 = (bf16[256,256]{1,0:T(8,128)(2,1)S(1)}, bf16[256,256]{1,0:T(8,128)(2,1)S(1)}, u32[]{:S(2)}, u32[]{:S(2)}) collective-permute-start(bf16[256,256]{1,0:T(8,128)(2,1)S(1)} %copy-done.23), channel_id=1, source_target_pairs={{0,5},{1,6},{2,7},{3,0},{4,1},{5,2},{6,3},{7,4},{8,13},{9,14},{10,... | collective-permute-start | bytes 393224 | tf_op jit(solution)/shard_map/ppermute | solution.py:338
  288.5 18.2 %collective-permute-start.19 = (bf16[256,256]{1,0:T(8,128)(2,1)S(1)}, bf16[256,256]{1,0:T(8,128)(2,1)S(1)}, u32[]{:S(2)}, u32[]{:S(2)}) collective-permute-start(bf16[256,256]{1,0:T(8,128)(2,1)S(1)} %copy-done.21), channel_id=1, source_target_pairs={{0,6},{1,7},{2,0},{3,1},{4,2},{5,3},{6,4},{7,5},{8,14},{9,15},{10,... | collective-permute-start | bytes 393224 | tf_op jit(solution)/shard_map/ppermute | solution.py:338
  315.3 32.2 %all-to-all-start.8 = ((f32[128,8,128]{2,1,0:T(8,128)}), f32[128,8,128]{2,1,0:T(8,128)}, u32[]{:S(2)}, u32[]{:S(2)}) async-start(f32[128,8,128]{2,1,0:T(8,128)} %broadcast_in_dim.62), calls=%async_computation.8 | async-start | bytes 1048576 | tf_op jit(solution)/shard_map/all_to_all | solution.py:43
  328.9 23.2 %collective-permute-start.22 = (bf16[2048,256]{1,0:T(8,128)(2,1)S(1)}, bf16[2048,256]{1,0:T(8,128)(2,1)}, u32[]{:S(2)}, u32[]{:S(2)}) collective-permute-start(bf16[2048,256]{1,0:T(8,128)(2,1)S(1)} %bitcast.49), channel_id=1, source_target_pairs={{128,0},{129,1},{130,2},{131,3},{132,4},{133,5},{134,6},{135,7},{1... | collective-permute-start | bytes 3145736 | tf_op jit(solution)/shard_map/ppermute | solution.py:438
  332.9 21.0 %collective-permute-start.21 = (bf16[2048,256]{1,0:T(8,128)(2,1)S(1)}, bf16[2048,256]{1,0:T(8,128)(2,1)}, u32[]{:S(2)}, u32[]{:S(2)}) collective-permute-start(bf16[2048,256]{1,0:T(8,128)(2,1)S(1)} %bitcast.45), channel_id=1, source_target_pairs={{0,128},{1,129},{2,130},{3,131},{4,132},{5,133},{6,134},{7,135},{8... | collective-permute-start | bytes 3145736 | tf_op jit(solution)/shard_map/ppermute | solution.py:439
  (50 other events, 555.0 us)

commit v4 on v3

--- a/solution.py
+++ b/solution.py
@@ -91,7 +91,7 @@
         out_ref = refs[-1]
         for p in range(rows):
             if squares is None:
-                extra = x_ref[p, tokens:].astype(F32)
+                extra = x_ref[p, tokens : tokens + EXTRA].astype(F32)
                 total = extra[0:1] + extra[1:2] + extra[2:3]
             else:
                 total = refs[0][p : p + 1]
@@ -150,8 +150,8 @@
                 ).astype(BF16)
 
         for r in range(C1):
-            row = second_ref[r : r + 1]
-            out_ref[0, r * C2 : (r + 1) * C2] = spread_ref[r] * row
+            row = second_ref[r : r + 1].astype(F32)
+            out_ref[0, r * C2 : (r + 1) * C2] = (spread_ref[r].astype(F32) * row).astype(BF16)
 
     return pl.pallas_call(
         kernel,
@@ -214,16 +214,17 @@
     )(normed, gate_map)
 
 
-def out_stage(seq_out, gate, x_tok, out_map, gain=None, tensor_index=None):
+def out_stage(seq_out, gate, x_tok, out_map, gain=None):
     groups, n_blk, width, _ = seq_out.shape
     tokens = groups * width
+    height = tokens + EXTRA * (1 if gain is None else 2)
 
     def kernel(seq_ref, gate_ref, x_ref, map_ref, *refs):
         n = pl.program_id(0)
-        if gain is not None:
+        if gain is None:
+            res_ref, gated_ref = refs
+        else:
             gain_ref, res_ref, normed_ref, gated_ref = refs
-        else:
-            z_ref, *send_refs, rows_ref, res_ref, gated_ref = refs
 
         @pl.when(n == 0)
         def _():
@@ -236,16 +237,17 @@
 
         @pl.when(n == n_blk - 1)
         def _():
+            blocks = [res_ref[z, :tokens] for z in range(n_blk)]
+            place = lax.broadcasted_iota(jnp.int32, (EXTRA, BLK), 0)
+            scored = jnp.zeros((EXTRA, BLK), F32)
+            for z in range(n_blk):
+                for q in range(tokens // STRIDE):
+                    row = blocks[z][q * STRIDE : q * STRIDE + 1].astype(F32)
+                    scored = jnp.where(place == q * n_blk + z, row, scored)
+            for z in range(n_blk):
+                res_ref[z, height - EXTRA :] = scored.astype(BF16)
             if gain is None:
-                for d in range(n_blk):
-                    send_refs[d][...] = res_ref[(z_ref[0] + d) % n_blk]
-                for z in range(n_blk):
-                    for q in range(tokens // STRIDE):
-                        rows_ref[q : q + 1, z * BLK : (z + 1) * BLK] = res_ref[
-                            z, q * STRIDE : q * STRIDE + 1
-                        ]
                 return
-            blocks = [res_ref[z, :tokens] for z in range(n_blk)]
 
             def store(z, value):
                 normed_ref[:, z * BLK : (z + 1) * BLK] = value
@@ -259,7 +261,7 @@
             rest = jnp.where(row == 1, mid, jnp.where(row == 2, total - high - mid, 0.0))
             packed = jnp.where(row == 0, high, rest).astype(BF16)
             for z in range(n_blk):
-                res_ref[z, tokens:] = packed
+                res_ref[z, tokens : tokens + EXTRA] = packed
 
     in_specs = [
         whole(seq_out.shape),
@@ -268,41 +270,92 @@
         pl.BlockSpec((1, D, BLK), lambda n: (n, 0, 0)),
     ]
     operands = [seq_out, gate, x_tok, out_map]
-    scratch = [pltpu.VMEM((tokens, D), BF16)]
+    out_shape = [shape_of((n_blk, height, BLK))]
     if gain is not None:
         operands.append(gain)
         in_specs.append(whole(gain.shape))
-        out_shape = [shape_of((n_blk, tokens + EXTRA, BLK)), shape_of((tokens, D))]
-    else:
-        operands.append(tensor_index)
-        in_specs.append(scalar_spec())
-        out_shape = [shape_of((tokens, BLK))] * n_blk + [shape_of((tokens // STRIDE, D))]
-        scratch = [pltpu.VMEM((n_blk, tokens, BLK), BF16)] + scratch
+        out_shape.append(shape_of((tokens, D)))
     return pl.pallas_call(
         kernel,
         grid=(n_blk,),
         in_specs=in_specs,
         out_specs=[whole(s.shape) for s in out_shape],
         out_shape=out_shape,
-        scratch_shapes=scratch,
+        scratch_shapes=[pltpu.VMEM((tokens, D), BF16)],
         compiler_params=params(),
     )(*operands)
 
 
-def place_stage(received, tensor_index):
-    n_blk = len(received)
-    tokens = received[0].shape[0]
-
-    def kernel(z_ref, *refs):
-        for d in range(n_blk):
-            refs[n_blk][(z_ref[0] + n_blk - d) % n_blk] = refs[d][...]
-
-    return pl.pallas_call(
-        kernel,
-        in_specs=[scalar_spec()] + [whole((tokens, BLK))] * n_blk,
-        out_shape=shape_of((n_blk, tokens, BLK)),
-        compiler_params=params(),
-    )(tensor_index, *received)
+def score_stage(row_sets, heads, labels, first_column, column_step):
+    n_blk = row_sets[0].shape[0]
+    per_ring = 2 * n_blk
+    count = len(row_sets) * per_ring
+    groups, _, width = heads.shape
+
+    def kernel(first_ref, head_ref, label_ref, *refs):
+        out_ref, rows_ref, exp_ref, target_ref = refs[-4:]
+        g = pl.program_id(0)
+
+        @pl.when(g == 0)
+        def _():
+            exp_ref[...] = jnp.zeros_like(exp_ref)
+            target_ref[...] = jnp.zeros_like(target_ref)
+            for m in range(len(row_sets)):
+                for z in range(n_blk):
+                    lines = refs[m][z].astype(F32)
+                    for q in range(2):
+                        at = m * per_ring + z * 2 + q
+                        for n in range(n_blk):
+                            line = q * n_blk + n
+                            rows_ref[at : at + 1, n * BLK : (n + 1) * BLK] = lines[line : line + 1]
+
+        logits = dot(rows_ref[...].astype(BF16), head_ref[0])
+        column = lax.broadcasted_iota(jnp.int32, (count, width), 1) + (first_ref[0] + g * column_step)
+        exp_ref[...] += jnp.sum(jnp.exp(logits), axis=1, keepdims=True)
+        target_ref[...] += jnp.sum(
+            jnp.where(column == label_ref[...], logits, 0.0), axis=1, keepdims=True
+        )
+
+        @pl.when(g == groups - 1)
+        def _():
+            row = lax.broadcasted_iota(jnp.int32, (count, 128), 0)
+            lane = lax.broadcasted_iota(jnp.int32, (count, 128), 1)
+            spread = jnp.where(lane == row, exp_ref[...], 0.0)
+            spread = spread + jnp.where(lane == row + count, target_ref[...], 0.0)
+            out_ref[...] = jnp.sum(spread, axis=0, keepdims=True)
+
+    return pl.pallas_call(
+        kernel,
+        grid=(groups,),
+        in_specs=[
+            scalar_spec(),
+            pl.BlockSpec((1, D, width), lambda g: (g, 0, 0)),
+            whole(labels.shape),
+        ]
+        + [whole(r.shape) for r in row_sets],
+        out_specs=whole((1, 128)),
+        out_shape=shape_of((1, 128), F32),
+        scratch_shapes=[
+            pltpu.VMEM((count, D), F32),
+            pltpu.VMEM((count, 1), F32),
+            pltpu.VMEM((count, 1), F32),
+        ],
+        compiler_params=params(),
+    )(first_column, heads, labels, *row_sets)
+
+
+def loss_stage(parts, groups, count):
+    def kernel(parts_ref, out_ref):
+        total = jnp.sum(parts_ref[...].reshape(groups, -1, 128), axis=1)
+        losses = jnp.log(total[:, :count]) - total[:, count : 2 * count]
+        for m in range(2):
+            out_ref[m] = losses[:, m * count // 2 : (m + 1) * count // 2]
+
+    return pl.pallas_call(
+        kernel,
+        out_shape=shape_of((2, groups, count // 2), F32),
+        compiler_params=params(),
+    )(parts)
 
 
 def body(
@@ -352,20 +405,14 @@
     gain_local = by_block(norm_gain)
     shared = jnp.concatenate([squares, *gain_local, jnp.zeros((6, BLK), F32)], axis=0)
 
-    shared, gate_own, out_own, second_own = tie(
-        (shared, gate_first[0], out_first[0], (gate_second, out_second))
-    )
-    gate_one, gate_two = by_block(gate_own)
-    out_one, out_two = by_block(out_own)
-    gate_sec = by_block(rows_second(second_own[0]))
-    out_sec = by_block(rows_second(second_own[1]))
+    shared, head_own = tie((shared, head[0]))
+    heads = lax.all_gather(head_own, "seq", axis=0)
+
     shared = gather_by_exchange(shared, "tensor")
-    gate_map_one = channel_map(gate_one, gate_sec[0], n_blk)
     squares = jnp.sum(shared[:, :rows_dev], axis=0)
     gains = [shared[:, rows_dev + b][:, None, :] for b in range(2)]
-
-    def mix_right(x_chan, squares, b):
-        return right_stage(x_chan, squares, gain_local[b], rights[b], seq_count)
+    lefts = by_block(left_blocks[0])
+    received = by_distance(sends)
 
     def exchange_seq(mix):
         return lax.all_to_all(mix, "seq", split_axis=0, concat_axis=0, tiled=True)
@@ -378,63 +425,57 @@
         out = lax.all_to_all(cols, everyone, split_axis=0, concat_axis=0, tiled=True)
         return out.reshape(seq_count, n_blk, j_dev, BLK)
 
-    mix = mix_right(x_own, squares, 0)
-    mix, left_own, gate_map_one, out_one = tie((mix, left_blocks[0], gate_map_one, out_one))
+    mix = right_stage(x_own, squares, gain_local[0], rights[0], seq_count)
+    near = [1, 2, n_blk - 2, n_blk - 1]
+    mix, near_blocks, gate_own, out_own, gate_sec_own, out_sec_own = tie(
+        (mix, [received[d] for d in near], gate_first[0], out_first[0], gate_second, out_second)
+    )
+    for d, block in zip(near, near_blocks):
+        received[d] = block
     cols = exchange_seq(mix)
-    lefts = by_block(left_own)
-    received = by_distance(sends)
-    out_map_one = channel_map(out_one, out_sec[0], n_blk)
+    gate_firsts = by_block(gate_own)
+    out_firsts = by_block(out_own)
+    gate_seconds = by_block(rows_second(gate_sec_own))
+    out_seconds = by_block(rows_second(out_sec_own))
 
     cols = mix_left(cols, 0)
-    cols, received, out_map_one, gate_two, out_two, head_own = tie(
-        (cols, received, out_map_one, gate_two, out_two, head[0])
+    cols, received, gate_firsts, out_firsts, gate_seconds, out_seconds = tie(
+        (cols, received, gate_firsts, out_firsts, gate_seconds, out_seconds)
     )
     seq_out = exchange_all(cols)
     x_tok, normed = token_stage(received, gains[0], z_scalar)
-    gate = gate_stage(normed, gate_map_one)
-    gate_map_two = channel_map(gate_two, gate_sec[1], n_blk)
-    out_map_two = channel_map(out_two, out_sec[1], n_blk)
-    heads = by_block(head_own)
-    packed, normed = out_stage(seq_out, gate, x_tok, out_map_one, gain=gains[1])
-
-    rows_one = jnp.transpose(packed[:, :tokens:STRIDE], (1, 0, 2)).reshape(-1, D)
+    gate = gate_stage(normed, channel_map(gate_firsts[0], gate_seconds[0], n_blk))
+    out_map = channel_map(out_firsts[0], out_seconds[0], n_blk)
+    packed, normed = out_stage(seq_out, gate, x_tok, out_map, gain=gains[1])
+
+    packed, normed, gate_two, out_two, gate_sec, out_sec = tie(
+        (packed, normed, gate_firsts[1], out_firsts[1], gate_seconds[1], out_seconds[1])
+    )
     chan_one = lax.all_to_all(packed, "tensor", split_axis=0, concat_axis=0, tiled=True)
-    gate = gate_stage(normed, gate_map_two)
-    cols = exchange_seq(mix_right(chan_one, None, 1))
-    seq_out = exchange_all(mix_left(cols, 1))
-    *sends, rows_two = out_stage(seq_out, gate, packed, out_map_two, tensor_index=z_scalar)
-
-    pair = jnp.concatenate([rows_one, rows_two], axis=0)
-    near = gather_by_exchange(pair, "tensor").reshape(-1, D)
-    received = by_distance(sends)
-    scored = gather_by_exchange(near, "seq")
-    scored, received = tie((scored, received))
-    scored = scored.reshape(-1, D)
-
+    gate = gate_stage(normed, channel_map(gate_two, gate_sec, n_blk))
+    out_map = channel_map(out_two, out_sec, n_blk)
+    mix = right_stage(chan_one, None, gain_local[1], rights[1], seq_count)
+    mix, gate, out_map = tie((mix, gate, out_map))
+    seq_out = exchange_all(mix_left(exchange_seq(mix), 1))
+    seq_out, heads = tie((seq_out, heads))
+    (packed_two,) = out_stage(seq_out, gate, packed, out_map)
+    chan_two = lax.all_to_all(packed_two, "tensor", split_axis=0, concat_axis=0, tiled=True)
+
+    rows_one, rows_two = chan_one[:, -EXTRA:], chan_two[:, -EXTRA:]
+    kept = jnp.where(first, rows_one, rows_two)
+    got = lax.ppermute(jnp.where(first, rows_two, rows_one), "section", swap)
     vocab_dev = head.shape[2]
-    vocab_offset = lax.axis_index(everyone) * vocab_dev
-    vocab_ids = jnp.arange(vocab_dev, dtype=jnp.int32)[None, :] + vocab_offset
-    labels = jnp.where(first, targets[0], targets[1]).reshape(p_count, 1, -1)
-    labels = jnp.broadcast_to(labels, (p_count, 2, labels.shape[2]))
-    row_shape = labels.shape
-    is_target = vocab_ids == labels.reshape(-1)[:, None]
-    parts = []
-    for b in range(2):
-        logits = jnp.dot(scored, heads[b], preferred_element_type=F32)
-        exp_sums = jnp.sum(jnp.exp(logits), axis=1)
-        target_part = jnp.sum(jnp.where(is_target, logits, 0.0), axis=1)
-        parts.append(jnp.stack([exp_sums, target_part]))
-    row_block = lax.broadcasted_iota(jnp.int32, row_shape, 1).reshape(1, -1)
-    parts = jnp.where(row_block == 0, parts[0], parts[1]).reshape(-1, 128)
-    totals = jnp.sum(gather_by_exchange(parts, everyone), axis=0).reshape(2, -1)
-    losses = (jnp.log(totals[0]) - totals[1]).reshape(row_shape)
-    losses = [losses[:, b].reshape(-1) for b in range(2)]
-    kept = jnp.where(first, losses[0], losses[1])
-    got = lax.ppermute(jnp.where(first, losses[1], losses[0]), "section", swap)
-    aux_losses = jnp.where(first, jnp.stack([kept, got]), jnp.stack([got, kept]))[None]
+    labels = lax.dynamic_index_in_dim(
+        targets.reshape(2, seq_count, -1), lax.axis_index("seq"), 1, keepdims=False
+    )
+    labels = jnp.where(first, labels, labels[::-1]).reshape(-1, 1)
+    parts = score_stage((kept, got), heads, labels, z_scalar * vocab_dev, n_blk * vocab_dev)
+    parts = gather_by_exchange(parts, everyone).reshape(-1, 128)
+    losses = loss_stage(parts, seq_count, labels.shape[0])
+    aux_losses = jnp.where(first, losses, losses[::-1]).reshape(1, 2, -1)
 
     chan_one = chan_one[:, :tokens].reshape(rows_dev * tokens, BLK)
-    chan_two = place_stage(received, z_scalar).reshape(rows_dev * tokens, BLK)
+    chan_two = chan_two[:, :tokens].reshape(rows_dev * tokens, BLK)
     got_one = lax.ppermute(chan_one, "section", [(1, 0)])
     got_two = lax.ppermute(chan_two, "section", [(0, 1)])
     block_out = jnp.stack(

time: 363 us -> 319 us (0.88); the launches traced: 357 us -> 317 us
  waiting for transfers between devices: 68.6 us -> 42.4 us
  starting transfers between devices: 104 us -> 81.1 us
  Pallas kernels: 83.1 us -> 100 us
  between operations: 1.42 us -> 14.4 us
  local copies, waits for them, and re-layouts: 22.1 us -> 12.2 us
  matrix products: 5.17 us -> 0 us
  blocking collectives: 58.9 us -> 54 us
    ppermute x14 -> x7, waiting for transfers between devices: 33.1 us -> 0.87 us  [by_distance(): lax.ppermute(blocks[d], 'tensor', [(i, (i + d) % n_blk) for i in range(n_...]
    all_to_all x3 -> x2, starting transfers between devices: 35.9 us -> 12.6 us  [gather_by_exchange(): return lax.all_to_all(copies, axis, split_axis=0, concat_axis=0, tiled=True)]
    all_to_all x2 -> x1, waiting for transfers between devices: 16.2 us -> 0.01 us  [exchange_all(): lax.all_to_all(cols, everyone, split_axis=0, concat_axis=0, tiled=True)]
    all_to_all x0 -> x2, waiting for transfers between devices: none -> 14 us  [the longest x1 14 us: body(): lax.all_to_all(packed_two, 'tensor', split_axis=0, concat_axis=0, tiled=T...]
    pallas_call x1 -> x2, Pallas kernels: 0.07 us -> 14.1 us  [the longest x1 13.9 us: score_stage(): pl.pallas_call(kernel, grid=(groups,), in_specs=[scalar_spec(), pl.BlockS...]
    all_to_all x1, waiting for transfers between devices: 0.01 us -> 13.9 us  [exchange_seq(): return lax.all_to_all(mix, 'seq', split_axis=0, concat_axis=0, tiled=True)]
    all_to_all x2 -> x1, starting transfers between devices: 20.1 us -> 9.47 us  [exchange_all(): lax.all_to_all(cols, everyone, split_axis=0, concat_axis=0, tiled=True)]
    all_to_all x0 -> x2, starting transfers between devices: none -> 9.62 us  [the longest x1 5.93 us: body(): lax.all_to_all(packed, 'tensor', split_axis=0, concat_axis=0, tiled=True)]
  transfers between devices with their start and end apart: 31 -> 24, of which waited for: 10 -> 8; matrix products, arithmetic and copies ran while one was open for 4% -> 5% of each run, Pallas kernels for 17% -> 29%
where the time goes in v4:
time: 319 us; the launch traced here: 317 us
  Pallas kernels  100 us (31%)
  starting transfers between devices  81.1 us (25%)
  blocking collectives  54 us (17%)
  waiting for transfers between devices  42.4 us (13%)
  between operations  14.4 us (5%)
  other arithmetic  12.6 us (4%)
  local copies, waits for them, and re-layouts  12.2 us (4%)
    pallas_call x4, Pallas kernels, channel_map(): pl.pallas_call(kernel, grid=(n_blk,), in_specs=[whole((C1, C2, C2)), pl.B...  43.9 us
    all_to_all x1, blocking collectives, exchange_all(): lax.all_to_all(cols, everyone, split_axis=0, concat_axis=0, tiled=True)  35.4 us
    all_to_all x1, blocking collectives, exchange_seq(): return lax.all_to_all(mix, 'seq', split_axis=0, concat_axis=0, tiled=True)  18.6 us
    pallas_call x2, Pallas kernels, out_stage(): pl.pallas_call(kernel, grid=(n_blk,), in_specs=in_specs, out_specs=[whole...  18.3 us
    pallas_call x2, Pallas kernels, gate_stage(): pl.pallas_call(kernel, grid=(n_blk,), in_specs=[whole(normed.shape), pl.B...  14.9 us
    all_to_all x1, waiting for transfers between devices, body(): lax.all_to_all(packed_two, 'tensor', split_axis=0, concat_axis=0, tiled=T...  14 us
    pallas_call x1, Pallas kernels, score_stage(): pl.pallas_call(kernel, grid=(groups,), in_specs=[scalar_spec(), pl.BlockS...  13.9 us
    all_to_all x1, waiting for transfers between devices, exchange_seq(): return lax.all_to_all(mix, 'seq', split_axis=0, concat_axis=0, tiled=True)  13.9 us
  transfers between devices with their start and end apart: 24, of which 8 were waited for; matrix products, arithmetic and copies ran while one was open for 5% of the time, Pallas kernels for 29%

profile of v4, /device:TPU:1, one launch (start us, length us, event | category | flops | bytes accessed | tf_op | source)
XLA Modules:
  0.0 316.8 jit_solution(15067402677645657826)
XLA Ops:
  7.2 3.3 %collective-permute-start.1 = (f32[1,256]{1,0:T(1,128)}, f32[1,256]{1,0:T(1,128)S(1)}, u32[]{:S(2)}, u32[]{:S(2)}) collective-permute-start(f32[1,256]{1,0:T(1,128)} %param.11), channel_id=1, source_target_pairs={{0,128},{128,0},{1,129},{129,1},{2,130},{130,2},{3,131},{131,3},{4... | collective-permute-start | bytes 3080 | tf_op jit(solution)/shard_map/ppermute | solution.py:386
  15.0 6.5 %all-to-all-start = ((f32[8,16,256]{2,1,0:T(8,128)}), f32[8,16,256]{2,1,0:T(8,128)S(1)}, u32[]{:S(2)}, u32[]{:S(2)}) async-start(f32[8,16,256]{2,1,0:T(8,128)} %broadcast_in_dim.21), calls=%async_computation | async-start | bytes 262144 | tf_op jit(solution)/shard_map/all_to_all | solution.py:43
  42.5 4.9 %collective-permute-start.13 = (bf16[32,2048]{1,0:T(8,128)(2,1)S(1)}, bf16[32,2048]{1,0:T(8,128)(2,1)S(1)}, u32[]{:S(2)}, u32[]{:S(2)}) collective-permute-start(bf16[32,2048]{1,0:T(8,128)(2,1)S(1)} %reshape.62), channel_id=1, source_target_pairs={{0,128},{128,0},{1,129},{129,1},{2,130},{130,2},{3,131},{131,3},{4... | collective-permute-start | bytes 393224 | tf_op jit(solution)/shard_map/ppermute | solution.py:386
  49.8 6.8 %all-to-all-start.1 = ((bf16[16,8,16,256]{3,2,1,0:T(8,128)(2,1)}), bf16[16,8,16,256]{3,2,1,0:T(8,128)(2,1)S(1)}, u32[]{:S(2)}, u32[]{:S(2)}) async-start(bf16[16,8,16,256]{3,2,1,0:T(8,128)(2,1)} %shard_map.114), calls=%async_computation.1 | async-start | bytes 2097152 | tf_op jit(solution)/shard_map/all_to_all | solution.py:418
  62.0 13.9 %all-to-all-done.1 = bf16[16,8,16,256]{3,2,1,0:T(8,128)(2,1)S(1)} async-done(((bf16[16,8,16,256]{3,2,1,0:T(8,128)(2,1)}), bf16[16,8,16,256]{3,2,1,0:T(8,128)(2,1)S(1)}, u32[]{:S(2)}, u32[]{:S(2)}) %all-to-all-start.1) | async-done | bytes 1048608 | tf_op jit(solution)/shard_map/all_to_all | solution.py:418
  78.4 9.5 %all-to-all-start.2 = ((bf16[128,16,256]{2,1,0:T(8,128)(2,1)}), bf16[128,16,256]{2,1,0:T(8,128)(2,1)S(1)}, u32[]{:S(2)}, u32[]{:S(2)}) async-start(bf16[128,16,256]{2,1,0:T(8,128)(2,1)} %bitcast.8), calls=%async_computation.2 | async-start | bytes 2097152 | tf_op jit(solution)/shard_map/all_to_all | solution.py:425
  88.9 11.0 %shard_map.119.map_ref = bf16[8,2048,256]{2,1,0:T(8,128)(2,1)} custom-call(bf16[32,64,64]{2,1,0:T(8,128)(2,1)S(1)} %get-tuple-element.86.first_ref, bf16[32,2048]{1,0:T(8,128)(2,1)S(1)} %get-tuple-element.87.second_ref), custom_call_target="tpu_custom_call" | custom-call | tf_op jit(solution)/shard_map/pallas_call | solution.py:156
  99.9 10.9 %shard_map.117.map_ref = bf16[8,2048,256]{2,1,0:T(8,128)(2,1)} custom-call(bf16[32,64,64]{2,1,0:T(8,128)(2,1)S(1)} %copy-done.7, bf16[32,2048]{1,0:T(8,128)(2,1)S(1)} %copy-done.10), custom_call_target="tpu_custom_call" | custom-call | tf_op jit(solution)/shard_map/pallas_call | solution.py:156
  112.6 7.5 %shard_map.118.gate_ref = f32[8,256,256]{2,1,0:T(8,128)S(1)} custom-call(bf16[256,2048]{1,0:T(8,128)(2,1)S(1)} %get-tuple-element.82.normed_ref, bf16[8,2048,256]{2,1,0:T(8,128)(2,1)} %shard_map.117.map_ref), custom_call_target="tpu_custom_call" | custom-call | tf_op jit(solution)/shard_map/pallas_call | solution.py:207
  121.4 10.3 %shard_map.120 = (bf16[8,288,256]{2,1,0:T(8,128)(2,1)}, bf16[256,2048]{1,0:T(8,128)(2,1)S(1)}) custom-call(bf16[16,8,16,256]{3,2,1,0:T(8,128)(2,1)S(1)} %bitcast.44, f32[8,256,256]{2,1,0:T(8,128)} %copy-done.2, bf16[8,256,256]{2,1,0:T(8,128)(2,1)S(1)} %get-tuple-element.85.x_ref, bf16[8,2048,256]{2,1,0:T(8,128)(2,1)} %shard_map.119.map_ref, ...), custom_call_target="tpu_custom_call" | custom-call | tf_op jit(solution)/shard_map/pallas_call | solution.py:278
  132.6 5.9 %all-to-all-start.3 = ((bf16[8,288,256]{2,1,0:T(8,128)(2,1)}), bf16[8,288,256]{2,1,0:T(8,128)(2,1)S(1)}, u32[]{:S(2)}, u32[]{:S(2)}) async-start(bf16[8,288,256]{2,1,0:T(8,128)(2,1)} %get-tuple-element.94.x_ref), calls=%async_computation.3 | async-start | bytes 2359296 | tf_op jit(solution)/shard_map/all_to_all | solution.py:454
  138.6 11.0 %shard_map.124.map_ref = bf16[8,2048,256]{2,1,0:T(8,128)(2,1)} custom-call(bf16[32,64,64]{2,1,0:T(8,128)(2,1)S(1)} %get-tuple-element.98.first_ref, bf16[32,2048]{1,0:T(8,128)(2,1)S(1)} %get-tuple-element.99.second_ref), custom_call_target="tpu_custom_call" | custom-call | tf_op jit(solution)/shard_map/pallas_call | solution.py:156
  149.6 10.9 %shard_map.122.map_ref = bf16[8,2048,256]{2,1,0:T(8,128)(2,1)} custom-call(bf16[32,64,64]{2,1,0:T(8,128)(2,1)S(1)} %get-tuple-element.96.first_ref, bf16[32,2048]{1,0:T(8,128)(2,1)S(1)} %get-tuple-element.97.second_ref), custom_call_target="tpu_custom_call" | custom-call | tf_op jit(solution)/shard_map/pallas_call | solution.py:156
  160.5 7.4 %shard_map.123.gate_ref = f32[8,256,256]{2,1,0:T(8,128)S(1)} custom-call(bf16[256,2048]{1,0:T(8,128)(2,1)S(1)} %copy-done.9, bf16[8,2048,256]{2,1,0:T(8,128)(2,1)} %shard_map.122.map_ref), custom_call_target="tpu_custom_call" | custom-call | tf_op jit(solution)/shard_map/pallas_call | solution.py:207
  169.6 18.6 %all_to_all.40 = bf16[16,8,16,256]{3,2,1,0:T(8,128)(2,1)S(1)} all-to-all(bf16[16,8,16,256]{3,2,1,0:T(8,128)(2,1)S(1)} %shard_map.121), channel_id=1, replica_groups=mesh['section'=2,'seq'=16,'tensor'=8] {'seq'}, dimensions={0} | all-to-all | bytes 2097152 | tf_op jit(solution)/shard_map/all_to_all | solution.py:418
  189.8 35.4 %all_to_all.41 = bf16[128,16,256]{2,1,0:T(8,128)(2,1)} all-to-all(bf16[128,16,256]{2,1,0:T(8,128)(2,1)S(1)} %bitcast.43), channel_id=1, replica_groups=mesh['section'=2,'seq'=16,'tensor'=8] {'seq','tensor'}, dimensions={0} | all-to-all | bytes 2097152 | tf_op jit(solution)/shard_map/all_to_all | solution.py:425
  226.4 8.0 %shard_map.126 = bf16[8,272,256]{2,1,0:T(8,128)(2,1)S(1)} custom-call(bf16[16,8,16,256]{3,2,1,0:T(8,128)(2,1)S(1)} %bitcast.45, f32[8,256,256]{2,1,0:T(8,128)S(1)} %shard_map.123.gate_ref, bf16[8,288,256]{2,1,0:T(8,128)(2,1)} %get-tuple-element.94.x_ref, bf16[8,2048,256]{2,1,0:T(8,128)(2,1)} %shard_map.124.map_ref), custom_call_target="tpu_custom_call" | custom-call | tf_op jit(solution)/shard_map/pallas_call | solution.py:278
  235.4 3.7 %all-to-all-start.6 = ((bf16[8,272,256]{2,1,0:T(8,128)(2,1)}), bf16[8,272,256]{2,1,0:T(8,128)(2,1)S(1)}, u32[]{:S(2)}, u32[]{:S(2)}) async-start(bf16[8,272,256]{2,1,0:T(8,128)(2,1)} %copy-done.3), calls=%async_computation.6 | async-start | bytes 2228224 | tf_op jit(solution)/shard_map/all_to_all | solution.py:462
  239.2 10.6 %collective-permute-start.15 = (bf16[2048,256]{1,0:T(8,128)(2,1)S(1)}, bf16[2048,256]{1,0:T(8,128)(2,1)}, u32[]{:S(2)}, u32[]{:S(2)}) collective-permute-start(bf16[2048,256]{1,0:T(8,128)(2,1)S(1)} %bitcast.49), channel_id=1, source_target_pairs={{128,0},{129,1},{130,2},{131,3},{132,4},{133,5},{134,6},{135,7},{1... | collective-permute-start | bytes 3145736 | tf_op jit(solution)/shard_map/ppermute | solution.py:479
  249.9 14.0 %all-to-all-done.6 = bf16[8,272,256]{2,1,0:T(8,128)(2,1)S(1)} async-done(((bf16[8,272,256]{2,1,0:T(8,128)(2,1)}), bf16[8,272,256]{2,1,0:T(8,128)(2,1)S(1)}, u32[]{:S(2)}, u32[]{:S(2)}) %all-to-all-start.6) | async-done | bytes 1114144 | tf_op jit(solution)/shard_map/all_to_all | solution.py:462
  266.3 7.3 %collective-permute-start.16 = (bf16[8,16,256]{2,1,0:T(8,128)(2,1)S(1)}, bf16[8,16,256]{2,1,0:T(8,128)(2,1)S(1)}, u32[]{:S(2)}, u32[]{:S(2)}) collective-permute-start(bf16[8,16,256]{2,1,0:T(8,128)(2,1)S(1)} %get-tuple-element.106), channel_id=1, source_target_pairs={{0,128},{128,0},{1,129},{129,1},{2,130},{130,2},{3,131},{131,3},{4... | collective-permute-start | bytes 196616 | tf_op jit(solution)/shard_map/ppermute | solution.py:466
  274.7 13.9 %shard_map.127 = f32[1,128]{1,0:T(1,128)S(1)} custom-call(s32[1]{0:T(128)S(6)} %mul.3.first_ref, bf16[16,2048,256]{2,1,0:T(8,128)(2,1)} %bitcast.48, s32[32,1]{1,0:T(8,128)S(1)} %reshape.74.label_ref, bf16[8,16,256]{2,1,0:T(8,128)(2,1)S(1)} %get-tuple-element.107.refs_0_, bf16[8,16,256]{2,1,0:T(8,128)(2,1)S(1)} %collective-permute-done.16.refs_1_), custom_call_target="tpu_custom_call" | custom-call | tf_op jit(solution)/shard_map/pallas_call | solution.py:327
  289.3 6.2 %all-to-all-start.7 = ((f32[128,1,128]{2,1,0:T(1,128)}), f32[128,1,128]{2,1,0:T(1,128)S(1)}, u32[]{:S(2)}, u32[]{:S(2)}) async-start(f32[128,1,128]{2,1,0:T(1,128)} %broadcast_in_dim.24), calls=%async_computation.7 | async-start | bytes 131072 | tf_op jit(solution)/shard_map/all_to_all | solution.py:43
  297.9 8.3 %all-to-all-done.7 = f32[128,1,128]{2,1,0:T(1,128)S(1)} async-done(((f32[128,1,128]{2,1,0:T(1,128)}), f32[128,1,128]{2,1,0:T(1,128)S(1)}, u32[]{:S(2)}, u32[]{:S(2)}) %all-to-all-start.7) | async-done | bytes 65568 | tf_op jit(solution)/shard_map/all_to_all | solution.py:43
  (135 shorter events, 56.6 us)
Async XLA Ops:
  7.2 218.0 %all-gather.3.cloned.1.call-start = ((), (), s32[]{:S(2)}) async-start(), calls=%async_computation.8 | async-start | bytes 17825792 | tf_op jit(solution)/shard_map/all_gather | solution.py:409
  7.2 5.5 %collective-permute-start.1 = (f32[1,256]{1,0:T(1,128)}, f32[1,256]{1,0:T(1,128)S(1)}, u32[]{:S(2)}, u32[]{:S(2)}) collective-permute-start(f32[1,256]{1,0:T(1,128)} %param.11), channel_id=1, source_target_pairs={{0,128},{128,0},{1,129},{129,1},{2,130},{130,2},{3,131},{131,3},{4... | collective-permute-start | bytes 3080 | tf_op jit(solution)/shard_map/ppermute | solution.py:386
  12.8 17.2 %collective-permute-start.2 = (bf16[8,256,256]{2,1,0:T(8,128)(2,1)S(1)}, bf16[8,256,256]{2,1,0:T(8,128)(2,1)}, u32[]{:S(2)}, u32[]{:S(2)}) collective-permute-start(bf16[8,256,256]{2,1,0:T(8,128)(2,1)S(1)} %bitcast.50), channel_id=1, source_target_pairs={{0,128},{128,0},{1,129},{129,1},{2,130},{130,2},{3,131},{131,3},{4... | collective-permute-start | bytes 3145736 | tf_op jit(solution)/shard_map/ppermute | solution.py:386
  15.0 15.0 %all-to-all-start = ((f32[8,16,256]{2,1,0:T(8,128)}), f32[8,16,256]{2,1,0:T(8,128)S(1)}, u32[]{:S(2)}, u32[]{:S(2)}) async-start(f32[8,16,256]{2,1,0:T(8,128)} %broadcast_in_dim.21), calls=%async_computation | async-start | bytes 262144 | tf_op jit(solution)/shard_map/all_to_all | solution.py:43
  21.5 25.9 %collective-permute-start = (bf16[16,128,128]{2,1,0:T(8,128)(2,1)}, bf16[16,128,128]{2,1,0:T(8,128)(2,1)}, u32[]{:S(2)}, u32[]{:S(2)}) collective-permute-start(bf16[16,128,128]{2,1,0:T(8,128)(2,1)} %bitcast.52), channel_id=1, source_target_pairs={{0,128},{128,0},{1,129},{129,1},{2,130},{130,2},{3,131},{131,3},{4... | collective-permute-start | bytes 1572872 | tf_op jit(solution)/shard_map/ppermute | solution.py:386
  21.8 12.1 %collective-permute-start.3 = (bf16[256,256]{1,0:T(8,128)(2,1)S(1)}, bf16[256,256]{1,0:T(8,128)(2,1)S(1)}, u32[]{:S(2)}, u32[]{:S(2)}) collective-permute-start(bf16[256,256]{1,0:T(8,128)(2,1)S(1)} %get-tuple-element.56), channel_id=1, source_target_pairs={{0,1},{1,2},{2,3},{3,4},{4,5},{5,6},{6,7},{7,0},{8,9},{9,10},{10,1... | collective-permute-start | bytes 393224 | tf_op jit(solution)/shard_map/ppermute | solution.py:391
  23.5 11.9 %collective-permute-start.4 = (bf16[256,256]{1,0:T(8,128)(2,1)S(1)}, bf16[256,256]{1,0:T(8,128)(2,1)S(1)}, u32[]{:S(2)}, u32[]{:S(2)}) collective-permute-start(bf16[256,256]{1,0:T(8,128)(2,1)S(1)} %get-tuple-element.57), channel_id=1, source_target_pairs={{0,2},{1,3},{2,4},{3,5},{4,6},{5,7},{6,0},{7,1},{8,10},{9,11},{10,... | collective-permute-start | bytes 393224 | tf_op jit(solution)/shard_map/ppermute | solution.py:391
  25.6 12.6 %collective-permute-start.5 = (bf16[256,256]{1,0:T(8,128)(2,1)S(1)}, bf16[256,256]{1,0:T(8,128)(2,1)S(1)}, u32[]{:S(2)}, u32[]{:S(2)}) collective-permute-start(bf16[256,256]{1,0:T(8,128)(2,1)S(1)} %get-tuple-element.58), channel_id=1, source_target_pairs={{0,6},{1,7},{2,0},{3,1},{4,2},{5,3},{6,4},{7,5},{8,14},{9,15},{10,... | collective-permute-start | bytes 393224 | tf_op jit(solution)/shard_map/ppermute | solution.py:391
  30.0 11.4 %collective-permute-start.6 = (bf16[256,256]{1,0:T(8,128)(2,1)S(1)}, bf16[256,256]{1,0:T(8,128)(2,1)S(1)}, u32[]{:S(2)}, u32[]{:S(2)}) collective-permute-start(bf16[256,256]{1,0:T(8,128)(2,1)S(1)} %get-tuple-element.59), channel_id=1, source_target_pairs={{0,7},{1,0},{2,1},{3,2},{4,3},{5,4},{6,5},{7,6},{8,15},{9,8},{10,9... | collective-permute-start | bytes 393224 | tf_op jit(solution)/shard_map/ppermute | solution.py:391
  33.9 44.6 %collective-permute-start.7 = (bf16[256,256]{1,0:T(8,128)(2,1)}, bf16[256,256]{1,0:T(8,128)(2,1)}, u32[]{:S(2)}, u32[]{:S(2)}) collective-permute-start(bf16[256,256]{1,0:T(8,128)(2,1)} %get-tuple-element.64), channel_id=1, source_target_pairs={{0,3},{1,4},{2,5},{3,6},{4,7},{5,0},{6,1},{7,2},{8,11},{9,12},{10,... | collective-permute-start | bytes 393224 | tf_op jit(solution)/shard_map/ppermute | solution.py:391
  35.4 43.0 %collective-permute-start.8 = (bf16[256,256]{1,0:T(8,128)(2,1)}, bf16[256,256]{1,0:T(8,128)(2,1)}, u32[]{:S(2)}, u32[]{:S(2)}) collective-permute-start(bf16[256,256]{1,0:T(8,128)(2,1)} %get-tuple-element.65), channel_id=1, source_target_pairs={{0,4},{1,5},{2,6},{3,7},{4,0},{5,1},{6,2},{7,3},{8,12},{9,13},{10,... | collective-permute-start | bytes 393224 | tf_op jit(solution)/shard_map/ppermute | solution.py:391
  38.2 40.2 %collective-permute-start.9 = (bf16[256,256]{1,0:T(8,128)(2,1)}, bf16[256,256]{1,0:T(8,128)(2,1)}, u32[]{:S(2)}, u32[]{:S(2)}) collective-permute-start(bf16[256,256]{1,0:T(8,128)(2,1)} %get-tuple-element.66), channel_id=1, source_target_pairs={{0,5},{1,6},{2,7},{3,0},{4,1},{5,2},{6,3},{7,4},{8,13},{9,14},{10,... | collective-permute-start | bytes 393224 | tf_op jit(solution)/shard_map/ppermute | solution.py:391
  42.5 14.1 %collective-permute-start.13 = (bf16[32,2048]{1,0:T(8,128)(2,1)S(1)}, bf16[32,2048]{1,0:T(8,128)(2,1)S(1)}, u32[]{:S(2)}, u32[]{:S(2)}) collective-permute-start(bf16[32,2048]{1,0:T(8,128)(2,1)S(1)} %reshape.62), channel_id=1, source_target_pairs={{0,128},{128,0},{1,129},{129,1},{2,130},{130,2},{3,131},{131,3},{4... | collective-permute-start | bytes 393224 | tf_op jit(solution)/shard_map/ppermute | solution.py:386
  49.7 7.8 %collective-permute-start.12 = (bf16[32,2048]{1,0:T(8,128)(2,1)S(1)}, bf16[32,2048]{1,0:T(8,128)(2,1)S(1)}, u32[]{:S(2)}, u32[]{:S(2)}) collective-permute-start(bf16[32,2048]{1,0:T(8,128)(2,1)S(1)} %reshape.61), channel_id=1, source_target_pairs={{0,128},{128,0},{1,129},{129,1},{2,130},{130,2},{3,131},{131,3},{4... | collective-permute-start | bytes 393224 | tf_op jit(solution)/shard_map/ppermute | solution.py:386
  49.8 26.1 %all-to-all-start.1 = ((bf16[16,8,16,256]{3,2,1,0:T(8,128)(2,1)}), bf16[16,8,16,256]{3,2,1,0:T(8,128)(2,1)S(1)}, u32[]{:S(2)}, u32[]{:S(2)}) async-start(bf16[16,8,16,256]{3,2,1,0:T(8,128)(2,1)} %shard_map.114), calls=%async_computation.1 | async-start | bytes 2097152 | tf_op jit(solution)/shard_map/all_to_all | solution.py:418
  56.6 2.4 collective-permute-start.11
  57.5 2.5 collective-permute-start.10
  78.4 42.9 %all-to-all-start.2 = ((bf16[128,16,256]{2,1,0:T(8,128)(2,1)}), bf16[128,16,256]{2,1,0:T(8,128)(2,1)S(1)}, u32[]{:S(2)}, u32[]{:S(2)}) async-start(bf16[128,16,256]{2,1,0:T(8,128)(2,1)} %bitcast.8), calls=%async_computation.2 | async-start | bytes 2097152 | tf_op jit(solution)/shard_map/all_to_all | solution.py:425
  132.6 35.3 %all-to-all-start.3 = ((bf16[8,288,256]{2,1,0:T(8,128)(2,1)}), bf16[8,288,256]{2,1,0:T(8,128)(2,1)S(1)}, u32[]{:S(2)}, u32[]{:S(2)}) async-start(bf16[8,288,256]{2,1,0:T(8,128)(2,1)} %get-tuple-element.94.x_ref), calls=%async_computation.3 | async-start | bytes 2359296 | tf_op jit(solution)/shard_map/all_to_all | solution.py:454
  235.4 28.6 %all-to-all-start.6 = ((bf16[8,272,256]{2,1,0:T(8,128)(2,1)}), bf16[8,272,256]{2,1,0:T(8,128)(2,1)S(1)}, u32[]{:S(2)}, u32[]{:S(2)}) async-start(bf16[8,272,256]{2,1,0:T(8,128)(2,1)} %copy-done.3), calls=%async_computation.6 | async-start | bytes 2228224 | tf_op jit(solution)/shard_map/all_to_all | solution.py:462
  239.2 56.3 %collective-permute-start.15 = (bf16[2048,256]{1,0:T(8,128)(2,1)S(1)}, bf16[2048,256]{1,0:T(8,128)(2,1)}, u32[]{:S(2)}, u32[]{:S(2)}) collective-permute-start(bf16[2048,256]{1,0:T(8,128)(2,1)S(1)} %bitcast.49), channel_id=1, source_target_pairs={{128,0},{129,1},{130,2},{131,3},{132,4},{133,5},{134,6},{135,7},{1... | collective-permute-start | bytes 3145736 | tf_op jit(solution)/shard_map/ppermute | solution.py:479
  265.0 41.9 %collective-permute-start.14 = (bf16[2048,256]{1,0:T(8,128)(2,1)}, bf16[2048,256]{1,0:T(8,128)(2,1)}, u32[]{:S(2)}, u32[]{:S(2)}) collective-permute-start(bf16[2048,256]{1,0:T(8,128)(2,1)} %bitcast.19), channel_id=1, source_target_pairs={{0,128},{1,129},{2,130},{3,131},{4,132},{5,133},{6,134},{7,135},{8... | collective-permute-start | bytes 3145736 | tf_op jit(solution)/shard_map/ppermute | solution.py:480
  266.3 8.4 %collective-permute-start.16 = (bf16[8,16,256]{2,1,0:T(8,128)(2,1)S(1)}, bf16[8,16,256]{2,1,0:T(8,128)(2,1)S(1)}, u32[]{:S(2)}, u32[]{:S(2)}) collective-permute-start(bf16[8,16,256]{2,1,0:T(8,128)(2,1)S(1)} %get-tuple-element.106), channel_id=1, source_target_pairs={{0,128},{128,0},{1,129},{129,1},{2,130},{130,2},{3,131},{131,3},{4... | collective-permute-start | bytes 196616 | tf_op jit(solution)/shard_map/ppermute | solution.py:466
  289.3 16.8 %all-to-all-start.7 = ((f32[128,1,128]{2,1,0:T(1,128)}), f32[128,1,128]{2,1,0:T(1,128)S(1)}, u32[]{:S(2)}, u32[]{:S(2)}) async-start(f32[128,1,128]{2,1,0:T(1,128)} %broadcast_in_dim.24), calls=%async_computation.7 | async-start | bytes 131072 | tf_op jit(solution)/shard_map/all_to_all | solution.py:43
  (30 other events, 242.7 us)
Sparse Core Ops, SparseCore 0:
  12.9 138.0 all-gather.2

commit v5 on v4

--- a/solution.py
+++ b/solution.py
@@ -12,6 +12,7 @@
 EPS = 1e-05
 BLK = 256
 EXTRA = 16
+PER = BLK // C2
 VMEM_LIMIT = 48 * 1024 * 1024
 F32 = jnp.float32
 BF16 = jnp.bfloat16
@@ -59,42 +60,56 @@
     return total
 
 
-def split_stage(x_own, tensor_index):
+def split3(value):
+    high = value.astype(BF16).astype(F32)
+    mid = (value - high).astype(BF16).astype(F32)
+    return high, mid, value - high - mid
+
+
+def pack_stage(x_own, gains):
     rows, tokens, _ = x_own.shape
 
-    def kernel(z_ref, x_ref, squares_ref, *send_refs):
-        z = z_ref[0]
-        row = lax.broadcasted_iota(jnp.int32, (8, tokens), 0)
-        squares = jnp.zeros((8, tokens), F32)
+    def kernel(x_ref, gain_a_ref, gain_b_ref, out_ref):
+        row = lax.broadcasted_iota(jnp.int32, (rows, tokens), 0)
+        squares = jnp.zeros((rows, tokens), F32)
         for p in range(rows):
             squares = jnp.where(row == p, squares_by_lane([x_ref[p]]), squares)
-        squares_ref[...] = squares
-        for d in range(rows):
-            send_refs[d][...] = x_ref[(z + d) % rows]
-
-    outs = [shape_of((rows, tokens), F32)] + [shape_of((tokens, BLK))] * rows
-    return pl.pallas_call(
-        kernel,
-        in_specs=[scalar_spec(), whole(x_own.shape)],
-        out_shape=outs,
-        compiler_params=params(),
-    )(tensor_index, x_own)
-
-
-def right_stage(x_chan, squares, gain_local, right, groups):
+        gain_rows = jnp.zeros((rows, BLK), F32)
+        for b, gain_ref in enumerate((gain_a_ref, gain_b_ref)):
+            for part, value in enumerate(split3(gain_ref[...])):
+                gain_rows = jnp.where(row == b * 3 + part, value, gain_rows)
+        planes = jnp.concatenate([*split3(squares), gain_rows], axis=0).astype(BF16)
+        for p in range(rows):
+            out_ref[p, :tokens] = x_ref[p]
+            out_ref[p, tokens:] = planes
+
+    return pl.pallas_call(
+        kernel,
+        out_shape=shape_of((rows, tokens + 4 * rows, BLK)),
+        compiler_params=params(),
+    )(x_own, *gains)
+
+
+def right_stage(x_chan, gain_local, right, groups, shared=None):
     rows = right.shape[0]
     tokens = right.shape[1]
     width = tokens // groups
-    operands = [x_chan, gain_local, right] + ([] if squares is None else [squares])
+    operands = [x_chan, gain_local, right] + ([] if shared is None else [shared])
 
     def kernel(x_ref, gain_ref, right_ref, *refs):
         out_ref = refs[-1]
+        if shared is not None:
+            squares = jnp.zeros((rows, tokens), F32)
+            for z in range(shared.shape[0]):
+                planes = refs[0][z, tokens:].astype(F32)
+                for part in range(3):
+                    squares = squares + planes[part * rows : (part + 1) * rows]
         for p in range(rows):
-            if squares is None:
+            if shared is None:
                 extra = x_ref[p, tokens : tokens + EXTRA].astype(F32)
                 total = extra[0:1] + extra[1:2] + extra[2:3]
             else:
-                total = refs[0][p : p + 1]
+                total = squares[p : p + 1]
             scale = lax.rsqrt(total / D + EPS)
             scaled = (right_ref[p].astype(F32) * scale).astype(BF16)
             mix = dot(scaled, x_ref[p, :tokens]) * gain_ref[...]
@@ -140,14 +155,18 @@
     def kernel(first_ref, second_ref, out_ref, spread_ref):
         @pl.when(pl.program_id(0) == 0)
         def _():
-            lane = lax.broadcasted_iota(jnp.int32, (C2, BLK), 1) % C2
-            pick = (lane == lax.broadcasted_iota(jnp.int32, (C2, BLK), 0)).astype(BF16)
-
-            @pl.loop(0, C1)
-            def _(r):
-                spread_ref[r] = lax.dot_general(
-                    first_ref[r], pick, (((0,), (0,)), ((), ())), preferred_element_type=F32
+            lane = lax.broadcasted_iota(jnp.int32, (BLK, PER * BLK), 1)
+            wanted = (lane // BLK) * C2 + lane % C2
+            pick = (wanted == lax.broadcasted_iota(jnp.int32, (BLK, PER * BLK), 0)).astype(BF16)
+            for g in range(C1 // PER):
+                spread = lax.dot_general(
+                    first_ref[g * PER : (g + 1) * PER].reshape(BLK, C2),
+                    pick,
+                    (((0,), (0,)), ((), ())),
+                    preferred_element_type=F32,
                 ).astype(BF16)
+                for r in range(PER):
+                    spread_ref[g * PER + r] = spread[:, r * BLK : (r + 1) * BLK]
 
         for r in range(C1):
             row = second_ref[r : r + 1].astype(F32)
@@ -174,26 +193,20 @@
         store(n, (x.astype(F32) * scale * gain_ref[n]).astype(BF16))
 
 
-def token_stage(received, gain, tensor_index):
-    n_blk = len(received)
-    tokens = received[0].shape[0]
-
-    def kernel(z_ref, gain_ref, *refs):
-        x_ref, normed_ref = refs[n_blk:]
-        for d in range(n_blk):
-            x_ref[(z_ref[0] + n_blk - d) % n_blk] = refs[d][...]
-
+def token_stage(x_tok, gain, tokens):
+    n_blk = x_tok.shape[0]
+
+    def kernel(gain_ref, x_ref, normed_ref):
         def store(n, value):
             normed_ref[:, n * BLK : (n + 1) * BLK] = value
 
-        normalize([x_ref[n] for n in range(n_blk)], gain_ref, tokens, store)
-
-    return pl.pallas_call(
-        kernel,
-        in_specs=[scalar_spec(), whole(gain.shape)] + [whole((tokens, BLK))] * n_blk,
-        out_shape=(shape_of((n_blk, tokens, BLK)), shape_of((tokens, D))),
-        compiler_params=params(),
-    )(tensor_index, gain, *received)
+        normalize([x_ref[n, :tokens] for n in range(n_blk)], gain_ref, tokens, store)
+
+    return pl.pallas_call(
+        kernel,
+        out_shape=shape_of((tokens, D)),
+        compiler_params=params(),
+    )(gain, x_tok)
 
 
 def gate_stage(normed, gate_map):
@@ -255,10 +268,9 @@
             normalize(blocks, gain_ref, tokens, store)
             total = squares_by_lane(blocks)
             total = jnp.concatenate([total, total], axis=0)
-            high = total.astype(BF16).astype(F32)
-            mid = (total - high).astype(BF16).astype(F32)
+            high, mid, low = split3(total)
             row = lax.broadcasted_iota(jnp.int32, (EXTRA, tokens), 0)
-            rest = jnp.where(row == 1, mid, jnp.where(row == 2, total - high - mid, 0.0))
+            rest = jnp.where(row == 1, mid, jnp.where(row == 2, low, 0.0))
             packed = jnp.where(row == 0, high, rest).astype(BF16)
             for z in range(n_blk):
                 res_ref[z, tokens : tokens + EXTRA] = packed
@@ -291,6 +303,7 @@
     per_ring = 2 * n_blk
     count = len(row_sets) * per_ring
     groups, _, width = heads.shape
+    per_step = 2
 
     def kernel(first_ref, head_ref, label_ref, *refs):
         out_ref, rows_ref, exp_ref, target_ref = refs[-4:]
@@ -309,14 +322,16 @@
                             line = q * n_blk + n
                             rows_ref[at : at + 1, n * BLK : (n + 1) * BLK] = lines[line : line + 1]
 
-        logits = dot(rows_ref[...].astype(BF16), head_ref[0])
-        column = lax.broadcasted_iota(jnp.int32, (count, width), 1) + (first_ref[0] + g * column_step)
-        exp_ref[...] += jnp.sum(jnp.exp(logits), axis=1, keepdims=True)
-        target_ref[...] += jnp.sum(
-            jnp.where(column == label_ref[...], logits, 0.0), axis=1, keepdims=True
-        )
-
-        @pl.when(g == groups - 1)
+        for part in range(per_step):
+            logits = dot(rows_ref[...].astype(BF16), head_ref[part])
+            start = first_ref[0] + (g * per_step + part) * column_step
+            column = lax.broadcasted_iota(jnp.int32, (count, width), 1) + start
+            exp_ref[...] += jnp.sum(jnp.exp(logits), axis=1, keepdims=True)
+            target_ref[...] += jnp.sum(
+                jnp.where(column == label_ref[...], logits, 0.0), axis=1, keepdims=True
+            )
+
+        @pl.when(g == groups // per_step - 1)
         def _():
             row = lax.broadcasted_iota(jnp.int32, (count, 128), 0)
             lane = lax.broadcasted_iota(jnp.int32, (count, 128), 1)
@@ -326,10 +341,10 @@
 
     return pl.pallas_call(
         kernel,
-        grid=(groups,),
+        grid=(groups // per_step,),
         in_specs=[
             scalar_spec(),
-            pl.BlockSpec((1, D, width), lambda g: (g, 0, 0)),
+            pl.BlockSpec((per_step, D, width), lambda g: (g, 0, 0)),
             whole(labels.shape),
         ]
         + [whole(r.shape) for r in row_sets],
@@ -386,12 +401,6 @@
         other = lax.ppermute(own, "section", swap)
         return jnp.where(first, own, other), jnp.where(first, other, own)
 
-    def by_distance(blocks):
-        return [blocks[0]] + [
-            lax.ppermute(blocks[d], "tensor", [(i, (i + d) % n_blk) for i in range(n_blk)])
-            for d in range(1, n_blk)
-        ]
-
     def rows_second(factor):
         return jnp.transpose(factor[0], (2, 1, 0)).reshape(C1, D)
 
@@ -400,19 +409,26 @@
     x_own = lax.dynamic_index_in_dim(x_in, section, 0, keepdims=False).reshape(
         rows_dev, tokens, BLK
     )
-    squares, *sends = split_stage(x_own, z_scalar)
-    rights = by_block(right_blocks[0])
     gain_local = by_block(norm_gain)
-    shared = jnp.concatenate([squares, *gain_local, jnp.zeros((6, BLK), F32)], axis=0)
-
-    shared, head_own = tie((shared, head[0]))
-    heads = lax.all_gather(head_own, "seq", axis=0)
-
-    shared = gather_by_exchange(shared, "tensor")
-    squares = jnp.sum(shared[:, :rows_dev], axis=0)
-    gains = [shared[:, rows_dev + b][:, None, :] for b in range(2)]
-    lefts = by_block(left_blocks[0])
-    received = by_distance(sends)
+
+    packed = pack_stage(x_own, gain_local)
+    packed, *own = tie(
+        (
+            packed,
+            right_blocks[0],
+            left_blocks[0],
+            gate_first[0],
+            out_first[0],
+            gate_second,
+            out_second,
+        )
+    )
+    rights, lefts, gate_firsts, out_firsts = (by_block(w) for w in own[:4])
+    gate_seconds, out_seconds = (by_block(rows_second(w)) for w in own[4:])
+    x_tok = lax.all_to_all(packed, "tensor", split_axis=0, concat_axis=0, tiled=True)
+    gain_rows = x_tok[:, tokens + 3 * rows_dev :][:, :6].astype(F32)
+    gain_rows = jnp.sum(gain_rows.reshape(n_blk, 2, 3, BLK), axis=2)
+    gains = [gain_rows[:, b : b + 1] for b in range(2)]
 
     def exchange_seq(mix):
         return lax.all_to_all(mix, "seq", split_axis=0, concat_axis=0, tiled=True)
@@ -425,25 +441,19 @@
         out = lax.all_to_all(cols, everyone, split_axis=0, concat_axis=0, tiled=True)
         return out.reshape(seq_count, n_blk, j_dev, BLK)
 
-    mix = right_stage(x_own, squares, gain_local[0], rights[0], seq_count)
-    near = [1, 2, n_blk - 2, n_blk - 1]
-    mix, near_blocks, gate_own, out_own, gate_sec_own, out_sec_own = tie(
-        (mix, [received[d] for d in near], gate_first[0], out_first[0], gate_second, out_second)
-    )
-    for d, block in zip(near, near_blocks):
-        received[d] = block
+    mix = right_stage(x_own, gain_local[0], rights[0], seq_count, shared=x_tok)
+    mix, head_own, lefts, gate_firsts, out_firsts, gate_seconds, out_seconds = tie(
+        (mix, head[0], lefts, gate_firsts, out_firsts, gate_seconds, out_seconds)
+    )
+    heads = lax.all_gather(head_own, "seq", axis=0)
     cols = exchange_seq(mix)
-    gate_firsts = by_block(gate_own)
-    out_firsts = by_block(out_own)
-    gate_seconds = by_block(rows_second(gate_sec_own))
-    out_seconds = by_block(rows_second(out_sec_own))
 
     cols = mix_left(cols, 0)
-    cols, received, gate_firsts, out_firsts, gate_seconds, out_seconds = tie(
-        (cols, received, gate_firsts, out_firsts, gate_seconds, out_seconds)
+    cols, gate_firsts, out_firsts, gate_seconds, out_seconds = tie(
+        (cols, gate_firsts, out_firsts, gate_seconds, out_seconds)
     )
     seq_out = exchange_all(cols)
-    x_tok, normed = token_stage(received, gains[0], z_scalar)
+    normed = token_stage(x_tok, gains[0], tokens)
     gate = gate_stage(normed, channel_map(gate_firsts[0], gate_seconds[0], n_blk))
     out_map = channel_map(out_firsts[0], out_seconds[0], n_blk)
     packed, normed = out_stage(seq_out, gate, x_tok, out_map, gain=gains[1])
@@ -454,7 +464,7 @@
     chan_one = lax.all_to_all(packed, "tensor", split_axis=0, concat_axis=0, tiled=True)
     gate = gate_stage(normed, channel_map(gate_two, gate_sec, n_blk))
     out_map = channel_map(out_two, out_sec, n_blk)
-    mix = right_stage(chan_one, None, gain_local[1], rights[1], seq_count)
+    mix = right_stage(chan_one, gain_local[1], rights[1], seq_count)
     mix, gate, out_map = tie((mix, gate, out_map))
     seq_out = exchange_all(mix_left(exchange_seq(mix), 1))
     seq_out, heads = tie((seq_out, heads))

time: 319 us -> 318 us (level)
  blocking collectives: 54 us -> 90.6 us
  starting transfers between devices: 81.1 us -> 48.2 us
  Pallas kernels: 100 us -> 73.8 us
  waiting for transfers between devices: 42.4 us -> 57.3 us
  other arithmetic: 12.6 us -> 17.2 us
    all_to_all x1 -> x2, blocking collectives: 18.6 us -> 52.1 us  [exchange_seq(): return lax.all_to_all(mix, 'seq', split_axis=0, concat_axis=0, tiled=True)]
    all_to_all x1 -> x2, waiting for transfers between devices: 0.01 us -> 23.3 us  [body(): lax.all_to_all(packed, 'tensor', split_axis=0, concat_axis=0, tiled=True)]
    pallas_call x4, Pallas kernels: 43.9 us -> 24.3 us  [channel_map(): pl.pallas_call(kernel, grid=(n_blk,), in_specs=[whole((C1, C2, C2)), pl.B...]
    all_to_all x1 -> x0, waiting for transfers between devices: 13.9 us -> none  [exchange_seq(): return lax.all_to_all(mix, 'seq', split_axis=0, concat_axis=0, tiled=True)]
    ppermute x7 -> x0, starting transfers between devices: 12.1 us -> none  [by_distance(): lax.ppermute(blocks[d], 'tensor', [(i, (i + d) % n_blk) for i in range(n_...]
    all_to_all x1 -> x0, starting transfers between devices: 6.76 us -> none  [exchange_seq(): return lax.all_to_all(mix, 'seq', split_axis=0, concat_axis=0, tiled=True)]
    all_to_all x2 -> x1, starting transfers between devices: 12.6 us -> 6.16 us  [gather_by_exchange(): return lax.all_to_all(copies, axis, split_axis=0, concat_axis=0, tiled=True)]
    ppermute x7, starting transfers between devices: 11.3 us -> 5.46 us  [by_block(): other = lax.ppermute(own, 'section', swap)]
  transfers between devices with their start and end apart: 24 -> 16, of which waited for: 8 -> 8; matrix products, arithmetic and copies ran while one was open for 5% -> 6% of each run, Pallas kernels for 29% -> 20%
where the time goes in v5:
time: 318 us; the launch traced here: 316 us
  blocking collectives  90.6 us (28%)
  Pallas kernels  73.8 us (23%)
  waiting for transfers between devices  57.3 us (18%)
  starting transfers between devices  48.2 us (15%)
  other arithmetic  17.2 us (5%)
  local copies, waits for them, and re-layouts  14.8 us (5%)
  between operations  14.4 us (5%)
    all_to_all x2, blocking collectives, exchange_seq(): return lax.all_to_all(mix, 'seq', split_axis=0, concat_axis=0, tiled=True)  52.1 us
    all_to_all x1, blocking collectives, exchange_all(): lax.all_to_all(cols, everyone, split_axis=0, concat_axis=0, tiled=True)  38.5 us
    pallas_call x4, Pallas kernels, channel_map(): pl.pallas_call(kernel, grid=(n_blk,), in_specs=[whole((C1, C2, C2)), pl.B...  24.3 us
    all_to_all x2, waiting for transfers between devices, body(): lax.all_to_all(packed, 'tensor', split_axis=0, concat_axis=0, tiled=True)  23.3 us
    all_to_all x1, waiting for transfers between devices, body(): lax.all_to_all(packed_two, 'tensor', split_axis=0, concat_axis=0, tiled=T...  18.6 us
    pallas_call x2, Pallas kernels, out_stage(): pl.pallas_call(kernel, grid=(n_blk,), in_specs=in_specs, out_specs=[whole...  18.3 us
    pallas_call x2, Pallas kernels, gate_stage(): pl.pallas_call(kernel, grid=(n_blk,), in_specs=[whole(normed.shape), pl.B...  15 us
    select_n x7, other arithmetic, by_block(): return (jnp.where(first, own, other), jnp.where(first, other, own))  11.8 us
  transfers between devices with their start and end apart: 16, of which 8 were waited for; matrix products, arithmetic and copies ran while one was open for 6% of the time, Pallas kernels for 20%

profile of v5, /device:TPU:1, one launch (start us, length us, event | category | flops | bytes accessed | tf_op | source)
XLA Modules:
  0.0 316.2 jit_solution(1967602895821820838)
XLA Ops:
  14.4 6.5 %all-to-all-start = ((bf16[8,288,256]{2,1,0:T(8,128)(2,1)}), bf16[8,288,256]{2,1,0:T(8,128)(2,1)S(1)}, u32[]{:S(2)}, u32[]{:S(2)}) async-start(bf16[8,288,256]{2,1,0:T(8,128)(2,1)} %copy-done.3), calls=%async_computation | async-start | bytes 2359296 | tf_op jit(solution)/shard_map/all_to_all | solution.py:428
  37.3 15.6 %all-to-all-done.refs_0_.x_ref = bf16[8,288,256]{2,1,0:T(8,128)(2,1)S(1)} async-done(((bf16[8,288,256]{2,1,0:T(8,128)(2,1)}), bf16[8,288,256]{2,1,0:T(8,128)(2,1)S(1)}, u32[]{:S(2)}, u32[]{:S(2)}) %all-to-all-start) | async-done | bytes 1179680 | tf_op jit(solution)/shard_map/all_to_all | solution.py:428
  55.6 27.6 %all_to_all.40 = bf16[16,8,16,256]{3,2,1,0:T(8,128)(2,1)S(1)} all-to-all(bf16[16,8,16,256]{3,2,1,0:T(8,128)(2,1)} %copy-done.7), channel_id=1, replica_groups=mesh['section'=2,'seq'=16,'tensor'=8] {'seq'}, dimensions={0} | all-to-all | bytes 2097152 | tf_op jit(solution)/shard_map/all_to_all | solution.py:434
  85.8 7.9 %all-to-all-start.2 = ((bf16[128,16,256]{2,1,0:T(8,128)(2,1)}), bf16[128,16,256]{2,1,0:T(8,128)(2,1)S(1)}, u32[]{:S(2)}, u32[]{:S(2)}) async-start(bf16[128,16,256]{2,1,0:T(8,128)(2,1)} %bitcast.11), calls=%async_computation.2 | async-start | bytes 2097152 | tf_op jit(solution)/shard_map/all_to_all | solution.py:441
  94.3 6.1 %shard_map.119.map_ref = bf16[8,2048,256]{2,1,0:T(8,128)(2,1)} custom-call(bf16[32,64,64]{2,1,0:T(8,128)(2,1)S(1)} %copy-done.12, bf16[32,2048]{1,0:T(8,128)(2,1)S(1)} %get-tuple-element.64.second_ref), custom_call_target="tpu_custom_call" | custom-call | tf_op jit(solution)/shard_map/pallas_call | solution.py:175
  100.4 6.0 %shard_map.117.map_ref = bf16[8,2048,256]{2,1,0:T(8,128)(2,1)} custom-call(bf16[32,64,64]{2,1,0:T(8,128)(2,1)S(1)} %copy-done.13, bf16[32,2048]{1,0:T(8,128)(2,1)S(1)} %copy-done.16), custom_call_target="tpu_custom_call" | custom-call | tf_op jit(solution)/shard_map/pallas_call | solution.py:175
  106.4 7.4 %shard_map.118.gate_ref = f32[8,256,256]{2,1,0:T(8,128)S(1)} custom-call(bf16[256,2048]{1,0:T(8,128)(2,1)S(1)} %shard_map.116.normed_ref, bf16[8,2048,256]{2,1,0:T(8,128)(2,1)} %shard_map.117.map_ref), custom_call_target="tpu_custom_call" | custom-call | tf_op jit(solution)/shard_map/pallas_call | solution.py:220
  115.2 4.9 %all-to-all-done.2 = bf16[128,16,256]{2,1,0:T(8,128)(2,1)S(1)} async-done(((bf16[128,16,256]{2,1,0:T(8,128)(2,1)}), bf16[128,16,256]{2,1,0:T(8,128)(2,1)S(1)}, u32[]{:S(2)}, u32[]{:S(2)}) %all-to-all-start.2) | async-done | bytes 1048608 | tf_op jit(solution)/shard_map/all_to_all | solution.py:441
  120.1 10.3 %shard_map.120 = (bf16[8,288,256]{2,1,0:T(8,128)(2,1)}, bf16[256,2048]{1,0:T(8,128)(2,1)S(1)}) custom-call(bf16[16,8,16,256]{3,2,1,0:T(8,128)(2,1)S(1)} %bitcast.41, f32[8,256,256]{2,1,0:T(8,128)} %copy-done.2, bf16[8,288,256]{2,1,0:T(8,128)(2,1)S(1)} %all-to-all-done.refs_0_.x_ref, bf16[8,2048,256]{2,1,0:T(8,128)(2,1)} %shard_map.119.map_ref, ...), custom_call_target="tpu_custom_call" | custom-call | tf_op jit(solution)/shard_map/pallas_call | solution.py:290
  131.4 3.7 %all-to-all-start.3 = ((bf16[8,288,256]{2,1,0:T(8,128)(2,1)}), bf16[8,288,256]{2,1,0:T(8,128)(2,1)S(1)}, u32[]{:S(2)}, u32[]{:S(2)}) async-start(bf16[8,288,256]{2,1,0:T(8,128)(2,1)} %get-tuple-element.71.x_ref), calls=%async_computation.3 | async-start | bytes 2359296 | tf_op jit(solution)/shard_map/all_to_all | solution.py:464
  135.1 6.1 %shard_map.124.map_ref = bf16[8,2048,256]{2,1,0:T(8,128)(2,1)} custom-call(bf16[32,64,64]{2,1,0:T(8,128)(2,1)S(1)} %copy-done.10, bf16[32,2048]{1,0:T(8,128)(2,1)S(1)} %get-tuple-element.77.second_ref), custom_call_target="tpu_custom_call" | custom-call | tf_op jit(solution)/shard_map/pallas_call | solution.py:175
  141.2 6.0 %shard_map.122.map_ref = bf16[8,2048,256]{2,1,0:T(8,128)(2,1)} custom-call(bf16[32,64,64]{2,1,0:T(8,128)(2,1)S(1)} %copy-done.11, bf16[32,2048]{1,0:T(8,128)(2,1)S(1)} %get-tuple-element.75.second_ref), custom_call_target="tpu_custom_call" | custom-call | tf_op jit(solution)/shard_map/pallas_call | solution.py:175
  147.3 7.5 %shard_map.123.gate_ref = f32[8,256,256]{2,1,0:T(8,128)S(1)} custom-call(bf16[256,2048]{1,0:T(8,128)(2,1)S(1)} %copy-done.15, bf16[8,2048,256]{2,1,0:T(8,128)(2,1)} %shard_map.122.map_ref), custom_call_target="tpu_custom_call" | custom-call | tf_op jit(solution)/shard_map/pallas_call | solution.py:220
  154.8 7.7 %all-to-all-done.3.x_ref = bf16[8,288,256]{2,1,0:T(8,128)(2,1)S(1)} async-done(((bf16[8,288,256]{2,1,0:T(8,128)(2,1)}), bf16[8,288,256]{2,1,0:T(8,128)(2,1)S(1)}, u32[]{:S(2)}, u32[]{:S(2)}) %all-to-all-start.3) | async-done | bytes 1179680 | tf_op jit(solution)/shard_map/all_to_all | solution.py:464
  164.2 24.5 %all_to_all.41 = bf16[16,8,16,256]{3,2,1,0:T(8,128)(2,1)S(1)} all-to-all(bf16[16,8,16,256]{3,2,1,0:T(8,128)(2,1)S(1)} %shard_map.121), channel_id=1, replica_groups=mesh['section'=2,'seq'=16,'tensor'=8] {'seq'}, dimensions={0} | all-to-all | bytes 2097152 | tf_op jit(solution)/shard_map/all_to_all | solution.py:434
  190.1 38.5 %all_to_all.42 = bf16[128,16,256]{2,1,0:T(8,128)(2,1)} all-to-all(bf16[128,16,256]{2,1,0:T(8,128)(2,1)S(1)} %bitcast.40), channel_id=1, replica_groups=mesh['section'=2,'seq'=16,'tensor'=8] {'seq','tensor'}, dimensions={0} | all-to-all | bytes 2097152 | tf_op jit(solution)/shard_map/all_to_all | solution.py:441
  229.8 8.0 %shard_map.126 = bf16[8,272,256]{2,1,0:T(8,128)(2,1)S(1)} custom-call(bf16[16,8,16,256]{3,2,1,0:T(8,128)(2,1)S(1)} %bitcast.42, f32[8,256,256]{2,1,0:T(8,128)S(1)} %shard_map.123.gate_ref, bf16[8,288,256]{2,1,0:T(8,128)(2,1)} %get-tuple-element.71.x_ref, bf16[8,2048,256]{2,1,0:T(8,128)(2,1)} %shard_map.124.map_ref), custom_call_target="tpu_custom_call" | custom-call | tf_op jit(solution)/shard_map/pallas_call | solution.py:290
  238.8 3.7 %all-to-all-start.6 = ((bf16[8,272,256]{2,1,0:T(8,128)(2,1)}), bf16[8,272,256]{2,1,0:T(8,128)(2,1)S(1)}, u32[]{:S(2)}, u32[]{:S(2)}) async-start(bf16[8,272,256]{2,1,0:T(8,128)(2,1)} %copy-done.4), calls=%async_computation.6 | async-start | bytes 2228224 | tf_op jit(solution)/shard_map/all_to_all | solution.py:472
  242.6 7.7 %collective-permute-start.8 = (bf16[2048,256]{1,0:T(8,128)(2,1)S(1)}, bf16[2048,256]{1,0:T(8,128)(2,1)}, u32[]{:S(2)}, u32[]{:S(2)}) collective-permute-start(bf16[2048,256]{1,0:T(8,128)(2,1)S(1)} %bitcast.46), channel_id=1, source_target_pairs={{128,0},{129,1},{130,2},{131,3},{132,4},{133,5},{134,6},{135,7},{1... | collective-permute-start | bytes 3145736 | tf_op jit(solution)/shard_map/ppermute | solution.py:489
  250.4 18.6 %all-to-all-done.6 = bf16[8,272,256]{2,1,0:T(8,128)(2,1)S(1)} async-done(((bf16[8,272,256]{2,1,0:T(8,128)(2,1)}), bf16[8,272,256]{2,1,0:T(8,128)(2,1)S(1)}, u32[]{:S(2)}, u32[]{:S(2)}) %all-to-all-start.6) | async-done | bytes 1114144 | tf_op jit(solution)/shard_map/all_to_all | solution.py:472
  271.4 5.8 %collective-permute-start.9 = (bf16[8,16,256]{2,1,0:T(8,128)(2,1)S(1)}, bf16[8,16,256]{2,1,0:T(8,128)(2,1)S(1)}, u32[]{:S(2)}, u32[]{:S(2)}) collective-permute-start(bf16[8,16,256]{2,1,0:T(8,128)(2,1)S(1)} %get-tuple-element.84), channel_id=1, source_target_pairs={{0,128},{128,0},{1,129},{129,1},{2,130},{130,2},{3,131},{131,3},{4... | collective-permute-start | bytes 196616 | tf_op jit(solution)/shard_map/ppermute | solution.py:476
  278.1 9.9 %shard_map.127 = f32[1,128]{1,0:T(1,128)S(1)} custom-call(s32[1]{0:T(128)} %bitcast.23.first_ref, bf16[16,2048,256]{2,1,0:T(8,128)(2,1)} %bitcast.45, s32[32,1]{1,0:T(8,128)S(1)} %reshape.82.label_ref, bf16[8,16,256]{2,1,0:T(8,128)(2,1)S(1)} %get-tuple-element.85.refs_0_, bf16[8,16,256]{2,1,0:T(8,128)(2,1)S(1)} %collective-permute-done.9.refs_1_), custom_call_target="tpu_custom_call" | custom-call | tf_op jit(solution)/shard_map/pallas_call | solution.py:342
  288.7 6.2 %all-to-all-start.7 = ((f32[128,1,128]{2,1,0:T(1,128)}), f32[128,1,128]{2,1,0:T(1,128)S(1)}, u32[]{:S(2)}, u32[]{:S(2)}) async-start(f32[128,1,128]{2,1,0:T(1,128)} %broadcast_in_dim.13), calls=%async_computation.7 | async-start | bytes 131072 | tf_op jit(solution)/shard_map/all_to_all | solution.py:44
  297.2 8.2 %all-to-all-done.7 = f32[128,1,128]{2,1,0:T(1,128)S(1)} async-done(((f32[128,1,128]{2,1,0:T(1,128)}), f32[128,1,128]{2,1,0:T(1,128)S(1)}, u32[]{:S(2)}, u32[]{:S(2)}) %all-to-all-start.7) | async-done | bytes 65568 | tf_op jit(solution)/shard_map/all_to_all | solution.py:44
  (108 shorter events, 47.4 us)
Async XLA Ops:
  7.2 4.4 %collective-permute-start = (f32[1,256]{1,0:T(1,128)}, f32[1,256]{1,0:T(1,128)S(1)}, u32[]{:S(2)}, u32[]{:S(2)}) collective-permute-start(f32[1,256]{1,0:T(1,128)} %param.11), channel_id=1, source_target_pairs={{0,128},{128,0},{1,129},{129,1},{2,130},{130,2},{3,131},{131,3},{4... | collective-permute-start | bytes 3080 | tf_op jit(solution)/shard_map/ppermute | solution.py:401
  13.3 7.6 %copy-start.18 = (bf16[1,32,64,64]{3,2,1,0:T(8,128)(2,1)S(1)}, bf16[1,32,64,64]{3,2,1,0:T(8,128)(2,1)}, u32[]{:S(2)}) copy-start(bf16[1,32,64,64]{3,2,1,0:T(8,128)(2,1)} %param.16) | copy-start | bytes 786436
  13.7 10.5 %collective-permute-start.6 = (bf16[32,2048]{1,0:T(8,128)(2,1)S(1)}, bf16[32,2048]{1,0:T(8,128)(2,1)S(1)}, u32[]{:S(2)}, u32[]{:S(2)}) collective-permute-start(bf16[32,2048]{1,0:T(8,128)(2,1)S(1)} %reshape.64), channel_id=1, source_target_pairs={{0,128},{128,0},{1,129},{129,1},{2,130},{130,2},{3,131},{131,3},{4... | collective-permute-start | bytes 393224 | tf_op jit(solution)/shard_map/ppermute | solution.py:401
  14.3 20.0 %collective-permute-start.1 = (bf16[8,256,256]{2,1,0:T(8,128)(2,1)}, bf16[8,256,256]{2,1,0:T(8,128)(2,1)}, u32[]{:S(2)}, u32[]{:S(2)}) collective-permute-start(bf16[8,256,256]{2,1,0:T(8,128)(2,1)} %bitcast.1), channel_id=1, source_target_pairs={{0,128},{128,0},{1,129},{129,1},{2,130},{130,2},{3,131},{131,3},{4... | collective-permute-start | bytes 3145736 | tf_op jit(solution)/shard_map/ppermute | solution.py:401
  14.4 38.5 %all-to-all-start = ((bf16[8,288,256]{2,1,0:T(8,128)(2,1)}), bf16[8,288,256]{2,1,0:T(8,128)(2,1)S(1)}, u32[]{:S(2)}, u32[]{:S(2)}) async-start(bf16[8,288,256]{2,1,0:T(8,128)(2,1)} %copy-done.3), calls=%async_computation | async-start | bytes 2359296 | tf_op jit(solution)/shard_map/all_to_all | solution.py:428
  20.9 207.8 %all-gather.3.cloned.1.call-start = ((), (), s32[]{:S(2)}) async-start(), calls=%async_computation.8 | async-start | bytes 17825792 | tf_op jit(solution)/shard_map/all_gather | solution.py:448
  20.9 7.1 %collective-permute-start.4 = (bf16[32,64,64]{2,1,0:T(8,128)(2,1)S(1)}, bf16[32,64,64]{2,1,0:T(8,128)(2,1)}, u32[]{:S(2)}, u32[]{:S(2)}) collective-permute-start(bf16[32,64,64]{2,1,0:T(8,128)(2,1)S(1)} %bitcast.48), channel_id=1, source_target_pairs={{0,128},{128,0},{1,129},{129,1},{2,130},{130,2},{3,131},{131,3},{4... | collective-permute-start | bytes 786440 | tf_op jit(solution)/shard_map/ppermute | solution.py:401
  21.7 8.4 %collective-permute-start.3 = (bf16[32,64,64]{2,1,0:T(8,128)(2,1)}, bf16[32,64,64]{2,1,0:T(8,128)(2,1)}, u32[]{:S(2)}, u32[]{:S(2)}) collective-permute-start(bf16[32,64,64]{2,1,0:T(8,128)(2,1)} %bitcast.50), channel_id=1, source_target_pairs={{0,128},{128,0},{1,129},{129,1},{2,130},{130,2},{3,131},{131,3},{4... | collective-permute-start | bytes 786440 | tf_op jit(solution)/shard_map/ppermute | solution.py:401
  21.8 10.6 %collective-permute-start.2 = (bf16[16,128,128]{2,1,0:T(8,128)(2,1)}, bf16[16,128,128]{2,1,0:T(8,128)(2,1)}, u32[]{:S(2)}, u32[]{:S(2)}) collective-permute-start(bf16[16,128,128]{2,1,0:T(8,128)(2,1)} %bitcast.52), channel_id=1, source_target_pairs={{0,128},{128,0},{1,129},{129,1},{2,130},{130,2},{3,131},{131,3},{4... | collective-permute-start | bytes 1572872 | tf_op jit(solution)/shard_map/ppermute | solution.py:401
  24.8 1.6 collective-permute-start.5
  85.8 8.5 %copy-start.12 = (bf16[32,64,64]{2,1,0:T(8,128)(2,1)S(1)}, bf16[32,64,64]{2,1,0:T(8,128)(2,1)}, u32[]{:S(2)}) copy-start(bf16[32,64,64]{2,1,0:T(8,128)(2,1)} %get-tuple-element.63.first_ref) | copy-start | bytes 786436
  85.8 34.3 %all-to-all-start.2 = ((bf16[128,16,256]{2,1,0:T(8,128)(2,1)}), bf16[128,16,256]{2,1,0:T(8,128)(2,1)S(1)}, u32[]{:S(2)}, u32[]{:S(2)}) async-start(bf16[128,16,256]{2,1,0:T(8,128)(2,1)} %bitcast.11), calls=%async_computation.2 | async-start | bytes 2097152 | tf_op jit(solution)/shard_map/all_to_all | solution.py:441
  94.3 6.1 %copy-start.13 = (bf16[32,64,64]{2,1,0:T(8,128)(2,1)S(1)}, bf16[32,64,64]{2,1,0:T(8,128)(2,1)}, u32[]{:S(2)}) copy-start(bf16[32,64,64]{2,1,0:T(8,128)(2,1)} %get-tuple-element.61.first_ref) | copy-start | bytes 786436
  94.3 6.1 %copy-start.16 = (bf16[32,2048]{1,0:T(8,128)(2,1)S(1)}, bf16[32,2048]{1,0:T(8,128)(2,1)}, u32[]{:S(2)}) copy-start(bf16[32,2048]{1,0:T(8,128)(2,1)} %get-tuple-element.62.second_ref) | copy-start | bytes 393220
  131.4 31.1 %all-to-all-start.3 = ((bf16[8,288,256]{2,1,0:T(8,128)(2,1)}), bf16[8,288,256]{2,1,0:T(8,128)(2,1)S(1)}, u32[]{:S(2)}, u32[]{:S(2)}) async-start(bf16[8,288,256]{2,1,0:T(8,128)(2,1)} %get-tuple-element.71.x_ref), calls=%async_computation.3 | async-start | bytes 2359296 | tf_op jit(solution)/shard_map/all_to_all | solution.py:464
  135.1 6.1 %copy-start.11 = (bf16[32,64,64]{2,1,0:T(8,128)(2,1)S(1)}, bf16[32,64,64]{2,1,0:T(8,128)(2,1)}, u32[]{:S(2)}) copy-start(bf16[32,64,64]{2,1,0:T(8,128)(2,1)} %get-tuple-element.74.first_ref) | copy-start | bytes 786436
  141.2 6.0 %copy-start.15 = (bf16[256,2048]{1,0:T(8,128)(2,1)S(1)}, bf16[256,2048]{1,0:T(8,128)(2,1)}, u32[]{:S(2)}) copy-start(bf16[256,2048]{1,0:T(8,128)(2,1)} %copy-done.14) | copy-start | bytes 3145732
  163.7 24.9 %copy-start.9 = (bf16[16,128,128]{2,1,0:T(8,128)(2,1)S(1)}, bf16[16,128,128]{2,1,0:T(8,128)(2,1)}, u32[]{:S(2)}) copy-start(bf16[16,128,128]{2,1,0:T(8,128)(2,1)} %get-tuple-element.72.left_ref) | copy-start | bytes 1572868
  238.8 11.5 %copy-start.22 = (s32[2,256]{1,0:T(2,128)S(1)}, s32[2,256]{1,0:T(2,128)}, u32[]{:S(2)}) copy-start(s32[2,256]{1,0:T(2,128)} %param.19) | copy-start | bytes 6148
  238.8 30.2 %all-to-all-start.6 = ((bf16[8,272,256]{2,1,0:T(8,128)(2,1)}), bf16[8,272,256]{2,1,0:T(8,128)(2,1)S(1)}, u32[]{:S(2)}, u32[]{:S(2)}) async-start(bf16[8,272,256]{2,1,0:T(8,128)(2,1)} %copy-done.4), calls=%async_computation.6 | async-start | bytes 2228224 | tf_op jit(solution)/shard_map/all_to_all | solution.py:472
  242.6 52.3 %collective-permute-start.8 = (bf16[2048,256]{1,0:T(8,128)(2,1)S(1)}, bf16[2048,256]{1,0:T(8,128)(2,1)}, u32[]{:S(2)}, u32[]{:S(2)}) collective-permute-start(bf16[2048,256]{1,0:T(8,128)(2,1)S(1)} %bitcast.46), channel_id=1, source_target_pairs={{128,0},{129,1},{130,2},{131,3},{132,4},{133,5},{134,6},{135,7},{1... | collective-permute-start | bytes 3145736 | tf_op jit(solution)/shard_map/ppermute | solution.py:489
  270.1 36.3 %collective-permute-start.7 = (bf16[2048,256]{1,0:T(8,128)(2,1)}, bf16[2048,256]{1,0:T(8,128)(2,1)}, u32[]{:S(2)}, u32[]{:S(2)}) collective-permute-start(bf16[2048,256]{1,0:T(8,128)(2,1)} %bitcast.19), channel_id=1, source_target_pairs={{0,128},{1,129},{2,130},{3,131},{4,132},{5,133},{6,134},{7,135},{8... | collective-permute-start | bytes 3145736 | tf_op jit(solution)/shard_map/ppermute | solution.py:490
  271.4 6.8 %collective-permute-start.9 = (bf16[8,16,256]{2,1,0:T(8,128)(2,1)S(1)}, bf16[8,16,256]{2,1,0:T(8,128)(2,1)S(1)}, u32[]{:S(2)}, u32[]{:S(2)}) collective-permute-start(bf16[8,16,256]{2,1,0:T(8,128)(2,1)S(1)} %get-tuple-element.84), channel_id=1, source_target_pairs={{0,128},{128,0},{1,129},{129,1},{2,130},{130,2},{3,131},{131,3},{4... | collective-permute-start | bytes 196616 | tf_op jit(solution)/shard_map/ppermute | solution.py:476
  288.7 16.7 %all-to-all-start.7 = ((f32[128,1,128]{2,1,0:T(1,128)}), f32[128,1,128]{2,1,0:T(1,128)S(1)}, u32[]{:S(2)}, u32[]{:S(2)}) async-start(f32[128,1,128]{2,1,0:T(1,128)} %broadcast_in_dim.13), calls=%async_computation.7 | async-start | bytes 131072 | tf_op jit(solution)/shard_map/all_to_all | solution.py:44
  (16 other events, 32.8 us)
Sparse Core Ops, SparseCore 0:
  55.8 132.2 all-gather.2

commit v6 on v5

--- a/solution.py
+++ b/solution.py
@@ -298,77 +298,68 @@
     )(*operands)
 
 
-def score_stage(row_sets, heads, labels, first_column, column_step):
-    n_blk = row_sets[0].shape[0]
-    per_ring = 2 * n_blk
-    count = len(row_sets) * per_ring
-    groups, _, width = heads.shape
-    per_step = 2
-
-    def kernel(first_ref, head_ref, label_ref, *refs):
-        out_ref, rows_ref, exp_ref, target_ref = refs[-4:]
-        g = pl.program_id(0)
-
-        @pl.when(g == 0)
-        def _():
-            exp_ref[...] = jnp.zeros_like(exp_ref)
-            target_ref[...] = jnp.zeros_like(target_ref)
-            for m in range(len(row_sets)):
-                for z in range(n_blk):
-                    lines = refs[m][z].astype(F32)
-                    for q in range(2):
-                        at = m * per_ring + z * 2 + q
-                        for n in range(n_blk):
-                            line = q * n_blk + n
-                            rows_ref[at : at + 1, n * BLK : (n + 1) * BLK] = lines[line : line + 1]
-
-        for part in range(per_step):
-            logits = dot(rows_ref[...].astype(BF16), head_ref[part])
-            start = first_ref[0] + (g * per_step + part) * column_step
-            column = lax.broadcasted_iota(jnp.int32, (count, width), 1) + start
-            exp_ref[...] += jnp.sum(jnp.exp(logits), axis=1, keepdims=True)
-            target_ref[...] += jnp.sum(
+def score_stage(row_sets, heads, labels, places):
+    x_count = len(row_sets)
+    pairs = row_sets[0].shape[0]
+    n_blk = pairs // 2
+    per_set = 2 * pairs
+    count = x_count * per_set
+    width = heads[0].shape[1]
+
+    def kernel(place_ref, label_ref, *refs):
+        out_ref, rows_ref = refs[-2:]
+        head_refs = refs[x_count : x_count + len(heads)]
+        for d in range(x_count):
+            first_row = place_ref[d] * per_set
+            for z in range(0, pairs, 4):
+                lines = [refs[d][z + k].astype(F32) for k in range(4)]
+                group = [lines[k][q * n_blk : (q + 1) * n_blk] for k in range(4) for q in range(2)]
+                at = pl.multiple_of(first_row + 2 * z, 8)
+                for n in range(n_blk):
+                    block = jnp.concatenate([g[n : n + 1] for g in group], axis=0)
+                    rows_ref[pl.ds(at, 8), n * BLK : (n + 1) * BLK] = block
+        rows = rows_ref[...].astype(BF16)
+        exp_sum = jnp.zeros((count, 1), F32)
+        target = jnp.zeros((count, 1), F32)
+        for d, head_ref in enumerate(head_refs):
+            logits = dot(rows, head_ref[...])
+            column = lax.broadcasted_iota(jnp.int32, (count, width), 1) + place_ref[x_count + d]
+            exp_sum = exp_sum + jnp.sum(jnp.exp(logits), axis=1, keepdims=True)
+            target = target + jnp.sum(
                 jnp.where(column == label_ref[...], logits, 0.0), axis=1, keepdims=True
             )
-
-        @pl.when(g == groups // per_step - 1)
-        def _():
-            row = lax.broadcasted_iota(jnp.int32, (count, 128), 0)
-            lane = lax.broadcasted_iota(jnp.int32, (count, 128), 1)
-            spread = jnp.where(lane == row, exp_ref[...], 0.0)
-            spread = spread + jnp.where(lane == row + count, target_ref[...], 0.0)
-            out_ref[...] = jnp.sum(spread, axis=0, keepdims=True)
-
-    return pl.pallas_call(
-        kernel,
-        grid=(groups // per_step,),
-        in_specs=[
-            scalar_spec(),
-            pl.BlockSpec((per_step, D, width), lambda g: (g, 0, 0)),
-            whole(labels.shape),
-        ]
-        + [whole(r.shape) for r in row_sets],
-        out_specs=whole((1, 128)),
-        out_shape=shape_of((1, 128), F32),
-        scratch_shapes=[
-            pltpu.VMEM((count, D), F32),
-            pltpu.VMEM((count, 1), F32),
-            pltpu.VMEM((count, 1), F32),
-        ],
-        compiler_params=params(),
-    )(first_column, heads, labels, *row_sets)
-
-
-def loss_stage(parts, groups, count):
+        row = lax.broadcasted_iota(jnp.int32, (count, count), 0)
+        lane = lax.broadcasted_iota(jnp.int32, (count, count), 1)
+        out_ref[0:1] = jnp.sum(jnp.where(lane == row, exp_sum, 0.0), axis=0, keepdims=True)
+        out_ref[1:2] = jnp.sum(jnp.where(lane == row, target, 0.0), axis=0, keepdims=True)
+
+    return pl.pallas_call(
+        kernel,
+        in_specs=[scalar_spec(), whole(labels.shape)]
+        + [whole(r.shape) for r in row_sets]
+        + [whole(h.shape) for h in heads],
+        out_shape=shape_of((2, count), F32),
+        scratch_shapes=[pltpu.VMEM((count, D), F32)],
+        compiler_params=params(),
+    )(places, labels, *row_sets, *heads)
+
+
+def loss_stage(parts, x_count, y_count):
+    count = parts.shape[-1]
+    ring = count // (2 * x_count)
+
     def kernel(parts_ref, out_ref):
-        total = jnp.sum(parts_ref[...].reshape(groups, -1, 128), axis=1)
-        losses = jnp.log(total[:, :count]) - total[:, count : 2 * count]
+        by_place = parts_ref[...].reshape(x_count, y_count, -1, 2, count)
+        total = jnp.sum(jnp.sum(by_place, axis=2), axis=0)
+        losses = jnp.log(total[:, 0]) - total[:, 1]
         for m in range(2):
-            out_ref[m] = losses[:, m * count // 2 : (m + 1) * count // 2]
-
-    return pl.pallas_call(
-        kernel,
-        out_shape=shape_of((2, groups, count // 2), F32),
+            for x in range(x_count):
+                at = (x * 2 + m) * ring
+                out_ref[m, x] = losses[:, at : at + ring]
+
+    return pl.pallas_call(
+        kernel,
+        out_shape=shape_of((2, x_count, y_count, ring), F32),
         compiler_params=params(),
     )(parts)
 
@@ -390,6 +381,8 @@
     tensor_index = lax.axis_index("tensor")
     z_scalar = tensor_index.astype(jnp.int32).reshape(1)
     seq_count = lax.axis_size("seq")
+    y_count = 4
+    x_count = seq_count // y_count
     n_blk = lax.axis_size("tensor")
     everyone = ("seq", "tensor")
     swap = [(0, 1), (1, 0)]
@@ -400,6 +393,14 @@
     def by_block(own):
         other = lax.ppermute(own, "section", swap)
         return jnp.where(first, own, other), jnp.where(first, other, own)
+
+    def along_y(block, distance):
+        route = [(i, i - i % y_count + (i + distance) % y_count) for i in range(seq_count)]
+        return lax.ppermute(block, "seq", route)
+
+    def along_x(block, distance):
+        route = [(i, (i + distance * y_count) % seq_count) for i in range(seq_count)]
+        return lax.ppermute(block, "seq", route)
 
     def rows_second(factor):
         return jnp.transpose(factor[0], (2, 1, 0)).reshape(C1, D)
@@ -421,10 +422,12 @@
             out_first[0],
             gate_second,
             out_second,
+            head[0],
         )
     )
     rights, lefts, gate_firsts, out_firsts = (by_block(w) for w in own[:4])
-    gate_seconds, out_seconds = (by_block(rows_second(w)) for w in own[4:])
+    gate_seconds, out_seconds = (by_block(rows_second(w)) for w in own[4:6])
+    heads = [own[6], along_y(own[6], 1), None, along_y(own[6], 3)]
     x_tok = lax.all_to_all(packed, "tensor", split_axis=0, concat_axis=0, tiled=True)
     gain_rows = x_tok[:, tokens + 3 * rows_dev :][:, :6].astype(F32)
     gain_rows = jnp.sum(gain_rows.reshape(n_blk, 2, 3, BLK), axis=2)
@@ -442,10 +445,9 @@
         return out.reshape(seq_count, n_blk, j_dev, BLK)
 
     mix = right_stage(x_own, gain_local[0], rights[0], seq_count, shared=x_tok)
-    mix, head_own, lefts, gate_firsts, out_firsts, gate_seconds, out_seconds = tie(
-        (mix, head[0], lefts, gate_firsts, out_firsts, gate_seconds, out_seconds)
+    mix, heads[1], heads[3], lefts, gate_firsts, out_firsts, gate_seconds, out_seconds = tie(
+        (mix, heads[1], heads[3], lefts, gate_firsts, out_firsts, gate_seconds, out_seconds)
     )
-    heads = lax.all_gather(head_own, "seq", axis=0)
     cols = exchange_seq(mix)
 
     cols = mix_left(cols, 0)
@@ -458,30 +460,36 @@
     out_map = channel_map(out_firsts[0], out_seconds[0], n_blk)
     packed, normed = out_stage(seq_out, gate, x_tok, out_map, gain=gains[1])
 
-    packed, normed, gate_two, out_two, gate_sec, out_sec = tie(
-        (packed, normed, gate_firsts[1], out_firsts[1], gate_seconds[1], out_seconds[1])
+    packed, normed, heads[0], gate_two, out_two, gate_sec, out_sec = tie(
+        (packed, normed, heads[0], gate_firsts[1], out_firsts[1], gate_seconds[1], out_seconds[1])
     )
+    heads[2] = along_y(heads[0], 2)
     chan_one = lax.all_to_all(packed, "tensor", split_axis=0, concat_axis=0, tiled=True)
     gate = gate_stage(normed, channel_map(gate_two, gate_sec, n_blk))
     out_map = channel_map(out_two, out_sec, n_blk)
     mix = right_stage(chan_one, gain_local[1], rights[1], seq_count)
-    mix, gate, out_map = tie((mix, gate, out_map))
+    mix, gate, out_map, heads[2] = tie((mix, gate, out_map, heads[2]))
     seq_out = exchange_all(mix_left(exchange_seq(mix), 1))
-    seq_out, heads = tie((seq_out, heads))
     (packed_two,) = out_stage(seq_out, gate, packed, out_map)
     chan_two = lax.all_to_all(packed_two, "tensor", split_axis=0, concat_axis=0, tiled=True)
 
     rows_one, rows_two = chan_one[:, -EXTRA:], chan_two[:, -EXTRA:]
     kept = jnp.where(first, rows_one, rows_two)
     got = lax.ppermute(jnp.where(first, rows_two, rows_one), "section", swap)
+    rows = jnp.concatenate([kept, got], axis=0)
+    row_sets = [rows] + [along_x(rows, d) for d in range(1, x_count)]
+    seq_index = lax.axis_index("seq").astype(jnp.int32)
+    x_index, y_index = seq_index // y_count, seq_index % y_count
     vocab_dev = head.shape[2]
-    labels = lax.dynamic_index_in_dim(
-        targets.reshape(2, seq_count, -1), lax.axis_index("seq"), 1, keepdims=False
-    )
-    labels = jnp.where(first, labels, labels[::-1]).reshape(-1, 1)
-    parts = score_stage((kept, got), heads, labels, z_scalar * vocab_dev, n_blk * vocab_dev)
-    parts = gather_by_exchange(parts, everyone).reshape(-1, 128)
-    losses = loss_stage(parts, seq_count, labels.shape[0])
+    labels = targets.reshape(2, x_count, y_count, -1)
+    labels = lax.dynamic_index_in_dim(labels, y_index, 2, keepdims=False)
+    labels = jnp.transpose(jnp.where(first, labels, labels[::-1]), (1, 0, 2)).reshape(-1, 1)
+    places = [(x_index + x_count - d) % x_count for d in range(x_count)]
+    for d in range(y_count):
+        source = x_index * y_count + (y_index + y_count - d) % y_count
+        places.append((source * n_blk + z_scalar[0]) * vocab_dev)
+    parts = score_stage(row_sets, heads, labels, jnp.stack(places))
+    losses = loss_stage(gather_by_exchange(parts, everyone), x_count, y_count)
     aux_losses = jnp.where(first, losses, losses[::-1]).reshape(1, 2, -1)
 
     chan_one = chan_one[:, :tokens].reshape(rows_dev * tokens, BLK)

time: 318 us -> 287 us (0.903)
  blocking collectives: 90.6 us -> 69.4 us
  between operations: 14.4 us -> 1.04 us
  waiting for transfers between devices: 57.3 us -> 64.4 us
  Pallas kernels: 73.8 us -> 67.5 us
  starting transfers between devices: 48.2 us -> 53 us
    all_to_all x2, blocking collectives: 52.1 us -> 37.2 us  [exchange_seq(): return lax.all_to_all(mix, 'seq', split_axis=0, concat_axis=0, tiled=True)]
    ppermute x0 -> x6, starting transfers between devices: none -> 6.69 us  [the longest x3 3.9 us: along_x(): return lax.ppermute(block, 'seq', route)]
    pallas_call x2, Pallas kernels: 10.1 us -> 3.65 us  [the longest x1 3.53 us: score_stage(): pl.pallas_call(kernel, in_specs=[scalar_spec(), whole(labels.shape)] + [w...]
    all_to_all x1, blocking collectives: 38.5 us -> 32.2 us  [exchange_all(): lax.all_to_all(cols, everyone, split_axis=0, concat_axis=0, tiled=True)]
    ppermute x0 -> x6, waiting for transfers between devices: none -> 3.89 us  [the longest x3 3.89 us: along_x(): return lax.ppermute(block, 'seq', route)]
    unnamed x50 -> x46, local copies, waits for them, and re-layouts: 9.69 us -> 7.52 us
  transfers between devices with their start and end apart: 16 -> 21, of which waited for: 8 -> 11; matrix products, arithmetic and copies ran while one was open for 6% -> 6% of each run, Pallas kernels for 20% -> 16%
where the time goes in v6:
time: 287 us; the launch traced here: 284 us
  blocking collectives  69.4 us (24%)
  Pallas kernels  67.5 us (24%)
  waiting for transfers between devices  64.4 us (22%)
  starting transfers between devices  53 us (18%)
  other arithmetic  16 us (6%)
  local copies, waits for them, and re-layouts  12.7 us (4%)
    all_to_all x2, blocking collectives, exchange_seq(): return lax.all_to_all(mix, 'seq', split_axis=0, concat_axis=0, tiled=True)  37.2 us
    all_to_all x1, blocking collectives, exchange_all(): lax.all_to_all(cols, everyone, split_axis=0, concat_axis=0, tiled=True)  32.2 us
    all_to_all x2, waiting for transfers between devices, body(): lax.all_to_all(packed, 'tensor', split_axis=0, concat_axis=0, tiled=True)  25.7 us
    pallas_call x4, Pallas kernels, channel_map(): pl.pallas_call(kernel, grid=(n_blk,), in_specs=[whole((C1, C2, C2)), pl.B...  24.4 us
    pallas_call x2, Pallas kernels, out_stage(): pl.pallas_call(kernel, grid=(n_blk,), in_specs=in_specs, out_specs=[whole...  18.2 us
    all_to_all x1, waiting for transfers between devices, body(): lax.all_to_all(packed_two, 'tensor', split_axis=0, concat_axis=0, tiled=T...  16.6 us
    pallas_call x2, Pallas kernels, gate_stage(): pl.pallas_call(kernel, grid=(n_blk,), in_specs=[whole(normed.shape), pl.B...  15 us
    select_n x7, other arithmetic, by_block(): return (jnp.where(first, own, other), jnp.where(first, other, own))  10.6 us
  transfers between devices with their start and end apart: 21, of which 11 were waited for; matrix products, arithmetic and copies ran while one was open for 6% of the time, Pallas kernels for 16%

profile of v6, /device:TPU:1, one launch (start us, length us, event | category | flops | bytes accessed | tf_op | source)
XLA Modules:
  0.0 284.0 jit_solution(10254481426962229215)
XLA Ops:
  11.1 6.5 %all-to-all-start = ((bf16[8,288,256]{2,1,0:T(8,128)(2,1)}), bf16[8,288,256]{2,1,0:T(8,128)(2,1)S(1)}, u32[]{:S(2)}, u32[]{:S(2)}) async-start(bf16[8,288,256]{2,1,0:T(8,128)(2,1)} %copy-done.3), calls=%async_computation | async-start | bytes 2359296 | tf_op jit(solution)/shard_map/all_to_all | solution.py:431
  33.2 16.5 %all-to-all-done.refs_0_.x_ref = bf16[8,288,256]{2,1,0:T(8,128)(2,1)S(1)} async-done(((bf16[8,288,256]{2,1,0:T(8,128)(2,1)}), bf16[8,288,256]{2,1,0:T(8,128)(2,1)S(1)}, u32[]{:S(2)}, u32[]{:S(2)}) %all-to-all-start) | async-done | bytes 1179680 | tf_op jit(solution)/shard_map/all_to_all | solution.py:431
  51.4 21.3 %all_to_all.40 = bf16[16,8,16,256]{3,2,1,0:T(8,128)(2,1)S(1)} all-to-all(bf16[16,8,16,256]{3,2,1,0:T(8,128)(2,1)S(1)} %shard_map.114), channel_id=1, replica_groups=mesh['section'=2,'seq'=16,'tensor'=8] {'seq'}, dimensions={0} | all-to-all | bytes 2097152 | tf_op jit(solution)/shard_map/all_to_all | solution.py:437
  75.2 6.5 %all-to-all-start.2 = ((bf16[128,16,256]{2,1,0:T(8,128)(2,1)}), bf16[128,16,256]{2,1,0:T(8,128)(2,1)S(1)}, u32[]{:S(2)}, u32[]{:S(2)}) async-start(bf16[128,16,256]{2,1,0:T(8,128)(2,1)} %bitcast.11), calls=%async_computation.2 | async-start | bytes 2097152 | tf_op jit(solution)/shard_map/all_to_all | solution.py:444
  82.4 6.1 %shard_map.117.map_ref = bf16[8,2048,256]{2,1,0:T(8,128)(2,1)} custom-call(bf16[32,64,64]{2,1,0:T(8,128)(2,1)S(1)} %copy-done.10, bf16[32,2048]{1,0:T(8,128)(2,1)S(1)} %get-tuple-element.65.second_ref), custom_call_target="tpu_custom_call" | custom-call | tf_op jit(solution)/shard_map/pallas_call | solution.py:175
  88.5 7.5 %shard_map.118.gate_ref = f32[8,256,256]{2,1,0:T(8,128)S(1)} custom-call(bf16[256,2048]{1,0:T(8,128)(2,1)S(1)} %shard_map.116.normed_ref, bf16[8,2048,256]{2,1,0:T(8,128)(2,1)} %shard_map.117.map_ref), custom_call_target="tpu_custom_call" | custom-call | tf_op jit(solution)/shard_map/pallas_call | solution.py:220
  97.3 6.1 %shard_map.119.map_ref = bf16[8,2048,256]{2,1,0:T(8,128)(2,1)} custom-call(bf16[32,64,64]{2,1,0:T(8,128)(2,1)S(1)} %copy-done.11, bf16[32,2048]{1,0:T(8,128)(2,1)S(1)} %copy-done.14), custom_call_target="tpu_custom_call" | custom-call | tf_op jit(solution)/shard_map/pallas_call | solution.py:175
  103.4 7.2 %all-to-all-done.2 = bf16[128,16,256]{2,1,0:T(8,128)(2,1)S(1)} async-done(((bf16[128,16,256]{2,1,0:T(8,128)(2,1)}), bf16[128,16,256]{2,1,0:T(8,128)(2,1)S(1)}, u32[]{:S(2)}, u32[]{:S(2)}) %all-to-all-start.2) | async-done | bytes 1048608 | tf_op jit(solution)/shard_map/all_to_all | solution.py:444
  110.6 10.2 %shard_map.120 = (bf16[8,288,256]{2,1,0:T(8,128)(2,1)}, bf16[256,2048]{1,0:T(8,128)(2,1)S(1)}) custom-call(bf16[16,8,16,256]{3,2,1,0:T(8,128)(2,1)S(1)} %bitcast.47, f32[8,256,256]{2,1,0:T(8,128)} %copy-done.2, bf16[8,288,256]{2,1,0:T(8,128)(2,1)S(1)} %all-to-all-done.refs_0_.x_ref, bf16[8,2048,256]{2,1,0:T(8,128)(2,1)} %shard_map.119.map_ref, ...), custom_call_target="tpu_custom_call" | custom-call | tf_op jit(solution)/shard_map/pallas_call | solution.py:290
  121.8 3.7 %all-to-all-start.3 = ((bf16[8,288,256]{2,1,0:T(8,128)(2,1)}), bf16[8,288,256]{2,1,0:T(8,128)(2,1)S(1)}, u32[]{:S(2)}, u32[]{:S(2)}) async-start(bf16[8,288,256]{2,1,0:T(8,128)(2,1)} %get-tuple-element.74.x_ref), calls=%async_computation.3 | async-start | bytes 2359296 | tf_op jit(solution)/shard_map/all_to_all | solution.py:467
  125.6 6.1 %shard_map.122.map_ref = bf16[8,2048,256]{2,1,0:T(8,128)(2,1)} custom-call(bf16[32,64,64]{2,1,0:T(8,128)(2,1)S(1)} %copy-done.8, bf16[32,2048]{1,0:T(8,128)(2,1)S(1)} %get-tuple-element.78.second_ref), custom_call_target="tpu_custom_call" | custom-call | tf_op jit(solution)/shard_map/pallas_call | solution.py:175
  131.7 7.5 %shard_map.123.gate_ref = f32[8,256,256]{2,1,0:T(8,128)S(1)} custom-call(bf16[256,2048]{1,0:T(8,128)(2,1)S(1)} %copy-done.13, bf16[8,2048,256]{2,1,0:T(8,128)(2,1)} %shard_map.122.map_ref), custom_call_target="tpu_custom_call" | custom-call | tf_op jit(solution)/shard_map/pallas_call | solution.py:220
  139.2 6.1 %shard_map.124.map_ref = bf16[8,2048,256]{2,1,0:T(8,128)(2,1)} custom-call(bf16[32,64,64]{2,1,0:T(8,128)(2,1)S(1)} %copy-done.9, bf16[32,2048]{1,0:T(8,128)(2,1)S(1)} %get-tuple-element.80.second_ref), custom_call_target="tpu_custom_call" | custom-call | tf_op jit(solution)/shard_map/pallas_call | solution.py:175
  145.3 9.2 %all-to-all-done.3.x_ref = bf16[8,288,256]{2,1,0:T(8,128)(2,1)S(1)} async-done(((bf16[8,288,256]{2,1,0:T(8,128)(2,1)}), bf16[8,288,256]{2,1,0:T(8,128)(2,1)S(1)}, u32[]{:S(2)}, u32[]{:S(2)}) %all-to-all-start.3) | async-done | bytes 1179680 | tf_op jit(solution)/shard_map/all_to_all | solution.py:467
  156.3 15.9 %all_to_all.41 = bf16[16,8,16,256]{3,2,1,0:T(8,128)(2,1)S(1)} all-to-all(bf16[16,8,16,256]{3,2,1,0:T(8,128)(2,1)S(1)} %shard_map.121), channel_id=1, replica_groups=mesh['section'=2,'seq'=16,'tensor'=8] {'seq'}, dimensions={0} | all-to-all | bytes 2097152 | tf_op jit(solution)/shard_map/all_to_all | solution.py:437
  173.7 32.2 %all_to_all.42 = bf16[128,16,256]{2,1,0:T(8,128)(2,1)S(1)} all-to-all(bf16[128,16,256]{2,1,0:T(8,128)(2,1)S(1)} %bitcast.46), channel_id=1, replica_groups=mesh['section'=2,'seq'=16,'tensor'=8] {'seq','tensor'}, dimensions={0} | all-to-all | bytes 2097152 | tf_op jit(solution)/shard_map/all_to_all | solution.py:444
  205.9 8.0 %shard_map.126 = bf16[8,272,256]{2,1,0:T(8,128)(2,1)S(1)} custom-call(bf16[16,8,16,256]{3,2,1,0:T(8,128)(2,1)S(1)} %bitcast.48, f32[8,256,256]{2,1,0:T(8,128)S(1)} %shard_map.123.gate_ref, bf16[8,288,256]{2,1,0:T(8,128)(2,1)} %get-tuple-element.74.x_ref, bf16[8,2048,256]{2,1,0:T(8,128)(2,1)} %shard_map.124.map_ref), custom_call_target="tpu_custom_call" | custom-call | tf_op jit(solution)/shard_map/pallas_call | solution.py:290
  214.9 3.9 %all-to-all-start.6 = ((bf16[8,272,256]{2,1,0:T(8,128)(2,1)}), bf16[8,272,256]{2,1,0:T(8,128)(2,1)S(1)}, u32[]{:S(2)}, u32[]{:S(2)}) async-start(bf16[8,272,256]{2,1,0:T(8,128)(2,1)} %copy-done.4), calls=%async_computation.6 | async-start | bytes 2228224 | tf_op jit(solution)/shard_map/all_to_all | solution.py:474
  218.9 9.2 %collective-permute-start.11 = (bf16[2048,256]{1,0:T(8,128)(2,1)S(1)}, bf16[2048,256]{1,0:T(8,128)(2,1)}, u32[]{:S(2)}, u32[]{:S(2)}) collective-permute-start(bf16[2048,256]{1,0:T(8,128)(2,1)S(1)} %bitcast.49), channel_id=1, source_target_pairs={{128,0},{129,1},{130,2},{131,3},{132,4},{133,5},{134,6},{135,7},{1... | collective-permute-start | bytes 3145736 | tf_op jit(solution)/shard_map/ppermute | solution.py:497
  228.1 16.6 %all-to-all-done.6 = bf16[8,272,256]{2,1,0:T(8,128)(2,1)S(1)} async-done(((bf16[8,272,256]{2,1,0:T(8,128)(2,1)}), bf16[8,272,256]{2,1,0:T(8,128)(2,1)S(1)}, u32[]{:S(2)}, u32[]{:S(2)}) %all-to-all-start.6) | async-done | bytes 1114144 | tf_op jit(solution)/shard_map/all_to_all | solution.py:474
  244.7 3.6 %collective-permute-start.12 = (bf16[8,16,256]{2,1,0:T(8,128)(2,1)S(1)}, bf16[8,16,256]{2,1,0:T(8,128)(2,1)S(1)}, u32[]{:S(2)}, u32[]{:S(2)}) collective-permute-start(bf16[8,16,256]{2,1,0:T(8,128)(2,1)S(1)} %get-tuple-element.89), channel_id=1, source_target_pairs={{0,128},{128,0},{1,129},{129,1},{2,130},{130,2},{3,131},{131,3},{4... | collective-permute-start | bytes 196616 | tf_op jit(solution)/shard_map/ppermute | solution.py:478
  258.7 3.5 %shard_map.127 = f32[2,128]{1,0:T(2,128)S(1)} custom-call(s32[8]{0:T(128)S(1)} %stack.47.place_ref, s32[128,1]{1,0:T(8,128)S(1)} %reshape.72.label_ref, bf16[16,16,256]{2,1,0:T(8,128)(2,1)S(1)} %pad_maximum_fusion.refs_0_, bf16[16,16,256]{2,1,0:T(8,128)(2,1)S(1)} %collective-permute-done.13.refs_1_, ...), custom_call_target="tpu_custom_call" | custom-call | tf_op jit(solution)/shard_map/pallas_call | solution.py:336
  262.9 6.2 %all-to-all-start.7 = ((f32[128,2,128]{2,1,0:T(2,128)}), f32[128,2,128]{2,1,0:T(2,128)S(1)}, u32[]{:S(2)}, u32[]{:S(2)}) async-start(f32[128,2,128]{2,1,0:T(2,128)} %broadcast_in_dim.10), calls=%async_computation.7 | async-start | bytes 262144 | tf_op jit(solution)/shard_map/all_to_all | solution.py:44
  271.4 8.8 %all-to-all-done.7.parts_ref = f32[128,2,128]{2,1,0:T(2,128)S(1)} async-done(((f32[128,2,128]{2,1,0:T(2,128)}), f32[128,2,128]{2,1,0:T(2,128)S(1)}, u32[]{:S(2)}, u32[]{:S(2)}) %all-to-all-start.7) | async-done | bytes 131104 | tf_op jit(solution)/shard_map/all_to_all | solution.py:44
  (115 shorter events, 54.8 us)
Async XLA Ops:
  0.7 4.4 %collective-permute-start = (f32[1,256]{1,0:T(1,128)}, f32[1,256]{1,0:T(1,128)S(1)}, u32[]{:S(2)}, u32[]{:S(2)}) collective-permute-start(f32[1,256]{1,0:T(1,128)} %param.11), channel_id=1, source_target_pairs={{0,128},{128,0},{1,129},{129,1},{2,130},{130,2},{3,131},{131,3},{4... | collective-permute-start | bytes 3080 | tf_op jit(solution)/shard_map/ppermute | solution.py:394
  6.8 15.2 %copy-start.16 = (bf16[1,32,64,64]{3,2,1,0:T(8,128)(2,1)S(1)}, bf16[1,32,64,64]{3,2,1,0:T(8,128)(2,1)}, u32[]{:S(2)}) copy-start(bf16[1,32,64,64]{3,2,1,0:T(8,128)(2,1)} %param.14) | copy-start | bytes 786436
  7.1 12.7 %collective-permute-start.7 = (bf16[32,2048]{1,0:T(8,128)(2,1)S(1)}, bf16[32,2048]{1,0:T(8,128)(2,1)S(1)}, u32[]{:S(2)}, u32[]{:S(2)}) collective-permute-start(bf16[32,2048]{1,0:T(8,128)(2,1)S(1)} %reshape.55), channel_id=1, source_target_pairs={{0,128},{128,0},{1,129},{129,1},{2,130},{130,2},{3,131},{131,3},{4... | collective-permute-start | bytes 393224 | tf_op jit(solution)/shard_map/ppermute | solution.py:394
  7.8 43.6 %collective-permute-start.2 = (bf16[2048,256]{1,0:T(8,128)(2,1)}, bf16[2048,256]{1,0:T(8,128)(2,1)}, u32[]{:S(2)}, u32[]{:S(2)}) collective-permute-start(bf16[2048,256]{1,0:T(8,128)(2,1)} %bitcast.5.refs_4_), channel_id=1, source_target_pairs={{0,8},{8,16},{16,24},{24,0},{32,40},{40,48},{48,56},{56,32},{64,72... | collective-permute-start | bytes 3145736 | tf_op jit(solution)/shard_map/ppermute | solution.py:399
  7.8 43.6 %collective-permute-start.3 = (bf16[2048,256]{1,0:T(8,128)(2,1)}, bf16[2048,256]{1,0:T(8,128)(2,1)}, u32[]{:S(2)}, u32[]{:S(2)}) collective-permute-start(bf16[2048,256]{1,0:T(8,128)(2,1)} %bitcast.5.refs_4_), channel_id=1, source_target_pairs={{0,24},{8,0},{16,8},{24,16},{32,56},{40,32},{48,40},{56,48},{64,88... | collective-permute-start | bytes 3145736 | tf_op jit(solution)/shard_map/ppermute | solution.py:399
  10.5 19.6 %collective-permute-start.1 = (bf16[8,256,256]{2,1,0:T(8,128)(2,1)}, bf16[8,256,256]{2,1,0:T(8,128)(2,1)}, u32[]{:S(2)}, u32[]{:S(2)}) collective-permute-start(bf16[8,256,256]{2,1,0:T(8,128)(2,1)} %bitcast.1), channel_id=1, source_target_pairs={{0,128},{128,0},{1,129},{129,1},{2,130},{130,2},{3,131},{131,3},{4... | collective-permute-start | bytes 3145736 | tf_op jit(solution)/shard_map/ppermute | solution.py:394
  11.1 38.5 %all-to-all-start = ((bf16[8,288,256]{2,1,0:T(8,128)(2,1)}), bf16[8,288,256]{2,1,0:T(8,128)(2,1)S(1)}, u32[]{:S(2)}, u32[]{:S(2)}) async-start(bf16[8,288,256]{2,1,0:T(8,128)(2,1)} %copy-done.3), calls=%async_computation | async-start | bytes 2359296 | tf_op jit(solution)/shard_map/all_to_all | solution.py:431
  17.6 10.6 %collective-permute-start.4 = (bf16[16,128,128]{2,1,0:T(8,128)(2,1)}, bf16[16,128,128]{2,1,0:T(8,128)(2,1)}, u32[]{:S(2)}, u32[]{:S(2)}) collective-permute-start(bf16[16,128,128]{2,1,0:T(8,128)(2,1)} %bitcast.54), channel_id=1, source_target_pairs={{0,128},{128,0},{1,129},{129,1},{2,130},{130,2},{3,131},{131,3},{4... | collective-permute-start | bytes 1572872 | tf_op jit(solution)/shard_map/ppermute | solution.py:394
  20.5 1.6 collective-permute-start.8
  22.1 1.9 collective-permute-start.5
  24.0 2.1 collective-permute-start.6
  75.2 35.4 %all-to-all-start.2 = ((bf16[128,16,256]{2,1,0:T(8,128)(2,1)}), bf16[128,16,256]{2,1,0:T(8,128)(2,1)S(1)}, u32[]{:S(2)}, u32[]{:S(2)}) async-start(bf16[128,16,256]{2,1,0:T(8,128)(2,1)} %bitcast.11), calls=%async_computation.2 | async-start | bytes 2097152 | tf_op jit(solution)/shard_map/all_to_all | solution.py:444
  121.8 32.8 %all-to-all-start.3 = ((bf16[8,288,256]{2,1,0:T(8,128)(2,1)}), bf16[8,288,256]{2,1,0:T(8,128)(2,1)S(1)}, u32[]{:S(2)}, u32[]{:S(2)}) async-start(bf16[8,288,256]{2,1,0:T(8,128)(2,1)} %get-tuple-element.74.x_ref), calls=%async_computation.3 | async-start | bytes 2359296 | tf_op jit(solution)/shard_map/all_to_all | solution.py:467
  125.5 30.8 %collective-permute-start.9 = (bf16[2048,256]{1,0:T(8,128)(2,1)}, bf16[2048,256]{1,0:T(8,128)(2,1)}, u32[]{:S(2)}, u32[]{:S(2)}) collective-permute-start(bf16[2048,256]{1,0:T(8,128)(2,1)} %bitcast.5.refs_4_), channel_id=1, source_target_pairs={{0,16},{8,24},{16,0},{24,8},{32,48},{40,56},{48,32},{56,40},{64,80... | collective-permute-start | bytes 3145736 | tf_op jit(solution)/shard_map/ppermute | solution.py:399
  155.8 16.4 %copy-start.7 = (bf16[16,128,128]{2,1,0:T(8,128)(2,1)S(1)}, bf16[16,128,128]{2,1,0:T(8,128)(2,1)}, u32[]{:S(2)}) copy-start(bf16[16,128,128]{2,1,0:T(8,128)(2,1)} %get-tuple-element.75.left_ref) | copy-start | bytes 1572868
  214.9 13.2 %copy-start.20 = (s32[2,256]{1,0:T(2,128)S(1)}, s32[2,256]{1,0:T(2,128)}, u32[]{:S(2)}) copy-start(s32[2,256]{1,0:T(2,128)} %param.19) | copy-start | bytes 6148
  214.9 29.8 %all-to-all-start.6 = ((bf16[8,272,256]{2,1,0:T(8,128)(2,1)}), bf16[8,272,256]{2,1,0:T(8,128)(2,1)S(1)}, u32[]{:S(2)}, u32[]{:S(2)}) async-start(bf16[8,272,256]{2,1,0:T(8,128)(2,1)} %copy-done.4), calls=%async_computation.6 | async-start | bytes 2228224 | tf_op jit(solution)/shard_map/all_to_all | solution.py:474
  218.9 50.2 %collective-permute-start.11 = (bf16[2048,256]{1,0:T(8,128)(2,1)S(1)}, bf16[2048,256]{1,0:T(8,128)(2,1)}, u32[]{:S(2)}, u32[]{:S(2)}) collective-permute-start(bf16[2048,256]{1,0:T(8,128)(2,1)S(1)} %bitcast.49), channel_id=1, source_target_pairs={{128,0},{129,1},{130,2},{131,3},{132,4},{133,5},{134,6},{135,7},{1... | collective-permute-start | bytes 3145736 | tf_op jit(solution)/shard_map/ppermute | solution.py:497
  244.7 5.9 %collective-permute-start.12 = (bf16[8,16,256]{2,1,0:T(8,128)(2,1)S(1)}, bf16[8,16,256]{2,1,0:T(8,128)(2,1)S(1)}, u32[]{:S(2)}, u32[]{:S(2)}) collective-permute-start(bf16[8,16,256]{2,1,0:T(8,128)(2,1)S(1)} %get-tuple-element.89), channel_id=1, source_target_pairs={{0,128},{128,0},{1,129},{129,1},{2,130},{130,2},{3,131},{131,3},{4... | collective-permute-start | bytes 196616 | tf_op jit(solution)/shard_map/ppermute | solution.py:478
  249.3 31.6 %collective-permute-start.10 = (bf16[2048,256]{1,0:T(8,128)(2,1)}, bf16[2048,256]{1,0:T(8,128)(2,1)}, u32[]{:S(2)}, u32[]{:S(2)}) collective-permute-start(bf16[2048,256]{1,0:T(8,128)(2,1)} %bitcast.18), channel_id=1, source_target_pairs={{0,128},{1,129},{2,130},{3,131},{4,132},{5,133},{6,134},{7,135},{8... | collective-permute-start | bytes 3145736 | tf_op jit(solution)/shard_map/ppermute | solution.py:498
  250.7 5.1 %collective-permute-start.13 = (bf16[16,16,256]{2,1,0:T(8,128)(2,1)S(1)}, bf16[16,16,256]{2,1,0:T(8,128)(2,1)S(1)}, u32[]{:S(2)}, u32[]{:S(2)}) collective-permute-start(bf16[16,16,256]{2,1,0:T(8,128)(2,1)S(1)} %pad_maximum_fusion.refs_0_), channel_id=1, source_target_pairs={{0,32},{8,40},{16,48},{24,56},{32,64},{40,72},{48,80},{56,88},{64,... | collective-permute-start | bytes 393224 | tf_op jit(solution)/shard_map/ppermute | solution.py:403
  252.1 6.6 %collective-permute-start.14 = (bf16[16,16,256]{2,1,0:T(8,128)(2,1)S(1)}, bf16[16,16,256]{2,1,0:T(8,128)(2,1)S(1)}, u32[]{:S(2)}, u32[]{:S(2)}) collective-permute-start(bf16[16,16,256]{2,1,0:T(8,128)(2,1)S(1)} %pad_maximum_fusion.refs_0_), channel_id=1, source_target_pairs={{0,64},{8,72},{16,80},{24,88},{32,96},{40,104},{48,112},{56,120},{... | collective-permute-start | bytes 393224 | tf_op jit(solution)/shard_map/ppermute | solution.py:403
  252.3 6.4 %collective-permute-start.15 = (bf16[16,16,256]{2,1,0:T(8,128)(2,1)S(1)}, bf16[16,16,256]{2,1,0:T(8,128)(2,1)S(1)}, u32[]{:S(2)}, u32[]{:S(2)}) collective-permute-start(bf16[16,16,256]{2,1,0:T(8,128)(2,1)S(1)} %pad_maximum_fusion.refs_0_), channel_id=1, source_target_pairs={{0,96},{8,104},{16,112},{24,120},{32,0},{40,8},{48,16},{56,24},{64... | collective-permute-start | bytes 393224 | tf_op jit(solution)/shard_map/ppermute | solution.py:403
  262.9 17.3 %all-to-all-start.7 = ((f32[128,2,128]{2,1,0:T(2,128)}), f32[128,2,128]{2,1,0:T(2,128)S(1)}, u32[]{:S(2)}, u32[]{:S(2)}) async-start(f32[128,2,128]{2,1,0:T(2,128)} %broadcast_in_dim.10), calls=%async_computation.7 | async-start | bytes 262144 | tf_op jit(solution)/shard_map/all_to_all | solution.py:44
  (19 other events, 69.1 us)

commit v7 on v6

--- a/solution.py
+++ b/solution.py
@@ -230,14 +230,14 @@
 def out_stage(seq_out, gate, x_tok, out_map, gain=None):
     groups, n_blk, width, _ = seq_out.shape
     tokens = groups * width
-    height = tokens + EXTRA * (1 if gain is None else 2)
+    height = tokens + (0 if gain is None else EXTRA)
 
     def kernel(seq_ref, gate_ref, x_ref, map_ref, *refs):
         n = pl.program_id(0)
         if gain is None:
-            res_ref, gated_ref = refs
+            rows_ref, res_ref, gated_ref = refs
         else:
-            gain_ref, res_ref, normed_ref, gated_ref = refs
+            gain_ref, rows_ref, res_ref, normed_ref, gated_ref = refs
 
         @pl.when(n == 0)
         def _():
@@ -251,14 +251,11 @@
         @pl.when(n == n_blk - 1)
         def _():
             blocks = [res_ref[z, :tokens] for z in range(n_blk)]
-            place = lax.broadcasted_iota(jnp.int32, (EXTRA, BLK), 0)
-            scored = jnp.zeros((EXTRA, BLK), F32)
             for z in range(n_blk):
                 for q in range(tokens // STRIDE):
-                    row = blocks[z][q * STRIDE : q * STRIDE + 1].astype(F32)
-                    scored = jnp.where(place == q * n_blk + z, row, scored)
-            for z in range(n_blk):
-                res_ref[z, height - EXTRA :] = scored.astype(BF16)
+                    rows_ref[q : q + 1, z * BLK : (z + 1) * BLK] = blocks[z][
+                        q * STRIDE : q * STRIDE + 1
+                    ]
             if gain is None:
                 return
 
@@ -282,7 +279,7 @@
         pl.BlockSpec((1, D, BLK), lambda n: (n, 0, 0)),
     ]
     operands = [seq_out, gate, x_tok, out_map]
-    out_shape = [shape_of((n_blk, height, BLK))]
+    out_shape = [shape_of((tokens // STRIDE, D)), shape_of((n_blk, height, BLK))]
     if gain is not None:
         operands.append(gain)
         in_specs.append(whole(gain.shape))
@@ -300,9 +297,7 @@
 
 def score_stage(row_sets, heads, labels, places):
     x_count = len(row_sets)
-    pairs = row_sets[0].shape[0]
-    n_blk = pairs // 2
-    per_set = 2 * pairs
+    per_set = row_sets[0].shape[0]
     count = x_count * per_set
     width = heads[0].shape[1]
 
@@ -310,15 +305,8 @@
         out_ref, rows_ref = refs[-2:]
         head_refs = refs[x_count : x_count + len(heads)]
         for d in range(x_count):
-            first_row = place_ref[d] * per_set
-            for z in range(0, pairs, 4):
-                lines = [refs[d][z + k].astype(F32) for k in range(4)]
-                group = [lines[k][q * n_blk : (q + 1) * n_blk] for k in range(4) for q in range(2)]
-                at = pl.multiple_of(first_row + 2 * z, 8)
-                for n in range(n_blk):
-                    block = jnp.concatenate([g[n : n + 1] for g in group], axis=0)
-                    rows_ref[pl.ds(at, 8), n * BLK : (n + 1) * BLK] = block
-        rows = rows_ref[...].astype(BF16)
+            rows_ref[place_ref[d]] = refs[d][...]
+        rows = rows_ref[...].reshape(count, D)
         exp_sum = jnp.zeros((count, 1), F32)
         target = jnp.zeros((count, 1), F32)
         for d, head_ref in enumerate(head_refs):
@@ -339,7 +327,7 @@
         + [whole(r.shape) for r in row_sets]
         + [whole(h.shape) for h in heads],
         out_shape=shape_of((2, count), F32),
-        scratch_shapes=[pltpu.VMEM((count, D), F32)],
+        scratch_shapes=[pltpu.VMEM((x_count, per_set, D), BF16)],
         compiler_params=params(),
     )(places, labels, *row_sets, *heads)
 
@@ -362,6 +350,32 @@
         out_shape=shape_of((2, x_count, y_count, ring), F32),
         compiler_params=params(),
     )(parts)
+
+
+def result_stage(section, chan_one, got_one, got_two, chan_two, tokens):
+    rows = chan_one.shape[0]
+
+    def kernel(section_ref, *refs):
+        out_ref = refs[-1]
+
+        @pl.when(section_ref[0] == 0)
+        def _():
+            out_ref[0] = refs[0][...]
+            out_ref[1] = refs[1][...]
+
+        @pl.when(section_ref[0] != 0)
+        def _():
+            out_ref[0] = refs[2][...]
+            out_ref[1] = refs[3][...]
+
+    return pl.pallas_call(
+        kernel,
+        grid=(rows,),
+        in_specs=[scalar_spec()] + [pl.BlockSpec((1, tokens, BLK), lambda p: (p, 0, 0))] * 4,
+        out_specs=pl.BlockSpec((2, 1, tokens, BLK), lambda p: (0, p, 0, 0)),
+        out_shape=shape_of((2, rows, tokens, BLK)),
+        compiler_params=params(),
+    )(section, chan_one, got_one, got_two, chan_two)
 
 
 def body(
@@ -427,7 +441,8 @@
     )
     rights, lefts, gate_firsts, out_firsts = (by_block(w) for w in own[:4])
     gate_seconds, out_seconds = (by_block(rows_second(w)) for w in own[4:6])
-    heads = [own[6], along_y(own[6], 1), None, along_y(own[6], 3)]
+    lefts, head_own = tie((lefts, own[6]))
+    heads = [head_own, along_y(head_own, 1), None, along_y(head_own, 3)]
     x_tok = lax.all_to_all(packed, "tensor", split_axis=0, concat_axis=0, tiled=True)
     gain_rows = x_tok[:, tokens + 3 * rows_dev :][:, :6].astype(F32)
     gain_rows = jnp.sum(gain_rows.reshape(n_blk, 2, 3, BLK), axis=2)
@@ -458,7 +473,7 @@
     normed = token_stage(x_tok, gains[0], tokens)
     gate = gate_stage(normed, channel_map(gate_firsts[0], gate_seconds[0], n_blk))
     out_map = channel_map(out_firsts[0], out_seconds[0], n_blk)
-    packed, normed = out_stage(seq_out, gate, x_tok, out_map, gain=gains[1])
+    rows_one, packed, normed = out_stage(seq_out, gate, x_tok, out_map, gain=gains[1])
 
     packed, normed, heads[0], gate_two, out_two, gate_sec, out_sec = tie(
         (packed, normed, heads[0], gate_firsts[1], out_firsts[1], gate_seconds[1], out_seconds[1])
@@ -470,35 +485,37 @@
     mix = right_stage(chan_one, gain_local[1], rights[1], seq_count)
     mix, gate, out_map, heads[2] = tie((mix, gate, out_map, heads[2]))
     seq_out = exchange_all(mix_left(exchange_seq(mix), 1))
-    (packed_two,) = out_stage(seq_out, gate, packed, out_map)
-    chan_two = lax.all_to_all(packed_two, "tensor", split_axis=0, concat_axis=0, tiled=True)
-
-    rows_one, rows_two = chan_one[:, -EXTRA:], chan_two[:, -EXTRA:]
-    kept = jnp.where(first, rows_one, rows_two)
-    got = lax.ppermute(jnp.where(first, rows_two, rows_one), "section", swap)
-    rows = jnp.concatenate([kept, got], axis=0)
+    rows_two, result = out_stage(seq_out, gate, packed, out_map)
+
+    pair = jnp.stack([rows_one, rows_two])[:, None]
+    pair = jnp.broadcast_to(pair, (2, n_blk) + rows_two.shape).reshape((-1,) + rows_two.shape)
+    rows = lax.all_to_all(pair, ("section", "tensor"), split_axis=0, concat_axis=0, tiled=True)
+    rows, result = tie((rows, result))
+    chan_two = lax.all_to_all(result, "tensor", split_axis=0, concat_axis=0, tiled=True)
+
+    rows = rows.reshape(-1, D)
     row_sets = [rows] + [along_x(rows, d) for d in range(1, x_count)]
     seq_index = lax.axis_index("seq").astype(jnp.int32)
     x_index, y_index = seq_index // y_count, seq_index % y_count
     vocab_dev = head.shape[2]
     labels = targets.reshape(2, x_count, y_count, -1)
     labels = lax.dynamic_index_in_dim(labels, y_index, 2, keepdims=False)
-    labels = jnp.transpose(jnp.where(first, labels, labels[::-1]), (1, 0, 2)).reshape(-1, 1)
+    labels = jnp.transpose(labels, (1, 0, 2)).reshape(-1, 1)
     places = [(x_index + x_count - d) % x_count for d in range(x_count)]
     for d in range(y_count):
         source = x_index * y_count + (y_index + y_count - d) % y_count
         places.append((source * n_blk + z_scalar[0]) * vocab_dev)
     parts = score_stage(row_sets, heads, labels, jnp.stack(places))
-    losses = loss_stage(gather_by_exchange(parts, everyone), x_count, y_count)
-    aux_losses = jnp.where(first, losses, losses[::-1]).reshape(1, 2, -1)
-
-    chan_one = chan_one[:, :tokens].reshape(rows_dev * tokens, BLK)
-    chan_two = chan_two[:, :tokens].reshape(rows_dev * tokens, BLK)
+    parts, chan_two = tie((parts, chan_two))
+    sums = gather_by_exchange(parts, everyone)
+
     got_one = lax.ppermute(chan_one, "section", [(1, 0)])
     got_two = lax.ppermute(chan_two, "section", [(0, 1)])
-    block_out = jnp.stack(
-        [jnp.where(first, chan_one, got_two), jnp.where(first, got_one, chan_two)]
-    )[None]
+    scalar = section.astype(jnp.int32).reshape(1)
+    block_out = result_stage(scalar, chan_one, got_one, got_two, chan_two, tokens)
+    sums, block_out = tie((sums, block_out))
+    aux_losses = loss_stage(sums, x_count, y_count).reshape(1, 2, -1)
+    block_out = block_out.reshape(1, 2, rows_dev * tokens, BLK)
     return (block_out, aux_losses)
 
 

time: 287 us -> 284 us (0.990)
  blocking collectives: 69.4 us -> 87.9 us
  waiting for transfers between devices: 64.4 us -> 46.5 us
  starting transfers between devices: 53 us -> 46.3 us
  other arithmetic: 16 us -> 10.7 us
  local copies, waits for them, and re-layouts: 12.7 us -> 17.7 us
  Pallas kernels: 67.5 us -> 70.9 us
    all_to_all x0 -> x1, blocking collectives: none -> 16.3 us  [body(): lax.all_to_all(pair, ('section', 'tensor'), split_axis=0, concat_axis=0,...]
    unnamed x46 -> x66, local copies, waits for them, and re-layouts: 7.52 us -> 14.2 us
    all_to_all x1, waiting for transfers between devices: 8.76 us -> 3.01 us  [gather_by_exchange(): return lax.all_to_all(copies, axis, split_axis=0, concat_axis=0, tiled=True)]
    pallas_call x0 -> x1, Pallas kernels: none -> 5.74 us  [result_stage(): pl.pallas_call(kernel, grid=(rows,), in_specs=[scalar_spec()] + [pl.Block...]
    ppermute x1, starting transfers between devices: 9.18 us -> 4.73 us  [body(): got_one = lax.ppermute(chan_one, 'section', [(1, 0)])]
    ppermute x3, waiting for transfers between devices: 3.89 us -> 0.01 us  [along_x(): return lax.ppermute(block, 'seq', route)]
    another operation x2 -> x1, other arithmetic: 3.81 us -> 0.03 us  [body(): pair = jnp.stack([rows_one, rows_two])[:, None]]
    all_to_all x1, waiting for transfers between devices: 16.6 us -> 13 us  [body(): lax.all_to_all(result, 'tensor', split_axis=0, concat_axis=0, tiled=True)]
  transfers between devices with their start and end apart: 21 -> 20, of which waited for: 11 -> 6; matrix products, arithmetic and copies ran while one was open for 6% -> 5% of each run, Pallas kernels for 16% -> 18%
where the time goes in v7:
time: 284 us; the launch traced here: 281 us
  blocking collectives  87.9 us (31%)
  Pallas kernels  70.9 us (25%)
  waiting for transfers between devices  46.5 us (16%)
  starting transfers between devices  46.3 us (16%)
  local copies, waits for them, and re-layouts  17.7 us (6%)
  other arithmetic  10.7 us (4%)
    all_to_all x2, blocking collectives, exchange_seq(): return lax.all_to_all(mix, 'seq', split_axis=0, concat_axis=0, tiled=True)  39.3 us
    all_to_all x1, blocking collectives, exchange_all(): lax.all_to_all(cols, everyone, split_axis=0, concat_axis=0, tiled=True)  32.3 us
    pallas_call x4, Pallas kernels, channel_map(): pl.pallas_call(kernel, grid=(n_blk,), in_specs=[whole((C1, C2, C2)), pl.B...  24.7 us
    all_to_all x2, waiting for transfers between devices, body(): lax.all_to_all(packed, 'tensor', split_axis=0, concat_axis=0, tiled=True)  23.4 us
    pallas_call x2, Pallas kernels, out_stage(): pl.pallas_call(kernel, grid=(n_blk,), in_specs=in_specs, out_specs=[whole...  17.2 us
    all_to_all x1, blocking collectives, body(): lax.all_to_all(pair, ('section', 'tensor'), split_axis=0, concat_axis=0,...  16.3 us
    pallas_call x2, Pallas kernels, gate_stage(): pl.pallas_call(kernel, grid=(n_blk,), in_specs=[whole(normed.shape), pl.B...  15 us
    unnamed x66, local copies, waits for them, and re-layouts  14.2 us
  transfers between devices with their start and end apart: 20, of which 6 were waited for; matrix products, arithmetic and copies ran while one was open for 5% of the time, Pallas kernels for 18%

profile of v7, /device:TPU:1, one launch (start us, length us, event | category | flops | bytes accessed | tf_op | source)
XLA Modules:
  0.0 281.2 jit_solution(11246988875372921600)
XLA Ops:
  0.7 3.3 %collective-permute-start = (f32[1,256]{1,0:T(1,128)}, f32[1,256]{1,0:T(1,128)S(1)}, u32[]{:S(2)}, u32[]{:S(2)}) collective-permute-start(f32[1,256]{1,0:T(1,128)} %param.11), channel_id=1, source_target_pairs={{0,128},{128,0},{1,129},{129,1},{2,130},{130,2},{3,131},{131,3},{4... | collective-permute-start | bytes 3080 | tf_op jit(solution)/shard_map/ppermute | solution.py:408
  8.3 6.5 %all-to-all-start = ((bf16[8,288,256]{2,1,0:T(8,128)(2,1)}), bf16[8,288,256]{2,1,0:T(8,128)(2,1)S(1)}, u32[]{:S(2)}, u32[]{:S(2)}) async-start(bf16[8,288,256]{2,1,0:T(8,128)(2,1)} %copy-done.3), calls=%async_computation | async-start | bytes 2359296 | tf_op jit(solution)/shard_map/all_to_all | solution.py:446
  30.5 16.3 %all-to-all-done.refs_0_.x_ref = bf16[8,288,256]{2,1,0:T(8,128)(2,1)S(1)} async-done(((bf16[8,288,256]{2,1,0:T(8,128)(2,1)}), bf16[8,288,256]{2,1,0:T(8,128)(2,1)S(1)}, u32[]{:S(2)}, u32[]{:S(2)}) %all-to-all-start) | async-done | bytes 1179680 | tf_op jit(solution)/shard_map/all_to_all | solution.py:446
  48.6 22.6 %all_to_all.45 = bf16[16,8,16,256]{3,2,1,0:T(8,128)(2,1)S(1)} all-to-all(bf16[16,8,16,256]{3,2,1,0:T(8,128)(2,1)S(1)} %shard_map.114), channel_id=1, replica_groups=mesh['section'=2,'seq'=16,'tensor'=8] {'seq'}, dimensions={0} | all-to-all | bytes 2097152 | tf_op jit(solution)/shard_map/all_to_all | solution.py:452
  73.7 8.6 %all-to-all-start.2 = ((bf16[128,16,256]{2,1,0:T(8,128)(2,1)}), bf16[128,16,256]{2,1,0:T(8,128)(2,1)}, u32[]{:S(2)}, u32[]{:S(2)}) async-start(bf16[128,16,256]{2,1,0:T(8,128)(2,1)} %bitcast.40), calls=%async_computation.2 | async-start | bytes 2097152 | tf_op jit(solution)/shard_map/all_to_all | solution.py:459
  82.9 6.2 %shard_map.117.map_ref = bf16[8,2048,256]{2,1,0:T(8,128)(2,1)} custom-call(bf16[32,64,64]{2,1,0:T(8,128)(2,1)S(1)} %copy-done.12, bf16[32,2048]{1,0:T(8,128)(2,1)S(1)} %copy-done.20), custom_call_target="tpu_custom_call" | custom-call | tf_op jit(solution)/shard_map/pallas_call | solution.py:175
  89.1 7.5 %shard_map.118.gate_ref = f32[8,256,256]{2,1,0:T(8,128)S(1)} custom-call(bf16[256,2048]{1,0:T(8,128)(2,1)S(1)} %shard_map.116.normed_ref, bf16[8,2048,256]{2,1,0:T(8,128)(2,1)} %shard_map.117.map_ref), custom_call_target="tpu_custom_call" | custom-call | tf_op jit(solution)/shard_map/pallas_call | solution.py:220
  97.9 6.2 %shard_map.119.map_ref = bf16[8,2048,256]{2,1,0:T(8,128)(2,1)} custom-call(bf16[32,64,64]{2,1,0:T(8,128)(2,1)S(1)} %copy-done.13, bf16[32,2048]{1,0:T(8,128)(2,1)S(1)} %copy-done.21), custom_call_target="tpu_custom_call" | custom-call | tf_op jit(solution)/shard_map/pallas_call | solution.py:175
  104.1 6.2 %all-to-all-done.2 = bf16[128,16,256]{2,1,0:T(8,128)(2,1)} async-done(((bf16[128,16,256]{2,1,0:T(8,128)(2,1)}), bf16[128,16,256]{2,1,0:T(8,128)(2,1)}, u32[]{:S(2)}, u32[]{:S(2)}) %all-to-all-start.2) | async-done | bytes 1048608 | tf_op jit(solution)/shard_map/all_to_all | solution.py:459
  110.3 9.6 %shard_map.120 = (bf16[2,2048]{1,0:T(2,128)(2,1)S(1)}, bf16[8,272,256]{2,1,0:T(8,128)(2,1)S(1)}, bf16[256,2048]{1,0:T(8,128)(2,1)S(1)}) custom-call(bf16[16,8,16,256]{3,2,1,0:T(8,128)(2,1)} %bitcast.22.seq_ref, f32[8,256,256]{2,1,0:T(8,128)} %copy-done.2, bf16[8,288,256]{2,1,0:T(8,128)(2,1)S(1)} %all-to-all-done.refs_0_.x_ref, ...), custom_call_target="tpu_custom_call" | custom-call | tf_op jit(solution)/shard_map/pallas_call | solution.py:287
  121.9 3.7 %all-to-all-start.3 = ((bf16[8,272,256]{2,1,0:T(8,128)(2,1)}), bf16[8,272,256]{2,1,0:T(8,128)(2,1)S(1)}, u32[]{:S(2)}, u32[]{:S(2)}) async-start(bf16[8,272,256]{2,1,0:T(8,128)(2,1)} %copy-done.4), calls=%async_computation.3 | async-start | bytes 2228224 | tf_op jit(solution)/shard_map/all_to_all | solution.py:482
  125.7 6.2 %shard_map.122.map_ref = bf16[8,2048,256]{2,1,0:T(8,128)(2,1)} custom-call(bf16[32,64,64]{2,1,0:T(8,128)(2,1)S(1)} %copy-done.10, bf16[32,2048]{1,0:T(8,128)(2,1)S(1)} %get-tuple-element.94.second_ref), custom_call_target="tpu_custom_call" | custom-call | tf_op jit(solution)/shard_map/pallas_call | solution.py:175
  131.9 7.5 %shard_map.123.gate_ref = f32[8,256,256]{2,1,0:T(8,128)S(1)} custom-call(bf16[256,2048]{1,0:T(8,128)(2,1)S(1)} %copy-done.19, bf16[8,2048,256]{2,1,0:T(8,128)(2,1)} %shard_map.122.map_ref), custom_call_target="tpu_custom_call" | custom-call | tf_op jit(solution)/shard_map/pallas_call | solution.py:220
  139.4 6.2 %shard_map.124.map_ref = bf16[8,2048,256]{2,1,0:T(8,128)(2,1)} custom-call(bf16[32,64,64]{2,1,0:T(8,128)(2,1)S(1)} %copy-done.11, bf16[32,2048]{1,0:T(8,128)(2,1)S(1)} %get-tuple-element.96.second_ref), custom_call_target="tpu_custom_call" | custom-call | tf_op jit(solution)/shard_map/pallas_call | solution.py:175
  145.6 7.0 %all-to-all-done.3.x_ref.refs_0_ = bf16[8,272,256]{2,1,0:T(8,128)(2,1)S(1)} async-done(((bf16[8,272,256]{2,1,0:T(8,128)(2,1)}), bf16[8,272,256]{2,1,0:T(8,128)(2,1)S(1)}, u32[]{:S(2)}, u32[]{:S(2)}) %all-to-all-start.3) | async-done | bytes 1114144 | tf_op jit(solution)/shard_map/all_to_all | solution.py:482
  154.3 16.7 %all_to_all.46 = bf16[16,8,16,256]{3,2,1,0:T(8,128)(2,1)S(1)} all-to-all(bf16[16,8,16,256]{3,2,1,0:T(8,128)(2,1)S(1)} %shard_map.121), channel_id=1, replica_groups=mesh['section'=2,'seq'=16,'tensor'=8] {'seq'}, dimensions={0} | all-to-all | bytes 2097152 | tf_op jit(solution)/shard_map/all_to_all | solution.py:452
  172.6 32.3 %all_to_all.47 = bf16[128,16,256]{2,1,0:T(8,128)(2,1)S(1)} all-to-all(bf16[128,16,256]{2,1,0:T(8,128)(2,1)S(1)} %bitcast.43), channel_id=1, replica_groups=mesh['section'=2,'seq'=16,'tensor'=8] {'seq','tensor'}, dimensions={0} | all-to-all | bytes 2097152 | tf_op jit(solution)/shard_map/all_to_all | solution.py:459
  204.9 7.6 %shard_map.126 = (bf16[2,2048]{1,0:T(2,128)(2,1)S(1)}, bf16[8,256,256]{2,1,0:T(8,128)(2,1)S(1)}) custom-call(bf16[16,8,16,256]{3,2,1,0:T(8,128)(2,1)S(1)} %bitcast.39, f32[8,256,256]{2,1,0:T(8,128)S(1)} %shard_map.123.gate_ref, bf16[8,272,256]{2,1,0:T(8,128)(2,1)S(1)} %copy-done.5, bf16[8,2048,256]{2,1,0:T(8,128)(2,1)} %shard_map.124.map_ref), custom_call_target="tpu_custom_call" | custom-call | tf_op jit(solution)/shard_map/pallas_call | solution.py:287
  213.5 16.3 %all_to_all.48 = bf16[16,2,2048]{2,1,0:T(2,128)(2,1)S(1)} all-to-all(bf16[16,2,2048]{2,1,0:T(2,128)(2,1)S(1)} %bitcast.55), channel_id=1, replica_groups=mesh['section'=2,'seq'=16,'tensor'=8] {'section','tensor'}, dimensions={0} | all-to-all | bytes 262144 | tf_op jit(solution)/shard_map/all_to_all | solution.py:492
  229.8 4.2 %all-to-all-start.7 = ((bf16[8,256,256]{2,1,0:T(8,128)(2,1)}), bf16[8,256,256]{2,1,0:T(8,128)(2,1)}, u32[]{:S(2)}, u32[]{:S(2)}) async-start(bf16[8,256,256]{2,1,0:T(8,128)(2,1)} %copy-done.17), calls=%async_computation.7 | async-start | bytes 2097152 | tf_op jit(solution)/shard_map/all_to_all | solution.py:494
  237.0 4.7 %collective-permute-start.13 = (bf16[8,272,256]{2,1,0:T(8,128)(2,1)S(1)}, bf16[8,272,256]{2,1,0:T(8,128)(2,1)}, u32[]{:S(2)}, u32[]{:S(2)}) collective-permute-start(bf16[8,272,256]{2,1,0:T(8,128)(2,1)S(1)} %all-to-all-done.3.x_ref.refs_0_), channel_id=1, source_target_pairs={{128,0},{129,1},{130,2},{131,3},{132,4},{133,5},{134,6},{135,7},{1... | collective-permute-start | bytes 3342344 | tf_op jit(solution)/shard_map/ppermute | solution.py:512
  248.1 13.0 %all-to-all-done.7.refs_3_ = bf16[8,256,256]{2,1,0:T(8,128)(2,1)} async-done(((bf16[8,256,256]{2,1,0:T(8,128)(2,1)}), bf16[8,256,256]{2,1,0:T(8,128)(2,1)}, u32[]{:S(2)}, u32[]{:S(2)}) %all-to-all-start.7) | async-done | bytes 1048608 | tf_op jit(solution)/shard_map/all_to_all | solution.py:494
  263.1 6.1 %all-to-all-start.8 = ((f32[128,2,128]{2,1,0:T(2,128)}), f32[128,2,128]{2,1,0:T(2,128)S(1)}, u32[]{:S(2)}, u32[]{:S(2)}) async-start(f32[128,2,128]{2,1,0:T(2,128)} %broadcast_in_dim.5), calls=%async_computation.8 | async-start | bytes 262144 | tf_op jit(solution)/shard_map/all_to_all | solution.py:44
  271.6 5.7 %shard_map.128 = bf16[2,8,256,256]{3,2,1,0:T(8,128)(2,1)} custom-call(s32[1]{0:T(128)} %bitcast.30.section_ref, bf16[8,272,256]{2,1,0:T(8,128)(2,1)S(1)} %all-to-all-done.3.x_ref.refs_0_, bf16[8,272,256]{2,1,0:T(8,128)(2,1)} %collective-permute-done.13.refs_1_, bf16[8,256,256]{2,1,0:T(8,128)(2,1)S(1)} %copy-done.16, bf16[8,256,256]{2,1,0:T(8,128)(2,1)} %all-to-all-done.7.refs_3_), custom_call_target="tpu_custom_call" | custom-call | tf_op jit(solution)/shard_map/pallas_call | solution.py:371
  (129 shorter events, 49.8 us)
Async XLA Ops:
  0.7 4.4 %collective-permute-start = (f32[1,256]{1,0:T(1,128)}, f32[1,256]{1,0:T(1,128)S(1)}, u32[]{:S(2)}, u32[]{:S(2)}) collective-permute-start(f32[1,256]{1,0:T(1,128)} %param.11), channel_id=1, source_target_pairs={{0,128},{128,0},{1,129},{129,1},{2,130},{130,2},{3,131},{131,3},{4... | collective-permute-start | bytes 3080 | tf_op jit(solution)/shard_map/ppermute | solution.py:408
  7.1 9.5 %collective-permute-start.7 = (bf16[32,2048]{1,0:T(8,128)(2,1)S(1)}, bf16[32,2048]{1,0:T(8,128)(2,1)S(1)}, u32[]{:S(2)}, u32[]{:S(2)}) collective-permute-start(bf16[32,2048]{1,0:T(8,128)(2,1)S(1)} %reshape.64), channel_id=1, source_target_pairs={{0,128},{128,0},{1,129},{129,1},{2,130},{130,2},{3,131},{131,3},{4... | collective-permute-start | bytes 393224 | tf_op jit(solution)/shard_map/ppermute | solution.py:408
  7.8 10.0 %collective-permute-start.2 = (bf16[16,128,128]{2,1,0:T(8,128)(2,1)S(1)}, bf16[16,128,128]{2,1,0:T(8,128)(2,1)}, u32[]{:S(2)}, u32[]{:S(2)}) collective-permute-start(bf16[16,128,128]{2,1,0:T(8,128)(2,1)S(1)} %bitcast.49), channel_id=1, source_target_pairs={{0,128},{128,0},{1,129},{129,1},{2,130},{130,2},{3,131},{131,3},{4... | collective-permute-start | bytes 1572872 | tf_op jit(solution)/shard_map/ppermute | solution.py:408
  7.9 19.9 %collective-permute-start.1 = (bf16[8,256,256]{2,1,0:T(8,128)(2,1)}, bf16[8,256,256]{2,1,0:T(8,128)(2,1)}, u32[]{:S(2)}, u32[]{:S(2)}) collective-permute-start(bf16[8,256,256]{2,1,0:T(8,128)(2,1)} %bitcast.47), channel_id=1, source_target_pairs={{0,128},{128,0},{1,129},{129,1},{2,130},{130,2},{3,131},{131,3},{4... | collective-permute-start | bytes 3145736 | tf_op jit(solution)/shard_map/ppermute | solution.py:408
  8.3 38.5 %all-to-all-start = ((bf16[8,288,256]{2,1,0:T(8,128)(2,1)}), bf16[8,288,256]{2,1,0:T(8,128)(2,1)S(1)}, u32[]{:S(2)}, u32[]{:S(2)}) async-start(bf16[8,288,256]{2,1,0:T(8,128)(2,1)} %copy-done.3), calls=%async_computation | async-start | bytes 2359296 | tf_op jit(solution)/shard_map/all_to_all | solution.py:446
  14.8 8.6 %collective-permute-start.5 = (bf16[32,64,64]{2,1,0:T(8,128)(2,1)}, bf16[32,64,64]{2,1,0:T(8,128)(2,1)}, u32[]{:S(2)}, u32[]{:S(2)}) collective-permute-start(bf16[32,64,64]{2,1,0:T(8,128)(2,1)} %bitcast.51), channel_id=1, source_target_pairs={{0,128},{128,0},{1,129},{129,1},{2,130},{130,2},{3,131},{131,3},{4... | collective-permute-start | bytes 786440 | tf_op jit(solution)/shard_map/ppermute | solution.py:408
  15.1 10.6 %collective-permute-start.6 = (bf16[32,64,64]{2,1,0:T(8,128)(2,1)}, bf16[32,64,64]{2,1,0:T(8,128)(2,1)}, u32[]{:S(2)}, u32[]{:S(2)}) collective-permute-start(bf16[32,64,64]{2,1,0:T(8,128)(2,1)} %bitcast.53), channel_id=1, source_target_pairs={{0,128},{128,0},{1,129},{129,1},{2,130},{130,2},{3,131},{131,3},{4... | collective-permute-start | bytes 786440 | tf_op jit(solution)/shard_map/ppermute | solution.py:408
  16.6 4.6 %collective-permute-start.8 = (bf16[32,2048]{1,0:T(8,128)(2,1)S(1)}, bf16[32,2048]{1,0:T(8,128)(2,1)S(1)}, u32[]{:S(2)}, u32[]{:S(2)}) collective-permute-start(bf16[32,2048]{1,0:T(8,128)(2,1)S(1)} %reshape.65), channel_id=1, source_target_pairs={{0,128},{128,0},{1,129},{129,1},{2,130},{130,2},{3,131},{131,3},{4... | collective-permute-start | bytes 393224 | tf_op jit(solution)/shard_map/ppermute | solution.py:408
  19.9 28.7 %collective-permute-start.3 = (bf16[2048,256]{1,0:T(8,128)(2,1)}, bf16[2048,256]{1,0:T(8,128)(2,1)}, u32[]{:S(2)}, u32[]{:S(2)}) collective-permute-start(bf16[2048,256]{1,0:T(8,128)(2,1)} %bitcast.15.refs_4_), channel_id=1, source_target_pairs={{0,8},{8,16},{16,24},{24,0},{32,40},{40,48},{48,56},{56,32},{64,72... | collective-permute-start | bytes 3145736 | tf_op jit(solution)/shard_map/ppermute | solution.py:413
  21.2 27.4 %collective-permute-start.4 = (bf16[2048,256]{1,0:T(8,128)(2,1)}, bf16[2048,256]{1,0:T(8,128)(2,1)}, u32[]{:S(2)}, u32[]{:S(2)}) collective-permute-start(bf16[2048,256]{1,0:T(8,128)(2,1)} %bitcast.15.refs_4_), channel_id=1, source_target_pairs={{0,24},{8,0},{16,8},{24,16},{32,56},{40,32},{48,40},{56,48},{64,88... | collective-permute-start | bytes 3145736 | tf_op jit(solution)/shard_map/ppermute | solution.py:413
  48.6 22.6 %copy-start.14 = (bf16[16,128,128]{2,1,0:T(8,128)(2,1)S(1)}, bf16[16,128,128]{2,1,0:T(8,128)(2,1)}, u32[]{:S(2)}) copy-start(bf16[16,128,128]{2,1,0:T(8,128)(2,1)} %get-tuple-element.68.left_ref) | copy-start | bytes 1572868
  73.7 36.7 %all-to-all-start.2 = ((bf16[128,16,256]{2,1,0:T(8,128)(2,1)}), bf16[128,16,256]{2,1,0:T(8,128)(2,1)}, u32[]{:S(2)}, u32[]{:S(2)}) async-start(bf16[128,16,256]{2,1,0:T(8,128)(2,1)} %bitcast.40), calls=%async_computation.2 | async-start | bytes 2097152 | tf_op jit(solution)/shard_map/all_to_all | solution.py:459
  121.9 30.7 %all-to-all-start.3 = ((bf16[8,272,256]{2,1,0:T(8,128)(2,1)}), bf16[8,272,256]{2,1,0:T(8,128)(2,1)S(1)}, u32[]{:S(2)}, u32[]{:S(2)}) async-start(bf16[8,272,256]{2,1,0:T(8,128)(2,1)} %copy-done.4), calls=%async_computation.3 | async-start | bytes 2228224 | tf_op jit(solution)/shard_map/all_to_all | solution.py:482
  125.6 28.7 %collective-permute-start.9 = (bf16[2048,256]{1,0:T(8,128)(2,1)}, bf16[2048,256]{1,0:T(8,128)(2,1)}, u32[]{:S(2)}, u32[]{:S(2)}) collective-permute-start(bf16[2048,256]{1,0:T(8,128)(2,1)} %bitcast.15.refs_4_), channel_id=1, source_target_pairs={{0,16},{8,24},{16,0},{24,8},{32,48},{40,56},{48,32},{56,40},{64,80... | collective-permute-start | bytes 3145736 | tf_op jit(solution)/shard_map/ppermute | solution.py:413
  153.8 17.2 %copy-start.9 = (bf16[16,128,128]{2,1,0:T(8,128)(2,1)S(1)}, bf16[16,128,128]{2,1,0:T(8,128)(2,1)}, u32[]{:S(2)}) copy-start(bf16[16,128,128]{2,1,0:T(8,128)(2,1)} %get-tuple-element.84.left_ref) | copy-start | bytes 1572868
  171.1 33.8 %copy-start.5 = (bf16[8,272,256]{2,1,0:T(8,128)(2,1)S(1)}, bf16[8,272,256]{2,1,0:T(8,128)(2,1)}, u32[]{:S(2)}) copy-start(bf16[8,272,256]{2,1,0:T(8,128)(2,1)} %copy-done.4) | copy-start | bytes 3342340
  213.4 23.5 %copy-start.30 = (s32[2,256]{1,0:T(2,128)S(1)}, s32[2,256]{1,0:T(2,128)}, u32[]{:S(2)}) copy-start(s32[2,256]{1,0:T(2,128)} %param.19) | copy-start | bytes 6148
  229.8 31.3 %all-to-all-start.7 = ((bf16[8,256,256]{2,1,0:T(8,128)(2,1)}), bf16[8,256,256]{2,1,0:T(8,128)(2,1)}, u32[]{:S(2)}, u32[]{:S(2)}) async-start(bf16[8,256,256]{2,1,0:T(8,128)(2,1)} %copy-done.17), calls=%async_computation.7 | async-start | bytes 2097152 | tf_op jit(solution)/shard_map/all_to_all | solution.py:494
  234.1 7.8 %collective-permute-start.10 = (bf16[32,2048]{1,0:T(8,128)(2,1)S(1)}, bf16[32,2048]{1,0:T(8,128)(2,1)S(1)}, u32[]{:S(2)}, u32[]{:S(2)}) collective-permute-start(bf16[32,2048]{1,0:T(8,128)(2,1)S(1)} %reshape.75.refs_0_), channel_id=1, source_target_pairs={{0,32},{8,40},{16,48},{24,56},{32,64},{40,72},{48,80},{56,88},{64,... | collective-permute-start | bytes 393224 | tf_op jit(solution)/shard_map/ppermute | solution.py:417
  234.2 7.7 %collective-permute-start.11 = (bf16[32,2048]{1,0:T(8,128)(2,1)S(1)}, bf16[32,2048]{1,0:T(8,128)(2,1)S(1)}, u32[]{:S(2)}, u32[]{:S(2)}) collective-permute-start(bf16[32,2048]{1,0:T(8,128)(2,1)S(1)} %reshape.75.refs_0_), channel_id=1, source_target_pairs={{0,64},{8,72},{16,80},{24,88},{32,96},{40,104},{48,112},{56,120},{... | collective-permute-start | bytes 393224 | tf_op jit(solution)/shard_map/ppermute | solution.py:417
  235.8 6.9 %collective-permute-start.12 = (bf16[32,2048]{1,0:T(8,128)(2,1)S(1)}, bf16[32,2048]{1,0:T(8,128)(2,1)S(1)}, u32[]{:S(2)}, u32[]{:S(2)}) collective-permute-start(bf16[32,2048]{1,0:T(8,128)(2,1)S(1)} %reshape.75.refs_0_), channel_id=1, source_target_pairs={{0,96},{8,104},{16,112},{24,120},{32,0},{40,8},{48,16},{56,24},{64... | collective-permute-start | bytes 393224 | tf_op jit(solution)/shard_map/ppermute | solution.py:417
  237.0 32.3 %collective-permute-start.13 = (bf16[8,272,256]{2,1,0:T(8,128)(2,1)S(1)}, bf16[8,272,256]{2,1,0:T(8,128)(2,1)}, u32[]{:S(2)}, u32[]{:S(2)}) collective-permute-start(bf16[8,272,256]{2,1,0:T(8,128)(2,1)S(1)} %all-to-all-done.3.x_ref.refs_0_), channel_id=1, source_target_pairs={{128,0},{129,1},{130,2},{131,3},{132,4},{133,5},{134,6},{135,7},{1... | collective-permute-start | bytes 3342344 | tf_op jit(solution)/shard_map/ppermute | solution.py:512
  261.1 8.1 %collective-permute-start.14 = (bf16[8,256,256]{2,1,0:T(8,128)(2,1)}, bf16[8,256,256]{2,1,0:T(8,128)(2,1)S(1)}, u32[]{:S(2)}, u32[]{:S(2)}) collective-permute-start(bf16[8,256,256]{2,1,0:T(8,128)(2,1)} %all-to-all-done.7.refs_3_), channel_id=1, source_target_pairs={{0,128},{1,129},{2,130},{3,131},{4,132},{5,133},{6,134},{7,135},{8... | collective-permute-start | bytes 3145736 | tf_op jit(solution)/shard_map/ppermute | solution.py:513
  263.1 17.3 %all-to-all-start.8 = ((f32[128,2,128]{2,1,0:T(2,128)}), f32[128,2,128]{2,1,0:T(2,128)S(1)}, u32[]{:S(2)}, u32[]{:S(2)}) async-start(f32[128,2,128]{2,1,0:T(2,128)} %broadcast_in_dim.5), calls=%async_computation.8 | async-start | bytes 262144 | tf_op jit(solution)/shard_map/all_to_all | solution.py:44
  (28 other events, 105.4 us)

commit v8 on v7

--- a/solution.py
+++ b/solution.py
@@ -66,28 +66,26 @@
     return high, mid, value - high - mid
 
 
-def pack_stage(x_own, gains):
+def split_stage(x_own, gains, tensor_index):
     rows, tokens, _ = x_own.shape
 
-    def kernel(x_ref, gain_a_ref, gain_b_ref, out_ref):
+    def kernel(z_ref, gain_a_ref, gain_b_ref, x_ref, shared_ref, *send_refs):
         row = lax.broadcasted_iota(jnp.int32, (rows, tokens), 0)
         squares = jnp.zeros((rows, tokens), F32)
         for p in range(rows):
             squares = jnp.where(row == p, squares_by_lane([x_ref[p]]), squares)
-        gain_rows = jnp.zeros((rows, BLK), F32)
-        for b, gain_ref in enumerate((gain_a_ref, gain_b_ref)):
-            for part, value in enumerate(split3(gain_ref[...])):
-                gain_rows = jnp.where(row == b * 3 + part, value, gain_rows)
-        planes = jnp.concatenate([*split3(squares), gain_rows], axis=0).astype(BF16)
-        for p in range(rows):
-            out_ref[p, :tokens] = x_ref[p]
-            out_ref[p, tokens:] = planes
-
-    return pl.pallas_call(
-        kernel,
-        out_shape=shape_of((rows, tokens + 4 * rows, BLK)),
-        compiler_params=params(),
-    )(x_own, *gains)
+        shared_ref[:rows] = squares
+        shared_ref[rows:] = jnp.where(row == 0, gain_a_ref[...], gain_b_ref[...])
+        for d in range(rows):
+            send_refs[d][...] = x_ref[(z_ref[0] + d) % rows]
+
+    outs = [shape_of((2 * rows, tokens), F32)] + [shape_of((tokens, BLK))] * rows
+    return pl.pallas_call(
+        kernel,
+        in_specs=[scalar_spec()] + [whole((1, BLK))] * 2 + [whole(x_own.shape)],
+        out_shape=outs,
+        compiler_params=params(),
+    )(tensor_index, *gains, x_own)
 
 
 def right_stage(x_chan, gain_local, right, groups, shared=None):
@@ -99,11 +97,9 @@
     def kernel(x_ref, gain_ref, right_ref, *refs):
         out_ref = refs[-1]
         if shared is not None:
-            squares = jnp.zeros((rows, tokens), F32)
-            for z in range(shared.shape[0]):
-                planes = refs[0][z, tokens:].astype(F32)
-                for part in range(3):
-                    squares = squares + planes[part * rows : (part + 1) * rows]
+            squares = refs[0][0, :rows]
+            for z in range(1, shared.shape[0]):
+                squares = squares + refs[0][z, :rows]
         for p in range(rows):
             if shared is None:
                 extra = x_ref[p, tokens : tokens + EXTRA].astype(F32)
@@ -193,20 +189,26 @@
         store(n, (x.astype(F32) * scale * gain_ref[n]).astype(BF16))
 
 
-def token_stage(x_tok, gain, tokens):
-    n_blk = x_tok.shape[0]
-
-    def kernel(gain_ref, x_ref, normed_ref):
+def token_stage(received, gain, tensor_index):
+    n_blk = len(received)
+    tokens = received[0].shape[0]
+
+    def kernel(z_ref, gain_ref, *refs):
+        x_ref, normed_ref = refs[n_blk:]
+        for d in range(n_blk):
+            x_ref[(z_ref[0] + n_blk - d) % n_blk] = refs[d][...]
+
         def store(n, value):
             normed_ref[:, n * BLK : (n + 1) * BLK] = value
 
-        normalize([x_ref[n, :tokens] for n in range(n_blk)], gain_ref, tokens, store)
-
-    return pl.pallas_call(
-        kernel,
-        out_shape=shape_of((tokens, D)),
-        compiler_params=params(),
-    )(gain, x_tok)
+        normalize([x_ref[n] for n in range(n_blk)], gain_ref, tokens, store)
+
+    return pl.pallas_call(
+        kernel,
+        in_specs=[scalar_spec(), whole(gain.shape)] + [whole((tokens, BLK))] * n_blk,
+        out_shape=(shape_of((n_blk, tokens, BLK)), shape_of((tokens, D))),
+        compiler_params=params(),
+    )(tensor_index, gain, *received)
 
 
 def gate_stage(normed, gate_map):
@@ -412,6 +414,9 @@
         route = [(i, i - i % y_count + (i + distance) % y_count) for i in range(seq_count)]
         return lax.ppermute(block, "seq", route)
 
+    def along_z(block, distance):
+        return lax.ppermute(block, "tensor", [(i, (i + distance) % n_blk) for i in range(n_blk)])
+
     def along_x(block, distance):
         route = [(i, (i + distance * y_count) % seq_count) for i in range(seq_count)]
         return lax.ppermute(block, "seq", route)
@@ -426,27 +431,15 @@
     )
     gain_local = by_block(norm_gain)
 
-    packed = pack_stage(x_own, gain_local)
-    packed, *own = tie(
-        (
-            packed,
-            right_blocks[0],
-            left_blocks[0],
-            gate_first[0],
-            out_first[0],
-            gate_second,
-            out_second,
-            head[0],
-        )
-    )
-    rights, lefts, gate_firsts, out_firsts = (by_block(w) for w in own[:4])
-    gate_seconds, out_seconds = (by_block(rows_second(w)) for w in own[4:6])
-    lefts, head_own = tie((lefts, own[6]))
-    heads = [head_own, along_y(head_own, 1), None, along_y(head_own, 3)]
-    x_tok = lax.all_to_all(packed, "tensor", split_axis=0, concat_axis=0, tiled=True)
-    gain_rows = x_tok[:, tokens + 3 * rows_dev :][:, :6].astype(F32)
-    gain_rows = jnp.sum(gain_rows.reshape(n_blk, 2, 3, BLK), axis=2)
-    gains = [gain_rows[:, b : b + 1] for b in range(2)]
+    shared, *sends = split_stage(x_own, gain_local, z_scalar)
+    shared, right_own, left_own = tie((shared, right_blocks[0], left_blocks[0]))
+    rights = by_block(right_own)
+    near = [1, 2, n_blk - 2, n_blk - 1]
+    received = [sends[0]] + [None] * (n_blk - 1)
+    for d in near:
+        received[d] = along_z(sends[d], d)
+    shared = gather_by_exchange(shared, "tensor")
+    gains = [shared[:, rows_dev + b][:, None] for b in range(2)]
 
     def exchange_seq(mix):
         return lax.all_to_all(mix, "seq", split_axis=0, concat_axis=0, tiled=True)
@@ -459,32 +452,41 @@
         out = lax.all_to_all(cols, everyone, split_axis=0, concat_axis=0, tiled=True)
         return out.reshape(seq_count, n_blk, j_dev, BLK)
 
-    mix = right_stage(x_own, gain_local[0], rights[0], seq_count, shared=x_tok)
-    mix, heads[1], heads[3], lefts, gate_firsts, out_firsts, gate_seconds, out_seconds = tie(
-        (mix, heads[1], heads[3], lefts, gate_firsts, out_firsts, gate_seconds, out_seconds)
-    )
+    mix = right_stage(x_own, gain_local[0], rights[0], seq_count, shared=shared)
+    mix, left_own, sends, near_blocks = tie((mix, left_own, sends, [received[d] for d in near]))
+    for d, block in zip(near, near_blocks):
+        received[d] = block
     cols = exchange_seq(mix)
+    lefts = by_block(left_own)
+    for d in range(3, n_blk - 2):
+        received[d] = along_z(sends[d], d)
 
     cols = mix_left(cols, 0)
-    cols, gate_firsts, out_firsts, gate_seconds, out_seconds = tie(
-        (cols, gate_firsts, out_firsts, gate_seconds, out_seconds)
+    cols, received, *own = tie(
+        (cols, received, gate_first[0], out_first[0], gate_second, out_second)
     )
     seq_out = exchange_all(cols)
-    normed = token_stage(x_tok, gains[0], tokens)
+    gate_firsts, out_firsts = (by_block(w) for w in own[:2])
+    gate_seconds, out_seconds = (by_block(rows_second(w)) for w in own[2:])
+    x_tok, normed = token_stage(received, gains[0], z_scalar)
     gate = gate_stage(normed, channel_map(gate_firsts[0], gate_seconds[0], n_blk))
     out_map = channel_map(out_firsts[0], out_seconds[0], n_blk)
     rows_one, packed, normed = out_stage(seq_out, gate, x_tok, out_map, gain=gains[1])
 
-    packed, normed, heads[0], gate_two, out_two, gate_sec, out_sec = tie(
-        (packed, normed, heads[0], gate_firsts[1], out_firsts[1], gate_seconds[1], out_seconds[1])
+    packed, normed, head_own, gate_two, out_two, gate_sec, out_sec = tie(
+        (packed, normed, head[0], gate_firsts[1], out_firsts[1], gate_seconds[1], out_seconds[1])
     )
-    heads[2] = along_y(heads[0], 2)
+    heads = [head_own, along_y(head_own, 1), None, along_y(head_own, 3)]
     chan_one = lax.all_to_all(packed, "tensor", split_axis=0, concat_axis=0, tiled=True)
     gate = gate_stage(normed, channel_map(gate_two, gate_sec, n_blk))
     out_map = channel_map(out_two, out_sec, n_blk)
     mix = right_stage(chan_one, gain_local[1], rights[1], seq_count)
-    mix, gate, out_map, heads[2] = tie((mix, gate, out_map, heads[2]))
-    seq_out = exchange_all(mix_left(exchange_seq(mix), 1))
+    mix, gate, out_map, heads = tie((mix, gate, out_map, [heads[0], heads[1], heads[3]]))
+    cols = mix_left(exchange_seq(mix), 1)
+    cols, heads = tie((cols, heads))
+    seq_out = exchange_all(cols)
+    seq_out, far_head = tie((seq_out, along_y(heads[0], 2)))
+    heads = [*heads[:2], far_head, heads[2]]
     rows_two, result = out_stage(seq_out, gate, packed, out_map)
 
     pair = jnp.stack([rows_one, rows_two])[:, None]

time: 284 us -> 305 us (1.074)
  blocking collectives: 87.9 us -> 36.7 us
  starting transfers between devices: 46.3 us -> 88 us
  waiting for transfers between devices: 46.5 us -> 72.6 us
  Pallas kernels: 70.9 us -> 75.3 us
  local copies, waits for them, and re-layouts: 17.7 us -> 22 us
    ppermute x3, waiting for transfers between devices: 0.01 us -> 35.1 us  [along_y(): return lax.ppermute(block, 'seq', route)]
    all_to_all x1 -> x0, blocking collectives: 32.3 us -> none  [exchange_all(): lax.all_to_all(cols, everyone, split_axis=0, concat_axis=0, tiled=True)]
    all_to_all x2 -> x1, blocking collectives: 39.3 us -> 22.6 us  [exchange_seq(): return lax.all_to_all(mix, 'seq', split_axis=0, concat_axis=0, tiled=True)]
    all_to_all x2 -> x1, waiting for transfers between devices: 23.4 us -> 8.1 us  [body(): lax.all_to_all(packed, 'tensor', split_axis=0, concat_axis=0, tiled=True)]
    all_to_all x1 -> x2, starting transfers between devices: 8.63 us -> 22.5 us  [exchange_all(): lax.all_to_all(cols, everyone, split_axis=0, concat_axis=0, tiled=True)]
    ppermute x0 -> x7, starting transfers between devices: none -> 13.2 us  [along_z(): lax.ppermute(block, 'tensor', [(i, (i + distance) % n_blk) for i in range...]
    ppermute x0 -> x7, waiting for transfers between devices: none -> 7.82 us  [along_z(): lax.ppermute(block, 'tensor', [(i, (i + distance) % n_blk) for i in range...]
    all_to_all x1 -> x2, starting transfers between devices: 6.15 us -> 13.3 us  [gather_by_exchange(): return lax.all_to_all(copies, axis, split_axis=0, concat_axis=0, tiled=True)]
  transfers between devices with their start and end apart: 20 -> 29, of which waited for: 6 -> 11; matrix products, arithmetic and copies ran while one was open for 5% -> 4% of each run, Pallas kernels for 18% -> 18%
where the time goes in v8:
time: 305 us; the launch traced here: 304 us
  starting transfers between devices  88 us (29%)
  Pallas kernels  75.3 us (25%)
  waiting for transfers between devices  72.6 us (24%)
  blocking collectives  36.7 us (12%)
  local copies, waits for them, and re-layouts  22 us (7%)
  other arithmetic  8.22 us (3%)
    ppermute x3, waiting for transfers between devices, along_y(): return lax.ppermute(block, 'seq', route)  35.1 us
    pallas_call x4, Pallas kernels, channel_map(): pl.pallas_call(kernel, grid=(n_blk,), in_specs=[whole((C1, C2, C2)), pl.B...  24.3 us
    all_to_all x1, blocking collectives, exchange_seq(): return lax.all_to_all(mix, 'seq', split_axis=0, concat_axis=0, tiled=True)  22.6 us
    all_to_all x2, starting transfers between devices, exchange_all(): lax.all_to_all(cols, everyone, split_axis=0, concat_axis=0, tiled=True)  22.5 us
    pallas_call x2, Pallas kernels, out_stage(): pl.pallas_call(kernel, grid=(n_blk,), in_specs=in_specs, out_specs=[whole...  18.8 us
    unnamed x76, local copies, waits for them, and re-layouts  18.1 us
    pallas_call x2, Pallas kernels, gate_stage(): pl.pallas_call(kernel, grid=(n_blk,), in_specs=[whole(normed.shape), pl.B...  14.9 us
    all_to_all x1, blocking collectives, body(): lax.all_to_all(pair, ('section', 'tensor'), split_axis=0, concat_axis=0,...  14 us
  transfers between devices with their start and end apart: 29, of which 11 were waited for; matrix products, arithmetic and copies ran while one was open for 4% of the time, Pallas kernels for 18%

profile of v8, /device:TPU:1, one launch (start us, length us, event | category | flops | bytes accessed | tf_op | source)
XLA Modules:
  0.0 303.8 jit_solution(12706813457202601963)
XLA Ops:
  7.7 6.4 %all-to-all-start = ((f32[8,16,256]{2,1,0:T(8,128)}), f32[8,16,256]{2,1,0:T(8,128)S(1)}, u32[]{:S(2)}, u32[]{:S(2)}) async-start(f32[8,16,256]{2,1,0:T(8,128)} %broadcast_in_dim.6), calls=%async_computation | async-start | bytes 262144 | tf_op jit(solution)/shard_map/all_to_all | solution.py:44
  24.1 4.3 %collective-permute-done.3.refs_2_ = bf16[256,256]{1,0:T(8,128)(2,1)} collective-permute-done((bf16[256,256]{1,0:T(8,128)(2,1)}, bf16[256,256]{1,0:T(8,128)(2,1)}, u32[]{:S(2)}, u32[]{:S(2)}) %collective-permute-start.3) | collective-permute-done | bytes 131104 | tf_op jit(solution)/shard_map/ppermute | solution.py:418
  29.5 6.8 %all-to-all-start.1 = ((bf16[16,8,16,256]{3,2,1,0:T(8,128)(2,1)}), bf16[16,8,16,256]{3,2,1,0:T(8,128)(2,1)S(1)}, u32[]{:S(2)}, u32[]{:S(2)}) async-start(bf16[16,8,16,256]{3,2,1,0:T(8,128)(2,1)} %shard_map.114), calls=%async_computation.1 | async-start | bytes 2097152 | tf_op jit(solution)/shard_map/all_to_all | solution.py:445
  37.7 3.7 %collective-permute-start.7 = (bf16[256,256]{1,0:T(8,128)(2,1)}, bf16[256,256]{1,0:T(8,128)(2,1)S(1)}, u32[]{:S(2)}, u32[]{:S(2)}) collective-permute-start(bf16[256,256]{1,0:T(8,128)(2,1)} %get-tuple-element.84), channel_id=1, source_target_pairs={{0,3},{1,4},{2,5},{3,6},{4,7},{5,0},{6,1},{7,2},{8,11},{9,12},{10,... | collective-permute-start | bytes 393224 | tf_op jit(solution)/shard_map/ppermute | solution.py:418
  46.7 4.9 %all-to-all-done.1 = bf16[16,8,16,256]{3,2,1,0:T(8,128)(2,1)S(1)} async-done(((bf16[16,8,16,256]{3,2,1,0:T(8,128)(2,1)}), bf16[16,8,16,256]{3,2,1,0:T(8,128)(2,1)S(1)}, u32[]{:S(2)}, u32[]{:S(2)}) %all-to-all-start.1) | async-done | bytes 1048608 | tf_op jit(solution)/shard_map/all_to_all | solution.py:445
  56.5 15.2 %all-to-all-start.2 = ((bf16[128,16,256]{2,1,0:T(8,128)(2,1)}), bf16[128,16,256]{2,1,0:T(8,128)(2,1)}, u32[]{:S(2)}, u32[]{:S(2)}) async-start(bf16[128,16,256]{2,1,0:T(8,128)(2,1)} %bitcast.15), calls=%async_computation.2 | async-start | bytes 2097152 | tf_op jit(solution)/shard_map/all_to_all | solution.py:452
  82.0 6.1 %shard_map.117.map_ref = bf16[8,2048,256]{2,1,0:T(8,128)(2,1)} custom-call(bf16[32,64,64]{2,1,0:T(8,128)(2,1)S(1)} %get-tuple-element.139.first_ref, bf16[32,2048]{1,0:T(8,128)(2,1)S(1)} %get-tuple-element.145.second_ref), custom_call_target="tpu_custom_call" | custom-call | tf_op jit(solution)/shard_map/pallas_call | solution.py:171
  88.1 7.4 %shard_map.118.gate_ref = f32[8,256,256]{2,1,0:T(8,128)S(1)} custom-call(bf16[256,2048]{1,0:T(8,128)(2,1)S(1)} %get-tuple-element.98.normed_ref, bf16[8,2048,256]{2,1,0:T(8,128)(2,1)} %shard_map.117.map_ref), custom_call_target="tpu_custom_call" | custom-call | tf_op jit(solution)/shard_map/pallas_call | solution.py:222
  98.9 6.1 %shard_map.119.map_ref = bf16[8,2048,256]{2,1,0:T(8,128)(2,1)} custom-call(bf16[32,64,64]{2,1,0:T(8,128)(2,1)S(1)} %get-tuple-element.137.first_ref, bf16[32,2048]{1,0:T(8,128)(2,1)S(1)} %get-tuple-element.143.second_ref), custom_call_target="tpu_custom_call" | custom-call | tf_op jit(solution)/shard_map/pallas_call | solution.py:171
  105.0 10.6 %shard_map.120 = (bf16[2,2048]{1,0:T(2,128)(2,1)S(1)}, bf16[8,272,256]{2,1,0:T(8,128)(2,1)}, bf16[256,2048]{1,0:T(8,128)(2,1)S(1)}) custom-call(bf16[16,8,16,256]{3,2,1,0:T(8,128)(2,1)} %bitcast.18.seq_ref, f32[8,256,256]{2,1,0:T(8,128)} %copy-done.2, bf16[8,256,256]{2,1,0:T(8,128)(2,1)S(1)} %copy-done.16, bf16[8,2048,256]{2,1,0:T(8,128)(2,1)} %shard_map.119.map_ref, ...), custom_call_target="tpu_custom_call" | custom-call | tf_op jit(solution)/shard_map/pallas_call | solution.py:289
  116.5 6.1 %all-to-all-start.3 = ((bf16[8,272,256]{2,1,0:T(8,128)(2,1)}), bf16[8,272,256]{2,1,0:T(8,128)(2,1)S(1)}, u32[]{:S(2)}, u32[]{:S(2)}) async-start(bf16[8,272,256]{2,1,0:T(8,128)(2,1)} %get-tuple-element.107.x_ref), calls=%async_computation.3 | async-start | bytes 2228224 | tf_op jit(solution)/shard_map/all_to_all | solution.py:480
  125.5 6.1 %shard_map.122.map_ref = bf16[8,2048,256]{2,1,0:T(8,128)(2,1)} custom-call(bf16[32,64,64]{2,1,0:T(8,128)(2,1)S(1)} %copy-done.8, bf16[32,2048]{1,0:T(8,128)(2,1)S(1)} %get-tuple-element.110.second_ref), custom_call_target="tpu_custom_call" | custom-call | tf_op jit(solution)/shard_map/pallas_call | solution.py:171
  131.6 7.5 %shard_map.123.gate_ref = f32[8,256,256]{2,1,0:T(8,128)S(1)} custom-call(bf16[256,2048]{1,0:T(8,128)(2,1)S(1)} %copy-done.18, bf16[8,2048,256]{2,1,0:T(8,128)(2,1)} %shard_map.122.map_ref), custom_call_target="tpu_custom_call" | custom-call | tf_op jit(solution)/shard_map/pallas_call | solution.py:222
  139.1 6.1 %shard_map.124.map_ref = bf16[8,2048,256]{2,1,0:T(8,128)(2,1)} custom-call(bf16[32,64,64]{2,1,0:T(8,128)(2,1)S(1)} %copy-done.9, bf16[32,2048]{1,0:T(8,128)(2,1)S(1)} %get-tuple-element.112.second_ref), custom_call_target="tpu_custom_call" | custom-call | tf_op jit(solution)/shard_map/pallas_call | solution.py:171
  145.2 8.1 %all-to-all-done.3.x_ref.refs_0_ = bf16[8,272,256]{2,1,0:T(8,128)(2,1)S(1)} async-done(((bf16[8,272,256]{2,1,0:T(8,128)(2,1)}), bf16[8,272,256]{2,1,0:T(8,128)(2,1)S(1)}, u32[]{:S(2)}, u32[]{:S(2)}) %all-to-all-start.3) | async-done | bytes 1114144 | tf_op jit(solution)/shard_map/all_to_all | solution.py:480
  155.0 22.6 %all_to_all.45 = bf16[16,8,16,256]{3,2,1,0:T(8,128)(2,1)S(1)} all-to-all(bf16[16,8,16,256]{3,2,1,0:T(8,128)(2,1)S(1)} %shard_map.121), channel_id=1, replica_groups=mesh['section'=2,'seq'=16,'tensor'=8] {'seq'}, dimensions={0} | all-to-all | bytes 2097152 | tf_op jit(solution)/shard_map/all_to_all | solution.py:445
  180.1 7.3 %all-to-all-start.5 = ((bf16[128,16,256]{2,1,0:T(8,128)(2,1)}), bf16[128,16,256]{2,1,0:T(8,128)(2,1)}, u32[]{:S(2)}, u32[]{:S(2)}) async-start(bf16[128,16,256]{2,1,0:T(8,128)(2,1)} %bitcast.40), calls=%async_computation.5 | async-start | bytes 2097152 | tf_op jit(solution)/shard_map/all_to_all | solution.py:452
  189.5 35.1 %collective-permute-done.16.refs_6_ = bf16[2048,256]{1,0:T(8,128)(2,1)S(1)} collective-permute-done((bf16[2048,256]{1,0:T(8,128)(2,1)}, bf16[2048,256]{1,0:T(8,128)(2,1)S(1)}, u32[]{:S(2)}, u32[]{:S(2)}) %collective-permute-start.16) | collective-permute-done | bytes 1048608 | tf_op jit(solution)/shard_map/ppermute | solution.py:415
  225.6 8.3 %shard_map.126 = (bf16[2,2048]{1,0:T(2,128)(2,1)S(1)}, bf16[8,256,256]{2,1,0:T(8,128)(2,1)S(1)}) custom-call(bf16[16,8,16,256]{3,2,1,0:T(8,128)(2,1)} %bitcast.27.seq_ref, f32[8,256,256]{2,1,0:T(8,128)S(1)} %shard_map.123.gate_ref, bf16[8,272,256]{2,1,0:T(8,128)(2,1)} %get-tuple-element.107.x_ref, bf16[8,2048,256]{2,1,0:T(8,128)(2,1)} %shard_map.124.map_ref), custom_call_target="tpu_custom_call" | custom-call | tf_op jit(solution)/shard_map/pallas_call | solution.py:289
  235.0 14.0 %all_to_all.46 = bf16[16,2,2048]{2,1,0:T(2,128)(2,1)S(1)} all-to-all(bf16[16,2,2048]{2,1,0:T(2,128)(2,1)S(1)} %bitcast.51), channel_id=1, replica_groups=mesh['section'=2,'seq'=16,'tensor'=8] {'section','tensor'}, dimensions={0} | all-to-all | bytes 262144 | tf_op jit(solution)/shard_map/all_to_all | solution.py:494
  257.2 5.0 %collective-permute-start.20 = (bf16[8,272,256]{2,1,0:T(8,128)(2,1)S(1)}, bf16[8,272,256]{2,1,0:T(8,128)(2,1)}, u32[]{:S(2)}, u32[]{:S(2)}) collective-permute-start(bf16[8,272,256]{2,1,0:T(8,128)(2,1)S(1)} %all-to-all-done.3.x_ref.refs_0_), channel_id=1, source_target_pairs={{128,0},{129,1},{130,2},{131,3},{132,4},{133,5},{134,6},{135,7},{1... | collective-permute-start | bytes 3342344 | tf_op jit(solution)/shard_map/ppermute | solution.py:514
  269.6 12.2 %all-to-all-done.7.refs_3_ = bf16[8,256,256]{2,1,0:T(8,128)(2,1)S(1)} async-done(((bf16[8,256,256]{2,1,0:T(8,128)(2,1)}), bf16[8,256,256]{2,1,0:T(8,128)(2,1)S(1)}, u32[]{:S(2)}, u32[]{:S(2)}) %all-to-all-start.7) | async-done | bytes 1048608 | tf_op jit(solution)/shard_map/all_to_all | solution.py:496
  284.7 6.9 %all-to-all-start.8 = ((f32[128,2,128]{2,1,0:T(2,128)}), f32[128,2,128]{2,1,0:T(2,128)S(1)}, u32[]{:S(2)}, u32[]{:S(2)}) async-start(f32[128,2,128]{2,1,0:T(2,128)} %broadcast_in_dim.8), calls=%async_computation.8 | async-start | bytes 262144 | tf_op jit(solution)/shard_map/all_to_all | solution.py:44
  295.2 5.4 %shard_map.128 = bf16[2,8,256,256]{3,2,1,0:T(8,128)(2,1)} custom-call(s32[1]{0:T(128)} %bitcast.30.section_ref, bf16[8,272,256]{2,1,0:T(8,128)(2,1)S(1)} %all-to-all-done.3.x_ref.refs_0_, bf16[8,272,256]{2,1,0:T(8,128)(2,1)} %collective-permute-done.20.refs_1_, bf16[8,256,256]{2,1,0:T(8,128)(2,1)S(1)} %copy-done.11, bf16[8,256,256]{2,1,0:T(8,128)(2,1)S(1)} %copy-done.4), custom_call_target="tpu_custom_call" | custom-call | tf_op jit(solution)/shard_map/pallas_call | solution.py:373
  (153 shorter events, 80.7 us)
Async XLA Ops:
  6.5 12.8 %collective-permute-start.1 = (bf16[8,256,256]{2,1,0:T(8,128)(2,1)}, bf16[8,256,256]{2,1,0:T(8,128)(2,1)}, u32[]{:S(2)}, u32[]{:S(2)}) collective-permute-start(bf16[8,256,256]{2,1,0:T(8,128)(2,1)} %bitcast.45), channel_id=1, source_target_pairs={{0,128},{128,0},{1,129},{129,1},{2,130},{130,2},{3,131},{131,3},{4... | collective-permute-start | bytes 3145736 | tf_op jit(solution)/shard_map/ppermute | solution.py:410
  7.7 14.9 %all-to-all-start = ((f32[8,16,256]{2,1,0:T(8,128)}), f32[8,16,256]{2,1,0:T(8,128)S(1)}, u32[]{:S(2)}, u32[]{:S(2)}) async-start(f32[8,16,256]{2,1,0:T(8,128)} %broadcast_in_dim.6), calls=%async_computation | async-start | bytes 262144 | tf_op jit(solution)/shard_map/all_to_all | solution.py:44
  14.2 9.9 %collective-permute-start.2 = (bf16[256,256]{1,0:T(8,128)(2,1)}, bf16[256,256]{1,0:T(8,128)(2,1)}, u32[]{:S(2)}, u32[]{:S(2)}) collective-permute-start(bf16[256,256]{1,0:T(8,128)(2,1)} %get-tuple-element.73), channel_id=1, source_target_pairs={{0,1},{1,2},{2,3},{3,4},{4,5},{5,6},{6,7},{7,0},{8,9},{9,10},{10,1... | collective-permute-start | bytes 393224 | tf_op jit(solution)/shard_map/ppermute | solution.py:418
  15.6 12.7 %collective-permute-start.3 = (bf16[256,256]{1,0:T(8,128)(2,1)}, bf16[256,256]{1,0:T(8,128)(2,1)}, u32[]{:S(2)}, u32[]{:S(2)}) collective-permute-start(bf16[256,256]{1,0:T(8,128)(2,1)} %get-tuple-element.74), channel_id=1, source_target_pairs={{0,2},{1,3},{2,4},{3,5},{4,6},{5,7},{6,0},{7,1},{8,10},{9,11},{10,... | collective-permute-start | bytes 393224 | tf_op jit(solution)/shard_map/ppermute | solution.py:418
  17.7 10.7 %collective-permute-start.4 = (bf16[256,256]{1,0:T(8,128)(2,1)}, bf16[256,256]{1,0:T(8,128)(2,1)}, u32[]{:S(2)}, u32[]{:S(2)}) collective-permute-start(bf16[256,256]{1,0:T(8,128)(2,1)} %get-tuple-element.78), channel_id=1, source_target_pairs={{0,6},{1,7},{2,0},{3,1},{4,2},{5,3},{6,4},{7,5},{8,14},{9,15},{10,... | collective-permute-start | bytes 393224 | tf_op jit(solution)/shard_map/ppermute | solution.py:418
  19.2 10.3 %collective-permute-start.5 = (bf16[256,256]{1,0:T(8,128)(2,1)}, bf16[256,256]{1,0:T(8,128)(2,1)}, u32[]{:S(2)}, u32[]{:S(2)}) collective-permute-start(bf16[256,256]{1,0:T(8,128)(2,1)} %get-tuple-element.79), channel_id=1, source_target_pairs={{0,7},{1,0},{2,1},{3,2},{4,3},{5,4},{6,5},{7,6},{8,15},{9,8},{10,9... | collective-permute-start | bytes 393224 | tf_op jit(solution)/shard_map/ppermute | solution.py:418
  29.5 22.0 %all-to-all-start.1 = ((bf16[16,8,16,256]{3,2,1,0:T(8,128)(2,1)}), bf16[16,8,16,256]{3,2,1,0:T(8,128)(2,1)S(1)}, u32[]{:S(2)}, u32[]{:S(2)}) async-start(bf16[16,8,16,256]{3,2,1,0:T(8,128)(2,1)} %shard_map.114), calls=%async_computation.1 | async-start | bytes 2097152 | tf_op jit(solution)/shard_map/all_to_all | solution.py:445
  36.3 9.5 %collective-permute-start.6 = (bf16[16,128,128]{2,1,0:T(8,128)(2,1)S(1)}, bf16[16,128,128]{2,1,0:T(8,128)(2,1)S(1)}, u32[]{:S(2)}, u32[]{:S(2)}) collective-permute-start(bf16[16,128,128]{2,1,0:T(8,128)(2,1)S(1)} %bitcast.47), channel_id=1, source_target_pairs={{0,128},{128,0},{1,129},{129,1},{2,130},{130,2},{3,131},{131,3},{4... | collective-permute-start | bytes 1572872 | tf_op jit(solution)/shard_map/ppermute | solution.py:410
  37.7 16.4 %collective-permute-start.7 = (bf16[256,256]{1,0:T(8,128)(2,1)}, bf16[256,256]{1,0:T(8,128)(2,1)S(1)}, u32[]{:S(2)}, u32[]{:S(2)}) collective-permute-start(bf16[256,256]{1,0:T(8,128)(2,1)} %get-tuple-element.84), channel_id=1, source_target_pairs={{0,3},{1,4},{2,5},{3,6},{4,7},{5,0},{6,1},{7,2},{8,11},{9,12},{10,... | collective-permute-start | bytes 393224 | tf_op jit(solution)/shard_map/ppermute | solution.py:418
  41.3 14.5 %collective-permute-start.8 = (bf16[256,256]{1,0:T(8,128)(2,1)}, bf16[256,256]{1,0:T(8,128)(2,1)S(1)}, u32[]{:S(2)}, u32[]{:S(2)}) collective-permute-start(bf16[256,256]{1,0:T(8,128)(2,1)} %get-tuple-element.85), channel_id=1, source_target_pairs={{0,4},{1,5},{2,6},{3,7},{4,0},{5,1},{6,2},{7,3},{8,12},{9,13},{10,... | collective-permute-start | bytes 393224 | tf_op jit(solution)/shard_map/ppermute | solution.py:418
  42.4 14.1 %collective-permute-start.9 = (bf16[256,256]{1,0:T(8,128)(2,1)S(1)}, bf16[256,256]{1,0:T(8,128)(2,1)S(1)}, u32[]{:S(2)}, u32[]{:S(2)}) collective-permute-start(bf16[256,256]{1,0:T(8,128)(2,1)S(1)} %copy-done.30), channel_id=1, source_target_pairs={{0,5},{1,6},{2,7},{3,0},{4,1},{5,2},{6,3},{7,4},{8,13},{9,14},{10,... | collective-permute-start | bytes 393224 | tf_op jit(solution)/shard_map/ppermute | solution.py:418
  56.5 48.5 %all-to-all-start.2 = ((bf16[128,16,256]{2,1,0:T(8,128)(2,1)}), bf16[128,16,256]{2,1,0:T(8,128)(2,1)}, u32[]{:S(2)}, u32[]{:S(2)}) async-start(bf16[128,16,256]{2,1,0:T(8,128)(2,1)} %bitcast.15), calls=%async_computation.2 | async-start | bytes 2097152 | tf_op jit(solution)/shard_map/all_to_all | solution.py:452
  73.0 23.8 %collective-permute-start.12 = (bf16[32,64,64]{2,1,0:T(8,128)(2,1)}, bf16[32,64,64]{2,1,0:T(8,128)(2,1)}, u32[]{:S(2)}, u32[]{:S(2)}) collective-permute-start(bf16[32,64,64]{2,1,0:T(8,128)(2,1)} %bitcast.17), channel_id=1, source_target_pairs={{0,128},{128,0},{1,129},{129,1},{2,130},{130,2},{3,131},{131,3},{4... | collective-permute-start | bytes 786440 | tf_op jit(solution)/shard_map/ppermute | solution.py:410
  116.5 36.7 %all-to-all-start.3 = ((bf16[8,272,256]{2,1,0:T(8,128)(2,1)}), bf16[8,272,256]{2,1,0:T(8,128)(2,1)S(1)}, u32[]{:S(2)}, u32[]{:S(2)}) async-start(bf16[8,272,256]{2,1,0:T(8,128)(2,1)} %get-tuple-element.107.x_ref), calls=%async_computation.3 | async-start | bytes 2228224 | tf_op jit(solution)/shard_map/all_to_all | solution.py:480
  122.6 32.3 %collective-permute-start.14 = (bf16[2048,256]{1,0:T(8,128)(2,1)}, bf16[2048,256]{1,0:T(8,128)(2,1)}, u32[]{:S(2)}, u32[]{:S(2)}) collective-permute-start(bf16[2048,256]{1,0:T(8,128)(2,1)} %bitcast.24.refs_4_), channel_id=1, source_target_pairs={{0,8},{8,16},{16,24},{24,0},{32,40},{40,48},{48,56},{56,32},{64,72... | collective-permute-start | bytes 3145736 | tf_op jit(solution)/shard_map/ppermute | solution.py:415
  123.9 31.1 %collective-permute-start.15 = (bf16[2048,256]{1,0:T(8,128)(2,1)}, bf16[2048,256]{1,0:T(8,128)(2,1)}, u32[]{:S(2)}, u32[]{:S(2)}) collective-permute-start(bf16[2048,256]{1,0:T(8,128)(2,1)} %bitcast.24.refs_4_), channel_id=1, source_target_pairs={{0,24},{8,0},{16,8},{24,16},{32,56},{40,32},{48,40},{56,48},{64,88... | collective-permute-start | bytes 3145736 | tf_op jit(solution)/shard_map/ppermute | solution.py:415
  180.1 45.5 %all-to-all-start.5 = ((bf16[128,16,256]{2,1,0:T(8,128)(2,1)}), bf16[128,16,256]{2,1,0:T(8,128)(2,1)}, u32[]{:S(2)}, u32[]{:S(2)}) async-start(bf16[128,16,256]{2,1,0:T(8,128)(2,1)} %bitcast.40), calls=%async_computation.5 | async-start | bytes 2097152 | tf_op jit(solution)/shard_map/all_to_all | solution.py:452
  187.4 37.2 %collective-permute-start.16 = (bf16[2048,256]{1,0:T(8,128)(2,1)}, bf16[2048,256]{1,0:T(8,128)(2,1)S(1)}, u32[]{:S(2)}, u32[]{:S(2)}) collective-permute-start(bf16[2048,256]{1,0:T(8,128)(2,1)} %bitcast.24.refs_4_), channel_id=1, source_target_pairs={{0,16},{8,24},{16,0},{24,8},{32,48},{40,56},{48,32},{56,40},{64,80... | collective-permute-start | bytes 3145736 | tf_op jit(solution)/shard_map/ppermute | solution.py:415
  249.0 32.7 %all-to-all-start.7 = ((bf16[8,256,256]{2,1,0:T(8,128)(2,1)}), bf16[8,256,256]{2,1,0:T(8,128)(2,1)S(1)}, u32[]{:S(2)}, u32[]{:S(2)}) async-start(bf16[8,256,256]{2,1,0:T(8,128)(2,1)} %copy-done.12), calls=%async_computation.7 | async-start | bytes 2097152 | tf_op jit(solution)/shard_map/all_to_all | solution.py:496
  252.6 9.9 %collective-permute-start.17 = (bf16[32,2048]{1,0:T(8,128)(2,1)S(1)}, bf16[32,2048]{1,0:T(8,128)(2,1)S(1)}, u32[]{:S(2)}, u32[]{:S(2)}) collective-permute-start(bf16[32,2048]{1,0:T(8,128)(2,1)S(1)} %reshape.72.refs_0_), channel_id=1, source_target_pairs={{0,32},{8,40},{16,48},{24,56},{32,64},{40,72},{48,80},{56,88},{64,... | collective-permute-start | bytes 393224 | tf_op jit(solution)/shard_map/ppermute | solution.py:422
  253.7 8.8 %collective-permute-start.18 = (bf16[32,2048]{1,0:T(8,128)(2,1)S(1)}, bf16[32,2048]{1,0:T(8,128)(2,1)S(1)}, u32[]{:S(2)}, u32[]{:S(2)}) collective-permute-start(bf16[32,2048]{1,0:T(8,128)(2,1)S(1)} %reshape.72.refs_0_), channel_id=1, source_target_pairs={{0,64},{8,72},{16,80},{24,88},{32,96},{40,104},{48,112},{56,120},{... | collective-permute-start | bytes 393224 | tf_op jit(solution)/shard_map/ppermute | solution.py:422
  257.2 34.4 %collective-permute-start.20 = (bf16[8,272,256]{2,1,0:T(8,128)(2,1)S(1)}, bf16[8,272,256]{2,1,0:T(8,128)(2,1)}, u32[]{:S(2)}, u32[]{:S(2)}) collective-permute-start(bf16[8,272,256]{2,1,0:T(8,128)(2,1)S(1)} %all-to-all-done.3.x_ref.refs_0_), channel_id=1, source_target_pairs={{128,0},{129,1},{130,2},{131,3},{132,4},{133,5},{134,6},{135,7},{1... | collective-permute-start | bytes 3342344 | tf_op jit(solution)/shard_map/ppermute | solution.py:514
  281.8 9.9 %collective-permute-start.21 = (bf16[8,256,256]{2,1,0:T(8,128)(2,1)S(1)}, bf16[8,256,256]{2,1,0:T(8,128)(2,1)S(1)}, u32[]{:S(2)}, u32[]{:S(2)}) collective-permute-start(bf16[8,256,256]{2,1,0:T(8,128)(2,1)S(1)} %all-to-all-done.7.refs_3_), channel_id=1, source_target_pairs={{0,128},{1,129},{2,130},{3,131},{4,132},{5,133},{6,134},{7,135},{8... | collective-permute-start | bytes 3145736 | tf_op jit(solution)/shard_map/ppermute | solution.py:515
  284.7 18.3 %all-to-all-start.8 = ((f32[128,2,128]{2,1,0:T(2,128)}), f32[128,2,128]{2,1,0:T(2,128)S(1)}, u32[]{:S(2)}, u32[]{:S(2)}) async-start(f32[128,2,128]{2,1,0:T(2,128)} %broadcast_in_dim.8), calls=%async_computation.8 | async-start | bytes 262144 | tf_op jit(solution)/shard_map/all_to_all | solution.py:44
  (43 other events, 320.3 us)

commit v9 on v8

--- a/solution.py
+++ b/solution.py
@@ -60,6 +60,10 @@
     return total
 
 
+def choose(mine_ref, own, other):
+    return jnp.where(mine_ref[0] == 1, own.astype(F32), other.astype(F32))
+
+
 def split3(value):
     high = value.astype(BF16).astype(F32)
     mid = (value - high).astype(BF16).astype(F32)
@@ -88,13 +92,13 @@
     )(tensor_index, *gains, x_own)
 
 
-def right_stage(x_chan, gain_local, right, groups, shared=None):
-    rows = right.shape[0]
-    tokens = right.shape[1]
+def right_stage(x_chan, gain_local, right, mine, groups, shared=None):
+    rows = right[0].shape[0]
+    tokens = right[0].shape[1]
     width = tokens // groups
-    operands = [x_chan, gain_local, right] + ([] if shared is None else [shared])
-
-    def kernel(x_ref, gain_ref, right_ref, *refs):
+    operands = [mine, *right, x_chan, gain_local] + ([] if shared is None else [shared])
+
+    def kernel(mine_ref, own_ref, other_ref, x_ref, gain_ref, *refs):
         out_ref = refs[-1]
         if shared is not None:
             squares = refs[0][0, :rows]
@@ -107,30 +111,33 @@
             else:
                 total = squares[p : p + 1]
             scale = lax.rsqrt(total / D + EPS)
-            scaled = (right_ref[p].astype(F32) * scale).astype(BF16)
+            right_row = choose(mine_ref, own_ref[p], other_ref[p])
+            scaled = (right_row * scale).astype(BF16)
             mix = dot(scaled, x_ref[p, :tokens]) * gain_ref[...]
             out_ref[:, p] = mix.astype(BF16).reshape(groups, width, BLK)
 
     return pl.pallas_call(
         kernel,
+        in_specs=[scalar_spec()] + [whole(o.shape) for o in operands[1:]],
         out_shape=shape_of((groups, rows, width, BLK)),
         compiler_params=params(),
     )(*operands)
 
 
-def left_stage(left, mix):
-    j_count, i_count, p_count = left.shape
+def left_stage(left, mine, mix):
+    j_count, i_count, p_count = left[0].shape
 
     half = BLK // 2
 
-    def kernel(left_ref, mix_ref, out_ref, wide_ref, acc_ref):
+    def kernel(mine_ref, own_ref, other_ref, mix_ref, out_ref, wide_ref, acc_ref):
         for h in range(2):
             wide_ref[h] = mix_ref[:, h * half : (h + 1) * half].astype(F32)
         for j in range(j_count):
             column = jnp.concatenate(
                 [wide_ref[h, pl.ds(j, p_count, stride=j_count), :] for h in range(2)], axis=1
             ).astype(BF16)
-            mixed = dot(left_ref[j], column)
+            factor = choose(mine_ref, own_ref[j], other_ref[j]).astype(BF16)
+            mixed = dot(factor, column)
             for h in range(2):
                 acc_ref[h, pl.ds(j, i_count, stride=j_count), :] = mixed[:, h * half : (h + 1) * half]
         for h in range(2):
@@ -138,45 +145,63 @@
 
     return pl.pallas_call(
         kernel,
+        in_specs=[scalar_spec()] + [whole(a.shape) for a in (*left, mix)],
         out_shape=shape_of((i_count * j_count, BLK)),
         scratch_shapes=[
             pltpu.VMEM((2, p_count * j_count, half), F32),
             pltpu.VMEM((2, i_count * j_count, half), F32),
         ],
         compiler_params=params(),
-    )(left, mix)
-
-
-def channel_map(first, second_rows, n_blk):
-    def kernel(first_ref, second_ref, out_ref, spread_ref):
+    )(mine, *left, mix)
+
+
+def spread_first(mine_ref, first_refs, spread_ref):
+    lane = lax.broadcasted_iota(jnp.int32, (BLK, PER * BLK), 1)
+    wanted = (lane // BLK) * C2 + lane % C2
+    pick = (wanted == lax.broadcasted_iota(jnp.int32, (BLK, PER * BLK), 0)).astype(BF16)
+    for g in range(C1 // PER):
+        group = [f[g * PER : (g + 1) * PER].reshape(BLK, C2) for f in first_refs]
+        spread = lax.dot_general(
+            choose(mine_ref, *group).astype(BF16),
+            pick,
+            (((0,), (0,)), ((), ())),
+            preferred_element_type=F32,
+        ).astype(BF16)
+        for r in range(PER):
+            spread_ref[g * PER + r] = spread[:, r * BLK : (r + 1) * BLK]
+
+
+def map_rows(spread_ref, second, r):
+    return (spread_ref[r].astype(F32) * second[r : r + 1]).astype(BF16)
+
+
+def factor_specs():
+    return (
+        [scalar_spec()]
+        + [whole((C1, C2, C2))] * 2
+        + [pl.BlockSpec((C1, BLK), lambda n: (0, n))] * 2
+    )
+
+
+def channel_map(first, second, mine, n_blk):
+    def kernel(mine_ref, first_a, first_b, second_a, second_b, out_ref, spread_ref):
         @pl.when(pl.program_id(0) == 0)
         def _():
-            lane = lax.broadcasted_iota(jnp.int32, (BLK, PER * BLK), 1)
-            wanted = (lane // BLK) * C2 + lane % C2
-            pick = (wanted == lax.broadcasted_iota(jnp.int32, (BLK, PER * BLK), 0)).astype(BF16)
-            for g in range(C1 // PER):
-                spread = lax.dot_general(
-                    first_ref[g * PER : (g + 1) * PER].reshape(BLK, C2),
-                    pick,
-                    (((0,), (0,)), ((), ())),
-                    preferred_element_type=F32,
-                ).astype(BF16)
-                for r in range(PER):
-                    spread_ref[g * PER + r] = spread[:, r * BLK : (r + 1) * BLK]
-
+            spread_first(mine_ref, (first_a, first_b), spread_ref)
+
+        second_rows = choose(mine_ref, second_a[...], second_b[...])
         for r in range(C1):
-            row = second_ref[r : r + 1].astype(F32)
-            out_ref[0, r * C2 : (r + 1) * C2] = (spread_ref[r].astype(F32) * row).astype(BF16)
+            out_ref[0, r * C2 : (r + 1) * C2] = map_rows(spread_ref, second_rows, r)
 
     return pl.pallas_call(
         kernel,
         grid=(n_blk,),
-        in_specs=[whole((C1, C2, C2)), pl.BlockSpec((C1, BLK), lambda n: (0, n))],
+        in_specs=factor_specs(),
         out_specs=pl.BlockSpec((1, D, BLK), lambda n: (n, 0, 0)),
         out_shape=shape_of((n_blk, D, BLK)),
         scratch_shapes=[pltpu.VMEM((C1, C2, BLK), BF16)],
         compiler_params=params(),
-    )(first, second_rows)
+    )(mine, *first, *second)
 
 
 def normalize(x_blocks, gain_ref, tokens, store):
@@ -211,22 +236,36 @@
     )(tensor_index, gain, *received)
 
 
-def gate_stage(normed, gate_map):
+def gate_stage(normed, first, second, mine, n_blk):
     tokens = normed.shape[0]
-    n_blk = gate_map.shape[0]
-
-    def kernel(normed_ref, map_ref, out_ref):
-        pre = dot(normed_ref[...], map_ref[0]).astype(BF16)
-        out_ref[0] = jax.nn.sigmoid(pre.astype(F32))
+    parts = 4
+    span = D // parts
+
+    def kernel(mine_ref, first_a, first_b, second_a, second_b, normed_ref, out_ref, *scratch):
+        spread_ref, *map_refs = scratch
+
+        @pl.when(pl.program_id(0) == 0)
+        def _():
+            spread_first(mine_ref, (first_a, first_b), spread_ref)
+
+        second_rows = choose(mine_ref, second_a[...], second_b[...])
+        pre = jnp.zeros((tokens, BLK), F32)
+        for part in range(parts):
+            for r in range(span // C2):
+                rows = map_rows(spread_ref, second_rows, part * span // C2 + r)
+                map_refs[part][r * C2 : (r + 1) * C2] = rows
+            pre = pre + dot(normed_ref[:, part * span : (part + 1) * span], map_refs[part][...])
+        out_ref[0] = jax.nn.sigmoid(pre.astype(BF16).astype(F32))
 
     return pl.pallas_call(
         kernel,
         grid=(n_blk,),
-        in_specs=[whole(normed.shape), pl.BlockSpec((1, D, BLK), lambda n: (n, 0, 0))],
+        in_specs=factor_specs() + [whole(normed.shape)],
         out_specs=pl.BlockSpec((1, tokens, BLK), lambda n: (n, 0, 0)),
         out_shape=shape_of((n_blk, tokens, BLK), F32),
-        compiler_params=params(),
-    )(normed, gate_map)
+        scratch_shapes=[pltpu.VMEM((C1, C2, BLK), BF16)] + [pltpu.VMEM((span, BLK), BF16)] * parts,
+        compiler_params=params(),
+    )(mine, *first, *second, normed)
 
 
 def out_stage(seq_out, gate, x_tok, out_map, gain=None):
@@ -406,9 +445,10 @@
     j_dev = left_blocks.shape[1]
     p_count = left_blocks.shape[2]
 
-    def by_block(own):
-        other = lax.ppermute(own, "section", swap)
-        return jnp.where(first, own, other), jnp.where(first, other, own)
+    mine = [(section == b).astype(jnp.int32).reshape(1) for b in range(2)]
+
+    def with_other(own):
+        return own, lax.ppermute(own, "section", swap)
 
     def along_y(block, distance):
         route = [(i, i - i % y_count + (i + distance) % y_count) for i in range(seq_count)]
@@ -429,11 +469,12 @@
     x_own = lax.dynamic_index_in_dim(x_in, section, 0, keepdims=False).reshape(
         rows_dev, tokens, BLK
     )
-    gain_local = by_block(norm_gain)
+    gain_other = lax.ppermute(norm_gain, "section", swap)
+    gain_local = [jnp.where(section == b, norm_gain, gain_other) for b in range(2)]
 
     shared, *sends = split_stage(x_own, gain_local, z_scalar)
     shared, right_own, left_own = tie((shared, right_blocks[0], left_blocks[0]))
-    rights = by_block(right_own)
+    right = with_other(right_own)
     near = [1, 2, n_blk - 2, n_blk - 1]
     received = [sends[0]] + [None] * (n_blk - 1)
     for d in near:
@@ -445,48 +486,46 @@
         return lax.all_to_all(mix, "seq", split_axis=0, concat_axis=0, tiled=True)
 
     def mix_left(cols, b):
-        out = left_stage(lefts[b], cols.reshape(p_count * j_dev, BLK))
+        out = left_stage(left, mine[b], cols.reshape(p_count * j_dev, BLK))
         return out.reshape(p_count, j_dev, BLK)
 
     def exchange_all(cols):
         out = lax.all_to_all(cols, everyone, split_axis=0, concat_axis=0, tiled=True)
         return out.reshape(seq_count, n_blk, j_dev, BLK)
 
-    mix = right_stage(x_own, gain_local[0], rights[0], seq_count, shared=shared)
+    mix = right_stage(x_own, gain_local[0], right, mine[0], seq_count, shared=shared)
     mix, left_own, sends, near_blocks = tie((mix, left_own, sends, [received[d] for d in near]))
     for d, block in zip(near, near_blocks):
         received[d] = block
     cols = exchange_seq(mix)
-    lefts = by_block(left_own)
+    left = with_other(left_own)
     for d in range(3, n_blk - 2):
         received[d] = along_z(sends[d], d)
 
     cols = mix_left(cols, 0)
-    cols, received, *own = tie(
-        (cols, received, gate_first[0], out_first[0], gate_second, out_second)
+    cols, received, head_own, *own = tie(
+        (cols, received, head[0], gate_first[0], out_first[0], gate_second, out_second)
     )
     seq_out = exchange_all(cols)
-    gate_firsts, out_firsts = (by_block(w) for w in own[:2])
-    gate_seconds, out_seconds = (by_block(rows_second(w)) for w in own[2:])
+    gate_first_pair, out_first_pair = (with_other(w) for w in own[:2])
+    gate_second_pair, out_second_pair = (with_other(rows_second(w)) for w in own[2:])
+    near_heads = [along_y(head_own, d) for d in (1, 3)]
     x_tok, normed = token_stage(received, gains[0], z_scalar)
-    gate = gate_stage(normed, channel_map(gate_firsts[0], gate_seconds[0], n_blk))
-    out_map = channel_map(out_firsts[0], out_seconds[0], n_blk)
+    gate = gate_stage(normed, gate_first_pair, gate_second_pair, mine[0], n_blk)
+    out_map = channel_map(out_first_pair, out_second_pair, mine[0], n_blk)
     rows_one, packed, normed = out_stage(seq_out, gate, x_tok, out_map, gain=gains[1])
 
-    packed, normed, head_own, gate_two, out_two, gate_sec, out_sec = tie(
-        (packed, normed, head[0], gate_firsts[1], out_firsts[1], gate_seconds[1], out_seconds[1])
+    packed, normed, head_own, near_heads, gate_first_pair, out_first_pair = tie(
+        (packed, normed, head_own, near_heads, gate_first_pair, out_first_pair)
     )
-    heads = [head_own, along_y(head_own, 1), None, along_y(head_own, 3)]
+    far_head = along_y(head_own, 2)
     chan_one = lax.all_to_all(packed, "tensor", split_axis=0, concat_axis=0, tiled=True)
-    gate = gate_stage(normed, channel_map(gate_two, gate_sec, n_blk))
-    out_map = channel_map(out_two, out_sec, n_blk)
-    mix = right_stage(chan_one, gain_local[1], rights[1], seq_count)
-    mix, gate, out_map, heads = tie((mix, gate, out_map, [heads[0], heads[1], heads[3]]))
-    cols = mix_left(exchange_seq(mix), 1)
-    cols, heads = tie((cols, heads))
-    seq_out = exchange_all(cols)
-    seq_out, far_head = tie((seq_out, along_y(heads[0], 2)))
-    heads = [*heads[:2], far_head, heads[2]]
+    gate = gate_stage(normed, gate_first_pair, gate_second_pair, mine[1], n_blk)
+    out_map = channel_map(out_first_pair, out_second_pair, mine[1], n_blk)
+    mix = right_stage(chan_one, gain_local[1], right, mine[1], seq_count)
+    mix, gate, out_map, far_head = tie((mix, gate, out_map, far_head))
+    heads = [head_own, near_heads[0], far_head, near_heads[1]]
+    seq_out = exchange_all(mix_left(exchange_seq(mix), 1))
     rows_two, result = out_stage(seq_out, gate, packed, out_map)
 
     pair = jnp.stack([rows_one, rows_two])[:, None]

time: 305 us -> 293 us (0.961)
  blocking collectives: 36.7 us -> 70 us
  waiting for transfers between devices: 72.6 us -> 47.6 us
  Pallas kernels: 75.3 us -> 62.7 us
  starting transfers between devices: 88 us -> 77.7 us
  local copies, waits for them, and re-layouts: 22 us -> 30.4 us
  other arithmetic: 8.22 us -> 0.03 us
    ppermute x3, waiting for transfers between devices: 35.1 us -> 0.01 us  [along_y(): return lax.ppermute(block, 'seq', route)]
    all_to_all x0 -> x1, blocking collectives: none -> 34.8 us  [exchange_all(): lax.all_to_all(cols, everyone, split_axis=0, concat_axis=0, tiled=True)]
    pallas_call x10 -> x8, Pallas kernels: 45.1 us -> 33.9 us  [the longest x2 14.8 us: channel_map(): pl.pallas_call(kernel, grid=(n_blk,), in_specs=factor_specs(), out_specs=...]
    select_n x7 -> x1, other arithmetic: 8.19 us -> 0.01 us  [body(): jnp.where(section == b, norm_gain, gain_other)]
    unnamed x76 -> x86, local copies, waits for them, and re-layouts: 18.1 us -> 26.2 us
    all_to_all x2 -> x1, starting transfers between devices: 22.5 us -> 15.3 us  [exchange_all(): lax.all_to_all(cols, everyone, split_axis=0, concat_axis=0, tiled=True)]
    all_to_all x1, waiting for transfers between devices: 8.1 us -> 13.2 us  [body(): lax.all_to_all(packed, 'tensor', split_axis=0, concat_axis=0, tiled=True)]
    all_to_all x2, waiting for transfers between devices: 3.48 us -> 8.57 us  [gather_by_exchange(): return lax.all_to_all(copies, axis, split_axis=0, concat_axis=0, tiled=True)]
  transfers between devices with their start and end apart: 29 -> 28, of which waited for: 11 -> 12; matrix products, arithmetic and copies ran while one was open for 4% -> 1% of each run, Pallas kernels for 18% -> 18%
where the time goes in v9:
time: 293 us; the launch traced here: 290 us
  starting transfers between devices  77.7 us (27%)
  blocking collectives  70 us (24%)
  Pallas kernels  62.7 us (21%)
  waiting for transfers between devices  47.6 us (16%)
  local copies, waits for them, and re-layouts  30.4 us (10%)
    all_to_all x1, blocking collectives, exchange_all(): lax.all_to_all(cols, everyone, split_axis=0, concat_axis=0, tiled=True)  34.8 us
    unnamed x86, local copies, waits for them, and re-layouts  26.2 us
    all_to_all x1, blocking collectives, exchange_seq(): return lax.all_to_all(mix, 'seq', split_axis=0, concat_axis=0, tiled=True)  21.6 us
    pallas_call x2, Pallas kernels, out_stage(): pl.pallas_call(kernel, grid=(n_blk,), in_specs=in_specs, out_specs=[whole...  17.2 us
    all_to_all x1, waiting for transfers between devices, body(): lax.all_to_all(result, 'tensor', split_axis=0, concat_axis=0, tiled=True)  15.5 us
    all_to_all x1, starting transfers between devices, exchange_all(): lax.all_to_all(cols, everyone, split_axis=0, concat_axis=0, tiled=True)  15.3 us
    pallas_call x2, Pallas kernels, channel_map(): pl.pallas_call(kernel, grid=(n_blk,), in_specs=factor_specs(), out_specs=...  14.8 us
    all_to_all x1, blocking collectives, body(): lax.all_to_all(pair, ('section', 'tensor'), split_axis=0, concat_axis=0,...  13.7 us
  transfers between devices with their start and end apart: 28, of which 12 were waited for; matrix products, arithmetic and copies ran while one was open for 1% of the time, Pallas kernels for 18%

profile of v9, /device:TPU:1, one launch (start us, length us, event | category | flops | bytes accessed | tf_op | source)
XLA Modules:
  0.0 289.6 jit_solution(14826063607248678958)
XLA Ops:
  12.2 6.4 %all-to-all-start = ((f32[8,16,256]{2,1,0:T(8,128)}), f32[8,16,256]{2,1,0:T(8,128)S(1)}, u32[]{:S(2)}, u32[]{:S(2)}) async-start(f32[8,16,256]{2,1,0:T(8,128)} %broadcast_in_dim.6), calls=%async_computation | async-start | bytes 262144 | tf_op jit(solution)/shard_map/all_to_all | solution.py:44
  23.7 3.5 %all-to-all-done.refs_0_ = f32[8,16,256]{2,1,0:T(8,128)S(1)} async-done(((f32[8,16,256]{2,1,0:T(8,128)}), f32[8,16,256]{2,1,0:T(8,128)S(1)}, u32[]{:S(2)}, u32[]{:S(2)}) %all-to-all-start) | async-done | bytes 131104 | tf_op jit(solution)/shard_map/all_to_all | solution.py:44
  34.0 6.8 %all-to-all-start.1 = ((bf16[16,8,16,256]{3,2,1,0:T(8,128)(2,1)}), bf16[16,8,16,256]{3,2,1,0:T(8,128)(2,1)S(1)}, u32[]{:S(2)}, u32[]{:S(2)}) async-start(bf16[16,8,16,256]{3,2,1,0:T(8,128)(2,1)} %copy-done.8), calls=%async_computation.1 | async-start | bytes 2097152 | tf_op jit(solution)/shard_map/all_to_all | solution.py:486
  42.1 3.7 %collective-permute-start.7 = (bf16[256,256]{1,0:T(8,128)(2,1)}, bf16[256,256]{1,0:T(8,128)(2,1)S(1)}, u32[]{:S(2)}, u32[]{:S(2)}) collective-permute-start(bf16[256,256]{1,0:T(8,128)(2,1)} %copy-done.34), channel_id=1, source_target_pairs={{0,3},{1,4},{2,5},{3,6},{4,7},{5,0},{6,1},{7,2},{8,11},{9,12},{10,... | collective-permute-start | bytes 393224 | tf_op jit(solution)/shard_map/ppermute | solution.py:458
  46.9 3.4 %collective-permute-start.9 = (bf16[256,256]{1,0:T(8,128)(2,1)}, bf16[256,256]{1,0:T(8,128)(2,1)}, u32[]{:S(2)}, u32[]{:S(2)}) collective-permute-start(bf16[256,256]{1,0:T(8,128)(2,1)} %copy-done.32), channel_id=1, source_target_pairs={{0,5},{1,6},{2,7},{3,0},{4,1},{5,2},{6,3},{7,4},{8,13},{9,14},{10,... | collective-permute-start | bytes 393224 | tf_op jit(solution)/shard_map/ppermute | solution.py:458
  51.0 5.0 %all-to-all-done.1 = bf16[16,8,16,256]{3,2,1,0:T(8,128)(2,1)S(1)} async-done(((bf16[16,8,16,256]{3,2,1,0:T(8,128)(2,1)}), bf16[16,8,16,256]{3,2,1,0:T(8,128)(2,1)S(1)}, u32[]{:S(2)}, u32[]{:S(2)}) %all-to-all-start.1) | async-done | bytes 1048608 | tf_op jit(solution)/shard_map/all_to_all | solution.py:486
  61.0 15.3 %all-to-all-start.2 = ((bf16[128,16,256]{2,1,0:T(8,128)(2,1)}), bf16[128,16,256]{2,1,0:T(8,128)(2,1)}, u32[]{:S(2)}, u32[]{:S(2)}) async-start(bf16[128,16,256]{2,1,0:T(8,128)(2,1)} %bitcast.45), calls=%async_computation.2 | async-start | bytes 2097152 | tf_op jit(solution)/shard_map/all_to_all | solution.py:493
  90.1 7.3 %shard_map.118.map_ref = bf16[8,2048,256]{2,1,0:T(8,128)(2,1)} custom-call(s32[1]{0:T(128)} %bitcast.10.mine_ref, bf16[32,64,64]{2,1,0:T(8,128)(2,1)} %bitcast.19.first_a, bf16[32,64,64]{2,1,0:T(8,128)(2,1)} %collective-permute-done.12.first_b, bf16[32,2048]{1,0:T(8,128)(2,1)S(1)} %reshape.79.second_a, bf16[32,2048]{1,0:T(8,128)(2,1)S(1)} %copy-done.22), custom_call_target="tpu_custom_call" | custom-call | tf_op jit(solution)/shard_map/pallas_call | solution.py:196
  97.5 6.2 %shard_map.117.gate_ref = f32[8,256,256]{2,1,0:T(8,128)S(1)} custom-call(s32[1]{0:T(128)} %bitcast.10.mine_ref, bf16[32,64,64]{2,1,0:T(8,128)(2,1)} %bitcast.18.first_a, bf16[32,64,64]{2,1,0:T(8,128)(2,1)} %collective-permute-done.10.first_b, bf16[32,2048]{1,0:T(8,128)(2,1)S(1)} %reshape.78.second_a, bf16[32,2048]{1,0:T(8,128)(2,1)S(1)} %collective-permute-done.11.second_b, ...), custom_call_target="tpu_custom_call" | custom-call | tf_op jit(solution)/shard_map/pallas_call | solution.py:260
  107.6 9.6 %shard_map.119 = (bf16[2,2048]{1,0:T(2,128)(2,1)S(1)}, bf16[8,272,256]{2,1,0:T(8,128)(2,1)S(1)}, bf16[256,2048]{1,0:T(8,128)(2,1)S(1)}) custom-call(bf16[16,8,16,256]{3,2,1,0:T(8,128)(2,1)} %bitcast.20.seq_ref, f32[8,256,256]{2,1,0:T(8,128)} %copy-done.3, bf16[8,256,256]{2,1,0:T(8,128)(2,1)S(1)} %copy-done.19, bf16[8,2048,256]{2,1,0:T(8,128)(2,1)} %shard_map.118.map_ref, ...), custom_call_target="tpu_custom_call" | custom-call | tf_op jit(solution)/shard_map/pallas_call | solution.py:328
  119.1 5.1 %all-to-all-start.3 = ((bf16[8,272,256]{2,1,0:T(8,128)(2,1)}), bf16[8,272,256]{2,1,0:T(8,128)(2,1)S(1)}, u32[]{:S(2)}, u32[]{:S(2)}) async-start(bf16[8,272,256]{2,1,0:T(8,128)(2,1)} %copy-done.4), calls=%async_computation.3 | async-start | bytes 2228224 | tf_op jit(solution)/shard_map/all_to_all | solution.py:522
  126.7 7.4 %shard_map.122.map_ref = bf16[8,2048,256]{2,1,0:T(8,128)(2,1)} custom-call(s32[1]{0:T(128)} %bitcast.26.mine_ref, bf16[32,64,64]{2,1,0:T(8,128)(2,1)} %bitcast.19.first_a, bf16[32,64,64]{2,1,0:T(8,128)(2,1)} %collective-permute-done.12.first_b, bf16[32,2048]{1,0:T(8,128)(2,1)S(1)} %reshape.79.second_a, bf16[32,2048]{1,0:T(8,128)(2,1)S(1)} %copy-done.23), custom_call_target="tpu_custom_call" | custom-call | tf_op jit(solution)/shard_map/pallas_call | solution.py:196
  134.1 6.2 %shard_map.121.gate_ref = f32[8,256,256]{2,1,0:T(8,128)S(1)} custom-call(s32[1]{0:T(128)} %bitcast.26.mine_ref, bf16[32,64,64]{2,1,0:T(8,128)(2,1)} %bitcast.18.first_a, bf16[32,64,64]{2,1,0:T(8,128)(2,1)} %collective-permute-done.10.first_b, bf16[32,2048]{1,0:T(8,128)(2,1)S(1)} %reshape.78.second_a, bf16[32,2048]{1,0:T(8,128)(2,1)S(1)} %copy-done.25, ...), custom_call_target="tpu_custom_call" | custom-call | tf_op jit(solution)/shard_map/pallas_call | solution.py:260
  141.7 13.2 %all-to-all-done.3.x_ref.refs_0_ = bf16[8,272,256]{2,1,0:T(8,128)(2,1)S(1)} async-done(((bf16[8,272,256]{2,1,0:T(8,128)(2,1)}), bf16[8,272,256]{2,1,0:T(8,128)(2,1)S(1)}, u32[]{:S(2)}, u32[]{:S(2)}) %all-to-all-start.3) | async-done | bytes 1114144 | tf_op jit(solution)/shard_map/all_to_all | solution.py:522
  158.0 21.6 %all_to_all.45 = bf16[16,8,16,256]{3,2,1,0:T(8,128)(2,1)S(1)} all-to-all(bf16[16,8,16,256]{3,2,1,0:T(8,128)(2,1)S(1)} %shard_map.120), channel_id=1, replica_groups=mesh['section'=2,'seq'=16,'tensor'=8] {'seq'}, dimensions={0} | all-to-all | bytes 2097152 | tf_op jit(solution)/shard_map/all_to_all | solution.py:486
  181.1 34.8 %all_to_all.46 = bf16[128,16,256]{2,1,0:T(8,128)(2,1)S(1)} all-to-all(bf16[128,16,256]{2,1,0:T(8,128)(2,1)S(1)} %bitcast.48), channel_id=1, replica_groups=mesh['section'=2,'seq'=16,'tensor'=8] {'seq','tensor'}, dimensions={0} | all-to-all | bytes 2097152 | tf_op jit(solution)/shard_map/all_to_all | solution.py:493
  215.9 7.6 %shard_map.124 = (bf16[2,2048]{1,0:T(2,128)(2,1)S(1)}, bf16[8,256,256]{2,1,0:T(8,128)(2,1)S(1)}) custom-call(bf16[16,8,16,256]{3,2,1,0:T(8,128)(2,1)S(1)} %bitcast.44, f32[8,256,256]{2,1,0:T(8,128)S(1)} %copy-done.2, bf16[8,272,256]{2,1,0:T(8,128)(2,1)S(1)} %copy-done.5, bf16[8,2048,256]{2,1,0:T(8,128)(2,1)} %shard_map.122.map_ref), custom_call_target="tpu_custom_call" | custom-call | tf_op jit(solution)/shard_map/pallas_call | solution.py:328
  224.6 13.7 %all_to_all.47 = bf16[16,2,2048]{2,1,0:T(2,128)(2,1)S(1)} all-to-all(bf16[16,2,2048]{2,1,0:T(2,128)(2,1)S(1)} %bitcast.55), channel_id=1, replica_groups=mesh['section'=2,'seq'=16,'tensor'=8] {'section','tensor'}, dimensions={0} | all-to-all | bytes 262144 | tf_op jit(solution)/shard_map/all_to_all | solution.py:533
  238.3 4.3 %all-to-all-start.7 = ((bf16[8,256,256]{2,1,0:T(8,128)(2,1)}), bf16[8,256,256]{2,1,0:T(8,128)(2,1)}, u32[]{:S(2)}, u32[]{:S(2)}) async-start(bf16[8,256,256]{2,1,0:T(8,128)(2,1)} %copy-done.17), calls=%async_computation.7 | async-start | bytes 2097152 | tf_op jit(solution)/shard_map/all_to_all | solution.py:535
  245.5 4.7 %collective-permute-start.20 = (bf16[8,272,256]{2,1,0:T(8,128)(2,1)S(1)}, bf16[8,272,256]{2,1,0:T(8,128)(2,1)}, u32[]{:S(2)}, u32[]{:S(2)}) collective-permute-start(bf16[8,272,256]{2,1,0:T(8,128)(2,1)S(1)} %all-to-all-done.3.x_ref.refs_0_), channel_id=1, source_target_pairs={{128,0},{129,1},{130,2},{131,3},{132,4},{133,5},{134,6},{135,7},{1... | collective-permute-start | bytes 3342344 | tf_op jit(solution)/shard_map/ppermute | solution.py:553
  254.1 15.5 %all-to-all-done.7.refs_3_ = bf16[8,256,256]{2,1,0:T(8,128)(2,1)} async-done(((bf16[8,256,256]{2,1,0:T(8,128)(2,1)}), bf16[8,256,256]{2,1,0:T(8,128)(2,1)}, u32[]{:S(2)}, u32[]{:S(2)}) %all-to-all-start.7) | async-done | bytes 1048608 | tf_op jit(solution)/shard_map/all_to_all | solution.py:535
  271.5 6.1 %all-to-all-start.8 = ((f32[128,2,128]{2,1,0:T(2,128)}), f32[128,2,128]{2,1,0:T(2,128)S(1)}, u32[]{:S(2)}, u32[]{:S(2)}) async-start(f32[128,2,128]{2,1,0:T(2,128)} %broadcast_in_dim.8), calls=%async_computation.8 | async-start | bytes 262144 | tf_op jit(solution)/shard_map/all_to_all | solution.py:44
  277.7 6.0 %shard_map.126 = bf16[2,8,256,256]{3,2,1,0:T(8,128)(2,1)} custom-call(s32[1]{0:T(128)} %bitcast.32.section_ref, bf16[8,272,256]{2,1,0:T(8,128)(2,1)S(1)} %all-to-all-done.3.x_ref.refs_0_, bf16[8,272,256]{2,1,0:T(8,128)(2,1)} %collective-permute-done.20.refs_1_, bf16[8,256,256]{2,1,0:T(8,128)(2,1)} %collective-permute-done.21.refs_2_, ...), custom_call_target="tpu_custom_call" | custom-call | tf_op jit(solution)/shard_map/pallas_call | solution.py:412
  283.7 5.1 %all-to-all-done.8.parts_ref = f32[128,2,128]{2,1,0:T(2,128)S(1)} async-done(((f32[128,2,128]{2,1,0:T(2,128)}), f32[128,2,128]{2,1,0:T(2,128)S(1)}, u32[]{:S(2)}, u32[]{:S(2)}) %all-to-all-start.8) | async-done | bytes 131104 | tf_op jit(solution)/shard_map/all_to_all | solution.py:44
  (154 shorter events, 70.0 us)
Async XLA Ops:
  10.9 16.2 %collective-permute-start.1 = (bf16[8,256,256]{2,1,0:T(8,128)(2,1)}, bf16[8,256,256]{2,1,0:T(8,128)(2,1)}, u32[]{:S(2)}, u32[]{:S(2)}) collective-permute-start(bf16[8,256,256]{2,1,0:T(8,128)(2,1)} %bitcast.41), channel_id=1, source_target_pairs={{0,128},{128,0},{1,129},{129,1},{2,130},{130,2},{3,131},{131,3},{4... | collective-permute-start | bytes 3145736 | tf_op jit(solution)/shard_map/ppermute | solution.py:451
  12.2 15.0 %all-to-all-start = ((f32[8,16,256]{2,1,0:T(8,128)}), f32[8,16,256]{2,1,0:T(8,128)S(1)}, u32[]{:S(2)}, u32[]{:S(2)}) async-start(f32[8,16,256]{2,1,0:T(8,128)} %broadcast_in_dim.6), calls=%async_computation | async-start | bytes 262144 | tf_op jit(solution)/shard_map/all_to_all | solution.py:44
  18.6 12.6 %collective-permute-start.2 = (bf16[256,256]{1,0:T(8,128)(2,1)}, bf16[256,256]{1,0:T(8,128)(2,1)S(1)}, u32[]{:S(2)}, u32[]{:S(2)}) collective-permute-start(bf16[256,256]{1,0:T(8,128)(2,1)} %copy-done.38), channel_id=1, source_target_pairs={{0,1},{1,2},{2,3},{3,4},{4,5},{5,6},{6,7},{7,0},{8,9},{9,10},{10,1... | collective-permute-start | bytes 393224 | tf_op jit(solution)/shard_map/ppermute | solution.py:458
  20.1 12.8 %collective-permute-start.3 = (bf16[256,256]{1,0:T(8,128)(2,1)}, bf16[256,256]{1,0:T(8,128)(2,1)}, u32[]{:S(2)}, u32[]{:S(2)}) collective-permute-start(bf16[256,256]{1,0:T(8,128)(2,1)} %copy-done.37), channel_id=1, source_target_pairs={{0,2},{1,3},{2,4},{3,5},{4,6},{5,7},{6,0},{7,1},{8,10},{9,11},{10,... | collective-permute-start | bytes 393224 | tf_op jit(solution)/shard_map/ppermute | solution.py:458
  22.2 10.7 %collective-permute-start.4 = (bf16[256,256]{1,0:T(8,128)(2,1)}, bf16[256,256]{1,0:T(8,128)(2,1)}, u32[]{:S(2)}, u32[]{:S(2)}) collective-permute-start(bf16[256,256]{1,0:T(8,128)(2,1)} %copy-done.36), channel_id=1, source_target_pairs={{0,6},{1,7},{2,0},{3,1},{4,2},{5,3},{6,4},{7,5},{8,14},{9,15},{10,... | collective-permute-start | bytes 393224 | tf_op jit(solution)/shard_map/ppermute | solution.py:458
  23.7 10.3 %collective-permute-start.5 = (bf16[256,256]{1,0:T(8,128)(2,1)}, bf16[256,256]{1,0:T(8,128)(2,1)}, u32[]{:S(2)}, u32[]{:S(2)}) collective-permute-start(bf16[256,256]{1,0:T(8,128)(2,1)} %copy-done.35), channel_id=1, source_target_pairs={{0,7},{1,0},{2,1},{3,2},{4,3},{5,4},{6,5},{7,6},{8,15},{9,8},{10,9... | collective-permute-start | bytes 393224 | tf_op jit(solution)/shard_map/ppermute | solution.py:458
  34.0 22.0 %all-to-all-start.1 = ((bf16[16,8,16,256]{3,2,1,0:T(8,128)(2,1)}), bf16[16,8,16,256]{3,2,1,0:T(8,128)(2,1)S(1)}, u32[]{:S(2)}, u32[]{:S(2)}) async-start(bf16[16,8,16,256]{3,2,1,0:T(8,128)(2,1)} %copy-done.8), calls=%async_computation.1 | async-start | bytes 2097152 | tf_op jit(solution)/shard_map/all_to_all | solution.py:486
  40.8 9.5 %collective-permute-start.6 = (bf16[16,128,128]{2,1,0:T(8,128)(2,1)}, bf16[16,128,128]{2,1,0:T(8,128)(2,1)S(1)}, u32[]{:S(2)}, u32[]{:S(2)}) collective-permute-start(bf16[16,128,128]{2,1,0:T(8,128)(2,1)} %bitcast.49), channel_id=1, source_target_pairs={{0,128},{128,0},{1,129},{129,1},{2,130},{130,2},{3,131},{131,3},{4... | collective-permute-start | bytes 1572872 | tf_op jit(solution)/shard_map/ppermute | solution.py:451
  42.1 18.6 %collective-permute-start.7 = (bf16[256,256]{1,0:T(8,128)(2,1)}, bf16[256,256]{1,0:T(8,128)(2,1)S(1)}, u32[]{:S(2)}, u32[]{:S(2)}) collective-permute-start(bf16[256,256]{1,0:T(8,128)(2,1)} %copy-done.34), channel_id=1, source_target_pairs={{0,3},{1,4},{2,5},{3,6},{4,7},{5,0},{6,1},{7,2},{8,11},{9,12},{10,... | collective-permute-start | bytes 393224 | tf_op jit(solution)/shard_map/ppermute | solution.py:458
  45.8 14.9 %collective-permute-start.8 = (bf16[256,256]{1,0:T(8,128)(2,1)}, bf16[256,256]{1,0:T(8,128)(2,1)}, u32[]{:S(2)}, u32[]{:S(2)}) collective-permute-start(bf16[256,256]{1,0:T(8,128)(2,1)} %copy-done.33), channel_id=1, source_target_pairs={{0,4},{1,5},{2,6},{3,7},{4,0},{5,1},{6,2},{7,3},{8,12},{9,13},{10,... | collective-permute-start | bytes 393224 | tf_op jit(solution)/shard_map/ppermute | solution.py:458
  46.9 14.1 %collective-permute-start.9 = (bf16[256,256]{1,0:T(8,128)(2,1)}, bf16[256,256]{1,0:T(8,128)(2,1)}, u32[]{:S(2)}, u32[]{:S(2)}) collective-permute-start(bf16[256,256]{1,0:T(8,128)(2,1)} %copy-done.32), channel_id=1, source_target_pairs={{0,5},{1,6},{2,7},{3,0},{4,1},{5,2},{6,3},{7,4},{8,13},{9,14},{10,... | collective-permute-start | bytes 393224 | tf_op jit(solution)/shard_map/ppermute | solution.py:458
  61.0 45.4 %all-to-all-start.2 = ((bf16[128,16,256]{2,1,0:T(8,128)(2,1)}), bf16[128,16,256]{2,1,0:T(8,128)(2,1)}, u32[]{:S(2)}, u32[]{:S(2)}) async-start(bf16[128,16,256]{2,1,0:T(8,128)(2,1)} %bitcast.45), calls=%async_computation.2 | async-start | bytes 2097152 | tf_op jit(solution)/shard_map/all_to_all | solution.py:493
  76.3 42.8 %collective-permute-start.14 = (bf16[2048,256]{1,0:T(8,128)(2,1)}, bf16[2048,256]{1,0:T(8,128)(2,1)}, u32[]{:S(2)}, u32[]{:S(2)}) collective-permute-start(bf16[2048,256]{1,0:T(8,128)(2,1)} %bitcast.17.refs_4_), channel_id=1, source_target_pairs={{0,8},{8,16},{16,24},{24,0},{32,40},{40,48},{48,56},{56,32},{64,72... | collective-permute-start | bytes 3145736 | tf_op jit(solution)/shard_map/ppermute | solution.py:455
  76.7 42.4 %collective-permute-start.15 = (bf16[2048,256]{1,0:T(8,128)(2,1)}, bf16[2048,256]{1,0:T(8,128)(2,1)}, u32[]{:S(2)}, u32[]{:S(2)}) collective-permute-start(bf16[2048,256]{1,0:T(8,128)(2,1)} %bitcast.17.refs_4_), channel_id=1, source_target_pairs={{0,24},{8,0},{16,8},{24,16},{32,56},{40,32},{48,40},{56,48},{64,88... | collective-permute-start | bytes 3145736 | tf_op jit(solution)/shard_map/ppermute | solution.py:455
  80.9 8.4 %collective-permute-start.12 = (bf16[32,64,64]{2,1,0:T(8,128)(2,1)}, bf16[32,64,64]{2,1,0:T(8,128)(2,1)}, u32[]{:S(2)}, u32[]{:S(2)}) collective-permute-start(bf16[32,64,64]{2,1,0:T(8,128)(2,1)} %bitcast.19.first_a), channel_id=1, source_target_pairs={{0,128},{128,0},{1,129},{129,1},{2,130},{130,2},{3,131},{131,3},{4... | collective-permute-start | bytes 786440 | tf_op jit(solution)/shard_map/ppermute | solution.py:451
  81.0 16.5 %collective-permute-start.10 = (bf16[32,64,64]{2,1,0:T(8,128)(2,1)}, bf16[32,64,64]{2,1,0:T(8,128)(2,1)}, u32[]{:S(2)}, u32[]{:S(2)}) collective-permute-start(bf16[32,64,64]{2,1,0:T(8,128)(2,1)} %bitcast.18.first_a), channel_id=1, source_target_pairs={{0,128},{128,0},{1,129},{129,1},{2,130},{130,2},{3,131},{131,3},{4... | collective-permute-start | bytes 786440 | tf_op jit(solution)/shard_map/ppermute | solution.py:451
  82.5 15.0 %collective-permute-start.11 = (bf16[32,2048]{1,0:T(8,128)(2,1)S(1)}, bf16[32,2048]{1,0:T(8,128)(2,1)S(1)}, u32[]{:S(2)}, u32[]{:S(2)}) collective-permute-start(bf16[32,2048]{1,0:T(8,128)(2,1)S(1)} %reshape.78.second_a), channel_id=1, source_target_pairs={{0,128},{128,0},{1,129},{129,1},{2,130},{130,2},{3,131},{131,3},{4... | collective-permute-start | bytes 393224 | tf_op jit(solution)/shard_map/ppermute | solution.py:451
  119.1 35.8 %all-to-all-start.3 = ((bf16[8,272,256]{2,1,0:T(8,128)(2,1)}), bf16[8,272,256]{2,1,0:T(8,128)(2,1)S(1)}, u32[]{:S(2)}, u32[]{:S(2)}) async-start(bf16[8,272,256]{2,1,0:T(8,128)(2,1)} %copy-done.4), calls=%async_computation.3 | async-start | bytes 2228224 | tf_op jit(solution)/shard_map/all_to_all | solution.py:522
  124.3 33.7 %collective-permute-start.16 = (bf16[2048,256]{1,0:T(8,128)(2,1)}, bf16[2048,256]{1,0:T(8,128)(2,1)}, u32[]{:S(2)}, u32[]{:S(2)}) collective-permute-start(bf16[2048,256]{1,0:T(8,128)(2,1)} %bitcast.17.refs_4_), channel_id=1, source_target_pairs={{0,16},{8,24},{16,0},{24,8},{32,48},{40,56},{48,32},{56,40},{64,80... | collective-permute-start | bytes 3145736 | tf_op jit(solution)/shard_map/ppermute | solution.py:455
  238.3 31.3 %all-to-all-start.7 = ((bf16[8,256,256]{2,1,0:T(8,128)(2,1)}), bf16[8,256,256]{2,1,0:T(8,128)(2,1)}, u32[]{:S(2)}, u32[]{:S(2)}) async-start(bf16[8,256,256]{2,1,0:T(8,128)(2,1)} %copy-done.17), calls=%async_computation.7 | async-start | bytes 2097152 | tf_op jit(solution)/shard_map/all_to_all | solution.py:535
  242.6 7.8 %collective-permute-start.17 = (bf16[32,2048]{1,0:T(8,128)(2,1)S(1)}, bf16[32,2048]{1,0:T(8,128)(2,1)S(1)}, u32[]{:S(2)}, u32[]{:S(2)}) collective-permute-start(bf16[32,2048]{1,0:T(8,128)(2,1)S(1)} %reshape.86.refs_0_), channel_id=1, source_target_pairs={{0,32},{8,40},{16,48},{24,56},{32,64},{40,72},{48,80},{56,88},{64,... | collective-permute-start | bytes 393224 | tf_op jit(solution)/shard_map/ppermute | solution.py:462
  245.5 32.2 %collective-permute-start.20 = (bf16[8,272,256]{2,1,0:T(8,128)(2,1)S(1)}, bf16[8,272,256]{2,1,0:T(8,128)(2,1)}, u32[]{:S(2)}, u32[]{:S(2)}) collective-permute-start(bf16[8,272,256]{2,1,0:T(8,128)(2,1)S(1)} %all-to-all-done.3.x_ref.refs_0_), channel_id=1, source_target_pairs={{128,0},{129,1},{130,2},{131,3},{132,4},{133,5},{134,6},{135,7},{1... | collective-permute-start | bytes 3342344 | tf_op jit(solution)/shard_map/ppermute | solution.py:553
  269.6 8.1 %collective-permute-start.21 = (bf16[8,256,256]{2,1,0:T(8,128)(2,1)}, bf16[8,256,256]{2,1,0:T(8,128)(2,1)}, u32[]{:S(2)}, u32[]{:S(2)}) collective-permute-start(bf16[8,256,256]{2,1,0:T(8,128)(2,1)} %all-to-all-done.7.refs_3_), channel_id=1, source_target_pairs={{0,128},{1,129},{2,130},{3,131},{4,132},{5,133},{6,134},{7,135},{8... | collective-permute-start | bytes 3145736 | tf_op jit(solution)/shard_map/ppermute | solution.py:554
  271.5 17.2 %all-to-all-start.8 = ((f32[128,2,128]{2,1,0:T(2,128)}), f32[128,2,128]{2,1,0:T(2,128)S(1)}, u32[]{:S(2)}, u32[]{:S(2)}) async-start(f32[128,2,128]{2,1,0:T(2,128)} %broadcast_in_dim.8), calls=%async_computation.8 | async-start | bytes 262144 | tf_op jit(solution)/shard_map/all_to_all | solution.py:44
  (47 other events, 295.9 us)

commit v10 on v9

--- a/solution.py
+++ b/solution.py
@@ -13,6 +13,7 @@
 BLK = 256
 EXTRA = 16
 PER = BLK // C2
+PARTS = 4
 VMEM_LIMIT = 48 * 1024 * 1024
 F32 = jnp.float32
 BF16 = jnp.bfloat16
@@ -73,21 +74,29 @@
 def split_stage(x_own, gains, tensor_index):
     rows, tokens, _ = x_own.shape
 
-    def kernel(z_ref, gain_a_ref, gain_b_ref, x_ref, shared_ref, *send_refs):
+    def kernel(z_ref, gain_a_ref, gain_b_ref, x_ref, shared_ref, *refs):
+        send_refs, sems = refs[:rows], refs[rows]
+        copies = [
+            pltpu.make_async_copy(x_ref.at[(z_ref[0] + d) % rows], send_refs[d], sems.at[d])
+            for d in range(rows)
+        ]
+        for copy in copies:
+            copy.start()
         row = lax.broadcasted_iota(jnp.int32, (rows, tokens), 0)
         squares = jnp.zeros((rows, tokens), F32)
         for p in range(rows):
             squares = jnp.where(row == p, squares_by_lane([x_ref[p]]), squares)
         shared_ref[:rows] = squares
         shared_ref[rows:] = jnp.where(row == 0, gain_a_ref[...], gain_b_ref[...])
-        for d in range(rows):
-            send_refs[d][...] = x_ref[(z_ref[0] + d) % rows]
-
-    outs = [shape_of((2 * rows, tokens), F32)] + [shape_of((tokens, BLK))] * rows
+        for copy in copies:
+            copy.wait()
+
     return pl.pallas_call(
         kernel,
         in_specs=[scalar_spec()] + [whole((1, BLK))] * 2 + [whole(x_own.shape)],
-        out_shape=outs,
+        out_specs=[whole((2 * rows, tokens))] + [pl.BlockSpec(memory_space=pltpu.HBM)] * rows,
+        out_shape=[shape_of((2 * rows, tokens), F32)] + [shape_of((tokens, BLK))] * rows,
+        scratch_shapes=[pltpu.SemaphoreType.DMA((rows,))],
         compiler_params=params(),
     )(tensor_index, *gains, x_own)
 
@@ -183,25 +192,18 @@
     )
 
 
-def channel_map(first, second, mine, n_blk):
-    def kernel(mine_ref, first_a, first_b, second_a, second_b, out_ref, spread_ref):
-        @pl.when(pl.program_id(0) == 0)
-        def _():
-            spread_first(mine_ref, (first_a, first_b), spread_ref)
-
-        second_rows = choose(mine_ref, second_a[...], second_b[...])
-        for r in range(C1):
-            out_ref[0, r * C2 : (r + 1) * C2] = map_rows(spread_ref, second_rows, r)
-
-    return pl.pallas_call(
-        kernel,
-        grid=(n_blk,),
-        in_specs=factor_specs(),
-        out_specs=pl.BlockSpec((1, D, BLK), lambda n: (n, 0, 0)),
-        out_shape=shape_of((n_blk, D, BLK)),
-        scratch_shapes=[pltpu.VMEM((C1, C2, BLK), BF16)],
-        compiler_params=params(),
-    )(mine, *first, *second)
+def mix_channels(values_ref, spread_ref, second, map_refs):
+    span = D // len(map_refs)
+    total = jnp.zeros((values_ref.shape[0], BLK), F32)
+    for part, map_ref in enumerate(map_refs):
+        for r in range(span // C2):
+            map_ref[r * C2 : (r + 1) * C2] = map_rows(spread_ref, second, part * span // C2 + r)
+        total = total + dot(values_ref[:, part * span : (part + 1) * span], map_ref[...])
+    return total.astype(BF16)
+
+
+def map_scratch():
+    return [pltpu.VMEM((C1, C2, BLK), BF16)] + [pltpu.VMEM((D // PARTS, BLK), BF16)] * PARTS
 
 
 def normalize(x_blocks, gain_ref, tokens, store):
@@ -238,8 +240,6 @@
 
 def gate_stage(normed, first, second, mine, n_blk):
     tokens = normed.shape[0]
-    parts = 4
-    span = D // parts
 
     def kernel(mine_ref, first_a, first_b, second_a, second_b, normed_ref, out_ref, *scratch):
         spread_ref, *map_refs = scratch
@@ -249,13 +249,8 @@
             spread_first(mine_ref, (first_a, first_b), spread_ref)
 
         second_rows = choose(mine_ref, second_a[...], second_b[...])
-        pre = jnp.zeros((tokens, BLK), F32)
-        for part in range(parts):
-            for r in range(span // C2):
-                rows = map_rows(spread_ref, second_rows, part * span // C2 + r)
-                map_refs[part][r * C2 : (r + 1) * C2] = rows
-            pre = pre + dot(normed_ref[:, part * span : (part + 1) * span], map_refs[part][...])
-        out_ref[0] = jax.nn.sigmoid(pre.astype(BF16).astype(F32))
+        pre = mix_channels(normed_ref, spread_ref, second_rows, map_refs)
+        out_ref[0] = jax.nn.sigmoid(pre.astype(F32))
 
     return pl.pallas_call(
         kernel,
@@ -263,30 +258,33 @@
         in_specs=factor_specs() + [whole(normed.shape)],
         out_specs=pl.BlockSpec((1, tokens, BLK), lambda n: (n, 0, 0)),
         out_shape=shape_of((n_blk, tokens, BLK), F32),
-        scratch_shapes=[pltpu.VMEM((C1, C2, BLK), BF16)] + [pltpu.VMEM((span, BLK), BF16)] * parts,
+        scratch_shapes=map_scratch(),
         compiler_params=params(),
     )(mine, *first, *second, normed)
 
 
-def out_stage(seq_out, gate, x_tok, out_map, gain=None):
+def out_stage(seq_out, gate, x_tok, first, second, mine, gain=None):
     groups, n_blk, width, _ = seq_out.shape
     tokens = groups * width
     height = tokens + (0 if gain is None else EXTRA)
 
-    def kernel(seq_ref, gate_ref, x_ref, map_ref, *refs):
+    def kernel(mine_ref, first_a, first_b, second_a, second_b, seq_ref, gate_ref, x_ref, *refs):
         n = pl.program_id(0)
+        gated_ref, spread_ref, *map_refs = refs[-2 - PARTS :]
         if gain is None:
-            rows_ref, res_ref, gated_ref = refs
+            rows_ref, res_ref = refs[:2]
         else:
-            gain_ref, rows_ref, res_ref, normed_ref, gated_ref = refs
+            gain_ref, rows_ref, res_ref, normed_ref = refs[:4]
 
         @pl.when(n == 0)
         def _():
+            spread_first(mine_ref, (first_a, first_b), spread_ref)
             for z in range(n_blk):
                 seq = seq_ref[:, z].reshape(tokens, BLK).astype(F32)
                 gated_ref[:, z * BLK : (z + 1) * BLK] = (seq * gate_ref[z]).astype(BF16)
 
-        mixed = dot(gated_ref[...], map_ref[0]).astype(BF16).astype(F32)
+        second_rows = choose(mine_ref, second_a[...], second_b[...])
+        mixed = mix_channels(gated_ref, spread_ref, second_rows, map_refs).astype(F32)
         res_ref[n, :tokens] = (x_ref[n, :tokens].astype(F32) + mixed).astype(BF16)
 
         @pl.when(n == n_blk - 1)
@@ -313,13 +311,8 @@
             for z in range(n_blk):
                 res_ref[z, tokens : tokens + EXTRA] = packed
 
-    in_specs = [
-        whole(seq_out.shape),
-        whole(gate.shape),
-        whole(x_tok.shape),
-        pl.BlockSpec((1, D, BLK), lambda n: (n, 0, 0)),
-    ]
-    operands = [seq_out, gate, x_tok, out_map]
+    in_specs = factor_specs() + [whole(a.shape) for a in (seq_out, gate, x_tok)]
+    operands = [mine, *first, *second, seq_out, gate, x_tok]
     out_shape = [shape_of((tokens // STRIDE, D)), shape_of((n_blk, height, BLK))]
     if gain is not None:
         operands.append(gain)
@@ -331,7 +324,7 @@
         in_specs=in_specs,
         out_specs=[whole(s.shape) for s in out_shape],
         out_shape=out_shape,
-        scratch_shapes=[pltpu.VMEM((tokens, D), BF16)],
+        scratch_shapes=[pltpu.VMEM((tokens, D), BF16)] + map_scratch(),
         compiler_params=params(),
     )(*operands)
 
@@ -512,8 +505,9 @@
     near_heads = [along_y(head_own, d) for d in (1, 3)]
     x_tok, normed = token_stage(received, gains[0], z_scalar)
     gate = gate_stage(normed, gate_first_pair, gate_second_pair, mine[0], n_blk)
-    out_map = channel_map(out_first_pair, out_second_pair, mine[0], n_blk)
-    rows_one, packed, normed = out_stage(seq_out, gate, x_tok, out_map, gain=gains[1])
+    rows_one, packed, normed = out_stage(
+        seq_out, gate, x_tok, out_first_pair, out_second_pair, mine[0], gain=gains[1]
+    )
 
     packed, normed, head_own, near_heads, gate_first_pair, out_first_pair = tie(
         (packed, normed, head_own, near_heads, gate_first_pair, out_first_pair)
@@ -521,12 +515,13 @@
     far_head = along_y(head_own, 2)
     chan_one = lax.all_to_all(packed, "tensor", split_axis=0, concat_axis=0, tiled=True)
     gate = gate_stage(normed, gate_first_pair, gate_second_pair, mine[1], n_blk)
-    out_map = channel_map(out_first_pair, out_second_pair, mine[1], n_blk)
     mix = right_stage(chan_one, gain_local[1], right, mine[1], seq_count)
-    mix, gate, out_map, far_head = tie((mix, gate, out_map, far_head))
+    mix, gate, far_head = tie((mix, gate, far_head))
     heads = [head_own, near_heads[0], far_head, near_heads[1]]
     seq_out = exchange_all(mix_left(exchange_seq(mix), 1))
-    rows_two, result = out_stage(seq_out, gate, packed, out_map)
+    rows_two, result = out_stage(
+        seq_out, gate, packed, out_first_pair, out_second_pair, mine[1]
+    )
 
     pair = jnp.stack([rows_one, rows_two])[:, None]
     pair = jnp.broadcast_to(pair, (2, n_blk) + rows_two.shape).reshape((-1,) + rows_two.shape)

time: 293 us -> 289 us (0.986)
  waiting for transfers between devices: 47.6 us -> 63.4 us
  Pallas kernels: 62.7 us -> 47.6 us
  starting transfers between devices: 77.7 us -> 74.6 us
    pallas_call x2 -> x0, Pallas kernels: 14.8 us -> none  [channel_map(): pl.pallas_call(kernel, grid=(n_blk,), in_specs=factor_specs(), out_specs=...]
    all_to_all x1, waiting for transfers between devices: 0.67 us -> 9.02 us  [exchange_all(): lax.all_to_all(cols, everyone, split_axis=0, concat_axis=0, tiled=True)]
    all_to_all x1, waiting for transfers between devices: 13.2 us -> 20.8 us  [body(): lax.all_to_all(packed, 'tensor', split_axis=0, concat_axis=0, tiled=True)]
  transfers between devices with their start and end apart: 28 -> 28, of which waited for: 12 -> 12; matrix products, arithmetic and copies ran while one was open for 1% -> 1% of each run, Pallas kernels for 18% -> 13%
where the time goes in v10:
time: 289 us; the launch traced here: 286 us
  starting transfers between devices  74.6 us (26%)
  blocking collectives  67.3 us (23%)
  waiting for transfers between devices  63.4 us (22%)
  Pallas kernels  47.6 us (16%)
  local copies, waits for them, and re-layouts  31.7 us (11%)
    all_to_all x1, blocking collectives, exchange_all(): lax.all_to_all(cols, everyone, split_axis=0, concat_axis=0, tiled=True)  34.8 us
    unnamed x86, local copies, waits for them, and re-layouts  27.5 us
    all_to_all x1, waiting for transfers between devices, body(): lax.all_to_all(packed, 'tensor', split_axis=0, concat_axis=0, tiled=True)  20.8 us
    all_to_all x1, blocking collectives, exchange_seq(): return lax.all_to_all(mix, 'seq', split_axis=0, concat_axis=0, tiled=True)  18.8 us
    all_to_all x1, waiting for transfers between devices, body(): lax.all_to_all(result, 'tensor', split_axis=0, concat_axis=0, tiled=True)  15.5 us
    pallas_call x2, Pallas kernels, out_stage(): pl.pallas_call(kernel, grid=(n_blk,), in_specs=in_specs, out_specs=[whole...  15.5 us
    all_to_all x1, starting transfers between devices, exchange_all(): lax.all_to_all(cols, everyone, split_axis=0, concat_axis=0, tiled=True)  15.1 us
    all_to_all x1, blocking collectives, body(): lax.all_to_all(pair, ('section', 'tensor'), split_axis=0, concat_axis=0,...  13.6 us
  transfers between devices with their start and end apart: 28, of which 12 were waited for; matrix products, arithmetic and copies ran while one was open for 1% of the time, Pallas kernels for 13%

profile of v10, /device:TPU:1, one launch (start us, length us, event | category | flops | bytes accessed | tf_op | source)
XLA Modules:
  0.0 285.8 jit_solution(11193014495343944436)
XLA Ops:
  0.7 3.3 %collective-permute-start = (f32[1,256]{1,0:T(1,128)}, f32[1,256]{1,0:T(1,128)S(1)}, u32[]{:S(2)}, u32[]{:S(2)}) collective-permute-start(f32[1,256]{1,0:T(1,128)} %param.11), channel_id=1, source_target_pairs={{0,128},{128,0},{1,129},{129,1},{2,130},{130,2},{3,131},{131,3},{4... | collective-permute-start | bytes 3080 | tf_op jit(solution)/shard_map/ppermute | solution.py:465
  13.7 6.4 %all-to-all-start = ((f32[8,16,256]{2,1,0:T(8,128)}), f32[8,16,256]{2,1,0:T(8,128)S(1)}, u32[]{:S(2)}, u32[]{:S(2)}) async-start(f32[8,16,256]{2,1,0:T(8,128)} %broadcast_in_dim.6), calls=%async_computation | async-start | bytes 262144 | tf_op jit(solution)/shard_map/all_to_all | solution.py:45
  25.2 3.5 %all-to-all-done.refs_0_ = f32[8,16,256]{2,1,0:T(8,128)S(1)} async-done(((f32[8,16,256]{2,1,0:T(8,128)}), f32[8,16,256]{2,1,0:T(8,128)S(1)}, u32[]{:S(2)}, u32[]{:S(2)}) %all-to-all-start) | async-done | bytes 131104 | tf_op jit(solution)/shard_map/all_to_all | solution.py:45
  35.5 6.8 %all-to-all-start.1 = ((bf16[16,8,16,256]{3,2,1,0:T(8,128)(2,1)}), bf16[16,8,16,256]{3,2,1,0:T(8,128)(2,1)S(1)}, u32[]{:S(2)}, u32[]{:S(2)}) async-start(bf16[16,8,16,256]{3,2,1,0:T(8,128)(2,1)} %copy-done.7), calls=%async_computation.1 | async-start | bytes 2097152 | tf_op jit(solution)/shard_map/all_to_all | solution.py:479
  43.6 3.7 %collective-permute-start.7 = (bf16[256,256]{1,0:T(8,128)(2,1)}, bf16[256,256]{1,0:T(8,128)(2,1)S(1)}, u32[]{:S(2)}, u32[]{:S(2)}) collective-permute-start(bf16[256,256]{1,0:T(8,128)(2,1)} %copy-done.34), channel_id=1, source_target_pairs={{0,3},{1,4},{2,5},{3,6},{4,7},{5,0},{6,1},{7,2},{8,11},{9,12},{10,... | collective-permute-start | bytes 393224 | tf_op jit(solution)/shard_map/ppermute | solution.py:451
  48.4 3.4 %collective-permute-start.9 = (bf16[256,256]{1,0:T(8,128)(2,1)}, bf16[256,256]{1,0:T(8,128)(2,1)}, u32[]{:S(2)}, u32[]{:S(2)}) collective-permute-start(bf16[256,256]{1,0:T(8,128)(2,1)} %copy-done.32), channel_id=1, source_target_pairs={{0,5},{1,6},{2,7},{3,0},{4,1},{5,2},{6,3},{7,4},{8,13},{9,14},{10,... | collective-permute-start | bytes 393224 | tf_op jit(solution)/shard_map/ppermute | solution.py:451
  52.6 5.0 %all-to-all-done.1 = bf16[16,8,16,256]{3,2,1,0:T(8,128)(2,1)S(1)} async-done(((bf16[16,8,16,256]{3,2,1,0:T(8,128)(2,1)}), bf16[16,8,16,256]{3,2,1,0:T(8,128)(2,1)S(1)}, u32[]{:S(2)}, u32[]{:S(2)}) %all-to-all-start.1) | async-done | bytes 1048608 | tf_op jit(solution)/shard_map/all_to_all | solution.py:479
  62.5 15.1 %all-to-all-start.2 = ((bf16[128,16,256]{2,1,0:T(8,128)(2,1)}), bf16[128,16,256]{2,1,0:T(8,128)(2,1)}, u32[]{:S(2)}, u32[]{:S(2)}) async-start(bf16[128,16,256]{2,1,0:T(8,128)(2,1)} %bitcast.44), calls=%async_computation.2 | async-start | bytes 2097152 | tf_op jit(solution)/shard_map/all_to_all | solution.py:486
  90.7 6.2 %shard_map.117.gate_ref = f32[8,256,256]{2,1,0:T(8,128)S(1)} custom-call(s32[1]{0:T(128)} %bitcast.10.mine_ref, bf16[32,64,64]{2,1,0:T(8,128)(2,1)} %bitcast.18.first_a, bf16[32,64,64]{2,1,0:T(8,128)(2,1)} %collective-permute-done.12.first_b, bf16[32,2048]{1,0:T(8,128)(2,1)S(1)} %reshape.79.second_a, bf16[32,2048]{1,0:T(8,128)(2,1)S(1)} %copy-done.24, ...), custom_call_target="tpu_custom_call" | custom-call | tf_op jit(solution)/shard_map/pallas_call | solution.py:255
  98.8 9.0 %all-to-all-done.2 = bf16[128,16,256]{2,1,0:T(8,128)(2,1)} async-done(((bf16[128,16,256]{2,1,0:T(8,128)(2,1)}), bf16[128,16,256]{2,1,0:T(8,128)(2,1)}, u32[]{:S(2)}, u32[]{:S(2)}) %all-to-all-start.2) | async-done | bytes 1048608 | tf_op jit(solution)/shard_map/all_to_all | solution.py:486
  110.0 8.4 %shard_map.118 = (bf16[2,2048]{1,0:T(2,128)(2,1)S(1)}, bf16[8,272,256]{2,1,0:T(8,128)(2,1)S(1)}, bf16[256,2048]{1,0:T(8,128)(2,1)S(1)}) custom-call(s32[1]{0:T(128)} %bitcast.10.mine_ref, bf16[32,64,64]{2,1,0:T(8,128)(2,1)} %bitcast.19.first_a, bf16[32,64,64]{2,1,0:T(8,128)(2,1)} %collective-permute-done.10.first_b, bf16[32,2048]{1,0:T(8,128)(2,1)S(1)} %reshape.77.second_a, ...), custom_call_target="tpu_custom_call" | custom-call | tf_op jit(solution)/shard_map/pallas_call | solution.py:321
  120.3 3.6 %all-to-all-start.3 = ((bf16[8,272,256]{2,1,0:T(8,128)(2,1)}), bf16[8,272,256]{2,1,0:T(8,128)(2,1)S(1)}, u32[]{:S(2)}, u32[]{:S(2)}) async-start(bf16[8,272,256]{2,1,0:T(8,128)(2,1)} %copy-done.3), calls=%async_computation.3 | async-start | bytes 2228224 | tf_op jit(solution)/shard_map/all_to_all | solution.py:516
  126.2 6.2 %shard_map.120.gate_ref = f32[8,256,256]{2,1,0:T(8,128)S(1)} custom-call(s32[1]{0:T(128)} %bitcast.26.mine_ref, bf16[32,64,64]{2,1,0:T(8,128)(2,1)} %bitcast.18.first_a, bf16[32,64,64]{2,1,0:T(8,128)(2,1)} %collective-permute-done.12.first_b, bf16[32,2048]{1,0:T(8,128)(2,1)S(1)} %reshape.79.second_a, bf16[32,2048]{1,0:T(8,128)(2,1)S(1)} %copy-done.25, ...), custom_call_target="tpu_custom_call" | custom-call | tf_op jit(solution)/shard_map/pallas_call | solution.py:255
  133.7 20.8 %all-to-all-done.3.x_ref.refs_0_ = bf16[8,272,256]{2,1,0:T(8,128)(2,1)S(1)} async-done(((bf16[8,272,256]{2,1,0:T(8,128)(2,1)}), bf16[8,272,256]{2,1,0:T(8,128)(2,1)S(1)}, u32[]{:S(2)}, u32[]{:S(2)}) %all-to-all-start.3) | async-done | bytes 1114144 | tf_op jit(solution)/shard_map/all_to_all | solution.py:516
  157.5 18.8 %all_to_all.45 = bf16[16,8,16,256]{3,2,1,0:T(8,128)(2,1)S(1)} all-to-all(bf16[16,8,16,256]{3,2,1,0:T(8,128)(2,1)S(1)} %shard_map.119), channel_id=1, replica_groups=mesh['section'=2,'seq'=16,'tensor'=8] {'seq'}, dimensions={0} | all-to-all | bytes 2097152 | tf_op jit(solution)/shard_map/all_to_all | solution.py:479
  177.9 34.8 %all_to_all.46 = bf16[128,16,256]{2,1,0:T(8,128)(2,1)S(1)} all-to-all(bf16[128,16,256]{2,1,0:T(8,128)(2,1)S(1)} %bitcast.47), channel_id=1, replica_groups=mesh['section'=2,'seq'=16,'tensor'=8] {'seq','tensor'}, dimensions={0} | all-to-all | bytes 2097152 | tf_op jit(solution)/shard_map/all_to_all | solution.py:486
  212.7 7.1 %shard_map.122 = (bf16[2,2048]{1,0:T(2,128)(2,1)S(1)}, bf16[8,256,256]{2,1,0:T(8,128)(2,1)S(1)}) custom-call(s32[1]{0:T(128)} %bitcast.26.mine_ref, bf16[32,64,64]{2,1,0:T(8,128)(2,1)} %bitcast.19.first_a, bf16[32,64,64]{2,1,0:T(8,128)(2,1)} %collective-permute-done.10.first_b, bf16[32,2048]{1,0:T(8,128)(2,1)S(1)} %reshape.77.second_a, ...), custom_call_target="tpu_custom_call" | custom-call | tf_op jit(solution)/shard_map/pallas_call | solution.py:321
  220.9 13.6 %all_to_all.47 = bf16[16,2,2048]{2,1,0:T(2,128)(2,1)S(1)} all-to-all(bf16[16,2,2048]{2,1,0:T(2,128)(2,1)S(1)} %bitcast.55), channel_id=1, replica_groups=mesh['section'=2,'seq'=16,'tensor'=8] {'section','tensor'}, dimensions={0} | all-to-all | bytes 262144 | tf_op jit(solution)/shard_map/all_to_all | solution.py:528
  234.5 4.3 %all-to-all-start.7 = ((bf16[8,256,256]{2,1,0:T(8,128)(2,1)}), bf16[8,256,256]{2,1,0:T(8,128)(2,1)}, u32[]{:S(2)}, u32[]{:S(2)}) async-start(bf16[8,256,256]{2,1,0:T(8,128)(2,1)} %copy-done.16), calls=%async_computation.7 | async-start | bytes 2097152 | tf_op jit(solution)/shard_map/all_to_all | solution.py:530
  241.7 4.7 %collective-permute-start.20 = (bf16[8,272,256]{2,1,0:T(8,128)(2,1)S(1)}, bf16[8,272,256]{2,1,0:T(8,128)(2,1)}, u32[]{:S(2)}, u32[]{:S(2)}) collective-permute-start(bf16[8,272,256]{2,1,0:T(8,128)(2,1)S(1)} %all-to-all-done.3.x_ref.refs_0_), channel_id=1, source_target_pairs={{128,0},{129,1},{130,2},{131,3},{132,4},{133,5},{134,6},{135,7},{1... | collective-permute-start | bytes 3342344 | tf_op jit(solution)/shard_map/ppermute | solution.py:548
  250.4 15.5 %all-to-all-done.7.refs_3_ = bf16[8,256,256]{2,1,0:T(8,128)(2,1)} async-done(((bf16[8,256,256]{2,1,0:T(8,128)(2,1)}), bf16[8,256,256]{2,1,0:T(8,128)(2,1)}, u32[]{:S(2)}, u32[]{:S(2)}) %all-to-all-start.7) | async-done | bytes 1048608 | tf_op jit(solution)/shard_map/all_to_all | solution.py:530
  267.8 6.1 %all-to-all-start.8 = ((f32[128,2,128]{2,1,0:T(2,128)}), f32[128,2,128]{2,1,0:T(2,128)S(1)}, u32[]{:S(2)}, u32[]{:S(2)}) async-start(f32[128,2,128]{2,1,0:T(2,128)} %broadcast_in_dim.8), calls=%async_computation.8 | async-start | bytes 262144 | tf_op jit(solution)/shard_map/all_to_all | solution.py:45
  273.9 6.0 %shard_map.124 = bf16[2,8,256,256]{3,2,1,0:T(8,128)(2,1)} custom-call(s32[1]{0:T(128)} %bitcast.32.section_ref, bf16[8,272,256]{2,1,0:T(8,128)(2,1)S(1)} %all-to-all-done.3.x_ref.refs_0_, bf16[8,272,256]{2,1,0:T(8,128)(2,1)} %collective-permute-done.20.refs_1_, bf16[8,256,256]{2,1,0:T(8,128)(2,1)} %collective-permute-done.21.refs_2_, ...), custom_call_target="tpu_custom_call" | custom-call | tf_op jit(solution)/shard_map/pallas_call | solution.py:405
  279.9 5.1 %all-to-all-done.8.parts_ref = f32[128,2,128]{2,1,0:T(2,128)S(1)} async-done(((f32[128,2,128]{2,1,0:T(2,128)}), f32[128,2,128]{2,1,0:T(2,128)S(1)}, u32[]{:S(2)}, u32[]{:S(2)}) %all-to-all-start.8) | async-done | bytes 131104 | tf_op jit(solution)/shard_map/all_to_all | solution.py:45
  (152 shorter events, 67.4 us)
Async XLA Ops:
  12.4 16.2 %collective-permute-start.1 = (bf16[8,256,256]{2,1,0:T(8,128)(2,1)}, bf16[8,256,256]{2,1,0:T(8,128)(2,1)}, u32[]{:S(2)}, u32[]{:S(2)}) collective-permute-start(bf16[8,256,256]{2,1,0:T(8,128)(2,1)} %bitcast.41), channel_id=1, source_target_pairs={{0,128},{128,0},{1,129},{129,1},{2,130},{130,2},{3,131},{131,3},{4... | collective-permute-start | bytes 3145736 | tf_op jit(solution)/shard_map/ppermute | solution.py:444
  13.7 15.0 %all-to-all-start = ((f32[8,16,256]{2,1,0:T(8,128)}), f32[8,16,256]{2,1,0:T(8,128)S(1)}, u32[]{:S(2)}, u32[]{:S(2)}) async-start(f32[8,16,256]{2,1,0:T(8,128)} %broadcast_in_dim.6), calls=%async_computation | async-start | bytes 262144 | tf_op jit(solution)/shard_map/all_to_all | solution.py:45
  20.1 12.6 %collective-permute-start.2 = (bf16[256,256]{1,0:T(8,128)(2,1)}, bf16[256,256]{1,0:T(8,128)(2,1)S(1)}, u32[]{:S(2)}, u32[]{:S(2)}) collective-permute-start(bf16[256,256]{1,0:T(8,128)(2,1)} %copy-done.38), channel_id=1, source_target_pairs={{0,1},{1,2},{2,3},{3,4},{4,5},{5,6},{6,7},{7,0},{8,9},{9,10},{10,1... | collective-permute-start | bytes 393224 | tf_op jit(solution)/shard_map/ppermute | solution.py:451
  21.6 12.8 %collective-permute-start.3 = (bf16[256,256]{1,0:T(8,128)(2,1)}, bf16[256,256]{1,0:T(8,128)(2,1)}, u32[]{:S(2)}, u32[]{:S(2)}) collective-permute-start(bf16[256,256]{1,0:T(8,128)(2,1)} %copy-done.37), channel_id=1, source_target_pairs={{0,2},{1,3},{2,4},{3,5},{4,6},{5,7},{6,0},{7,1},{8,10},{9,11},{10,... | collective-permute-start | bytes 393224 | tf_op jit(solution)/shard_map/ppermute | solution.py:451
  23.7 10.7 %collective-permute-start.4 = (bf16[256,256]{1,0:T(8,128)(2,1)}, bf16[256,256]{1,0:T(8,128)(2,1)}, u32[]{:S(2)}, u32[]{:S(2)}) collective-permute-start(bf16[256,256]{1,0:T(8,128)(2,1)} %copy-done.36), channel_id=1, source_target_pairs={{0,6},{1,7},{2,0},{3,1},{4,2},{5,3},{6,4},{7,5},{8,14},{9,15},{10,... | collective-permute-start | bytes 393224 | tf_op jit(solution)/shard_map/ppermute | solution.py:451
  25.2 10.3 %collective-permute-start.5 = (bf16[256,256]{1,0:T(8,128)(2,1)}, bf16[256,256]{1,0:T(8,128)(2,1)}, u32[]{:S(2)}, u32[]{:S(2)}) collective-permute-start(bf16[256,256]{1,0:T(8,128)(2,1)} %copy-done.35), channel_id=1, source_target_pairs={{0,7},{1,0},{2,1},{3,2},{4,3},{5,4},{6,5},{7,6},{8,15},{9,8},{10,9... | collective-permute-start | bytes 393224 | tf_op jit(solution)/shard_map/ppermute | solution.py:451
  35.5 22.0 %all-to-all-start.1 = ((bf16[16,8,16,256]{3,2,1,0:T(8,128)(2,1)}), bf16[16,8,16,256]{3,2,1,0:T(8,128)(2,1)S(1)}, u32[]{:S(2)}, u32[]{:S(2)}) async-start(bf16[16,8,16,256]{3,2,1,0:T(8,128)(2,1)} %copy-done.7), calls=%async_computation.1 | async-start | bytes 2097152 | tf_op jit(solution)/shard_map/all_to_all | solution.py:479
  42.3 9.5 %collective-permute-start.6 = (bf16[16,128,128]{2,1,0:T(8,128)(2,1)}, bf16[16,128,128]{2,1,0:T(8,128)(2,1)S(1)}, u32[]{:S(2)}, u32[]{:S(2)}) collective-permute-start(bf16[16,128,128]{2,1,0:T(8,128)(2,1)} %bitcast.49), channel_id=1, source_target_pairs={{0,128},{128,0},{1,129},{129,1},{2,130},{130,2},{3,131},{131,3},{4... | collective-permute-start | bytes 1572872 | tf_op jit(solution)/shard_map/ppermute | solution.py:444
  43.6 18.6 %collective-permute-start.7 = (bf16[256,256]{1,0:T(8,128)(2,1)}, bf16[256,256]{1,0:T(8,128)(2,1)S(1)}, u32[]{:S(2)}, u32[]{:S(2)}) collective-permute-start(bf16[256,256]{1,0:T(8,128)(2,1)} %copy-done.34), channel_id=1, source_target_pairs={{0,3},{1,4},{2,5},{3,6},{4,7},{5,0},{6,1},{7,2},{8,11},{9,12},{10,... | collective-permute-start | bytes 393224 | tf_op jit(solution)/shard_map/ppermute | solution.py:451
  47.3 14.9 %collective-permute-start.8 = (bf16[256,256]{1,0:T(8,128)(2,1)}, bf16[256,256]{1,0:T(8,128)(2,1)}, u32[]{:S(2)}, u32[]{:S(2)}) collective-permute-start(bf16[256,256]{1,0:T(8,128)(2,1)} %copy-done.33), channel_id=1, source_target_pairs={{0,4},{1,5},{2,6},{3,7},{4,0},{5,1},{6,2},{7,3},{8,12},{9,13},{10,... | collective-permute-start | bytes 393224 | tf_op jit(solution)/shard_map/ppermute | solution.py:451
  48.4 14.1 %collective-permute-start.9 = (bf16[256,256]{1,0:T(8,128)(2,1)}, bf16[256,256]{1,0:T(8,128)(2,1)}, u32[]{:S(2)}, u32[]{:S(2)}) collective-permute-start(bf16[256,256]{1,0:T(8,128)(2,1)} %copy-done.32), channel_id=1, source_target_pairs={{0,5},{1,6},{2,7},{3,0},{4,1},{5,2},{6,3},{7,4},{8,13},{9,14},{10,... | collective-permute-start | bytes 393224 | tf_op jit(solution)/shard_map/ppermute | solution.py:451
  62.5 45.4 %all-to-all-start.2 = ((bf16[128,16,256]{2,1,0:T(8,128)(2,1)}), bf16[128,16,256]{2,1,0:T(8,128)(2,1)}, u32[]{:S(2)}, u32[]{:S(2)}) async-start(bf16[128,16,256]{2,1,0:T(8,128)(2,1)} %bitcast.44), calls=%async_computation.2 | async-start | bytes 2097152 | tf_op jit(solution)/shard_map/all_to_all | solution.py:486
  77.6 42.7 %collective-permute-start.14 = (bf16[2048,256]{1,0:T(8,128)(2,1)}, bf16[2048,256]{1,0:T(8,128)(2,1)}, u32[]{:S(2)}, u32[]{:S(2)}) collective-permute-start(bf16[2048,256]{1,0:T(8,128)(2,1)} %bitcast.17.refs_4_), channel_id=1, source_target_pairs={{0,8},{8,16},{16,24},{24,0},{32,40},{40,48},{48,56},{56,32},{64,72... | collective-permute-start | bytes 3145736 | tf_op jit(solution)/shard_map/ppermute | solution.py:448
  78.2 42.1 %collective-permute-start.15 = (bf16[2048,256]{1,0:T(8,128)(2,1)}, bf16[2048,256]{1,0:T(8,128)(2,1)}, u32[]{:S(2)}, u32[]{:S(2)}) collective-permute-start(bf16[2048,256]{1,0:T(8,128)(2,1)} %bitcast.17.refs_4_), channel_id=1, source_target_pairs={{0,24},{8,0},{16,8},{24,16},{32,56},{40,32},{48,40},{56,48},{64,88... | collective-permute-start | bytes 3145736 | tf_op jit(solution)/shard_map/ppermute | solution.py:448
  82.3 16.6 %collective-permute-start.10 = (bf16[32,64,64]{2,1,0:T(8,128)(2,1)}, bf16[32,64,64]{2,1,0:T(8,128)(2,1)}, u32[]{:S(2)}, u32[]{:S(2)}) collective-permute-start(bf16[32,64,64]{2,1,0:T(8,128)(2,1)} %bitcast.19.first_a), channel_id=1, source_target_pairs={{0,128},{128,0},{1,129},{129,1},{2,130},{130,2},{3,131},{131,3},{4... | collective-permute-start | bytes 786440 | tf_op jit(solution)/shard_map/ppermute | solution.py:444
  83.8 14.4 %collective-permute-start.11 = (bf16[32,2048]{1,0:T(8,128)(2,1)S(1)}, bf16[32,2048]{1,0:T(8,128)(2,1)S(1)}, u32[]{:S(2)}, u32[]{:S(2)}) collective-permute-start(bf16[32,2048]{1,0:T(8,128)(2,1)S(1)} %reshape.77.second_a), channel_id=1, source_target_pairs={{0,128},{128,0},{1,129},{129,1},{2,130},{130,2},{3,131},{131,3},{4... | collective-permute-start | bytes 393224 | tf_op jit(solution)/shard_map/ppermute | solution.py:444
  120.3 34.1 %all-to-all-start.3 = ((bf16[8,272,256]{2,1,0:T(8,128)(2,1)}), bf16[8,272,256]{2,1,0:T(8,128)(2,1)S(1)}, u32[]{:S(2)}, u32[]{:S(2)}) async-start(bf16[8,272,256]{2,1,0:T(8,128)(2,1)} %copy-done.3), calls=%async_computation.3 | async-start | bytes 2228224 | tf_op jit(solution)/shard_map/all_to_all | solution.py:516
  123.9 33.6 %collective-permute-start.16 = (bf16[2048,256]{1,0:T(8,128)(2,1)}, bf16[2048,256]{1,0:T(8,128)(2,1)}, u32[]{:S(2)}, u32[]{:S(2)}) collective-permute-start(bf16[2048,256]{1,0:T(8,128)(2,1)} %bitcast.17.refs_4_), channel_id=1, source_target_pairs={{0,16},{8,24},{16,0},{24,8},{32,48},{40,56},{48,32},{56,40},{64,80... | collective-permute-start | bytes 3145736 | tf_op jit(solution)/shard_map/ppermute | solution.py:448
  234.5 31.3 %all-to-all-start.7 = ((bf16[8,256,256]{2,1,0:T(8,128)(2,1)}), bf16[8,256,256]{2,1,0:T(8,128)(2,1)}, u32[]{:S(2)}, u32[]{:S(2)}) async-start(bf16[8,256,256]{2,1,0:T(8,128)(2,1)} %copy-done.16), calls=%async_computation.7 | async-start | bytes 2097152 | tf_op jit(solution)/shard_map/all_to_all | solution.py:530
  238.9 7.8 %collective-permute-start.17 = (bf16[32,2048]{1,0:T(8,128)(2,1)S(1)}, bf16[32,2048]{1,0:T(8,128)(2,1)S(1)}, u32[]{:S(2)}, u32[]{:S(2)}) collective-permute-start(bf16[32,2048]{1,0:T(8,128)(2,1)S(1)} %reshape.86.refs_0_), channel_id=1, source_target_pairs={{0,32},{8,40},{16,48},{24,56},{32,64},{40,72},{48,80},{56,88},{64,... | collective-permute-start | bytes 393224 | tf_op jit(solution)/shard_map/ppermute | solution.py:455
  238.9 7.7 %collective-permute-start.18 = (bf16[32,2048]{1,0:T(8,128)(2,1)S(1)}, bf16[32,2048]{1,0:T(8,128)(2,1)}, u32[]{:S(2)}, u32[]{:S(2)}) collective-permute-start(bf16[32,2048]{1,0:T(8,128)(2,1)S(1)} %reshape.86.refs_0_), channel_id=1, source_target_pairs={{0,64},{8,72},{16,80},{24,88},{32,96},{40,104},{48,112},{56,120},{... | collective-permute-start | bytes 393224 | tf_op jit(solution)/shard_map/ppermute | solution.py:455
  241.7 32.2 %collective-permute-start.20 = (bf16[8,272,256]{2,1,0:T(8,128)(2,1)S(1)}, bf16[8,272,256]{2,1,0:T(8,128)(2,1)}, u32[]{:S(2)}, u32[]{:S(2)}) collective-permute-start(bf16[8,272,256]{2,1,0:T(8,128)(2,1)S(1)} %all-to-all-done.3.x_ref.refs_0_), channel_id=1, source_target_pairs={{128,0},{129,1},{130,2},{131,3},{132,4},{133,5},{134,6},{135,7},{1... | collective-permute-start | bytes 3342344 | tf_op jit(solution)/shard_map/ppermute | solution.py:548
  265.8 8.1 %collective-permute-start.21 = (bf16[8,256,256]{2,1,0:T(8,128)(2,1)}, bf16[8,256,256]{2,1,0:T(8,128)(2,1)}, u32[]{:S(2)}, u32[]{:S(2)}) collective-permute-start(bf16[8,256,256]{2,1,0:T(8,128)(2,1)} %all-to-all-done.7.refs_3_), channel_id=1, source_target_pairs={{0,128},{1,129},{2,130},{3,131},{4,132},{5,133},{6,134},{7,135},{8... | collective-permute-start | bytes 3145736 | tf_op jit(solution)/shard_map/ppermute | solution.py:549
  267.8 17.2 %all-to-all-start.8 = ((f32[128,2,128]{2,1,0:T(2,128)}), f32[128,2,128]{2,1,0:T(2,128)S(1)}, u32[]{:S(2)}, u32[]{:S(2)}) async-start(f32[128,2,128]{2,1,0:T(2,128)} %broadcast_in_dim.8), calls=%async_computation.8 | async-start | bytes 262144 | tf_op jit(solution)/shard_map/all_to_all | solution.py:45
  (47 other events, 285.5 us)

commit v11 on v10

--- a/solution.py
+++ b/solution.py
@@ -71,34 +71,28 @@
     return high, mid, value - high - mid
 
 
-def split_stage(x_own, gains, tensor_index):
+def pack_stage(x_own, gains):
     rows, tokens, _ = x_own.shape
 
-    def kernel(z_ref, gain_a_ref, gain_b_ref, x_ref, shared_ref, *refs):
-        send_refs, sems = refs[:rows], refs[rows]
-        copies = [
-            pltpu.make_async_copy(x_ref.at[(z_ref[0] + d) % rows], send_refs[d], sems.at[d])
-            for d in range(rows)
-        ]
-        for copy in copies:
-            copy.start()
+    def kernel(x_ref, gain_a_ref, gain_b_ref, out_ref):
         row = lax.broadcasted_iota(jnp.int32, (rows, tokens), 0)
         squares = jnp.zeros((rows, tokens), F32)
         for p in range(rows):
             squares = jnp.where(row == p, squares_by_lane([x_ref[p]]), squares)
-        shared_ref[:rows] = squares
-        shared_ref[rows:] = jnp.where(row == 0, gain_a_ref[...], gain_b_ref[...])
-        for copy in copies:
-            copy.wait()
-
-    return pl.pallas_call(
-        kernel,
-        in_specs=[scalar_spec()] + [whole((1, BLK))] * 2 + [whole(x_own.shape)],
-        out_specs=[whole((2 * rows, tokens))] + [pl.BlockSpec(memory_space=pltpu.HBM)] * rows,
-        out_shape=[shape_of((2 * rows, tokens), F32)] + [shape_of((tokens, BLK))] * rows,
-        scratch_shapes=[pltpu.SemaphoreType.DMA((rows,))],
-        compiler_params=params(),
-    )(tensor_index, *gains, x_own)
+        gain_rows = jnp.zeros((rows, BLK), F32)
+        for b, gain_ref in enumerate((gain_a_ref, gain_b_ref)):
+            for part, value in enumerate(split3(gain_ref[...])):
+                gain_rows = jnp.where(row == b * 3 + part, value, gain_rows)
+        planes = jnp.concatenate([*split3(squares), gain_rows], axis=0).astype(BF16)
+        for p in range(rows):
+            out_ref[p, :tokens] = x_ref[p]
+            out_ref[p, tokens:] = planes
+
+    return pl.pallas_call(
+        kernel,
+        out_shape=shape_of((rows, tokens + 4 * rows, BLK)),
+        compiler_params=params(),
+    )(x_own, *gains)
 
 
 def right_stage(x_chan, gain_local, right, mine, groups, shared=None):
@@ -110,9 +104,11 @@
     def kernel(mine_ref, own_ref, other_ref, x_ref, gain_ref, *refs):
         out_ref = refs[-1]
         if shared is not None:
-            squares = refs[0][0, :rows]
-            for z in range(1, shared.shape[0]):
-                squares = squares + refs[0][z, :rows]
+            squares = jnp.zeros((rows, tokens), F32)
+            for z in range(shared.shape[0]):
+                planes = refs[0][z, tokens:].astype(F32)
+                for part in range(3):
+                    squares = squares + planes[part * rows : (part + 1) * rows]
         for p in range(rows):
             if shared is None:
                 extra = x_ref[p, tokens : tokens + EXTRA].astype(F32)
@@ -216,26 +212,20 @@
         store(n, (x.astype(F32) * scale * gain_ref[n]).astype(BF16))
 
 
-def token_stage(received, gain, tensor_index):
-    n_blk = len(received)
-    tokens = received[0].shape[0]
-
-    def kernel(z_ref, gain_ref, *refs):
-        x_ref, normed_ref = refs[n_blk:]
-        for d in range(n_blk):
-            x_ref[(z_ref[0] + n_blk - d) % n_blk] = refs[d][...]
-
+def token_stage(x_tok, gain, tokens):
+    n_blk = x_tok.shape[0]
+
+    def kernel(gain_ref, x_ref, normed_ref):
         def store(n, value):
             normed_ref[:, n * BLK : (n + 1) * BLK] = value
 
-        normalize([x_ref[n] for n in range(n_blk)], gain_ref, tokens, store)
-
-    return pl.pallas_call(
-        kernel,
-        in_specs=[scalar_spec(), whole(gain.shape)] + [whole((tokens, BLK))] * n_blk,
-        out_shape=(shape_of((n_blk, tokens, BLK)), shape_of((tokens, D))),
-        compiler_params=params(),
-    )(tensor_index, gain, *received)
+        normalize([x_ref[n, :tokens] for n in range(n_blk)], gain_ref, tokens, store)
+
+    return pl.pallas_call(
+        kernel,
+        out_shape=shape_of((tokens, D)),
+        compiler_params=params(),
+    )(gain, x_tok)
 
 
 def gate_stage(normed, first, second, mine, n_blk):
@@ -447,9 +437,6 @@
         route = [(i, i - i % y_count + (i + distance) % y_count) for i in range(seq_count)]
         return lax.ppermute(block, "seq", route)
 
-    def along_z(block, distance):
-        return lax.ppermute(block, "tensor", [(i, (i + distance) % n_blk) for i in range(n_blk)])
-
     def along_x(block, distance):
         route = [(i, (i + distance * y_count) % seq_count) for i in range(seq_count)]
         return lax.ppermute(block, "seq", route)
@@ -465,15 +452,29 @@
     gain_other = lax.ppermute(norm_gain, "section", swap)
     gain_local = [jnp.where(section == b, norm_gain, gain_other) for b in range(2)]
 
-    shared, *sends = split_stage(x_own, gain_local, z_scalar)
-    shared, right_own, left_own = tie((shared, right_blocks[0], left_blocks[0]))
-    right = with_other(right_own)
-    near = [1, 2, n_blk - 2, n_blk - 1]
-    received = [sends[0]] + [None] * (n_blk - 1)
-    for d in near:
-        received[d] = along_z(sends[d], d)
-    shared = gather_by_exchange(shared, "tensor")
-    gains = [shared[:, rows_dev + b][:, None] for b in range(2)]
+    packed = pack_stage(x_own, gain_local)
+    packed, right_own, left_own, gate_own, out_own, gate_sec, out_sec, head_own = tie(
+        (
+            packed,
+            right_blocks[0],
+            left_blocks[0],
+            gate_first[0],
+            out_first[0],
+            gate_second,
+            out_second,
+            head[0],
+        )
+    )
+    right, left, gate_first_pair, out_first_pair = (
+        with_other(w) for w in (right_own, left_own, gate_own, out_own)
+    )
+    gate_second_pair, out_second_pair = (with_other(rows_second(w)) for w in (gate_sec, out_sec))
+    left, head_own = tie((left, head_own))
+    near_heads = [along_y(head_own, d) for d in (1, 3)]
+    x_tok = lax.all_to_all(packed, "tensor", split_axis=0, concat_axis=0, tiled=True)
+    gain_rows = x_tok[:, tokens + 3 * rows_dev :][:, :6].astype(F32)
+    gain_rows = jnp.sum(gain_rows.reshape(n_blk, 2, 3, BLK), axis=2)
+    gains = [gain_rows[:, b : b + 1] for b in range(2)]
 
     def exchange_seq(mix):
         return lax.all_to_all(mix, "seq", split_axis=0, concat_axis=0, tiled=True)
@@ -486,31 +487,21 @@
         out = lax.all_to_all(cols, everyone, split_axis=0, concat_axis=0, tiled=True)
         return out.reshape(seq_count, n_blk, j_dev, BLK)
 
-    mix = right_stage(x_own, gain_local[0], right, mine[0], seq_count, shared=shared)
-    mix, left_own, sends, near_blocks = tie((mix, left_own, sends, [received[d] for d in near]))
-    for d, block in zip(near, near_blocks):
-        received[d] = block
+    mix = right_stage(x_own, gain_local[0], right, mine[0], seq_count, shared=x_tok)
+    mix, near_heads, left, gate_first_pair, out_first_pair, gate_second_pair, out_second_pair = tie(
+        (mix, near_heads, left, gate_first_pair, out_first_pair, gate_second_pair, out_second_pair)
+    )
     cols = exchange_seq(mix)
-    left = with_other(left_own)
-    for d in range(3, n_blk - 2):
-        received[d] = along_z(sends[d], d)
-
-    cols = mix_left(cols, 0)
-    cols, received, head_own, *own = tie(
-        (cols, received, head[0], gate_first[0], out_first[0], gate_second, out_second)
-    )
-    seq_out = exchange_all(cols)
-    gate_first_pair, out_first_pair = (with_other(w) for w in own[:2])
-    gate_second_pair, out_second_pair = (with_other(rows_second(w)) for w in own[2:])
-    near_heads = [along_y(head_own, d) for d in (1, 3)]
-    x_tok, normed = token_stage(received, gains[0], z_scalar)
+
+    seq_out = exchange_all(mix_left(cols, 0))
+    normed = token_stage(x_tok, gains[0], tokens)
     gate = gate_stage(normed, gate_first_pair, gate_second_pair, mine[0], n_blk)
     rows_one, packed, normed = out_stage(
         seq_out, gate, x_tok, out_first_pair, out_second_pair, mine[0], gain=gains[1]
     )
 
-    packed, normed, head_own, near_heads, gate_first_pair, out_first_pair = tie(
-        (packed, normed, head_own, near_heads, gate_first_pair, out_first_pair)
+    packed, normed, head_own, gate_first_pair, out_first_pair = tie(
+        (packed, normed, head_own, gate_first_pair, out_first_pair)
     )
     far_head = along_y(head_own, 2)
     chan_one = lax.all_to_all(packed, "tensor", split_axis=0, concat_axis=0, tiled=True)

time: 289 us -> 291 us (level)
  starting transfers between devices: 74.6 us -> 46 us
  blocking collectives: 67.3 us -> 90.5 us
  waiting for transfers between devices: 63.4 us -> 75.6 us
  local copies, waits for them, and re-layouts: 31.7 us -> 27.1 us
    all_to_all x1 -> x2, blocking collectives: 18.8 us -> 42.1 us  [exchange_seq(): return lax.all_to_all(mix, 'seq', split_axis=0, concat_axis=0, tiled=True)]
    all_to_all x1 -> x2, waiting for transfers between devices: 20.8 us -> 34.3 us  [body(): lax.all_to_all(packed, 'tensor', split_axis=0, concat_axis=0, tiled=True)]
    ppermute x7 -> x0, starting transfers between devices: 13.2 us -> none  [along_z(): lax.ppermute(block, 'tensor', [(i, (i + distance) % n_blk) for i in range...]
    unnamed x86 -> x66, local copies, waits for them, and re-layouts: 27.5 us -> 18.9 us
    all_to_all x1, waiting for transfers between devices: 9.02 us -> 17.6 us  [exchange_all(): lax.all_to_all(cols, everyone, split_axis=0, concat_axis=0, tiled=True)]
    all_to_all x1, starting transfers between devices: 15.1 us -> 7.5 us  [exchange_all(): lax.all_to_all(cols, everyone, split_axis=0, concat_axis=0, tiled=True)]
    all_to_all x1 -> x0, starting transfers between devices: 6.76 us -> none  [exchange_seq(): return lax.all_to_all(mix, 'seq', split_axis=0, concat_axis=0, tiled=True)]
    all_to_all x1 -> x2, starting transfers between devices: 3.56 us -> 10.1 us  [body(): lax.all_to_all(packed, 'tensor', split_axis=0, concat_axis=0, tiled=True)]
  transfers between devices with their start and end apart: 28 -> 20, of which waited for: 12 -> 9; matrix products, arithmetic and copies ran while one was open for 1% -> 3% of each run, Pallas kernels for 13% -> 9%
where the time goes in v11:
time: 291 us; the launch traced here: 287 us
  blocking collectives  90.5 us (31%)
  waiting for transfers between devices  75.6 us (26%)
  starting transfers between devices  46 us (16%)
  Pallas kernels  45.4 us (16%)
  local copies, waits for them, and re-layouts  27.1 us (9%)
    all_to_all x2, blocking collectives, exchange_seq(): return lax.all_to_all(mix, 'seq', split_axis=0, concat_axis=0, tiled=True)  42.1 us
    all_to_all x2, waiting for transfers between devices, body(): lax.all_to_all(packed, 'tensor', split_axis=0, concat_axis=0, tiled=True)  34.3 us
    all_to_all x1, blocking collectives, exchange_all(): lax.all_to_all(cols, everyone, split_axis=0, concat_axis=0, tiled=True)  33.8 us
    unnamed x66, local copies, waits for them, and re-layouts  18.9 us
    all_to_all x1, waiting for transfers between devices, exchange_all(): lax.all_to_all(cols, everyone, split_axis=0, concat_axis=0, tiled=True)  17.6 us
    pallas_call x2, Pallas kernels, out_stage(): pl.pallas_call(kernel, grid=(n_blk,), in_specs=in_specs, out_specs=[whole...  16.5 us
    all_to_all x1, blocking collectives, body(): lax.all_to_all(pair, ('section', 'tensor'), split_axis=0, concat_axis=0,...  14.7 us
    all_to_all x1, waiting for transfers between devices, body(): lax.all_to_all(result, 'tensor', split_axis=0, concat_axis=0, tiled=True)  14.5 us
  transfers between devices with their start and end apart: 20, of which 9 were waited for; matrix products, arithmetic and copies ran while one was open for 3% of the time, Pallas kernels for 9%

profile of v11, /device:TPU:1, one launch (start us, length us, event | category | flops | bytes accessed | tf_op | source)
XLA Modules:
  0.0 287.2 jit_solution(11100815444218761166)
XLA Ops:
  0.7 3.3 %collective-permute-start = (f32[1,256]{1,0:T(1,128)}, f32[1,256]{1,0:T(1,128)S(1)}, u32[]{:S(2)}, u32[]{:S(2)}) collective-permute-start(f32[1,256]{1,0:T(1,128)} %param.11), channel_id=1, source_target_pairs={{0,128},{128,0},{1,129},{129,1},{2,130},{130,2},{3,131},{131,3},{4... | collective-permute-start | bytes 3080 | tf_op jit(solution)/shard_map/ppermute | solution.py:452
  6.7 6.6 %all-to-all-start = ((bf16[8,288,256]{2,1,0:T(8,128)(2,1)}), bf16[8,288,256]{2,1,0:T(8,128)(2,1)S(1)}, u32[]{:S(2)}, u32[]{:S(2)}) async-start(bf16[8,288,256]{2,1,0:T(8,128)(2,1)} %copy-done.5), calls=%async_computation | async-start | bytes 2359296 | tf_op jit(solution)/shard_map/all_to_all | solution.py:474
  27.7 17.7 %all-to-all-done.refs_0_.x_ref = bf16[8,288,256]{2,1,0:T(8,128)(2,1)S(1)} async-done(((bf16[8,288,256]{2,1,0:T(8,128)(2,1)}), bf16[8,288,256]{2,1,0:T(8,128)(2,1)S(1)}, u32[]{:S(2)}, u32[]{:S(2)}) %all-to-all-start) | async-done | bytes 1179680 | tf_op jit(solution)/shard_map/all_to_all | solution.py:474
  47.8 1.8 shard_map.114
  49.7 22.6 %all_to_all.45 = bf16[16,8,16,256]{3,2,1,0:T(8,128)(2,1)S(1)} all-to-all(bf16[16,8,16,256]{3,2,1,0:T(8,128)(2,1)S(1)} %shard_map.114), channel_id=1, replica_groups=mesh['section'=2,'seq'=16,'tensor'=8] {'seq'}, dimensions={0} | all-to-all | bytes 2097152 | tf_op jit(solution)/shard_map/all_to_all | solution.py:480
  74.9 7.5 %all-to-all-start.2 = ((bf16[128,16,256]{2,1,0:T(8,128)(2,1)}), bf16[128,16,256]{2,1,0:T(8,128)(2,1)}, u32[]{:S(2)}, u32[]{:S(2)}) async-start(bf16[128,16,256]{2,1,0:T(8,128)(2,1)} %bitcast.44), calls=%async_computation.2 | async-start | bytes 2097152 | tf_op jit(solution)/shard_map/all_to_all | solution.py:487
  85.8 6.1 %shard_map.117.gate_ref = f32[8,256,256]{2,1,0:T(8,128)S(1)} custom-call(s32[1]{0:T(128)} %bitcast.10.mine_ref, bf16[32,64,64]{2,1,0:T(8,128)(2,1)S(1)} %bitcast.50, bf16[32,64,64]{2,1,0:T(8,128)(2,1)} %collective-permute-done.5.first_b, bf16[32,2048]{1,0:T(8,128)(2,1)S(1)} %reshape.76.second_a, bf16[32,2048]{1,0:T(8,128)(2,1)S(1)} %copy-done.25, ...), custom_call_target="tpu_custom_call" | custom-call | tf_op jit(solution)/shard_map/pallas_call | solution.py:245
  93.2 17.6 %all-to-all-done.2 = bf16[128,16,256]{2,1,0:T(8,128)(2,1)} async-done(((bf16[128,16,256]{2,1,0:T(8,128)(2,1)}), bf16[128,16,256]{2,1,0:T(8,128)(2,1)}, u32[]{:S(2)}, u32[]{:S(2)}) %all-to-all-start.2) | async-done | bytes 1048608 | tf_op jit(solution)/shard_map/all_to_all | solution.py:487
  111.8 8.9 %shard_map.118 = (bf16[2,2048]{1,0:T(2,128)(2,1)S(1)}, bf16[8,272,256]{2,1,0:T(8,128)(2,1)S(1)}, bf16[256,2048]{1,0:T(8,128)(2,1)S(1)}) custom-call(s32[1]{0:T(128)} %bitcast.10.mine_ref, bf16[32,64,64]{2,1,0:T(8,128)(2,1)S(1)} %bitcast.53, bf16[32,64,64]{2,1,0:T(8,128)(2,1)} %collective-permute-done.6.first_b, bf16[32,2048]{1,0:T(8,128)(2,1)S(1)} %reshape.77.second_a, ...), custom_call_target="tpu_custom_call" | custom-call | tf_op jit(solution)/shard_map/pallas_call | solution.py:311
  123.3 3.6 %all-to-all-start.3 = ((bf16[8,272,256]{2,1,0:T(8,128)(2,1)}), bf16[8,272,256]{2,1,0:T(8,128)(2,1)S(1)}, u32[]{:S(2)}, u32[]{:S(2)}) async-start(bf16[8,272,256]{2,1,0:T(8,128)(2,1)} %copy-done.6), calls=%async_computation.3 | async-start | bytes 2228224 | tf_op jit(solution)/shard_map/all_to_all | solution.py:507
  130.2 6.0 %shard_map.120.gate_ref = f32[8,256,256]{2,1,0:T(8,128)S(1)} custom-call(s32[1]{0:T(128)} %bitcast.26.mine_ref, bf16[32,64,64]{2,1,0:T(8,128)(2,1)S(1)} %bitcast.51, bf16[32,64,64]{2,1,0:T(8,128)(2,1)} %collective-permute-done.5.first_b, bf16[32,2048]{1,0:T(8,128)(2,1)S(1)} %reshape.76.second_a, bf16[32,2048]{1,0:T(8,128)(2,1)S(1)} %copy-done.26, ...), custom_call_target="tpu_custom_call" | custom-call | tf_op jit(solution)/shard_map/pallas_call | solution.py:245
  137.5 16.7 %all-to-all-done.3.x_ref.refs_0_ = bf16[8,272,256]{2,1,0:T(8,128)(2,1)S(1)} async-done(((bf16[8,272,256]{2,1,0:T(8,128)(2,1)}), bf16[8,272,256]{2,1,0:T(8,128)(2,1)S(1)}, u32[]{:S(2)}, u32[]{:S(2)}) %all-to-all-start.3) | async-done | bytes 1114144 | tf_op jit(solution)/shard_map/all_to_all | solution.py:507
  155.4 1.8 shard_map.119
  157.3 19.5 %all_to_all.46 = bf16[16,8,16,256]{3,2,1,0:T(8,128)(2,1)S(1)} all-to-all(bf16[16,8,16,256]{3,2,1,0:T(8,128)(2,1)S(1)} %shard_map.119), channel_id=1, replica_groups=mesh['section'=2,'seq'=16,'tensor'=8] {'seq'}, dimensions={0} | all-to-all | bytes 2097152 | tf_op jit(solution)/shard_map/all_to_all | solution.py:480
  178.4 33.8 %all_to_all.47 = bf16[128,16,256]{2,1,0:T(8,128)(2,1)S(1)} all-to-all(bf16[128,16,256]{2,1,0:T(8,128)(2,1)S(1)} %bitcast.46), channel_id=1, replica_groups=mesh['section'=2,'seq'=16,'tensor'=8] {'seq','tensor'}, dimensions={0} | all-to-all | bytes 2097152 | tf_op jit(solution)/shard_map/all_to_all | solution.py:487
  212.1 7.6 %shard_map.122 = (bf16[2,2048]{1,0:T(2,128)(2,1)S(1)}, bf16[8,256,256]{2,1,0:T(8,128)(2,1)S(1)}) custom-call(s32[1]{0:T(128)} %bitcast.26.mine_ref, bf16[32,64,64]{2,1,0:T(8,128)(2,1)S(1)} %bitcast.54, bf16[32,64,64]{2,1,0:T(8,128)(2,1)} %collective-permute-done.6.first_b, bf16[32,2048]{1,0:T(8,128)(2,1)S(1)} %reshape.77.second_a, ...), custom_call_target="tpu_custom_call" | custom-call | tf_op jit(solution)/shard_map/pallas_call | solution.py:311
  220.8 14.7 %all_to_all.48 = bf16[16,2,2048]{2,1,0:T(2,128)(2,1)S(1)} all-to-all(bf16[16,2,2048]{2,1,0:T(2,128)(2,1)S(1)} %bitcast.65), channel_id=1, replica_groups=mesh['section'=2,'seq'=16,'tensor'=8] {'section','tensor'}, dimensions={0} | all-to-all | bytes 262144 | tf_op jit(solution)/shard_map/all_to_all | solution.py:519
  235.5 4.6 %all-to-all-start.7 = ((bf16[8,256,256]{2,1,0:T(8,128)(2,1)}), bf16[8,256,256]{2,1,0:T(8,128)(2,1)}, u32[]{:S(2)}, u32[]{:S(2)}) async-start(bf16[8,256,256]{2,1,0:T(8,128)(2,1)} %copy-done.22), calls=%async_computation.7 | async-start | bytes 2097152 | tf_op jit(solution)/shard_map/all_to_all | solution.py:521
  243.1 4.8 %collective-permute-start.13 = (bf16[8,272,256]{2,1,0:T(8,128)(2,1)S(1)}, bf16[8,272,256]{2,1,0:T(8,128)(2,1)}, u32[]{:S(2)}, u32[]{:S(2)}) collective-permute-start(bf16[8,272,256]{2,1,0:T(8,128)(2,1)S(1)} %all-to-all-done.3.x_ref.refs_0_), channel_id=1, source_target_pairs={{128,0},{129,1},{130,2},{131,3},{132,4},{133,5},{134,6},{135,7},{1... | collective-permute-start | bytes 3342344 | tf_op jit(solution)/shard_map/ppermute | solution.py:539
  249.8 2.9 shard_map.123
  252.6 14.5 %all-to-all-done.7.refs_3_ = bf16[8,256,256]{2,1,0:T(8,128)(2,1)} async-done(((bf16[8,256,256]{2,1,0:T(8,128)(2,1)}), bf16[8,256,256]{2,1,0:T(8,128)(2,1)}, u32[]{:S(2)}, u32[]{:S(2)}) %all-to-all-start.7) | async-done | bytes 1048608 | tf_op jit(solution)/shard_map/all_to_all | solution.py:521
  269.2 6.2 %all-to-all-start.8 = ((f32[128,2,128]{2,1,0:T(2,128)}), f32[128,2,128]{2,1,0:T(2,128)S(1)}, u32[]{:S(2)}, u32[]{:S(2)}) async-start(f32[128,2,128]{2,1,0:T(2,128)} %broadcast_in_dim.5), calls=%async_computation.8 | async-start | bytes 262144 | tf_op jit(solution)/shard_map/all_to_all | solution.py:45
  275.3 6.0 %shard_map.124 = bf16[2,8,256,256]{3,2,1,0:T(8,128)(2,1)} custom-call(s32[1]{0:T(128)} %bitcast.32.section_ref, bf16[8,272,256]{2,1,0:T(8,128)(2,1)S(1)} %all-to-all-done.3.x_ref.refs_0_, bf16[8,272,256]{2,1,0:T(8,128)(2,1)} %collective-permute-done.13.refs_1_, bf16[8,256,256]{2,1,0:T(8,128)(2,1)} %collective-permute-done.14.refs_2_, ...), custom_call_target="tpu_custom_call" | custom-call | tf_op jit(solution)/shard_map/pallas_call | solution.py:395
  281.3 5.1 %all-to-all-done.8.parts_ref = f32[128,2,128]{2,1,0:T(2,128)S(1)} async-done(((f32[128,2,128]{2,1,0:T(2,128)}), f32[128,2,128]{2,1,0:T(2,128)S(1)}, u32[]{:S(2)}, u32[]{:S(2)}) %all-to-all-start.8) | async-done | bytes 131104 | tf_op jit(solution)/shard_map/all_to_all | solution.py:45
  (119 shorter events, 46.4 us)
Async XLA Ops:
  0.7 4.4 %collective-permute-start = (f32[1,256]{1,0:T(1,128)}, f32[1,256]{1,0:T(1,128)S(1)}, u32[]{:S(2)}, u32[]{:S(2)}) collective-permute-start(f32[1,256]{1,0:T(1,128)} %param.11), channel_id=1, source_target_pairs={{0,128},{128,0},{1,129},{129,1},{2,130},{130,2},{3,131},{131,3},{4... | collective-permute-start | bytes 3080 | tf_op jit(solution)/shard_map/ppermute | solution.py:452
  6.7 38.6 %all-to-all-start = ((bf16[8,288,256]{2,1,0:T(8,128)(2,1)}), bf16[8,288,256]{2,1,0:T(8,128)(2,1)S(1)}, u32[]{:S(2)}, u32[]{:S(2)}) async-start(bf16[8,288,256]{2,1,0:T(8,128)(2,1)} %copy-done.5), calls=%async_computation | async-start | bytes 2359296 | tf_op jit(solution)/shard_map/all_to_all | solution.py:474
  13.3 2.6 collective-permute-start.2
  14.2 13.3 %collective-permute-start.1 = (bf16[8,256,256]{2,1,0:T(8,128)(2,1)}, bf16[8,256,256]{2,1,0:T(8,128)(2,1)}, u32[]{:S(2)}, u32[]{:S(2)}) collective-permute-start(bf16[8,256,256]{2,1,0:T(8,128)(2,1)} %bitcast.41), channel_id=1, source_target_pairs={{0,128},{128,0},{1,129},{129,1},{2,130},{130,2},{3,131},{131,3},{4... | collective-permute-start | bytes 3145736 | tf_op jit(solution)/shard_map/ppermute | solution.py:434
  16.7 32.9 %collective-permute-start.3 = (bf16[2048,256]{1,0:T(8,128)(2,1)}, bf16[2048,256]{1,0:T(8,128)(2,1)}, u32[]{:S(2)}, u32[]{:S(2)}) collective-permute-start(bf16[2048,256]{1,0:T(8,128)(2,1)} %bitcast.58), channel_id=1, source_target_pairs={{0,8},{8,16},{16,24},{24,0},{32,40},{40,48},{48,56},{56,32},{64,72... | collective-permute-start | bytes 3145736 | tf_op jit(solution)/shard_map/ppermute | solution.py:438
  18.0 31.7 %collective-permute-start.4 = (bf16[2048,256]{1,0:T(8,128)(2,1)}, bf16[2048,256]{1,0:T(8,128)(2,1)}, u32[]{:S(2)}, u32[]{:S(2)}) collective-permute-start(bf16[2048,256]{1,0:T(8,128)(2,1)} %bitcast.59), channel_id=1, source_target_pairs={{0,24},{8,0},{16,8},{24,16},{32,56},{40,32},{48,40},{56,48},{64,88... | collective-permute-start | bytes 3145736 | tf_op jit(solution)/shard_map/ppermute | solution.py:438
  21.5 1.9 collective-permute-start.7
  22.4 27.2 %collective-permute-start.5 = (bf16[32,64,64]{2,1,0:T(8,128)(2,1)}, bf16[32,64,64]{2,1,0:T(8,128)(2,1)}, u32[]{:S(2)}, u32[]{:S(2)}) collective-permute-start(bf16[32,64,64]{2,1,0:T(8,128)(2,1)} %bitcast.49), channel_id=1, source_target_pairs={{0,128},{128,0},{1,129},{129,1},{2,130},{130,2},{3,131},{131,3},{4... | collective-permute-start | bytes 786440 | tf_op jit(solution)/shard_map/ppermute | solution.py:434
  24.1 25.6 %collective-permute-start.6 = (bf16[32,64,64]{2,1,0:T(8,128)(2,1)}, bf16[32,64,64]{2,1,0:T(8,128)(2,1)}, u32[]{:S(2)}, u32[]{:S(2)}) collective-permute-start(bf16[32,64,64]{2,1,0:T(8,128)(2,1)} %bitcast.52), channel_id=1, source_target_pairs={{0,128},{128,0},{1,129},{129,1},{2,130},{130,2},{3,131},{131,3},{4... | collective-permute-start | bytes 786440 | tf_op jit(solution)/shard_map/ppermute | solution.py:434
  27.4 22.2 %collective-permute-start.8 = (bf16[32,2048]{1,0:T(8,128)(2,1)S(1)}, bf16[32,2048]{1,0:T(8,128)(2,1)}, u32[]{:S(2)}, u32[]{:S(2)}) collective-permute-start(bf16[32,2048]{1,0:T(8,128)(2,1)S(1)} %reshape.77.second_a), channel_id=1, source_target_pairs={{0,128},{128,0},{1,129},{129,1},{2,130},{130,2},{3,131},{131,3},{4... | collective-permute-start | bytes 393224 | tf_op jit(solution)/shard_map/ppermute | solution.py:434
  49.6 22.7 %copy-start.15 = (bf16[1,16,128,128]{3,2,1,0:T(8,128)(2,1)S(1)}, bf16[1,16,128,128]{3,2,1,0:T(8,128)(2,1)}, u32[]{:S(2)}) copy-start(bf16[1,16,128,128]{3,2,1,0:T(8,128)(2,1)} %param.13) | copy-start | bytes 1572868
  49.6 22.6 %copy-start.18 = (bf16[16,128,128]{2,1,0:T(8,128)(2,1)S(1)}, bf16[16,128,128]{2,1,0:T(8,128)(2,1)}, u32[]{:S(2)}) copy-start(bf16[16,128,128]{2,1,0:T(8,128)(2,1)} %copy-done.17) | copy-start | bytes 1572868
  74.9 35.9 %all-to-all-start.2 = ((bf16[128,16,256]{2,1,0:T(8,128)(2,1)}), bf16[128,16,256]{2,1,0:T(8,128)(2,1)}, u32[]{:S(2)}, u32[]{:S(2)}) async-start(bf16[128,16,256]{2,1,0:T(8,128)(2,1)} %bitcast.44), calls=%async_computation.2 | async-start | bytes 2097152 | tf_op jit(solution)/shard_map/all_to_all | solution.py:487
  123.3 30.8 %all-to-all-start.3 = ((bf16[8,272,256]{2,1,0:T(8,128)(2,1)}), bf16[8,272,256]{2,1,0:T(8,128)(2,1)S(1)}, u32[]{:S(2)}, u32[]{:S(2)}) async-start(bf16[8,272,256]{2,1,0:T(8,128)(2,1)} %copy-done.6), calls=%async_computation.3 | async-start | bytes 2228224 | tf_op jit(solution)/shard_map/all_to_all | solution.py:507
  126.9 30.4 %collective-permute-start.9 = (bf16[2048,256]{1,0:T(8,128)(2,1)}, bf16[2048,256]{1,0:T(8,128)(2,1)}, u32[]{:S(2)}, u32[]{:S(2)}) collective-permute-start(bf16[2048,256]{1,0:T(8,128)(2,1)} %bitcast.60), channel_id=1, source_target_pairs={{0,16},{8,24},{16,0},{24,8},{32,48},{40,56},{48,32},{56,40},{64,80... | collective-permute-start | bytes 3145736 | tf_op jit(solution)/shard_map/ppermute | solution.py:438
  178.3 33.8 %copy-start.7 = (bf16[8,272,256]{2,1,0:T(8,128)(2,1)S(1)}, bf16[8,272,256]{2,1,0:T(8,128)(2,1)}, u32[]{:S(2)}) copy-start(bf16[8,272,256]{2,1,0:T(8,128)(2,1)} %copy-done.6) | copy-start | bytes 3342340
  178.3 33.8 %copy-start.14 = (bf16[1,32,64,64]{3,2,1,0:T(8,128)(2,1)S(1)}, bf16[1,32,64,64]{3,2,1,0:T(8,128)(2,1)}, u32[]{:S(2)}) copy-start(bf16[1,32,64,64]{3,2,1,0:T(8,128)(2,1)} %param.16) | copy-start | bytes 786436
  235.5 31.6 %all-to-all-start.7 = ((bf16[8,256,256]{2,1,0:T(8,128)(2,1)}), bf16[8,256,256]{2,1,0:T(8,128)(2,1)}, u32[]{:S(2)}, u32[]{:S(2)}) async-start(bf16[8,256,256]{2,1,0:T(8,128)(2,1)} %copy-done.22), calls=%async_computation.7 | async-start | bytes 2097152 | tf_op jit(solution)/shard_map/all_to_all | solution.py:521
  240.2 7.9 %collective-permute-start.10 = (bf16[32,2048]{1,0:T(8,128)(2,1)S(1)}, bf16[32,2048]{1,0:T(8,128)(2,1)S(1)}, u32[]{:S(2)}, u32[]{:S(2)}) collective-permute-start(bf16[32,2048]{1,0:T(8,128)(2,1)S(1)} %reshape.89.refs_0_), channel_id=1, source_target_pairs={{0,32},{8,40},{16,48},{24,56},{32,64},{40,72},{48,80},{56,88},{64,... | collective-permute-start | bytes 393224 | tf_op jit(solution)/shard_map/ppermute | solution.py:442
  240.3 7.8 %collective-permute-start.11 = (bf16[32,2048]{1,0:T(8,128)(2,1)S(1)}, bf16[32,2048]{1,0:T(8,128)(2,1)}, u32[]{:S(2)}, u32[]{:S(2)}) collective-permute-start(bf16[32,2048]{1,0:T(8,128)(2,1)S(1)} %reshape.89.refs_0_), channel_id=1, source_target_pairs={{0,64},{8,72},{16,80},{24,88},{32,96},{40,104},{48,112},{56,120},{... | collective-permute-start | bytes 393224 | tf_op jit(solution)/shard_map/ppermute | solution.py:442
  241.8 6.7 %collective-permute-start.12 = (bf16[32,2048]{1,0:T(8,128)(2,1)S(1)}, bf16[32,2048]{1,0:T(8,128)(2,1)}, u32[]{:S(2)}, u32[]{:S(2)}) collective-permute-start(bf16[32,2048]{1,0:T(8,128)(2,1)S(1)} %reshape.89.refs_0_), channel_id=1, source_target_pairs={{0,96},{8,104},{16,112},{24,120},{32,0},{40,8},{48,16},{56,24},{64... | collective-permute-start | bytes 393224 | tf_op jit(solution)/shard_map/ppermute | solution.py:442
  243.1 32.3 %collective-permute-start.13 = (bf16[8,272,256]{2,1,0:T(8,128)(2,1)S(1)}, bf16[8,272,256]{2,1,0:T(8,128)(2,1)}, u32[]{:S(2)}, u32[]{:S(2)}) collective-permute-start(bf16[8,272,256]{2,1,0:T(8,128)(2,1)S(1)} %all-to-all-done.3.x_ref.refs_0_), channel_id=1, source_target_pairs={{128,0},{129,1},{130,2},{131,3},{132,4},{133,5},{134,6},{135,7},{1... | collective-permute-start | bytes 3342344 | tf_op jit(solution)/shard_map/ppermute | solution.py:539
  267.2 8.2 %collective-permute-start.14 = (bf16[8,256,256]{2,1,0:T(8,128)(2,1)}, bf16[8,256,256]{2,1,0:T(8,128)(2,1)}, u32[]{:S(2)}, u32[]{:S(2)}) collective-permute-start(bf16[8,256,256]{2,1,0:T(8,128)(2,1)} %all-to-all-done.7.refs_3_), channel_id=1, source_target_pairs={{0,128},{1,129},{2,130},{3,131},{4,132},{5,133},{6,134},{7,135},{8... | collective-permute-start | bytes 3145736 | tf_op jit(solution)/shard_map/ppermute | solution.py:540
  269.2 17.3 %all-to-all-start.8 = ((f32[128,2,128]{2,1,0:T(2,128)}), f32[128,2,128]{2,1,0:T(2,128)S(1)}, u32[]{:S(2)}, u32[]{:S(2)}) async-start(f32[128,2,128]{2,1,0:T(2,128)} %broadcast_in_dim.5), calls=%async_computation.8 | async-start | bytes 262144 | tf_op jit(solution)/shard_map/all_to_all | solution.py:45
  (28 other events, 99.8 us)

commit v12 on v7

--- a/solution.py
+++ b/solution.py
@@ -227,17 +227,14 @@
     )(normed, gate_map)
 
 
-def out_stage(seq_out, gate, x_tok, out_map, gain=None):
+def out_stage(seq_out, gate, x_tok, out_map, with_squares):
     groups, n_blk, width, _ = seq_out.shape
     tokens = groups * width
-    height = tokens + (0 if gain is None else EXTRA)
+    height = tokens + (EXTRA if with_squares else 0)
 
     def kernel(seq_ref, gate_ref, x_ref, map_ref, *refs):
         n = pl.program_id(0)
-        if gain is None:
-            rows_ref, res_ref, gated_ref = refs
-        else:
-            gain_ref, rows_ref, res_ref, normed_ref, gated_ref = refs
+        rows_ref, res_ref, gated_ref = refs
 
         @pl.when(n == 0)
         def _():
@@ -256,13 +253,8 @@
                     rows_ref[q : q + 1, z * BLK : (z + 1) * BLK] = blocks[z][
                         q * STRIDE : q * STRIDE + 1
                     ]
-            if gain is None:
+            if not with_squares:
                 return
-
-            def store(z, value):
-                normed_ref[:, z * BLK : (z + 1) * BLK] = value
-
-            normalize(blocks, gain_ref, tokens, store)
             total = squares_by_lane(blocks)
             total = jnp.concatenate([total, total], axis=0)
             high, mid, low = split3(total)
@@ -280,10 +272,6 @@
     ]
     operands = [seq_out, gate, x_tok, out_map]
     out_shape = [shape_of((tokens // STRIDE, D)), shape_of((n_blk, height, BLK))]
-    if gain is not None:
-        operands.append(gain)
-        in_specs.append(whole(gain.shape))
-        out_shape.append(shape_of((tokens, D)))
     return pl.pallas_call(
         kernel,
         grid=(n_blk,),
@@ -473,19 +461,20 @@
     normed = token_stage(x_tok, gains[0], tokens)
     gate = gate_stage(normed, channel_map(gate_firsts[0], gate_seconds[0], n_blk))
     out_map = channel_map(out_firsts[0], out_seconds[0], n_blk)
-    rows_one, packed, normed = out_stage(seq_out, gate, x_tok, out_map, gain=gains[1])
-
-    packed, normed, heads[0], gate_two, out_two, gate_sec, out_sec = tie(
-        (packed, normed, heads[0], gate_firsts[1], out_firsts[1], gate_seconds[1], out_seconds[1])
+    rows_one, packed = out_stage(seq_out, gate, x_tok, out_map, True)
+
+    packed, heads[0], gate_two, out_two, gate_sec, out_sec = tie(
+        (packed, heads[0], gate_firsts[1], out_firsts[1], gate_seconds[1], out_seconds[1])
     )
     heads[2] = along_y(heads[0], 2)
     chan_one = lax.all_to_all(packed, "tensor", split_axis=0, concat_axis=0, tiled=True)
+    normed = token_stage(packed, gains[1], tokens)
     gate = gate_stage(normed, channel_map(gate_two, gate_sec, n_blk))
     out_map = channel_map(out_two, out_sec, n_blk)
     mix = right_stage(chan_one, gain_local[1], rights[1], seq_count)
     mix, gate, out_map, heads[2] = tie((mix, gate, out_map, heads[2]))
     seq_out = exchange_all(mix_left(exchange_seq(mix), 1))
-    rows_two, result = out_stage(seq_out, gate, packed, out_map)
+    rows_two, result = out_stage(seq_out, gate, packed, out_map, False)
 
     pair = jnp.stack([rows_one, rows_two])[:, None]
     pair = jnp.broadcast_to(pair, (2, n_blk) + rows_two.shape).reshape((-1,) + rows_two.shape)
@@ -506,8 +495,9 @@
         source = x_index * y_count + (y_index + y_count - d) % y_count
         places.append((source * n_blk + z_scalar[0]) * vocab_dev)
     parts = score_stage(row_sets, heads, labels, jnp.stack(places))
+    parts = jnp.broadcast_to(parts[None], (p_count,) + parts.shape)
     parts, chan_two = tie((parts, chan_two))
-    sums = gather_by_exchange(parts, everyone)
+    sums = lax.all_to_all(parts, everyone, split_axis=0, concat_axis=0, tiled=True)
 
     got_one = lax.ppermute(chan_one, "section", [(1, 0)])
     got_two = lax.ppermute(chan_two, "section", [(0, 1)])

time: 284 us -> 286 us (level)
  local copies, waits for them, and re-layouts: 17.7 us -> 22.5 us
    unnamed x66 -> x70, local copies, waits for them, and re-layouts: 14.2 us -> 18 us
  transfers between devices with their start and end apart: 20 -> 20, of which waited for: 6 -> 5; matrix products, arithmetic and copies ran while one was open for 5% -> 5% of each run, Pallas kernels for 18% -> 18%
where the time goes in v12:
time: 286 us; the launch traced here: 283 us
  blocking collectives  87.3 us (31%)
  Pallas kernels  70 us (24%)
  starting transfers between devices  48 us (17%)
  waiting for transfers between devices  44 us (15%)
  local copies, waits for them, and re-layouts  22.5 us (8%)
  other arithmetic  10.3 us (4%)
    all_to_all x2, blocking collectives, exchange_seq(): return lax.all_to_all(mix, 'seq', split_axis=0, concat_axis=0, tiled=True)  38.9 us
    all_to_all x1, blocking collectives, exchange_all(): lax.all_to_all(cols, everyone, split_axis=0, concat_axis=0, tiled=True)  30.8 us
    pallas_call x4, Pallas kernels, channel_map(): pl.pallas_call(kernel, grid=(n_blk,), in_specs=[whole((C1, C2, C2)), pl.B...  24.5 us
    all_to_all x2, waiting for transfers between devices, body(): lax.all_to_all(packed, 'tensor', split_axis=0, concat_axis=0, tiled=True)  21.4 us
    unnamed x70, local copies, waits for them, and re-layouts  18 us
    all_to_all x1, blocking collectives, body(): lax.all_to_all(pair, ('section', 'tensor'), split_axis=0, concat_axis=0,...  17.6 us
    pallas_call x2, Pallas kernels, out_stage(): pl.pallas_call(kernel, grid=(n_blk,), in_specs=in_specs, out_specs=[whole...  16.2 us
    pallas_call x2, Pallas kernels, gate_stage(): pl.pallas_call(kernel, grid=(n_blk,), in_specs=[whole(normed.shape), pl.B...  15 us
  transfers between devices with their start and end apart: 20, of which 5 were waited for; matrix products, arithmetic and copies ran while one was open for 5% of the time, Pallas kernels for 18%

profile of v12, /device:TPU:1, one launch (start us, length us, event | category | flops | bytes accessed | tf_op | source)
XLA Modules:
  0.0 283.2 jit_solution(3436251618287845655)
XLA Ops:
  0.7 3.3 %collective-permute-start = (f32[1,256]{1,0:T(1,128)}, f32[1,256]{1,0:T(1,128)S(1)}, u32[]{:S(2)}, u32[]{:S(2)}) collective-permute-start(f32[1,256]{1,0:T(1,128)} %param.11), channel_id=1, source_target_pairs={{0,128},{128,0},{1,129},{129,1},{2,130},{130,2},{3,131},{131,3},{4... | collective-permute-start | bytes 3080 | tf_op jit(solution)/shard_map/ppermute | solution.py:396
  10.4 6.5 %all-to-all-start = ((bf16[8,288,256]{2,1,0:T(8,128)(2,1)}), bf16[8,288,256]{2,1,0:T(8,128)(2,1)S(1)}, u32[]{:S(2)}, u32[]{:S(2)}) async-start(bf16[8,288,256]{2,1,0:T(8,128)(2,1)} %copy-done.10), calls=%async_computation | async-start | bytes 2359296 | tf_op jit(solution)/shard_map/all_to_all | solution.py:434
  32.9 16.1 %all-to-all-done.refs_0_.x_ref = bf16[8,288,256]{2,1,0:T(8,128)(2,1)S(1)} async-done(((bf16[8,288,256]{2,1,0:T(8,128)(2,1)}), bf16[8,288,256]{2,1,0:T(8,128)(2,1)S(1)}, u32[]{:S(2)}, u32[]{:S(2)}) %all-to-all-start) | async-done | bytes 1179680 | tf_op jit(solution)/shard_map/all_to_all | solution.py:434
  50.7 22.4 %all_to_all.45 = bf16[16,8,16,256]{3,2,1,0:T(8,128)(2,1)S(1)} all-to-all(bf16[16,8,16,256]{3,2,1,0:T(8,128)(2,1)S(1)} %shard_map.114), channel_id=1, replica_groups=mesh['section'=2,'seq'=16,'tensor'=8] {'seq'}, dimensions={0} | all-to-all | bytes 2097152 | tf_op jit(solution)/shard_map/all_to_all | solution.py:440
  75.6 9.5 %all-to-all-start.2 = ((bf16[128,16,256]{2,1,0:T(8,128)(2,1)}), bf16[128,16,256]{2,1,0:T(8,128)(2,1)}, u32[]{:S(2)}, u32[]{:S(2)}) async-start(bf16[128,16,256]{2,1,0:T(8,128)(2,1)} %bitcast.40), calls=%async_computation.2 | async-start | bytes 2097152 | tf_op jit(solution)/shard_map/all_to_all | solution.py:447
  85.8 6.2 %shard_map.117.map_ref = bf16[8,2048,256]{2,1,0:T(8,128)(2,1)} custom-call(bf16[32,64,64]{2,1,0:T(8,128)(2,1)S(1)} %copy-done.17, bf16[32,2048]{1,0:T(8,128)(2,1)S(1)} %get-tuple-element.78.second_ref), custom_call_target="tpu_custom_call" | custom-call | tf_op jit(solution)/shard_map/pallas_call | solution.py:175
  92.0 7.5 %shard_map.118.gate_ref = f32[8,256,256]{2,1,0:T(8,128)S(1)} custom-call(bf16[256,2048]{1,0:T(8,128)(2,1)S(1)} %shard_map.116.normed_ref, bf16[8,2048,256]{2,1,0:T(8,128)(2,1)} %shard_map.117.map_ref), custom_call_target="tpu_custom_call" | custom-call | tf_op jit(solution)/shard_map/pallas_call | solution.py:220
  100.8 6.1 %shard_map.119.map_ref = bf16[8,2048,256]{2,1,0:T(8,128)(2,1)} custom-call(bf16[32,64,64]{2,1,0:T(8,128)(2,1)S(1)} %copy-done.18, bf16[32,2048]{1,0:T(8,128)(2,1)S(1)} %get-tuple-element.80.second_ref), custom_call_target="tpu_custom_call" | custom-call | tf_op jit(solution)/shard_map/pallas_call | solution.py:175
  106.9 6.3 %all-to-all-done.2 = bf16[128,16,256]{2,1,0:T(8,128)(2,1)} async-done(((bf16[128,16,256]{2,1,0:T(8,128)(2,1)}), bf16[128,16,256]{2,1,0:T(8,128)(2,1)}, u32[]{:S(2)}, u32[]{:S(2)}) %all-to-all-start.2) | async-done | bytes 1048608 | tf_op jit(solution)/shard_map/all_to_all | solution.py:447
  114.8 8.6 %shard_map.120 = (bf16[2,2048]{1,0:T(2,128)(2,1)S(1)}, bf16[8,272,256]{2,1,0:T(8,128)(2,1)S(1)}) custom-call(bf16[16,8,16,256]{3,2,1,0:T(8,128)(2,1)} %bitcast.22.seq_ref, f32[8,256,256]{2,1,0:T(8,128)S(1)} %copy-done.7, bf16[8,288,256]{2,1,0:T(8,128)(2,1)S(1)} %all-to-all-done.refs_0_.x_ref, bf16[8,2048,256]{2,1,0:T(8,128)(2,1)} %shard_map.119.map_ref), custom_call_target="tpu_custom_call" | custom-call | tf_op jit(solution)/shard_map/pallas_call | solution.py:275
  124.4 3.7 %all-to-all-start.3 = ((bf16[8,272,256]{2,1,0:T(8,128)(2,1)}), bf16[8,272,256]{2,1,0:T(8,128)(2,1)S(1)}, u32[]{:S(2)}, u32[]{:S(2)}) async-start(bf16[8,272,256]{2,1,0:T(8,128)(2,1)} %copy-done.2), calls=%async_computation.3 | async-start | bytes 2228224 | tf_op jit(solution)/shard_map/all_to_all | solution.py:470
  128.8 6.2 %shard_map.123.map_ref = bf16[8,2048,256]{2,1,0:T(8,128)(2,1)} custom-call(bf16[32,64,64]{2,1,0:T(8,128)(2,1)S(1)} %copy-done.15, bf16[32,2048]{1,0:T(8,128)(2,1)S(1)} %get-tuple-element.90.second_ref), custom_call_target="tpu_custom_call" | custom-call | tf_op jit(solution)/shard_map/pallas_call | solution.py:175
  134.9 7.5 %shard_map.124.gate_ref = f32[8,256,256]{2,1,0:T(8,128)S(1)} custom-call(bf16[256,2048]{1,0:T(8,128)(2,1)S(1)} %shard_map.122.normed_ref, bf16[8,2048,256]{2,1,0:T(8,128)(2,1)} %shard_map.123.map_ref), custom_call_target="tpu_custom_call" | custom-call | tf_op jit(solution)/shard_map/pallas_call | solution.py:220
  143.7 6.1 %shard_map.125.map_ref = bf16[8,2048,256]{2,1,0:T(8,128)(2,1)} custom-call(bf16[32,64,64]{2,1,0:T(8,128)(2,1)S(1)} %copy-done.16, bf16[32,2048]{1,0:T(8,128)(2,1)S(1)} %get-tuple-element.92.second_ref), custom_call_target="tpu_custom_call" | custom-call | tf_op jit(solution)/shard_map/pallas_call | solution.py:175
  149.9 5.3 %all-to-all-done.3.x_ref.refs_0_ = bf16[8,272,256]{2,1,0:T(8,128)(2,1)S(1)} async-done(((bf16[8,272,256]{2,1,0:T(8,128)(2,1)}), bf16[8,272,256]{2,1,0:T(8,128)(2,1)S(1)}, u32[]{:S(2)}, u32[]{:S(2)}) %all-to-all-start.3) | async-done | bytes 1114144 | tf_op jit(solution)/shard_map/all_to_all | solution.py:470
  156.9 16.5 %all_to_all.46 = bf16[16,8,16,256]{3,2,1,0:T(8,128)(2,1)S(1)} all-to-all(bf16[16,8,16,256]{3,2,1,0:T(8,128)(2,1)S(1)} %shard_map.121), channel_id=1, replica_groups=mesh['section'=2,'seq'=16,'tensor'=8] {'seq'}, dimensions={0} | all-to-all | bytes 2097152 | tf_op jit(solution)/shard_map/all_to_all | solution.py:440
  174.9 30.8 %all_to_all.47 = bf16[128,16,256]{2,1,0:T(8,128)(2,1)S(1)} all-to-all(bf16[128,16,256]{2,1,0:T(8,128)(2,1)S(1)} %bitcast.43), channel_id=1, replica_groups=mesh['section'=2,'seq'=16,'tensor'=8] {'seq','tensor'}, dimensions={0} | all-to-all | bytes 2097152 | tf_op jit(solution)/shard_map/all_to_all | solution.py:447
  205.7 7.6 %shard_map.127 = (bf16[2,2048]{1,0:T(2,128)(2,1)S(1)}, bf16[8,256,256]{2,1,0:T(8,128)(2,1)S(1)}) custom-call(bf16[16,8,16,256]{3,2,1,0:T(8,128)(2,1)S(1)} %bitcast.39, f32[8,256,256]{2,1,0:T(8,128)S(1)} %copy-done.9, bf16[8,272,256]{2,1,0:T(8,128)(2,1)S(1)} %copy-done.4, bf16[8,2048,256]{2,1,0:T(8,128)(2,1)} %shard_map.125.map_ref), custom_call_target="tpu_custom_call" | custom-call | tf_op jit(solution)/shard_map/pallas_call | solution.py:275
  214.4 17.6 %all_to_all.48 = bf16[16,2,2048]{2,1,0:T(2,128)(2,1)S(1)} all-to-all(bf16[16,2,2048]{2,1,0:T(2,128)(2,1)S(1)} %bitcast.59), channel_id=1, replica_groups=mesh['section'=2,'seq'=16,'tensor'=8] {'section','tensor'}, dimensions={0} | all-to-all | bytes 262144 | tf_op jit(solution)/shard_map/all_to_all | solution.py:481
  231.9 4.2 %all-to-all-start.7 = ((bf16[8,256,256]{2,1,0:T(8,128)(2,1)}), bf16[8,256,256]{2,1,0:T(8,128)(2,1)}, u32[]{:S(2)}, u32[]{:S(2)}) async-start(bf16[8,256,256]{2,1,0:T(8,128)(2,1)} %copy-done.21), calls=%async_computation.7 | async-start | bytes 2097152 | tf_op jit(solution)/shard_map/all_to_all | solution.py:483
  239.1 4.8 %collective-permute-start.13 = (bf16[8,272,256]{2,1,0:T(8,128)(2,1)S(1)}, bf16[8,272,256]{2,1,0:T(8,128)(2,1)}, u32[]{:S(2)}, u32[]{:S(2)}) collective-permute-start(bf16[8,272,256]{2,1,0:T(8,128)(2,1)S(1)} %all-to-all-done.3.x_ref.refs_0_), channel_id=1, source_target_pairs={{128,0},{129,1},{130,2},{131,3},{132,4},{133,5},{134,6},{135,7},{1... | collective-permute-start | bytes 3342344 | tf_op jit(solution)/shard_map/ppermute | solution.py:502
  249.9 13.3 %all-to-all-done.7.refs_3_ = bf16[8,256,256]{2,1,0:T(8,128)(2,1)} async-done(((bf16[8,256,256]{2,1,0:T(8,128)(2,1)}), bf16[8,256,256]{2,1,0:T(8,128)(2,1)}, u32[]{:S(2)}, u32[]{:S(2)}) %all-to-all-start.7) | async-done | bytes 1048608 | tf_op jit(solution)/shard_map/all_to_all | solution.py:483
  265.2 6.2 %all-to-all-start.8 = ((f32[128,2,128]{2,1,0:T(2,128)}), f32[128,2,128]{2,1,0:T(2,128)S(1)}, u32[]{:S(2)}, u32[]{:S(2)}) async-start(f32[128,2,128]{2,1,0:T(2,128)} %broadcast_in_dim.5), calls=%async_computation.8 | async-start | bytes 262144 | tf_op jit(solution)/shard_map/all_to_all | solution.py:500
  273.7 5.7 %shard_map.129 = bf16[2,8,256,256]{3,2,1,0:T(8,128)(2,1)} custom-call(s32[1]{0:T(128)} %bitcast.30.section_ref, bf16[8,272,256]{2,1,0:T(8,128)(2,1)S(1)} %all-to-all-done.3.x_ref.refs_0_, bf16[8,272,256]{2,1,0:T(8,128)(2,1)} %collective-permute-done.13.refs_1_, bf16[8,256,256]{2,1,0:T(8,128)(2,1)S(1)} %copy-done.20, bf16[8,256,256]{2,1,0:T(8,128)(2,1)} %all-to-all-done.7.refs_3_), custom_call_target="tpu_custom_call" | custom-call | tf_op jit(solution)/shard_map/pallas_call | solution.py:359
  (134 shorter events, 54.2 us)
Async XLA Ops:
  0.7 4.4 %collective-permute-start = (f32[1,256]{1,0:T(1,128)}, f32[1,256]{1,0:T(1,128)S(1)}, u32[]{:S(2)}, u32[]{:S(2)}) collective-permute-start(f32[1,256]{1,0:T(1,128)} %param.11), channel_id=1, source_target_pairs={{0,128},{128,0},{1,129},{129,1},{2,130},{130,2},{3,131},{131,3},{4... | collective-permute-start | bytes 3080 | tf_op jit(solution)/shard_map/ppermute | solution.py:396
  8.4 10.4 %collective-permute-start.7 = (bf16[32,2048]{1,0:T(8,128)(2,1)S(1)}, bf16[32,2048]{1,0:T(8,128)(2,1)S(1)}, u32[]{:S(2)}, u32[]{:S(2)}) collective-permute-start(bf16[32,2048]{1,0:T(8,128)(2,1)S(1)} %reshape.64), channel_id=1, source_target_pairs={{0,128},{128,0},{1,129},{129,1},{2,130},{130,2},{3,131},{131,3},{4... | collective-permute-start | bytes 393224 | tf_op jit(solution)/shard_map/ppermute | solution.py:396
  9.9 10.8 %collective-permute-start.2 = (bf16[16,128,128]{2,1,0:T(8,128)(2,1)S(1)}, bf16[16,128,128]{2,1,0:T(8,128)(2,1)}, u32[]{:S(2)}, u32[]{:S(2)}) collective-permute-start(bf16[16,128,128]{2,1,0:T(8,128)(2,1)S(1)} %bitcast.54), channel_id=1, source_target_pairs={{0,128},{128,0},{1,129},{129,1},{2,130},{130,2},{3,131},{131,3},{4... | collective-permute-start | bytes 1572872 | tf_op jit(solution)/shard_map/ppermute | solution.py:396
  10.0 20.1 %collective-permute-start.1 = (bf16[8,256,256]{2,1,0:T(8,128)(2,1)}, bf16[8,256,256]{2,1,0:T(8,128)(2,1)}, u32[]{:S(2)}, u32[]{:S(2)}) collective-permute-start(bf16[8,256,256]{2,1,0:T(8,128)(2,1)} %bitcast.51), channel_id=1, source_target_pairs={{0,128},{128,0},{1,129},{129,1},{2,130},{130,2},{3,131},{131,3},{4... | collective-permute-start | bytes 3145736 | tf_op jit(solution)/shard_map/ppermute | solution.py:396
  10.4 38.5 %all-to-all-start = ((bf16[8,288,256]{2,1,0:T(8,128)(2,1)}), bf16[8,288,256]{2,1,0:T(8,128)(2,1)S(1)}, u32[]{:S(2)}, u32[]{:S(2)}) async-start(bf16[8,288,256]{2,1,0:T(8,128)(2,1)} %copy-done.10), calls=%async_computation | async-start | bytes 2359296 | tf_op jit(solution)/shard_map/all_to_all | solution.py:434
  16.9 8.8 %collective-permute-start.5 = (bf16[32,64,64]{2,1,0:T(8,128)(2,1)}, bf16[32,64,64]{2,1,0:T(8,128)(2,1)}, u32[]{:S(2)}, u32[]{:S(2)}) collective-permute-start(bf16[32,64,64]{2,1,0:T(8,128)(2,1)} %bitcast.55), channel_id=1, source_target_pairs={{0,128},{128,0},{1,129},{129,1},{2,130},{130,2},{3,131},{131,3},{4... | collective-permute-start | bytes 786440 | tf_op jit(solution)/shard_map/ppermute | solution.py:396
  17.3 10.7 %collective-permute-start.6 = (bf16[32,64,64]{2,1,0:T(8,128)(2,1)}, bf16[32,64,64]{2,1,0:T(8,128)(2,1)}, u32[]{:S(2)}, u32[]{:S(2)}) collective-permute-start(bf16[32,64,64]{2,1,0:T(8,128)(2,1)} %bitcast.57), channel_id=1, source_target_pairs={{0,128},{128,0},{1,129},{129,1},{2,130},{130,2},{3,131},{131,3},{4... | collective-permute-start | bytes 786440 | tf_op jit(solution)/shard_map/ppermute | solution.py:396
  19.4 4.8 %collective-permute-start.8 = (bf16[32,2048]{1,0:T(8,128)(2,1)S(1)}, bf16[32,2048]{1,0:T(8,128)(2,1)S(1)}, u32[]{:S(2)}, u32[]{:S(2)}) collective-permute-start(bf16[32,2048]{1,0:T(8,128)(2,1)S(1)} %reshape.65), channel_id=1, source_target_pairs={{0,128},{128,0},{1,129},{129,1},{2,130},{130,2},{3,131},{131,3},{4... | collective-permute-start | bytes 393224 | tf_op jit(solution)/shard_map/ppermute | solution.py:396
  22.9 27.8 %collective-permute-start.3 = (bf16[2048,256]{1,0:T(8,128)(2,1)}, bf16[2048,256]{1,0:T(8,128)(2,1)}, u32[]{:S(2)}, u32[]{:S(2)}) collective-permute-start(bf16[2048,256]{1,0:T(8,128)(2,1)} %bitcast.44), channel_id=1, source_target_pairs={{0,8},{8,16},{16,24},{24,0},{32,40},{40,48},{48,56},{56,32},{64,72... | collective-permute-start | bytes 3145736 | tf_op jit(solution)/shard_map/ppermute | solution.py:401
  24.2 26.5 %collective-permute-start.4 = (bf16[2048,256]{1,0:T(8,128)(2,1)}, bf16[2048,256]{1,0:T(8,128)(2,1)}, u32[]{:S(2)}, u32[]{:S(2)}) collective-permute-start(bf16[2048,256]{1,0:T(8,128)(2,1)} %bitcast.45), channel_id=1, source_target_pairs={{0,24},{8,0},{16,8},{24,16},{32,56},{40,32},{48,40},{56,48},{64,88... | collective-permute-start | bytes 3145736 | tf_op jit(solution)/shard_map/ppermute | solution.py:401
  75.6 37.6 %all-to-all-start.2 = ((bf16[128,16,256]{2,1,0:T(8,128)(2,1)}), bf16[128,16,256]{2,1,0:T(8,128)(2,1)}, u32[]{:S(2)}, u32[]{:S(2)}) async-start(bf16[128,16,256]{2,1,0:T(8,128)(2,1)} %bitcast.40), calls=%async_computation.2 | async-start | bytes 2097152 | tf_op jit(solution)/shard_map/all_to_all | solution.py:447
  124.4 30.7 %all-to-all-start.3 = ((bf16[8,272,256]{2,1,0:T(8,128)(2,1)}), bf16[8,272,256]{2,1,0:T(8,128)(2,1)S(1)}, u32[]{:S(2)}, u32[]{:S(2)}) async-start(bf16[8,272,256]{2,1,0:T(8,128)(2,1)} %copy-done.2), calls=%async_computation.3 | async-start | bytes 2228224 | tf_op jit(solution)/shard_map/all_to_all | solution.py:470
  128.1 28.7 %collective-permute-start.9 = (bf16[2048,256]{1,0:T(8,128)(2,1)}, bf16[2048,256]{1,0:T(8,128)(2,1)}, u32[]{:S(2)}, u32[]{:S(2)}) collective-permute-start(bf16[2048,256]{1,0:T(8,128)(2,1)} %bitcast.46), channel_id=1, source_target_pairs={{0,16},{8,24},{16,0},{24,8},{32,48},{40,56},{48,32},{56,40},{64,80... | collective-permute-start | bytes 3145736 | tf_op jit(solution)/shard_map/ppermute | solution.py:401
  173.3 32.3 %copy-start.4 = (bf16[8,272,256]{2,1,0:T(8,128)(2,1)S(1)}, bf16[8,272,256]{2,1,0:T(8,128)(2,1)}, u32[]{:S(2)}) copy-start(bf16[8,272,256]{2,1,0:T(8,128)(2,1)} %copy-done.2) | copy-start | bytes 3342340
  173.3 32.3 %copy-start.9 = (f32[8,256,256]{2,1,0:T(8,128)S(1)}, f32[8,256,256]{2,1,0:T(8,128)}, u32[]{:S(2)}) copy-start(f32[8,256,256]{2,1,0:T(8,128)} %copy-done.8) | copy-start | bytes 6291460
  214.3 24.7 %copy-start.32 = (s32[2,256]{1,0:T(2,128)S(1)}, s32[2,256]{1,0:T(2,128)}, u32[]{:S(2)}) copy-start(s32[2,256]{1,0:T(2,128)} %param.19) | copy-start | bytes 6148
  214.3 31.1 %copy-start.22 = (bf16[1,2048,256]{2,1,0:T(8,128)(2,1)S(1)}, bf16[1,2048,256]{2,1,0:T(8,128)(2,1)}, u32[]{:S(2)}) copy-start(bf16[1,2048,256]{2,1,0:T(8,128)(2,1)} %param.18) | copy-start | bytes 3145732
  231.9 31.3 %all-to-all-start.7 = ((bf16[8,256,256]{2,1,0:T(8,128)(2,1)}), bf16[8,256,256]{2,1,0:T(8,128)(2,1)}, u32[]{:S(2)}, u32[]{:S(2)}) async-start(bf16[8,256,256]{2,1,0:T(8,128)(2,1)} %copy-done.21), calls=%async_computation.7 | async-start | bytes 2097152 | tf_op jit(solution)/shard_map/all_to_all | solution.py:483
  236.2 7.8 %collective-permute-start.10 = (bf16[32,2048]{1,0:T(8,128)(2,1)S(1)}, bf16[32,2048]{1,0:T(8,128)(2,1)S(1)}, u32[]{:S(2)}, u32[]{:S(2)}) collective-permute-start(bf16[32,2048]{1,0:T(8,128)(2,1)S(1)} %reshape.75.refs_0_), channel_id=1, source_target_pairs={{0,32},{8,40},{16,48},{24,56},{32,64},{40,72},{48,80},{56,88},{64,... | collective-permute-start | bytes 393224 | tf_op jit(solution)/shard_map/ppermute | solution.py:405
  236.3 7.8 %collective-permute-start.11 = (bf16[32,2048]{1,0:T(8,128)(2,1)S(1)}, bf16[32,2048]{1,0:T(8,128)(2,1)S(1)}, u32[]{:S(2)}, u32[]{:S(2)}) collective-permute-start(bf16[32,2048]{1,0:T(8,128)(2,1)S(1)} %reshape.75.refs_0_), channel_id=1, source_target_pairs={{0,64},{8,72},{16,80},{24,88},{32,96},{40,104},{48,112},{56,120},{... | collective-permute-start | bytes 393224 | tf_op jit(solution)/shard_map/ppermute | solution.py:405
  237.9 6.9 %collective-permute-start.12 = (bf16[32,2048]{1,0:T(8,128)(2,1)S(1)}, bf16[32,2048]{1,0:T(8,128)(2,1)S(1)}, u32[]{:S(2)}, u32[]{:S(2)}) collective-permute-start(bf16[32,2048]{1,0:T(8,128)(2,1)S(1)} %reshape.75.refs_0_), channel_id=1, source_target_pairs={{0,96},{8,104},{16,112},{24,120},{32,0},{40,8},{48,16},{56,24},{64... | collective-permute-start | bytes 393224 | tf_op jit(solution)/shard_map/ppermute | solution.py:405
  239.1 32.3 %collective-permute-start.13 = (bf16[8,272,256]{2,1,0:T(8,128)(2,1)S(1)}, bf16[8,272,256]{2,1,0:T(8,128)(2,1)}, u32[]{:S(2)}, u32[]{:S(2)}) collective-permute-start(bf16[8,272,256]{2,1,0:T(8,128)(2,1)S(1)} %all-to-all-done.3.x_ref.refs_0_), channel_id=1, source_target_pairs={{128,0},{129,1},{130,2},{131,3},{132,4},{133,5},{134,6},{135,7},{1... | collective-permute-start | bytes 3342344 | tf_op jit(solution)/shard_map/ppermute | solution.py:502
  263.9 7.5 %collective-permute-start.14 = (bf16[8,256,256]{2,1,0:T(8,128)(2,1)}, bf16[8,256,256]{2,1,0:T(8,128)(2,1)S(1)}, u32[]{:S(2)}, u32[]{:S(2)}) collective-permute-start(bf16[8,256,256]{2,1,0:T(8,128)(2,1)} %all-to-all-done.7.refs_3_), channel_id=1, source_target_pairs={{0,128},{1,129},{2,130},{3,131},{4,132},{5,133},{6,134},{7,135},{8... | collective-permute-start | bytes 3145736 | tf_op jit(solution)/shard_map/ppermute | solution.py:503
  265.2 17.3 %all-to-all-start.8 = ((f32[128,2,128]{2,1,0:T(2,128)}), f32[128,2,128]{2,1,0:T(2,128)S(1)}, u32[]{:S(2)}, u32[]{:S(2)}) async-start(f32[128,2,128]{2,1,0:T(2,128)} %broadcast_in_dim.5), calls=%async_computation.8 | async-start | bytes 262144 | tf_op jit(solution)/shard_map/all_to_all | solution.py:500
  (30 other events, 111.3 us)
